TPU v7x, 32 devices: a whole 2x2x4 slice. The times are simulated.
32 devices in a mesh: seq: 32 (over z, y, x, core).
Axes of the slice: x: 2, y: 2, z: 4, core: 2. Of those that a mesh axis runs over, the one named last changes fastest.
Arguments:
- tokens: bfloat16 [8192, 1536], P('seq'), may hold values from -6 to 6
- segment_ids: int32 [8192], P('seq'), may hold values from 0 to 3, never falling along the last dimension, each value on 1 to 4096 neighbouring positions
- out_grad: bfloat16 [8192, 1536], P('seq'), may hold values from -6 to 6
- attn_master: float32 [7079424], P('seq'), as said below
- attn_first: float32 [7079424], P('seq'), as said below
- attn_second: float32 [7079424], P('seq'), as said below
- ffn_master: float32 [18875904], P('seq'), as said below
- ffn_first: float32 [18875904], P('seq'), as said below
- ffn_second: float32 [18875904], P('seq'), as said below
Outputs:
- result: bfloat16 [8192, 1536], P('seq')
- input_grad: float32 [8192, 1536], P('seq')
- attn_master_new: float32 [7079424], P('seq')
- attn_first_new: float32 [7079424], P('seq')
- attn_second_new: float32 [7079424], P('seq')
- ffn_master_new: float32 [18875904], P('seq')
- ffn_first_new: float32 [18875904], P('seq')
- ffn_second_new: float32 [18875904], P('seq')
Inputs may be any that keep to these rules, and one draw needn't show every extreme that they name: `segment_ids`: item numbers never fall along the pack; each item has 1 to 4096 tokens and one has exactly 4096. `attn_master`: gains near 1, weights of mean 0. `ffn_master`: gains near 1, weights of mean 0. `attn_first`: both signs, none zero. `attn_second`: positive. `ffn_first`: both signs, none zero. `ffn_second`: positive.
All inputs are finite; a program needn't handle non-finite values.
Results may differ from a plain program's by a relative error of at most 0.015.
The roundings to bfloat16 on the way count: a program that leaves them out, or rounds other values in their place, can miss the bound.
Values may be sent and summed in bfloat16 or wider, within the bound.
No kernel may reach another device: no remote copies, remote signals or barrier semaphores. Data moves between devices by JAX's collectives and lax.ppermute only.
A program may use at most 448 MiB of HBM per device.

v0:
```python
import math

import jax
import jax.numpy as jnp
from jax import lax
from jax.sharding import PartitionSpec as P

D = 1536
HEADS = 16
KV_HEADS = 8
HEAD_DIM = 96
FF = 4096
SEG_MOST = 4096
STEP = 7


ROPE_BASE = 100000.0
NORM_EPS = 1e-05
BETA_ONE = 0.5
BETA_TWO = 0.5
LEARN_RATE = 0.04
DECAY = 0.1
ADAM_EPS = 1e-08
NEG_LARGE = -1e30


def passed_along(value, axis, steps):
    count = lax.axis_size(axis)
    leading, last = (max(0, -steps), min(count, count - steps))
    return lax.ppermute(value, axis, [(source, source + steps) for source in range(leading, last)])


def rms_norm(values, norm_gain):
    factor = lax.rsqrt(jnp.mean(values * values, axis=-1, keepdims=True) + NORM_EPS)
    return values * factor * norm_gain


def rotation(positions, head_dim):
    half_dim = head_dim // 2
    frequency = jnp.exp(
        jnp.arange(half_dim).astype(jnp.float32) * (-2.0 * math.log(ROPE_BASE) / head_dim)
    )
    angles = positions.astype(jnp.float32)[:, None] * frequency[None, :]
    return (jnp.cos(angles)[:, None, :], jnp.sin(angles)[:, None, :])


def rotate(values, cosine, sine_part):
    half_dim = values.shape[-1] // 2
    lower_part = values[..., :half_dim]
    upper_part = values[..., half_dim:]
    return jnp.concatenate(
        [
            lower_part * cosine - upper_part * sine_part,
            upper_part * cosine + lower_part * sine_part,
        ],
        axis=-1,
    )


def carve(flat_params, shapes):
    pieces = []
    offset = 0
    for shape_now in shapes:
        entries = math.prod(shape_now)
        pieces.append(flat_params[offset : offset + entries].reshape(shape_now))
        offset = offset + entries
    return tuple(pieces)


def split_attention(flat_params):
    q_width = HEADS * HEAD_DIM
    kv_width = KV_HEADS * HEAD_DIM
    return carve(flat_params, [(D,), (D, q_width), (D, kv_width), (D, kv_width), (q_width, D)])


def split_ffn(flat_params):
    return carve(flat_params, [(D,), (D, FF), (D, FF), (FF, D)])


def outer_sum(left, right):
    return lax.dot_general(
        left, right, (((0,), (0,)), ((), ())), preferred_element_type=jnp.float32
    )


def back_product(left, weight):
    return lax.dot_general(
        left, weight, (((1,), (1,)), ((), ())), preferred_element_type=jnp.float32
    )


def score_block(query_group, key_piece, live_mask):
    score_scale = 1.0 / math.sqrt(query_group.shape[-1])
    scores = (
        jnp.einsum("qkgd,tkd->kgqt", query_group, key_piece, preferred_element_type=jnp.float32)
        * score_scale
    )
    return jnp.where(live_mask, scores, NEG_LARGE)


def gather_window(key_low, value_low, seg_local, reach):
    key_win = jnp.zeros((reach + 1,) + key_low.shape, key_low.dtype).at[0].set(key_low)
    value_win = jnp.zeros((reach + 1,) + value_low.shape, value_low.dtype).at[0].set(value_low)
    seg_win = jnp.zeros((reach + 1,) + seg_local.shape, seg_local.dtype).at[0].set(seg_local)

    def advance(position, carried):
        key_win_now, value_win_now, seg_win_now, key_cur, value_cur, seg_cur = carried
        key_cur, value_cur, seg_cur = passed_along((key_cur, value_cur, seg_cur), "seq", 1)
        key_win_now = lax.dynamic_update_index_in_dim(key_win_now, key_cur, position, 0)
        value_win_now = lax.dynamic_update_index_in_dim(value_win_now, value_cur, position, 0)
        seg_win_now = lax.dynamic_update_index_in_dim(seg_win_now, seg_cur, position, 0)
        return (key_win_now, value_win_now, seg_win_now, key_cur, value_cur, seg_cur)

    finished = lax.fori_loop(
        1, reach + 1, advance, (key_win, value_win, seg_win, key_low, value_low, seg_local)
    )
    return (finished[0], finished[1], finished[2])


def return_window(contrib_key, contrib_value, reach):

    def retreat(step_count, carried):
        total_key, total_value = carried
        position = reach - 1 - step_count
        total_key, total_value = (
            passed_along(total_key.astype(jnp.bfloat16), "seq", -1).astype(total_key.dtype),
            passed_along(total_value.astype(jnp.bfloat16), "seq", -1).astype(total_value.dtype),
        )
        total_key = total_key + lax.dynamic_index_in_dim(contrib_key, position, 0, keepdims=False)
        total_value = total_value + lax.dynamic_index_in_dim(
            contrib_value, position, 0, keepdims=False
        )
        return (total_key, total_value)

    return lax.fori_loop(0, reach, retreat, (contrib_key[reach], contrib_value[reach]))


def adam_update(master, moment_one, moment_two, gradient):
    first_new = BETA_ONE * moment_one + (1.0 - BETA_ONE) * gradient
    second_new = BETA_TWO * moment_two + (1.0 - BETA_TWO) * gradient * gradient
    first_hat = first_new / (1.0 - BETA_ONE**STEP)
    second_hat = second_new / (1.0 - BETA_TWO**STEP)
    master_new = master - LEARN_RATE * (
        first_hat / (jnp.sqrt(second_hat) + ADAM_EPS) + DECAY * master
    )
    return (master_new, first_new, second_new)


def per_device(
    tokens,
    segment_ids,
    out_grad,
    attn_master,
    attn_first,
    attn_second,
    ffn_master,
    ffn_first,
    ffn_second,
):
    dev_index = lax.axis_index("seq")
    dev_count = lax.axis_size("seq")
    tok_rows = tokens.shape[0]
    reach = min((SEG_MOST + tok_rows - 2) // tok_rows, dev_count - 1)
    group_size = HEADS // KV_HEADS
    score_scale = 1.0 / math.sqrt(HEAD_DIM)
    attn_whole, ffn_whole = (
        lax.all_gather(attn_master.astype(jnp.bfloat16), "seq", axis=0, tiled=True),
        lax.all_gather(ffn_master.astype(jnp.bfloat16), "seq", axis=0, tiled=True),
    )
    norm_one, query_weight, key_weight, value_weight, out_weight = split_attention(attn_whole)
    norm_two, gate_weight, up_weight, down_weight = split_ffn(ffn_whole)
    gain_one = norm_one.astype(jnp.float32)
    gain_two = norm_two.astype(jnp.float32)
    row_index = jnp.arange(tok_rows, dtype=jnp.int32)
    query_pos = dev_index * tok_rows + row_index
    cosine, sine_part = rotation(query_pos, HEAD_DIM)
    inputs = tokens.astype(jnp.float32)
    normed_one = rms_norm(inputs, gain_one).astype(jnp.bfloat16)
    query_pre = jnp.dot(normed_one, query_weight, preferred_element_type=jnp.float32)
    key_pre = jnp.dot(normed_one, key_weight, preferred_element_type=jnp.float32)
    value_low = (
        jnp.dot(normed_one, value_weight, preferred_element_type=jnp.float32)
        .astype(jnp.bfloat16)
        .reshape(tok_rows, KV_HEADS, HEAD_DIM)
    )
    query_low = rotate(query_pre.reshape(tok_rows, HEADS, HEAD_DIM), cosine, sine_part).astype(
        jnp.bfloat16
    )
    query_group = query_low.reshape(tok_rows, KV_HEADS, group_size, HEAD_DIM)
    key_low = rotate(key_pre.reshape(tok_rows, KV_HEADS, HEAD_DIM), cosine, sine_part).astype(
        jnp.bfloat16
    )
    key_win, value_win, seg_win = gather_window(key_low, value_low, segment_ids, reach)
    distances = jnp.arange(reach + 1, dtype=jnp.int32)

    def piece_mask(seg_piece, distance):
        key_pos = (dev_index - distance) * tok_rows + row_index
        same_item = segment_ids[:, None] == seg_piece[None, :]
        return same_item & (key_pos[None, :] <= query_pos[:, None]) & (key_pos[None, :] >= 0)

    def first_pass(carried_state, piece):
        key_piece, seg_piece, distance = piece
        live_mask = piece_mask(seg_piece, distance)
        run_max, run_total = carried_state
        masked = score_block(query_group, key_piece, live_mask)
        new_max = jnp.maximum(run_max, jnp.max(masked, axis=-1))
        exp_terms = jnp.where(live_mask, jnp.exp(masked - new_max[..., None]), 0.0)
        return (
            (new_max, run_total * jnp.exp(run_max - new_max) + jnp.sum(exp_terms, axis=-1)),
            None,
        )

    heads_shape = (KV_HEADS, group_size, tok_rows)
    start_state = (
        jnp.full(heads_shape, NEG_LARGE, jnp.float32),
        jnp.zeros(heads_shape, jnp.float32),
    )
    (run_max, run_total), unused_first = lax.scan(
        first_pass, start_state, (key_win, seg_win, distances)
    )
    log_total = run_max + jnp.log(run_total)

    def second_pass(out_total, piece):
        key_piece, value_piece, seg_piece, distance = piece
        live_mask = piece_mask(seg_piece, distance)
        masked = score_block(query_group, key_piece, live_mask)
        weights_low = jnp.where(live_mask, jnp.exp(masked - log_total[..., None]), 0.0).astype(
            jnp.bfloat16
        )
        return (
            out_total
            + jnp.einsum(
                "kgqt,tkd->qkgd", weights_low, value_piece, preferred_element_type=jnp.float32
            ),
            None,
        )

    attn_out, unused_second = lax.scan(
        second_pass,
        jnp.zeros((tok_rows, KV_HEADS, group_size, HEAD_DIM), jnp.float32),
        (key_win, value_win, seg_win, distances),
    )
    attn_low = attn_out.reshape(tok_rows, HEADS * HEAD_DIM).astype(jnp.bfloat16)
    middle = inputs + jnp.dot(attn_low, out_weight, preferred_element_type=jnp.float32)
    normed_two = rms_norm(middle, gain_two).astype(jnp.bfloat16)
    gate_rows = jnp.dot(normed_two, gate_weight, preferred_element_type=jnp.float32)
    up_rows = jnp.dot(normed_two, up_weight, preferred_element_type=jnp.float32)
    hidden = (jax.nn.silu(gate_rows) * up_rows).astype(jnp.bfloat16)
    result = (middle + jnp.dot(hidden, down_weight, preferred_element_type=jnp.float32)).astype(
        jnp.bfloat16
    )
    grad_down = outer_sum(hidden, out_grad)
    hidden_grad = back_product(out_grad, down_weight)
    sigma_gate = jax.nn.sigmoid(gate_rows)
    silu_gate = gate_rows * sigma_gate
    gate_grad = (
        hidden_grad * up_rows * sigma_gate * (1.0 + gate_rows * (1.0 - sigma_gate))
    ).astype(jnp.bfloat16)
    up_grad = (hidden_grad * silu_gate).astype(jnp.bfloat16)
    grad_gate = outer_sum(normed_two, gate_grad)
    grad_up = outer_sum(normed_two, up_grad)
    normed_two_grad = back_product(gate_grad, gate_weight) + back_product(up_grad, up_weight)
    unused_norm, norm_pull = jax.vjp(rms_norm, middle, gain_two)
    middle_norm_grad, grad_two = norm_pull(normed_two_grad)
    middle_grad = out_grad.astype(jnp.float32) + middle_norm_grad
    ffn_flat = jnp.concatenate(
        [grad_two, grad_gate.reshape(-1), grad_up.reshape(-1), grad_down.reshape(-1)]
    )
    ffn_shard = lax.psum_scatter(ffn_flat, "seq", scatter_dimension=0, tiled=True)
    middle_low = middle_grad.astype(jnp.bfloat16)
    grad_out = outer_sum(attn_low, middle_low)
    dout_low = back_product(middle_low, out_weight).astype(jnp.bfloat16)
    dout_group = dout_low.reshape(tok_rows, KV_HEADS, group_size, HEAD_DIM)
    delta = jnp.transpose(jnp.sum(dout_group.astype(jnp.float32) * attn_out, axis=-1), (1, 2, 0))

    def back_pass(dq_total, piece):
        key_piece, value_piece, seg_piece, distance = piece
        live_mask = piece_mask(seg_piece, distance)
        masked = score_block(query_group, key_piece, live_mask)
        weights_exp = jnp.where(live_mask, jnp.exp(masked - log_total[..., None]), 0.0)
        weights_low = weights_exp.astype(jnp.bfloat16)
        prob_grad = jnp.einsum(
            "qkgd,tkd->kgqt", dout_group, value_piece, preferred_element_type=jnp.float32
        )
        dscore = (weights_exp * (prob_grad - delta[..., None])).astype(jnp.bfloat16)
        dq_next = (
            dq_total
            + jnp.einsum("kgqt,tkd->qkgd", dscore, key_piece, preferred_element_type=jnp.float32)
            * score_scale
        )
        dk_piece = (
            jnp.einsum("kgqt,qkgd->tkd", dscore, query_group, preferred_element_type=jnp.float32)
            * score_scale
        )
        dv_piece = jnp.einsum(
            "kgqt,qkgd->tkd", weights_low, dout_group, preferred_element_type=jnp.float32
        )
        return (dq_next, (dk_piece, dv_piece))

    dq_rot, (dk_stack, dv_stack) = lax.scan(
        back_pass,
        jnp.zeros((tok_rows, KV_HEADS, group_size, HEAD_DIM), jnp.float32),
        (key_win, value_win, seg_win, distances),
    )
    dk_rot, dv_total = return_window(dk_stack, dv_stack, reach)
    dquery_low = (
        rotate(dq_rot.reshape(tok_rows, HEADS, HEAD_DIM), cosine, -sine_part)
        .reshape(tok_rows, HEADS * HEAD_DIM)
        .astype(jnp.bfloat16)
    )
    dkey_low = (
        rotate(dk_rot, cosine, -sine_part)
        .reshape(tok_rows, KV_HEADS * HEAD_DIM)
        .astype(jnp.bfloat16)
    )
    dvalue_low = dv_total.reshape(tok_rows, KV_HEADS * HEAD_DIM).astype(jnp.bfloat16)
    grad_query = outer_sum(normed_one, dquery_low)
    grad_key = outer_sum(normed_one, dkey_low)
    grad_value = outer_sum(normed_one, dvalue_low)
    normed_one_grad = (
        back_product(dquery_low, query_weight)
        + back_product(dkey_low, key_weight)
        + back_product(dvalue_low, value_weight)
    )
    unused_first_norm, first_pull = jax.vjp(rms_norm, inputs, gain_one)
    input_norm_grad, grad_one = first_pull(normed_one_grad)
    input_grad = middle_grad + input_norm_grad
    attn_flat = jnp.concatenate(
        [
            grad_one,
            grad_query.reshape(-1),
            grad_key.reshape(-1),
            grad_value.reshape(-1),
            grad_out.reshape(-1),
        ]
    )
    attn_shard = lax.psum_scatter(attn_flat, "seq", scatter_dimension=0, tiled=True)
    attn_new, attn_one, attn_two = adam_update(attn_master, attn_first, attn_second, attn_shard)
    ffn_new, ffn_one, ffn_two = adam_update(ffn_master, ffn_first, ffn_second, ffn_shard)
    return (result, input_grad, attn_new, attn_one, attn_two, ffn_new, ffn_one, ffn_two)


def solution(mesh):
    in_specs = (
        P("seq", None),
        P("seq"),
        P("seq", None),
        P("seq"),
        P("seq"),
        P("seq"),
        P("seq"),
        P("seq"),
        P("seq"),
    )
    out_specs = (
        P("seq", None),
        P("seq", None),
        P("seq"),
        P("seq"),
        P("seq"),
        P("seq"),
        P("seq"),
        P("seq"),
    )
    return jax.shard_map(
        per_device, mesh=mesh, in_specs=in_specs, out_specs=out_specs, check_vma=False
    )
```

profile of v0, /device:TPU:7, one launch (start us, length us, event | category | flops | bytes accessed | tf_op | source)
XLA Modules:
  0.0 4161.3 jit_solution(1402043624521162144)
XLA Ops:
  15.4 7.6 dynamic-update-slice.9
  23.0 12.2 broadcast.292
  35.2 18.9 dynamic-update-slice.10
  56.4 745.2 %all-reduce.14.cloned.1.call-done = (bf16[7079424]{0:T(1024)(128)(2,1)}, bf16[18875904]{0:T(1024)(128)(2,1)}) async-done(((bf16[7079424]{0:T(1024)(128)(2,1)}, bf16[18875904]{0:T(1024)(128)(2,1)}), (bf16[7079424]{0:T(1024)(128)(2,1)}, bf16[18875904]{0:T(1024)(128)(2,1)})) %all-reduce.14.cloned.1.call-update) | async-done | bytes 51910672
  805.9 9.1 fusion.103
  815.8 24.5 fusion.102
  864.8 9.8 slice.177
  874.5 6.6 copy.72
  888.9 333.6 %while.82 = (s32[]{:T(128)}, bf16[17,256,8,96]{1,3,2,0:T(8,128)(2,1)}, bf16[17,256,8,96]{1,3,2,0:T(8,128)(2,1)}, s32[17,256]{1,0:T(8,128)S(1)}, bf16[256,8,96]{2...) while((s32[]{:T(128)}, ...), condition=%wide.region_2.0_spmd, body=%wide.region_1.0_spmd.sunk | while | flops 5 | bytes 7872787 | solution.py:114
  896.7 6.4 collective-permute-done.2
  916.3 8.0 collective-permute-done.2
  937.3 8.0 collective-permute-done.2
  958.4 8.0 collective-permute-done.2
  979.5 8.0 collective-permute-done.2
  1000.6 8.0 collective-permute-done.2
  1021.7 8.0 collective-permute-done.2
  1042.8 8.0 collective-permute-done.2
  1063.9 8.0 collective-permute-done.2
  1084.9 8.0 collective-permute-done.2
  1106.0 8.0 collective-permute-done.2
  1127.1 8.0 collective-permute-done.2
  1148.2 8.0 collective-permute-done.2
  1169.3 8.0 collective-permute-done.2
  1190.4 8.0 collective-permute-done.2
  1211.5 8.0 collective-permute-done.2
  1222.6 145.7 %while.84 = (s32[]{:T(128)}, f32[8,2,256]{2,1,0:T(2,128)S(1)}, f32[8,2,256]{2,1,0:T(2,128)S(1)}, s32[256]{0:T(256)S(1)}, s32[17,256]{1,0:T(8,128)S(1)}, /*index=...) while((s32[]{:T(128)}, f32[8,2,256]{2,1,0:T(2,128)S(1)}, ...), condition=%wide.region_6.7_spmd.clone, body=%wide.region_3.6_spmd.clone.sunk | while | flops 209998848 | bytes 9986760 | solution.py:218
  1368.3 76.4 %while.85 = (s32[]{:T(128)}, f32[256,8,2,96]{0,3,2,1:T(8,128)S(1)}, bf16[17,256,8,96]{1,3,2,0:T(8,128)(2,1)}, s32[256]{0:T(256)S(1)}, s32[17,256]{1,0:T(8,128)S(...) while((s32[]{:T(128)}, f32[256,8,2,96]{0,3,2,1:T(8,128)S(1)}, ...), condition=%wide.region_8.9_spmd.clone, body=%wide.region_7.8_spmd.clone.sunk | while | flops 408945664 | bytes 4876490 | solution.py:238
  1445.8 9.8 slice.181
  1459.6 19.6 reshape.392
  1479.2 19.3 reshape.393
  1498.7 10.4 fusion.105
  1514.2 23.6 slice.186
  1537.7 15.9 multiply_convert_fusion
  1553.6 9.1 fusion.107
  1562.7 10.6 multiply_reduce_fusion
  1580.3 304.3 %while.86 = (s32[]{:T(128)}, f32[256,8,2,96]{0,3,2,1:T(8,128)}, f32[17,256,8,96]{1,3,2,0:T(8,128)}, f32[17,256,8,96]{1,3,2,0:T(8,128)}, bf16[17,256,8,96]{1,3,2,...) while((s32[]{:T(128)}, f32[256,8,2,96]{0,3,2,1:T(8,128)}, ...), condition=%wide.region_13.14_spmd.clone, body=%wide.region_12.13_spmd.clone.sunk | while | flops 1020855296 | bytes 51241808 | solution.py:300
  1901.5 10.1 convolution_bitcast_fusion.1
  1911.6 10.4 convolution_bitcast_fusion.2
  1926.8 340.5 %while.83 = (s32[]{:T(128)}, f32[256,8,96]{2,1,0:T(8,128)}, bf16[256,8,96]{2,1,0:T(8,128)(2,1)}, f32[17,256,8,96]{1,3,2,0:T(8,128)}, f32[17,256,8,96]{1,3,2,0:T(...) while((s32[]{:T(128)}, f32[256,8,96]{2,1,0:T(8,128)}, bf16[256,8,96]{2,1,0:T(8,128)(2,1)}, ...), condition=%wide.region_15.16_spmd, body=%wide.region_14.15_spmd.sunk | while | flops 1179654 | bytes 14156007 | solution.py:135
  1934.3 6.9 collective-permute-done.3
  1956.3 6.2 collective-permute-done.3
  1977.5 6.2 collective-permute-done.3
  1998.7 6.2 collective-permute-done.3
  2020.0 6.2 collective-permute-done.3
  2041.2 6.2 collective-permute-done.3
  2062.5 6.2 collective-permute-done.3
  2083.7 6.2 collective-permute-done.3
  2104.9 6.2 collective-permute-done.3
  2126.2 6.2 collective-permute-done.3
  2147.4 6.2 collective-permute-done.3
  2280.3 10.5 reshape.396
  2302.3 10.7 reshape.399
  2313.0 10.2 fusion.109
  2323.2 26.2 reshape.402
  2349.3 20.9 copy.110
  2370.2 21.0 copy.109
  2392.6 80.5 %dynamic-update-slice.12 = f32[7079424]{0:T(1024)} dynamic-update-slice(f32[7079424]{0:T(1024)} %constant_dynamic-update-slice_fusion.2, f32[2359296]{0:T(1024)} %reshape.396, s32[]{} %constant.287) | dynamic-update-slice | bytes 18874372
  2473.1 41.0 dynamic-update-slice.13
  2514.1 41.0 dynamic-update-slice.14
  2555.1 80.4 %dynamic-update-slice.15 = f32[7079424]{0:T(1024)} dynamic-update-slice(f32[7079424]{0:T(1024)} %dynamic-update-slice.14, f32[2359296]{0:T(1024)} %reshape.399, s32[]{} %constant.290) | dynamic-update-slice | bytes 18874372 | tf_op jit(solution)/shard_map/concatenate | solution.py:328
  2635.5 62.9 %pad_maximum_fusion = f32[18875904]{0:T(1024)} fusion(f32[6291456]{0:T(1024)} %reshape.402, f32[6291456]{0:T(1024)} %bitcast.271, f32[6291456]{0:T(1024)} %bitcast.272, f32[1536]{0:T(1024)S(1)} %copy-done.45), kind=kLoop, calls=%fused_computation.83 | loop fusion | flops 56627712 | bytes 151007232 | tf_op jit(solution)/shard_map/concatenate | solution.py:266
  2703.2 8.3 fusion.70
  2711.5 1430.7 %all-reduce.12.cloned.1.call-done = (f32[7079424]{0:T(1024)}, f32[18875904]{0:T(1024)}) async-done(((f32[7079424]{0:T(1024)}, f32[18875904]{0:T(1024)}), (f32[7079424]{0:T(1024)}, f32[18875904]{0:T(1024)})) %all-reduce.12.cloned.1.call-update) | async-done | bytes 103821328
  4146.6 7.4 multiply_subtract_fusion
  (1075 shorter events, 1088.2 us)
Async XLA Ops:
  7.2 794.4 %all-reduce.14.cloned.1.call-start = ((), (), s32[]{:S(2)}) async-start(), calls=%async_computation.1 | async-start | bytes 103825408
  54.1 4088.1 %all-reduce.12.cloned.1.call-start = ((), (), s32[]{:S(2)}) async-start(), calls=%async_computation | async-start | bytes 207650816
  888.9 14.2 collective-permute-start
  891.3 12.2 collective-permute-start.1
  906.3 18.0 collective-permute-start
  912.4 12.2 collective-permute-start.1
  927.3 18.0 collective-permute-start
  933.5 12.2 collective-permute-start.1
  948.4 18.0 collective-permute-start
  954.5 12.2 collective-permute-start.1
  969.5 18.0 collective-permute-start
  975.6 12.2 collective-permute-start.1
  990.6 18.0 collective-permute-start
  996.7 12.2 collective-permute-start.1
  1011.7 18.0 collective-permute-start
  1017.8 12.2 collective-permute-start.1
  1032.8 18.0 collective-permute-start
  1038.9 12.2 collective-permute-start.1
  1053.9 18.0 collective-permute-start
  1075.0 18.0 collective-permute-start
  1081.1 12.2 collective-permute-start.1
  1096.1 18.0 collective-permute-start
  1102.2 12.2 collective-permute-start.1
  1117.1 18.0 collective-permute-start
  1123.2 12.2 collective-permute-start.1
  1138.2 18.0 collective-permute-start
  1159.3 18.0 collective-permute-start
  1165.4 12.2 collective-permute-start.1
  1180.4 18.0 collective-permute-start
  1186.5 12.2 collective-permute-start.1
  1201.5 18.0 collective-permute-start
  1207.6 12.2 collective-permute-start.1
  1928.1 13.1 collective-permute-start.3
  1930.0 16.8 collective-permute-start.4
  1950.0 12.4 collective-permute-start.3
  1952.0 16.1 collective-permute-start.4
  1971.3 12.4 collective-permute-start.3
  1973.2 16.1 collective-permute-start.4
  1992.5 12.4 collective-permute-start.3
  1994.4 16.1 collective-permute-start.4
  2013.8 12.4 collective-permute-start.3
  2015.7 16.1 collective-permute-start.4
  2035.0 12.4 collective-permute-start.3
  2036.9 16.1 collective-permute-start.4
  2056.2 12.4 collective-permute-start.3
  2058.2 16.1 collective-permute-start.4
  2077.5 12.4 collective-permute-start.3
  2079.4 16.1 collective-permute-start.4
  2098.7 12.4 collective-permute-start.3
  2100.6 16.1 collective-permute-start.4
  2119.9 12.4 collective-permute-start.3
  2121.9 16.1 collective-permute-start.4
  2141.2 12.4 collective-permute-start.3
  2143.1 16.1 collective-permute-start.4
  2162.4 12.4 collective-permute-start.3
  2164.4 16.1 collective-permute-start.4
  2183.7 12.4 collective-permute-start.3
  2185.6 16.1 collective-permute-start.4
  2204.9 12.4 collective-permute-start.3
  2206.8 16.1 collective-permute-start.4
  2226.2 12.4 collective-permute-start.3
  2228.1 16.1 collective-permute-start.4
  2247.4 12.4 collective-permute-start.3
  2249.3 16.1 collective-permute-start.4
  (118 other events, 5503.9 us)
Sparse Core Ops, SparseCore 0:
  54.2 747.3 all-reduce.13
  2698.6 1443.5 all-reduce.11
where the time goes:
time: 4200 us; the launch traced here: 4160 us
  waiting for transfers between devices  2460 us (59%)
  local copies, waits for them, and re-layouts  667 us (16%)
  matrix products  521 us (12%)
  other arithmetic  242 us (6%)
  starting transfers between devices  219 us (5%)
    unnamed x4, waiting for transfers between devices  2180 us
    ppermute x80, waiting for transfers between devices, passed_along(): lax.ppermute(value, axis, [(source, source + steps) for source in range(l...  282 us
    unnamed x108, local copies, waits for them, and re-layouts  253 us
    ppermute x80, starting transfers between devices, passed_along(): lax.ppermute(value, axis, [(source, source + steps) for source in range(l...  219 us
    dot_general x34, matrix products, score_block(): jnp.einsum('qkgd,tkd->kgqt', query_group, key_piece, preferred_element_ty...  132 us
    slice x8, local copies, waits for them, and re-layouts, carve(): pieces.append(flat_params[offset:offset + entries].reshape(shape_now))  91.8 us
  transfers between devices with their start and end apart: 82, of which 50 were waited for; matrix products, arithmetic and copies ran while one was open for 2% of the time, Pallas kernels for 0%

commit v1 on v0

v1 whole, which is shorter than its diff:
```python
import functools
import math

import jax
import jax.numpy as jnp
from jax import lax
from jax.experimental import pallas as pl
from jax.experimental.pallas import tpu as pltpu
from jax.sharding import PartitionSpec as P

D = 1536
HEADS = 16
KV_HEADS = 8
HEAD_DIM = 96
FF = 4096
SEG_MOST = 4096
STEP = 7


ROPE_BASE = 100000.0
NORM_EPS = 1e-05
BETA_ONE = 0.5
BETA_TWO = 0.5
LEARN_RATE = 0.04
DECAY = 0.1
ADAM_EPS = 1e-08
NEG_LARGE = -1e30
HALF_DIM = HEAD_DIM // 2
QUERY_TILE = 512
KEY_TILE = 1024
CHUNK = 8192
SCORE_BASE_TWO = math.log2(math.e) / math.sqrt(HEAD_DIM)
SCORE_SCALE = 1.0 / math.sqrt(HEAD_DIM)


def rms_norm(values, norm_gain):
    factor = lax.rsqrt(jnp.mean(values * values, axis=-1, keepdims=True) + NORM_EPS)
    return values * factor * norm_gain


def angle_tables(positions):
    frequency = jnp.exp(
        jnp.arange(HALF_DIM).astype(jnp.float32) * (-2.0 * math.log(ROPE_BASE) / HEAD_DIM)
    )
    angles = positions.astype(jnp.float32)[..., None, :] * frequency[:, None]
    return (jnp.cos(angles), jnp.sin(angles))


def rotate(values, cosine, sine_part):
    lower_part = values[..., :HALF_DIM, :]
    upper_part = values[..., HALF_DIM:, :]
    return jnp.concatenate(
        [
            lower_part * cosine - upper_part * sine_part,
            upper_part * cosine + lower_part * sine_part,
        ],
        axis=-2,
    )


def contract(left, left_dim, right, right_dim):
    return lax.dot_general(
        left,
        right,
        (((left_dim,), (right_dim,)), ((), ())),
        preferred_element_type=jnp.float32,
    )


def adam_update(master, moment_one, moment_two, gradient):
    first_new = BETA_ONE * moment_one + (1.0 - BETA_ONE) * gradient
    second_new = BETA_TWO * moment_two + (1.0 - BETA_TWO) * gradient * gradient
    first_hat = first_new / (1.0 - BETA_ONE**STEP)
    second_hat = second_new / (1.0 - BETA_TWO**STEP)
    master_new = master - LEARN_RATE * (
        first_hat / (jnp.sqrt(second_hat) + ADAM_EPS) + DECAY * master
    )
    return (master_new, first_new, second_new)


def units_from_shard(flat_low, index, count):
    edge = D // count
    block = flat_low.shape[0] - edge
    unit = block // 3
    following = lax.ppermute(flat_low[:D], "seq", [(i + 1, i) for i in range(count - 1)])
    extended = jnp.concatenate([flat_low, following])
    aligned = lax.dynamic_slice(extended, (D - edge * index,), (block,)).reshape(3, unit)
    dealt = jnp.stack(
        [
            lax.ppermute(aligned[j], "seq", [(i, (3 * i + j) % count) for i in range(count)])
            for j in range(3)
        ]
    )
    return [
        lax.dynamic_index_in_dim(dealt, slot_of_kind(index, kind, count), 0, keepdims=False)
        for kind in range(3)
    ]


def slot_of_kind(index, kind, count):
    return (index + count * kind) % 3


def shard_from_units(units, gain_grad, index, count):
    edge = D // count
    stacked = jnp.stack(units)
    unit = stacked.shape[1]
    returned = []
    for j in range(3):
        inverse = 1 if count % 3 == 1 else 2
        kind = ((j - index) * inverse) % 3
        piece = lax.dynamic_index_in_dim(stacked, kind, 0, keepdims=False)
        returned.append(
            lax.ppermute(piece, "seq", [((3 * i + j) % count, i) for i in range(count)])
        )
    block = jnp.concatenate(returned)
    before = lax.ppermute(block[-D:], "seq", [(i, i + 1) for i in range(count - 1)])
    before = jnp.where(index == 0, gain_grad.astype(before.dtype), before)
    extended = jnp.concatenate([before, block])
    return lax.dynamic_slice(extended, (edge * index,), (3 * unit + edge,))


AXES = ("z", "y", "x")
GATHER_ORDERS = (("z", "y", "x"), ("z", "x", "y"), ("y", "x", "z"))


def device_grid(count):
    chips = count // 2
    sides = {16: (4, 2, 2), 64: (4, 4, 4)}.get(chips, (chips, 1, 1))
    return dict(zip(AXES + ("core",), sides + (2,)))


def coordinates(index, grid):
    found = {}
    for axis in reversed(list(grid)):
        found[axis] = index % grid[axis]
        index = index // grid[axis]
    return found


def place(found, grid):
    index = 0
    for axis in grid:
        index = index * grid[axis] + found[axis]
    return index


def shifted(value, axis, steps, grid):
    pairs = []
    for source in range(math.prod(grid.values())):
        target = coordinates(source, grid)
        target[axis] = (target[axis] + steps) % grid[axis]
        pairs.append((source, place(target, grid)))
    return lax.ppermute(value, "seq", pairs)


def slot_table(index, grid, axes):
    here = coordinates(index, grid)
    entries = []
    for number in range(math.prod(grid.values())):
        slots = coordinates(number, {axis: grid[axis] for axis in axes})
        there = {axis: (here[axis] - slots[axis]) % grid[axis] for axis in grid}
        entries.append(place(there, grid))
    return jnp.stack(entries).astype(jnp.int32)


def place_kernel(table_ref, *refs, lengths, rows):
    piece_refs, out_ref, sems = (refs[:-2], refs[-2], refs[-1])
    copies = []
    for piece_ref, length in zip(piece_refs, lengths):
        for block in range(length):
            entry = len(copies)
            target = pl.ds(pl.multiple_of(table_ref[entry] * rows, rows), rows)
            copy = pltpu.make_async_copy(
                piece_ref.at[pl.ds(block * rows, rows), :], out_ref.at[target, :], sems.at[entry]
            )
            copy.start()
            copies.append(copy)
    for copy in copies:
        copy.wait()


def placed(pieces, table, rows):
    count = table.shape[0]
    width = pieces[0].shape[1]
    lengths = tuple(piece.shape[0] // rows for piece in pieces)
    anywhere = pl.BlockSpec(memory_space=pl.ANY)
    return pl.pallas_call(
        functools.partial(place_kernel, lengths=lengths, rows=rows),
        grid_spec=pltpu.PrefetchScalarGridSpec(
            num_scalar_prefetch=1,
            grid=(1,),
            in_specs=[anywhere] * len(pieces),
            out_specs=anywhere,
            scratch_shapes=[pltpu.SemaphoreType.DMA((count,))],
        ),
        out_shape=jax.ShapeDtypeStruct((count * rows, width), pieces[0].dtype),
        cost_estimate=pl.CostEstimate(
            flops=0, transcendentals=0, bytes_accessed=4 * count * rows * width
        ),
        name="place_blocks",
    )(table, *pieces)


def gather_rows(block, order, index, grid):
    rows = block.shape[0]
    held = block
    for axis in order:
        arrivals = [held]
        for _ in range(grid[axis] - 1):
            arrivals.append(shifted(arrivals[-1], axis, 1, grid))
        if axis != order[-1]:
            held = jnp.concatenate(arrivals)
    pieces = arrivals + [shifted(piece, "core", 1, grid) for piece in arrivals]
    table = slot_table(index, grid, ("core",) + tuple(reversed(order)))
    return placed(pieces, table, rows)


def reorder_kernel(table_ref, in_ref, out_ref, *, rows):
    for block in range(in_ref.shape[0] // rows):
        source = pl.ds(pl.multiple_of(table_ref[block] * rows, rows), rows)
        out_ref[block * rows : (block + 1) * rows, :] = in_ref[source, :]


def reordered(value, table):
    rows = value.shape[0] // table.shape[0]
    return pl.pallas_call(
        functools.partial(reorder_kernel, rows=rows),
        grid_spec=pltpu.PrefetchScalarGridSpec(
            num_scalar_prefetch=1,
            grid=(1,),
            in_specs=[whole_spec(value)],
            out_specs=whole_spec(value),
        ),
        out_shape=jax.ShapeDtypeStruct(value.shape, value.dtype),
        cost_estimate=pl.CostEstimate(
            flops=0, transcendentals=0, bytes_accessed=4 * value.size
        ),
        name="reorder_blocks",
    )(table, value)


def sum_scatter(left_cols, right, right_dim, order, index, grid):
    count = math.prod(grid.values())
    rows = left_cols.shape[0] // count
    order = ("core",) + tuple(reversed(order))
    left = reordered(left_cols, slot_table(index, grid, order))
    received = []

    def partial(first, last):
        span = slice(first * rows, last * rows)
        total = contract(left[span], 1, right, right_dim)
        for part in received:
            total = total + part[span]
        return total

    window = count
    for axis in order:
        window = window // grid[axis]
        passing = None
        for slot in range(grid[axis] - 1, 0, -1):
            own = partial(slot * window, (slot + 1) * window)
            total = own if passing is None else own + passing
            passing = shifted(total.astype(jnp.bfloat16), axis, -1, grid)
        if passing is not None:
            received.append(passing)
    return partial(0, 1)


def live_pairs(rel_ref, pos, start, base, queries):
    rel = rel_ref[...]
    rel = jnp.concatenate([rel] * (queries // rel.shape[1]), axis=1)
    return (rel >= start - base) & (rel <= pos - base)


def forward_kernel(
    low_ref, high_ref, query_ref, key_ref, value_ref, pos_ref, start_ref, rel_ref, out_ref, lse_ref
):
    tile = pl.program_id(0)
    query_cols = query_ref[0]
    queries = query_cols.shape[1]
    keys = rel_ref.shape[0]
    pos = pos_ref[0]
    start = start_ref[0]

    def body(step, carried):
        run_max, run_total, mixed = carried
        rows = pl.ds(pl.multiple_of(step * keys, keys), keys)
        scores = contract(key_ref[rows, :], 1, query_cols, 0)
        live = live_pairs(rel_ref, pos, start, step * keys, queries)
        scores = jnp.where(live, scores, NEG_LARGE)
        new_max = jnp.maximum(run_max, jnp.max(scores, axis=0, keepdims=True))
        weights = jnp.exp2((scores - new_max) * SCORE_BASE_TWO)
        keep = jnp.exp2((run_max - new_max) * SCORE_BASE_TWO)
        run_total = run_total * keep + jnp.sum(weights, axis=0, keepdims=True)
        mixed = mixed * keep + contract(value_ref[step], 1, weights.astype(jnp.bfloat16), 0)
        return (new_max, run_total, mixed)

    start_state = (
        jnp.full((1, queries), NEG_LARGE, jnp.float32),
        jnp.zeros((1, queries), jnp.float32),
        jnp.zeros((HEAD_DIM, queries), jnp.float32),
    )
    run_max, run_total, mixed = lax.fori_loop(low_ref[tile], high_ref[tile], body, start_state)
    out_ref[0] = mixed / run_total
    lse_ref[0] = run_max * SCORE_BASE_TWO + jnp.log2(run_total)


def backward_kernel(
    low_ref,
    high_ref,
    query_ref,
    query_row_ref,
    dout_ref,
    dout_row_ref,
    out_ref,
    lse_ref,
    key_ref,
    key_col_ref,
    value_ref,
    pos_ref,
    start_ref,
    rel_ref,
    dquery_ref,
    dkey_ref,
    dvalue_ref,
):
    tile = pl.program_id(0)

    @pl.when(tile == 0)
    def _():
        dkey_ref[...] = jnp.zeros_like(dkey_ref)
        dvalue_ref[...] = jnp.zeros_like(dvalue_ref)

    query_cols = query_ref[0]
    query_rows = query_row_ref[0]
    dout_cols = dout_ref[0]
    dout_rows = dout_row_ref[0]
    queries = query_cols.shape[1]
    keys = rel_ref.shape[0]
    pos = pos_ref[0]
    start = start_ref[0]
    lse = lse_ref[0]
    delta = jnp.sum(dout_cols.astype(jnp.float32) * out_ref[0], axis=0, keepdims=True)

    def body(step, dquery):
        rows = pl.ds(pl.multiple_of(step * keys, keys), keys)
        scores = contract(key_ref[rows, :], 1, query_cols, 0)
        live = live_pairs(rel_ref, pos, start, step * keys, queries)
        weights = jnp.where(live, jnp.exp2(scores * SCORE_BASE_TWO - lse), 0.0)
        weight_grad = contract(value_ref[rows, :], 1, dout_cols, 0)
        dscore = (weights * (weight_grad - delta)).astype(jnp.bfloat16)
        dvalue_ref[rows, :] += contract(weights.astype(jnp.bfloat16), 1, dout_rows, 0)
        dkey_ref[rows, :] += contract(dscore, 1, query_rows, 0)
        return dquery + contract(key_col_ref[step], 1, dscore, 0)

    dquery = lax.fori_loop(
        low_ref[tile], high_ref[tile], body, jnp.zeros((HEAD_DIM, queries), jnp.float32)
    )
    dquery_ref[0] = dquery * SCORE_SCALE

    @pl.when(tile == pl.num_programs(0) - 1)
    def _():
        dkey_ref[...] = dkey_ref[...] * SCORE_SCALE


def whole_spec(array):
    return pl.BlockSpec(array.shape, lambda i, *_: (0,) * array.ndim)


def tile_spec(array):
    return pl.BlockSpec((1,) + array.shape[1:], lambda i, *_: (i,) + (0,) * (array.ndim - 1))


def run_kernel(body, name, bounds, inputs, outputs, flops):
    spec = lambda item: tile_spec(item[0]) if item[1] else whole_spec(item[0])
    grid = next(array.shape[0] for array, cut in inputs if cut)
    return pl.pallas_call(
        body,
        grid_spec=pltpu.PrefetchScalarGridSpec(
            num_scalar_prefetch=2,
            grid=(grid,),
            in_specs=[spec(item) for item in inputs],
            out_specs=[spec(item) for item in outputs],
        ),
        out_shape=[item[0] for item in outputs],
        compiler_params=pltpu.CompilerParams(vmem_limit_bytes=52 << 20),
        cost_estimate=pl.CostEstimate(
            flops=flops, transcendentals=flops // 400, bytes_accessed=16 << 20
        ),
        name=name,
    )(*bounds, *[item[0] for item in inputs])


def attend(query_cols, key_rows, value_cols, pos, start, rel, low, high):
    tiles, _, queries = query_cols.shape
    return run_kernel(
        forward_kernel,
        "attention_forward",
        (low, high),
        [
            (query_cols, True),
            (key_rows, False),
            (value_cols, False),
            (pos, True),
            (start, True),
            (rel, False),
        ],
        [
            (jax.ShapeDtypeStruct((tiles, HEAD_DIM, queries), jnp.float32), True),
            (jax.ShapeDtypeStruct((tiles, 1, queries), jnp.float32), True),
        ],
        20_000_000_000,
    )


def attend_back(
    query_cols, dout_cols, out_cols, lse, key_rows, key_cols, value_rows, pos, start, rel, low, high
):
    tiles, _, queries = query_cols.shape
    grads = jax.ShapeDtypeStruct(key_rows.shape, jnp.float32)
    return run_kernel(
        backward_kernel,
        "attention_backward",
        (low, high),
        [
            (query_cols, True),
            (jnp.swapaxes(query_cols, 1, 2), True),
            (dout_cols, True),
            (jnp.swapaxes(dout_cols, 1, 2), True),
            (out_cols, True),
            (lse, True),
            (key_rows, False),
            (key_cols, False),
            (value_rows, False),
            (pos, True),
            (start, True),
            (rel, False),
        ],
        [
            (jax.ShapeDtypeStruct((tiles, HEAD_DIM, queries), jnp.float32), True),
            (grads, False),
            (grads, False),
        ],
        50_000_000_000,
    )


def per_device(
    tokens,
    segment_ids,
    out_grad,
    attn_master,
    attn_first,
    attn_second,
    ffn_master,
    ffn_first,
    ffn_second,
):
    index = lax.axis_index("seq")
    count = lax.axis_size("seq")
    rows = tokens.shape[0]
    total = rows * count
    group = count // KV_HEADS
    parts = group // 2
    span = rows // parts
    half = (index // parts) % 2
    part = index % parts

    def exchange(value):
        return lax.all_to_all(value, "seq", 0, 0, tiled=True)

    def swapped(value, bit):
        return lax.ppermute(value, "seq", [(i, i ^ bit) for i in range(count)])

    attn_low = attn_master.astype(jnp.bfloat16)
    ffn_low = ffn_master.astype(jnp.bfloat16)
    gains = lax.psum(
        jnp.where(
            index == 0, jnp.stack([attn_low[:D], ffn_low[:D]]).astype(jnp.float32), 0.0
        ),
        "seq",
    )
    gain_one, gain_two = (gains[0], gains[1])

    grid = device_grid(count)
    by_axes = (D // count) % 16 == 0

    def gathered(unit, width, color):
        block = unit.reshape(-1, width)
        if by_axes:
            return gather_rows(block, GATHER_ORDERS[color], index, grid)
        return lax.all_gather(block, "seq", axis=0, tiled=True)

    def scattered(left_cols, right, right_dim, color):
        if by_axes:
            return sum_scatter(
                left_cols, right, right_dim, GATHER_ORDERS[color], index, grid
            ).reshape(-1)
        whole = contract(left_cols, 1, right, right_dim).astype(jnp.bfloat16)
        return (
            lax.psum_scatter(whole, "seq", scatter_dimension=0, tiled=True)
            .reshape(-1)
            .astype(jnp.float32)
        )

    q_unit, kv_unit, o_unit = units_from_shard(attn_low, index, count)
    gate_unit, up_unit, down_unit = units_from_shard(ffn_low, index, count)
    query_weight = gathered(q_unit, HEADS * HEAD_DIM, 0)
    key_value_weight = gathered(kv_unit, KV_HEADS * HEAD_DIM, 1)
    key_weight, value_weight = (key_value_weight[:D], key_value_weight[D:])
    out_weight = gathered(o_unit, D, 2)
    gate_weight = gathered(gate_unit, FF, 0)
    up_weight = gathered(up_unit, FF, 1)
    down_weight = gathered(down_unit, D, 2)

    all_ids = lax.all_gather(segment_ids.reshape(1, rows), "seq", axis=0, tiled=True).reshape(-1)

    def item_starts(ids):
        return jnp.sum((all_ids < ids[..., None]).astype(jnp.int32), axis=-1)

    inputs = tokens.astype(jnp.float32)
    normed_one = rms_norm(inputs, gain_one).astype(jnp.bfloat16)
    own_places = index * rows + jnp.arange(rows, dtype=jnp.int32)
    own_cos, own_sin = angle_tables(own_places)
    query_pre = contract(query_weight, 0, normed_one, 1).reshape(HEADS, HEAD_DIM, rows)
    key_pre = contract(key_weight, 0, normed_one, 1).reshape(KV_HEADS, HEAD_DIM, rows)
    value_low = (
        contract(value_weight, 0, normed_one, 1)
        .astype(jnp.bfloat16)
        .reshape(KV_HEADS, HEAD_DIM, rows)
    )
    query_low = rotate(query_pre, own_cos, own_sin).astype(jnp.bfloat16)
    key_low = rotate(key_pre, own_cos, own_sin).astype(jnp.bfloat16)

    def by_owner(value):
        pieces = value.reshape(HEADS, HEAD_DIM, parts, span)
        return jnp.swapaxes(pieces, 1, 2).reshape(count, HEAD_DIM, span)

    def by_head(value):
        pieces = value.reshape(HEADS, parts, HEAD_DIM, span)
        return jnp.swapaxes(pieces, 1, 2).reshape(HEADS, HEAD_DIM, rows)

    def paired(key_part, value_part):
        return jnp.stack([key_part, value_part], axis=1).reshape(HEADS, HEAD_DIM, rows)

    received = exchange(
        jnp.concatenate([by_owner(query_low), by_owner(paired(key_low, value_low))], axis=1)
    )

    sources = QUERY_TILE // span
    tiles = count // sources

    def to_tiles(value):
        pieces = value.reshape(tiles, sources, value.shape[1], span)
        return jnp.swapaxes(pieces, 1, 2).reshape(tiles, value.shape[1], QUERY_TILE)

    def from_tiles(value):
        pieces = value.reshape(tiles, value.shape[1], sources, span)
        return jnp.swapaxes(pieces, 1, 2).reshape(count, value.shape[1], span)

    query_cols = to_tiles(received[:, :HEAD_DIM])
    own_kind = received[:, HEAD_DIM:]
    other_kind = swapped(own_kind, parts)
    pair = jnp.stack(
        [
            jnp.where(half == 0, own_kind, other_kind),
            jnp.where(half == 0, other_kind, own_kind),
        ]
    )[:, None]
    bit = 1
    while bit < parts:
        pair = jnp.concatenate([pair, swapped(pair, bit)], axis=1)
        bit = bit * 2
    key_all, value_all = (pair[0], pair[1])
    devices_per_tile = KEY_TILE // rows
    key_tiles = count // devices_per_tile

    def key_columns(value):
        pieces = value.reshape(parts, key_tiles, devices_per_tile, HEAD_DIM, span)
        return jnp.transpose(pieces, (1, 3, 2, 0, 4)).reshape(key_tiles, HEAD_DIM, KEY_TILE)

    def key_rows_of(value):
        return jnp.transpose(value, (1, 0, 3, 2)).reshape(total, HEAD_DIM)

    key_cols = key_columns(key_all)
    value_cols = key_columns(value_all)
    key_rows = key_rows_of(key_all)
    value_rows = key_rows_of(value_all)
    slot_parts = part ^ jnp.arange(parts, dtype=jnp.int32)
    within = jnp.arange(span, dtype=jnp.int32)
    rel = (
        rows * jnp.arange(devices_per_tile, dtype=jnp.int32)[:, None, None]
        + span * slot_parts[None, :, None]
        + within[None, None, :]
    ).reshape(KEY_TILE, 1)
    rel = jnp.broadcast_to(rel, (KEY_TILE, 128))
    held_places = (
        rows * jnp.arange(count, dtype=jnp.int32)[:, None] + span * part + within[None, :]
    )
    held_ids = lax.dynamic_index_in_dim(
        all_ids.reshape(count, parts, span), part, 1, keepdims=False
    )
    held_starts = item_starts(held_ids.reshape(-1))
    pos = held_places.reshape(tiles, 1, QUERY_TILE)
    start = held_starts.reshape(tiles, 1, QUERY_TILE)
    tile_span = sources * rows
    low = item_starts(all_ids[::tile_span]) // KEY_TILE
    high = (jnp.arange(1, tiles + 1, dtype=jnp.int32) * tile_span + KEY_TILE - 1) // KEY_TILE

    chunks = []
    chunk = min(CHUNK, total)
    for first in range(0, total, chunk):
        first_key = max(0, first - SEG_MOST) // KEY_TILE
        last_key = (first + chunk) // KEY_TILE
        chunks.append(
            (
                slice(first // tile_span, (first + chunk) // tile_span),
                slice(first_key, last_key),
                slice(first_key * KEY_TILE, last_key * KEY_TILE),
            )
        )

    pieces = []
    for of_tiles, of_key_tiles, of_keys in chunks:
        shift = of_key_tiles.start * KEY_TILE
        pieces.append(
            attend(
                query_cols[of_tiles],
                key_rows[of_keys],
                value_cols[of_key_tiles],
                pos[of_tiles] - shift,
                start[of_tiles] - shift,
                rel,
                low[of_tiles] - of_key_tiles.start,
                high[of_tiles] - of_key_tiles.start,
            )
        )
    out_cols = jnp.concatenate([piece[0] for piece in pieces])
    lse = jnp.concatenate([piece[1] for piece in pieces])

    mixed_low = by_head(exchange(from_tiles(out_cols.astype(jnp.bfloat16)))).reshape(
        HEADS * HEAD_DIM, rows
    )

    middle = inputs + contract(mixed_low, 0, out_weight, 0)
    normed_two = rms_norm(middle, gain_two).astype(jnp.bfloat16)
    gate_rows = contract(normed_two, 1, gate_weight, 0)
    up_rows = contract(normed_two, 1, up_weight, 0)
    hidden = (jax.nn.silu(gate_rows) * up_rows).astype(jnp.bfloat16)
    result = (middle + contract(hidden, 1, down_weight, 0)).astype(jnp.bfloat16)
    hidden_grad = contract(out_grad, 1, down_weight, 1)
    sigma_gate = jax.nn.sigmoid(gate_rows)
    silu_gate = gate_rows * sigma_gate
    gate_grad = (
        hidden_grad * up_rows * sigma_gate * (1.0 + gate_rows * (1.0 - sigma_gate))
    ).astype(jnp.bfloat16)
    up_grad = (hidden_grad * silu_gate).astype(jnp.bfloat16)
    normed_two_grad = contract(gate_grad, 1, gate_weight, 1) + contract(up_grad, 1, up_weight, 1)
    _, norm_pull = jax.vjp(rms_norm, middle, gain_two)
    middle_norm_grad, grad_two = norm_pull(normed_two_grad)
    middle_grad = out_grad.astype(jnp.float32) + middle_norm_grad
    middle_low = middle_grad.astype(jnp.bfloat16)

    dout_cols = to_tiles(
        exchange(
            by_owner(
                contract(out_weight, 1, middle_low, 1)
                .astype(jnp.bfloat16)
                .reshape(HEADS, HEAD_DIM, rows)
            )
        )
    )
    normed_two_cols = normed_two.T
    ffn_units = [
        scattered(normed_two_cols, gate_grad, 0, 0),
        scattered(normed_two_cols, up_grad, 0, 1),
        scattered(hidden.T, out_grad, 0, 2),
    ]
    out_unit = scattered(mixed_low, middle_low, 0, 2)

    pieces = []
    dkey_rows = jnp.zeros((total, HEAD_DIM), jnp.float32)
    dvalue_rows = jnp.zeros((total, HEAD_DIM), jnp.float32)
    for of_tiles, of_key_tiles, of_keys in chunks:
        shift = of_key_tiles.start * KEY_TILE
        dquery_piece, dkey_piece, dvalue_piece = attend_back(
            query_cols[of_tiles],
            dout_cols[of_tiles],
            out_cols[of_tiles],
            lse[of_tiles],
            key_rows[of_keys],
            key_cols[of_key_tiles],
            value_rows[of_keys],
            pos[of_tiles] - shift,
            start[of_tiles] - shift,
            rel,
            low[of_tiles] - of_key_tiles.start,
            high[of_tiles] - of_key_tiles.start,
        )
        pieces.append(dquery_piece)
        if len(chunks) == 1:
            dkey_rows, dvalue_rows = (dkey_piece, dvalue_piece)
        else:
            dkey_rows = dkey_rows.at[of_keys].add(dkey_piece)
            dvalue_rows = dvalue_rows.at[of_keys].add(dvalue_piece)
    dquery_rot = from_tiles(jnp.concatenate(pieces))
    held_cos, held_sin = angle_tables(held_places)
    dquery_held = rotate(dquery_rot, held_cos, -held_sin).astype(jnp.bfloat16)

    def by_slot(value):
        return jnp.transpose(value.reshape(count, parts, span, HEAD_DIM), (1, 0, 3, 2))

    grads = jnp.stack([by_slot(dkey_rows), by_slot(dvalue_rows)])
    bit = parts // 2
    while bit >= 1:
        grads = grads[:, :bit] + swapped(grads[:, bit:].astype(jnp.bfloat16), bit)
        bit = bit // 2
    dkey_held, dvalue_held = (grads[0, 0], grads[1, 0])
    sent_kind = jnp.where(half == 0, dvalue_held, dkey_held).astype(jnp.bfloat16)
    kept_kind = jnp.where(half == 0, dkey_held, dvalue_held) + swapped(sent_kind, parts)
    kept_low = jnp.where(half == 0, rotate(kept_kind, held_cos, -held_sin), kept_kind).astype(
        jnp.bfloat16
    )
    returned = exchange(jnp.concatenate([dquery_held, kept_low], axis=1))
    dquery_low = by_head(returned[:, :HEAD_DIM]).reshape(HEADS * HEAD_DIM, rows)
    pair_low = by_head(returned[:, HEAD_DIM:]).reshape(KV_HEADS, 2, HEAD_DIM, rows)
    dkey_low = pair_low[:, 0].reshape(KV_HEADS * HEAD_DIM, rows)
    dvalue_low = pair_low[:, 1].reshape(KV_HEADS * HEAD_DIM, rows)

    normed_one_cols = normed_one.T
    query_unit = scattered(normed_one_cols, dquery_low, 1, 0)
    nothing = jnp.zeros_like(normed_one_cols)
    key_value_cols = jnp.concatenate(
        [
            jnp.concatenate([normed_one_cols, nothing], axis=1),
            jnp.concatenate([nothing, normed_one_cols], axis=1),
        ]
    )
    key_value_unit = scattered(
        key_value_cols, jnp.concatenate([dkey_low, dvalue_low], axis=1), 1, 1
    )
    normed_one_grad = (
        contract(dquery_low, 0, query_weight, 1)
        + contract(dkey_low, 0, key_weight, 1)
        + contract(dvalue_low, 0, value_weight, 1)
    )
    _, first_pull = jax.vjp(rms_norm, inputs, gain_one)
    input_norm_grad, grad_one = first_pull(normed_one_grad)
    input_grad = middle_grad + input_norm_grad

    gain_grads = lax.psum(jnp.stack([grad_one, grad_two]), "seq")
    attn_shard = shard_from_units(
        [query_unit, key_value_unit, out_unit], gain_grads[0], index, count
    )
    ffn_shard = shard_from_units(ffn_units, gain_grads[1], index, count)
    attn_new, attn_one, attn_two = adam_update(
        attn_master, attn_first, attn_second, attn_shard
    )
    ffn_new, ffn_one, ffn_two = adam_update(
        ffn_master, ffn_first, ffn_second, ffn_shard
    )
    return (result, input_grad, attn_new, attn_one, attn_two, ffn_new, ffn_one, ffn_two)


def solution(mesh):
    rows_cut = P("seq", None)
    flat_cut = P("seq")
    in_specs = (rows_cut, flat_cut, rows_cut) + (flat_cut,) * 6
    out_specs = (rows_cut, rows_cut) + (flat_cut,) * 6
    return jax.shard_map(
        per_device, mesh=mesh, in_specs=in_specs, out_specs=out_specs, check_vma=False
    )
```

time: 4200 us -> 2720 us (0.65)
  waiting for transfers between devices: 2460 us -> 311 us
  Pallas kernels: 0 us -> 1660 us
  local copies, waits for them, and re-layouts: 667 us -> 135 us
  matrix products: 521 us -> 169 us
  other arithmetic: 242 us -> 107 us
  blocking collectives: 0 us -> 125 us
    unnamed x4 -> x0, waiting for transfers between devices: 2180 us -> none
    pallas_call x0 -> x14, Pallas kernels: none -> 1660 us  [the longest x6 1580 us: placed(): pl.pallas_call(functools.partial(place_kernel, lengths=lengths, rows=rows...]
    dot_general x140 -> x56, matrix products: 521 us -> 169 us  [contract(): lax.dot_general(left, right, (((left_dim,), (right_dim,)), ((), ())), pre...]
    unnamed x108 -> x205, local copies, waits for them, and re-layouts: 253 us -> 33.3 us
    psum x0 -> x2, blocking collectives: none -> 90.5 us  [the longest x1 47.6 us: per_device(): gain_grads = lax.psum(jnp.stack([grad_one, grad_two]), 'seq')]
    slice x8 -> x12, local copies, waits for them, and re-layouts: 91.8 us -> 4.37 us  [the longest x1 1.48 us: per_device(): dquery_low = by_head(returned[:, :HEAD_DIM]).reshape(HEADS * HEAD_DIM, rows)]
    add x103 -> x7, other arithmetic: 70.9 us -> 1.66 us  [the longest x3 0.63 us: per_device(): rows * jnp.arange(count, dtype=jnp.int32)[:, None] + span * part]
    concatenate x1 -> x6, local copies, waits for them, and re-layouts: 80.4 us -> 12 us  [gather_rows(): held = jnp.concatenate(arrivals)]
  transfers between devices with their start and end apart: 82 -> 106, of which waited for: 50 -> 32; matrix products, arithmetic and copies ran while one was open for 2% -> 11% of each run, Pallas kernels for 0% -> 61%
where the time goes in v1:
time: 2720 us; the launch traced here: 2710 us
  Pallas kernels  1660 us (61%)
  waiting for transfers between devices  311 us (11%)
  starting transfers between devices  195 us (7%)
  matrix products  169 us (6%)
  local copies, waits for them, and re-layouts  135 us (5%)
  blocking collectives  125 us (5%)
  other arithmetic  107 us (4%)
    pallas_call x6, Pallas kernels, placed(): pl.pallas_call(functools.partial(place_kernel, lengths=lengths, rows=rows...  1580 us
    ppermute x82, waiting for transfers between devices, shifted(): return lax.ppermute(value, 'seq', pairs)  285 us
    dot_general x56, matrix products, contract(): lax.dot_general(left, right, (((left_dim,), (right_dim,)), ((), ())), pre...  169 us
    ppermute x82, starting transfers between devices, shifted(): return lax.ppermute(value, 'seq', pairs)  122 us
    pallas_call x2, Pallas kernels, run_kernel(): pl.pallas_call(body, grid_spec=pltpu.PrefetchScalarGridSpec(num_scalar_pr...  56.2 us
  transfers between devices with their start and end apart: 106, of which 32 were waited for; matrix products, arithmetic and copies ran while one was open for 11% of the time, Pallas kernels for 61%

profile of v1, /device:TPU:7, one launch (start us, length us, event | category | flops | bytes accessed | tf_op | source)
XLA Modules:
  0.0 2706.1 jit_solution(5600598370658180412)
XLA Ops:
  9.9 34.9 %all-gather.1 = s32[32,1,256]{2,1,0:T(1,128)S(1)} all-gather(s32[1,1,256]{2,1,0:T(1,128)S(1)} %bitcast.332), channel_id=2, replica_groups=mesh['seq'=32] {'seq'}, dimensions={0}, use_global_device_ids=true | all-gather | bytes 33792 | tf_op jit(solution)/shard_map/all_gather | solution.py:517
  47.4 42.9 %psum.14 = f32[2,1536]{1,0:T(2,128)S(1)} all-reduce(f32[2,1536]{1,0:T(2,128)S(1)} %convert_select_fusion), channel_id=1, replica_groups=mesh['seq'=32] {'seq'}, use_global_device_ids=true, to_apply=%region_2.3 | all-reduce | flops 3072 | bytes 24576 | tf_op jit(solution)/shard_map/psum | solution.py:478
  100.7 4.6 collective-permute-start.3
  127.9 12.4 collective-permute-done.11
  152.4 8.4 dynamic-slice_reduce_fusion.2
  168.9 6.7 collective-permute-done.6
  191.9 5.2 collective-permute-start.16
  197.1 17.6 collective-permute-done.15.refs_1_
  225.9 145.0 %place_blocks.7 = bf16[3072,768]{1,0:T(8,128)(2,1)} custom-call(s32[32]{0:T(128)} %stack.152.table_ref, bf16[768,768]{1,0:T(8,128)(2,1)} %constant_dynamic-update-slice_fusion.5.refs_0_, bf16[768,768]{1,0:T(8,128)(2,1)} %copy-done.51, bf16[768,768]{1,0:T(8,128)(2,1)} %copy-done.52, bf16[768,768]{1,0:T(8,128)(2,1)} %copy-done.53), custom_call_target="tpu_custom_call" | custom-call | bytes 9437184 | tf_op jit(solution)/shard_map/place_blocks/pallas_call | solution.py:188
  377.9 145.0 %place_blocks.6 = bf16[1536,1536]{1,0:T(8,128)(2,1)} custom-call(s32[32]{0:T(128)} %stack.144.table_ref, bf16[384,1536]{1,0:T(8,128)(2,1)} %constant_dynamic-update-slice_fusion.refs_0_, bf16[384,1536]{1,0:T(8,128)(2,1)} %collective-permute-done.8.refs_1_, bf16[384,1536]{1,0:T(8,128)(2,1)} %collective-permute-done.9.refs_2_, ...), custom_call_target="tpu_custom_call" | custom-call | bytes 9437184 | tf_op jit(solution)/shard_map/place_blocks/pallas_call | solution.py:188
  528.8 6.1 all-to-all-start
  541.9 43.3 %collective-permute-done.42 = bf16[48,4096]{1,0:T(8,128)(2,1)S(1)} collective-permute-done((bf16[48,4096]{1,0:T(8,128)(2,1)S(1)}, bf16[48,4096]{1,0:T(8,128)(2,1)S(1)}, u32[]{:S(2)}, u32[]{:S(2)}) %collective-permute-start.42) | collective-permute-done | bytes 393248 | tf_op jit(solution)/shard_map/ppermute | solution.py:154
  586.9 6.8 collective-permute-done.35
  598.4 6.4 collective-permute-start.49
  606.9 16.6 collective-permute-done.43
  630.3 9.9 collective-permute-done.18
  642.9 6.7 collective-permute-start.24
  654.2 8.5 collective-permute-done.24.refs_3_
  666.0 30.4 %collective-permute-done.50.refs_2_ = bf16[512,1536]{1,0:T(8,128)(2,1)} collective-permute-done((bf16[512,1536]{1,0:T(8,128)(2,1)}, bf16[512,1536]{1,0:T(8,128)(2,1)}, u32[]{:S(2)}, u32[]{:S(2)}) %collective-permute-start.50) | collective-permute-done | bytes 1572896 | tf_op jit(solution)/shard_map/ppermute | solution.py:154
  697.2 18.8 convert_reduce_fusion
  736.2 21.5 attention_forward.1
  759.4 11.2 collective-permute-done.51.refs_3_
  779.0 145.0 %place_blocks.8 = bf16[1536,1536]{1,0:T(8,128)(2,1)} custom-call(s32[32]{0:T(128)} %stack.157.table_ref, bf16[192,1536]{1,0:T(8,128)(2,1)} %constant_dynamic-update-slice_fusion.10.refs_0_, bf16[192,1536]{1,0:T(8,128)(2,1)} %collective-permute-done.22.refs_1_, bf16[192,1536]{1,0:T(8,128)(2,1)} %collective-permute-done.23.refs_2_, ...), custom_call_target="tpu_custom_call" | custom-call | bytes 9437184 | tf_op jit(solution)/shard_map/place_blocks/pallas_call | solution.py:188
  924.0 383.4 %place_blocks.11 = bf16[4096,1536]{1,0:T(8,128)(2,1)} custom-call(s32[32]{0:T(128)} %stack.157.table_ref, bf16[512,1536]{1,0:T(8,128)(2,1)} %constant_dynamic-update-slice_fusion.23.refs_0_, bf16[512,1536]{1,0:T(8,128)(2,1)} %collective-permute-done.49.refs_1_, bf16[512,1536]{1,0:T(8,128)(2,1)} %collective-permute-done.50.refs_2_, ...), custom_call_target="tpu_custom_call" | custom-call | bytes 25165824 | tf_op jit(solution)/shard_map/place_blocks/pallas_call | solution.py:188
  1316.7 383.2 %place_blocks.9 = bf16[1536,4096]{1,0:T(8,128)(2,1)} custom-call(s32[32]{0:T(128)} %stack.144.table_ref, bf16[384,4096]{1,0:T(8,128)(2,1)} %constant_dynamic-update-slice_fusion.13.refs_0_, bf16[384,4096]{1,0:T(8,128)(2,1)} %collective-permute-done.37.refs_1_, bf16[384,4096]{1,0:T(8,128)(2,1)} %collective-permute-done.38.refs_2_, ...), custom_call_target="tpu_custom_call" | custom-call | bytes 25165824 | tf_op jit(solution)/shard_map/place_blocks/pallas_call | solution.py:188
  1699.9 383.2 %place_blocks.10 = bf16[1536,4096]{1,0:T(8,128)(2,1)} custom-call(s32[32]{0:T(128)} %stack.152.table_ref, bf16[384,4096]{1,0:T(8,128)(2,1)} %constant_dynamic-update-slice_fusion.18.refs_0_, bf16[384,4096]{1,0:T(8,128)(2,1)} %collective-permute-done.44.refs_1_, bf16[384,4096]{1,0:T(8,128)(2,1)} %collective-permute-done.45.refs_2_, ...), custom_call_target="tpu_custom_call" | custom-call | bytes 25165824 | tf_op jit(solution)/shard_map/place_blocks/pallas_call | solution.py:188
  2086.1 4.4 multiply_reduce_fusion.2
  2097.3 9.8 fusion.213
  2107.1 9.8 fusion.212
  2116.9 5.6 copy.164
  2122.5 5.7 copy.163
  2128.3 12.7 multiply_convert_fusion.1
  2150.2 7.4 fusion.214
  2157.7 10.7 multiply_reduce_fusion
  2178.2 4.6 convolution_convert_fusion.6
  2187.7 6.6 all-to-all-start.2
  2198.3 4.4 convolution_convert_fusion.1
  2207.1 4.4 convolution_convert_fusion
  2211.5 4.4 convolution_convert_fusion.2
  2220.3 34.6 %attention_backward.1 = (f32[8,96,512]{2,1,0:T(8,128)}, f32[8192,96]{1,0:T(8,128)}, f32[8192,96]{1,0:T(8,128)}) custom-call(s32[8]{0:T(128)S(1)} %get-tuple-element.126.low_ref, s32[8]{0:T(128)S(1)} %get-tuple-element.125.high_ref, bf16[8,96,512]{2,1,0:T(8,128)(2,1)S(1)} %copy.142.query_ref, bf16[8,512,96]{2,1,0:T(8,128)(2,1)} %bitcast.279, ...), custom_call_target="tpu_custom_call" | custom-call | flops 49999998976 | bytes 16777216 | tf_op jit(solution)/shard_map/attention_backward/pallas_call | solution.py:378
  2254.9 5.3 copy.156
  2260.3 5.5 copy.157
  2285.5 7.8 collective-permute-done.71
  2305.6 4.8 all-to-all-start.3
  2322.4 27.9 %collective-permute-done.73 = bf16[192,1536]{1,0:T(8,128)(2,1)S(1)} collective-permute-done((bf16[192,1536]{1,0:T(8,128)(2,1)S(1)}, bf16[192,1536]{1,0:T(8,128)(2,1)S(1)}, u32[]{:S(2)}, u32[]{:S(2)}) %collective-permute-start.73) | collective-permute-done | bytes 589856 | tf_op jit(solution)/shard_map/ppermute | solution.py:154
  2354.5 5.2 collective-permute-done.74
  2362.5 4.7 add_convert_fusion
  2367.8 4.6 add_convert_fusion.1
  2376.0 4.6 collective-permute-start.93
  2407.1 4.4 reorder_blocks.7
  2423.0 5.8 collective-permute-start.94
  2443.8 19.0 collective-permute-done.94
  2471.7 27.2 %collective-permute-done.88 = bf16[192,4096]{1,0:T(8,128)(2,1)S(1)} collective-permute-done((bf16[192,4096]{1,0:T(8,128)(2,1)S(1)}, bf16[192,4096]{1,0:T(8,128)(2,1)S(1)}, u32[]{:S(2)}, u32[]{:S(2)}) %collective-permute-start.88) | collective-permute-done | bytes 1572896 | tf_op jit(solution)/shard_map/ppermute | solution.py:154
  2500.6 5.0 collective-permute-start.89
  2507.3 5.1 collective-permute-start.83
  2517.4 8.0 collective-permute-done.61
  2553.5 4.7 collective-permute-done.84
  2563.5 7.1 collective-permute-done.91
  2571.9 7.1 collective-permute-done.85
  2592.4 13.3 fusion.12
  2608.2 47.6 %psum.15 = f32[2,1536]{1,0:T(2,128)S(1)} all-reduce(f32[2,1536]{1,0:T(2,128)S(1)} %pad_maximum_fusion.19), channel_id=1, replica_groups=mesh['seq'=32] {'seq'}, use_global_device_ids=true, to_apply=%region_9.10 | all-reduce | flops 3072 | bytes 24576 | tf_op jit(solution)/shard_map/psum | solution.py:752
  2673.3 7.1 collective-permute-start.99
  2685.5 13.7 collective-permute-done.101
  2699.2 6.7 multiply_subtract_fusion
  (578 shorter events, 421.6 us)
Async XLA Ops:
  1.9 90.8 %collective-permute-start = (bf16[1536]{0:T(1024)(128)(2,1)S(1)}, bf16[1536]{0:T(1024)(128)(2,1)S(1)}, u32[]{:S(2)}, u32[]{:S(2)}) collective-permute-start(bf16[1536]{0:T(1024)(128)(2,1)S(1)} %slice.693), channel_id=1, source_target_pairs={{1,0},{2,1},{3,2},{4,3},{5,4},{6,5},{7,6},{8,7},{9,8},{10,9},{11,1... | collective-permute-start | bytes 9224 | tf_op jit(solution)/shard_map/ppermute | solution.py:85
  6.4 98.9 %collective-permute-start.29 = (bf16[1536]{0:T(1024)(128)(2,1)S(1)}, bf16[1536]{0:T(1024)(128)(2,1)S(1)}, u32[]{:S(2)}, u32[]{:S(2)}) collective-permute-start(bf16[1536]{0:T(1024)(128)(2,1)S(1)} %slice.697), channel_id=1, source_target_pairs={{1,0},{2,1},{3,2},{4,3},{5,4},{6,5},{7,6},{8,7},{9,8},{10,9},{11,1... | collective-permute-start | bytes 9224 | tf_op jit(solution)/shard_map/ppermute | solution.py:85
  108.2 37.0 %collective-permute-start.30 = (bf16[196608]{0:T(1024)(128)(2,1)S(1)}, bf16[196608]{0:T(1024)(128)(2,1)}, u32[]{:S(2)}, u32[]{:S(2)}) collective-permute-start(bf16[196608]{0:T(1024)(128)(2,1)S(1)} %get-tuple-element.103), channel_id=1, source_target_pairs={{0,0},{1,3},{2,6},{3,9},{4,12},{5,15},{6,18},{7,21},{8,24},{9,27},... | collective-permute-start | bytes 1179656 | tf_op jit(solution)/shard_map/ppermute | solution.py:90
  111.3 36.3 %collective-permute-start.31 = (bf16[196608]{0:T(1024)(128)(2,1)S(1)}, bf16[196608]{0:T(1024)(128)(2,1)S(1)}, u32[]{:S(2)}, u32[]{:S(2)}) collective-permute-start(bf16[196608]{0:T(1024)(128)(2,1)S(1)} %get-tuple-element.104), channel_id=1, source_target_pairs={{0,1},{1,4},{2,7},{3,10},{4,13},{5,16},{6,19},{7,22},{8,25},{9,28}... | collective-permute-start | bytes 1179656 | tf_op jit(solution)/shard_map/ppermute | solution.py:90
  111.4 36.6 %collective-permute-start.32 = (bf16[196608]{0:T(1024)(128)(2,1)S(1)}, bf16[196608]{0:T(1024)(128)(2,1)}, u32[]{:S(2)}, u32[]{:S(2)}) collective-permute-start(bf16[196608]{0:T(1024)(128)(2,1)S(1)} %get-tuple-element.105), channel_id=1, source_target_pairs={{0,2},{1,5},{2,8},{3,11},{4,14},{5,17},{6,20},{7,23},{8,26},{9,29}... | collective-permute-start | bytes 1179656 | tf_op jit(solution)/shard_map/ppermute | solution.py:90
  140.2 51.6 %collective-permute-start.21 = (bf16[96,1536]{1,0:T(8,128)(2,1)}, bf16[96,1536]{1,0:T(8,128)(2,1)}, u32[]{:S(2)}, u32[]{:S(2)}) collective-permute-start(bf16[96,1536]{1,0:T(8,128)(2,1)} %pad_maximum_fusion.18), channel_id=1, source_target_pairs={{0,2},{1,3},{2,0},{3,1},{4,6},{5,7},{6,4},{7,5},{8,10},{9,11},{10,... | collective-permute-start | bytes 884744 | tf_op jit(solution)/shard_map/ppermute | solution.py:154
  161.0 59.3 %collective-permute-start.40 = (bf16[48,4096]{1,0:T(8,128)(2,1)S(1)}, bf16[48,4096]{1,0:T(8,128)(2,1)S(1)}, u32[]{:S(2)}, u32[]{:S(2)}) collective-permute-start(bf16[48,4096]{1,0:T(8,128)(2,1)S(1)} %reshape.418), channel_id=1, source_target_pairs={{0,8},{1,9},{2,10},{3,11},{4,12},{5,13},{6,14},{7,15},{8,16},{9,17... | collective-permute-start | bytes 1179656 | tf_op jit(solution)/shard_map/ppermute | solution.py:154
  167.2 52.1 %collective-permute-start.47 = (bf16[128,1536]{1,0:T(8,128)(2,1)S(1)}, bf16[128,1536]{1,0:T(8,128)(2,1)S(1)}, u32[]{:S(2)}, u32[]{:S(2)}) collective-permute-start(bf16[128,1536]{1,0:T(8,128)(2,1)S(1)} %reshape.419), channel_id=1, source_target_pairs={{0,4},{1,5},{2,6},{3,7},{4,0},{5,1},{6,2},{7,3},{8,12},{9,13},{10,... | collective-permute-start | bytes 1179656 | tf_op jit(solution)/shard_map/ppermute | solution.py:154
  182.3 32.4 %collective-permute-start.15 = (bf16[768,768]{1,0:T(8,128)(2,1)}, bf16[768,768]{1,0:T(8,128)(2,1)S(1)}, u32[]{:S(2)}, u32[]{:S(2)}) collective-permute-start(bf16[768,768]{1,0:T(8,128)(2,1)} %constant_dynamic-update-slice_fusion.5.refs_0_), channel_id=1, source_target_pairs={{0,4},{1,5},{2,6},{3,7},{4,0},{5,1},{6,2},{7,3},{8,12},{9,13},{10,... | collective-permute-start | bytes 3538952 | tf_op jit(solution)/shard_map/ppermute | solution.py:154
  190.2 31.4 %collective-permute-start.8 = (bf16[384,1536]{1,0:T(8,128)(2,1)}, bf16[384,1536]{1,0:T(8,128)(2,1)}, u32[]{:S(2)}, u32[]{:S(2)}) collective-permute-start(bf16[384,1536]{1,0:T(8,128)(2,1)} %constant_dynamic-update-slice_fusion.refs_0_), channel_id=1, source_target_pairs={{0,2},{1,3},{2,0},{3,1},{4,6},{5,7},{6,4},{7,5},{8,10},{9,11},{10,... | collective-permute-start | bytes 3538952 | tf_op jit(solution)/shard_map/ppermute | solution.py:154
  191.9 30.5 %collective-permute-start.16 = (bf16[768,768]{1,0:T(8,128)(2,1)S(1)}, bf16[768,768]{1,0:T(8,128)(2,1)S(1)}, u32[]{:S(2)}, u32[]{:S(2)}) collective-permute-start(bf16[768,768]{1,0:T(8,128)(2,1)S(1)} %copy-done.50), channel_id=1, source_target_pairs={{0,1},{1,0},{2,3},{3,2},{4,5},{5,4},{6,7},{7,6},{8,9},{9,8},{10,11... | collective-permute-start | bytes 3538952 | tf_op jit(solution)/shard_map/ppermute | solution.py:154
  219.3 156.4 %collective-permute-start.33 = (bf16[48,4096]{1,0:T(8,128)(2,1)S(1)}, bf16[48,4096]{1,0:T(8,128)(2,1)}, u32[]{:S(2)}, u32[]{:S(2)}) collective-permute-start(bf16[48,4096]{1,0:T(8,128)(2,1)S(1)} %reshape.417), channel_id=1, source_target_pairs={{0,8},{1,9},{2,10},{3,11},{4,12},{5,13},{6,14},{7,15},{8,16},{9,17... | collective-permute-start | bytes 1179656 | tf_op jit(solution)/shard_map/ppermute | solution.py:154
  221.1 155.6 %collective-permute-start.9 = (bf16[384,1536]{1,0:T(8,128)(2,1)}, bf16[384,1536]{1,0:T(8,128)(2,1)}, u32[]{:S(2)}, u32[]{:S(2)}) collective-permute-start(bf16[384,1536]{1,0:T(8,128)(2,1)} %constant_dynamic-update-slice_fusion.refs_0_), channel_id=1, source_target_pairs={{0,1},{1,0},{2,3},{3,2},{4,5},{5,4},{6,7},{7,6},{8,9},{9,8},{10,11... | collective-permute-start | bytes 3538952 | tf_op jit(solution)/shard_map/ppermute | solution.py:154
  221.6 156.3 %collective-permute-start.10 = (bf16[384,1536]{1,0:T(8,128)(2,1)}, bf16[384,1536]{1,0:T(8,128)(2,1)}, u32[]{:S(2)}, u32[]{:S(2)}) collective-permute-start(bf16[384,1536]{1,0:T(8,128)(2,1)} %collective-permute-done.8.refs_1_), channel_id=1, source_target_pairs={{0,1},{1,0},{2,3},{3,2},{4,5},{5,4},{6,7},{7,6},{8,9},{9,8},{10,11... | collective-permute-start | bytes 3538952 | tf_op jit(solution)/shard_map/ppermute | solution.py:154
  222.4 314.3 %collective-permute-start.22 = (bf16[192,1536]{1,0:T(8,128)(2,1)}, bf16[192,1536]{1,0:T(8,128)(2,1)}, u32[]{:S(2)}, u32[]{:S(2)}) collective-permute-start(bf16[192,1536]{1,0:T(8,128)(2,1)} %constant_dynamic-update-slice_fusion.10.refs_0_), channel_id=1, source_target_pairs={{0,8},{1,9},{2,10},{3,11},{4,12},{5,13},{6,14},{7,15},{8,16},{9,17... | collective-permute-start | bytes 1769480 | tf_op jit(solution)/shard_map/ppermute | solution.py:154
  225.7 370.6 %collective-permute-start.48 = (bf16[256,1536]{1,0:T(8,128)(2,1)}, bf16[256,1536]{1,0:T(8,128)(2,1)}, u32[]{:S(2)}, u32[]{:S(2)}) collective-permute-start(bf16[256,1536]{1,0:T(8,128)(2,1)} %pad_maximum_fusion.13), channel_id=1, source_target_pairs={{0,2},{1,3},{2,0},{3,1},{4,6},{5,7},{6,4},{7,5},{8,10},{9,11},{10,... | collective-permute-start | bytes 2359304 | tf_op jit(solution)/shard_map/ppermute | solution.py:154
  375.7 162.2 %collective-permute-start.41 = (bf16[48,4096]{1,0:T(8,128)(2,1)S(1)}, bf16[48,4096]{1,0:T(8,128)(2,1)S(1)}, u32[]{:S(2)}, u32[]{:S(2)}) collective-permute-start(bf16[48,4096]{1,0:T(8,128)(2,1)S(1)} %collective-permute-done.40), channel_id=1, source_target_pairs={{0,8},{1,9},{2,10},{3,11},{4,12},{5,13},{6,14},{7,15},{8,16},{9,17... | collective-permute-start | bytes 1179656 | tf_op jit(solution)/shard_map/ppermute | solution.py:154
  376.7 162.5 %collective-permute-start.34 = (bf16[48,4096]{1,0:T(8,128)(2,1)}, bf16[48,4096]{1,0:T(8,128)(2,1)S(1)}, u32[]{:S(2)}, u32[]{:S(2)}) collective-permute-start(bf16[48,4096]{1,0:T(8,128)(2,1)} %collective-permute-done.33), channel_id=1, source_target_pairs={{0,8},{1,9},{2,10},{3,11},{4,12},{5,13},{6,14},{7,15},{8,16},{9,17... | collective-permute-start | bytes 1179656 | tf_op jit(solution)/shard_map/ppermute | solution.py:154
  528.8 76.8 %all-to-all-start = ((bf16[32,192,128]{2,1,0:T(8,128)(2,1)}), bf16[32,192,128]{2,1,0:T(8,128)(2,1)S(1)}, u32[]{:S(2)}, u32[]{:S(2)}) async-start(bf16[32,192,128]{2,1,0:T(8,128)(2,1)} %pad_maximum_fusion.3), calls=%async_computation | async-start | bytes 3145728 | tf_op jit(solution)/shard_map/all_to_all | solution.py:471
  536.7 93.6 %collective-permute-start.23 = (bf16[192,1536]{1,0:T(8,128)(2,1)}, bf16[192,1536]{1,0:T(8,128)(2,1)}, u32[]{:S(2)}, u32[]{:S(2)}) collective-permute-start(bf16[192,1536]{1,0:T(8,128)(2,1)} %collective-permute-done.22.refs_1_), channel_id=1, source_target_pairs={{0,8},{1,9},{2,10},{3,11},{4,12},{5,13},{6,14},{7,15},{8,16},{9,17... | collective-permute-start | bytes 1769480 | tf_op jit(solution)/shard_map/ppermute | solution.py:154
  537.9 47.4 %collective-permute-start.42 = (bf16[48,4096]{1,0:T(8,128)(2,1)S(1)}, bf16[48,4096]{1,0:T(8,128)(2,1)S(1)}, u32[]{:S(2)}, u32[]{:S(2)}) collective-permute-start(bf16[48,4096]{1,0:T(8,128)(2,1)S(1)} %collective-permute-done.41), channel_id=1, source_target_pairs={{0,8},{1,9},{2,10},{3,11},{4,12},{5,13},{6,14},{7,15},{8,16},{9,17... | collective-permute-start | bytes 1179656 | tf_op jit(solution)/shard_map/ppermute | solution.py:154
  539.1 54.6 %collective-permute-start.35 = (bf16[48,4096]{1,0:T(8,128)(2,1)S(1)}, bf16[48,4096]{1,0:T(8,128)(2,1)S(1)}, u32[]{:S(2)}, u32[]{:S(2)}) collective-permute-start(bf16[48,4096]{1,0:T(8,128)(2,1)S(1)} %collective-permute-done.34), channel_id=1, source_target_pairs={{0,8},{1,9},{2,10},{3,11},{4,12},{5,13},{6,14},{7,15},{8,16},{9,17... | collective-permute-start | bytes 1179656 | tf_op jit(solution)/shard_map/ppermute | solution.py:154
  586.5 37.0 %collective-permute-start.43 = (bf16[192,4096]{1,0:T(8,128)(2,1)}, bf16[192,4096]{1,0:T(8,128)(2,1)}, u32[]{:S(2)}, u32[]{:S(2)}) collective-permute-start(bf16[192,4096]{1,0:T(8,128)(2,1)} %pad_maximum_fusion.6), channel_id=1, source_target_pairs={{0,2},{1,3},{2,0},{3,1},{4,6},{5,7},{6,4},{7,5},{8,10},{9,11},{10,... | collective-permute-start | bytes 4718600 | tf_op jit(solution)/shard_map/ppermute | solution.py:154
  596.1 53.7 %collective-permute-start.36 = (bf16[192,4096]{1,0:T(8,128)(2,1)}, bf16[192,4096]{1,0:T(8,128)(2,1)}, u32[]{:S(2)}, u32[]{:S(2)}) collective-permute-start(bf16[192,4096]{1,0:T(8,128)(2,1)} %pad_maximum_fusion.5), channel_id=1, source_target_pairs={{0,4},{1,5},{2,6},{3,7},{4,0},{5,1},{6,2},{7,3},{8,12},{9,13},{10,... | collective-permute-start | bytes 4718600 | tf_op jit(solution)/shard_map/ppermute | solution.py:154
  598.4 51.2 %collective-permute-start.49 = (bf16[512,1536]{1,0:T(8,128)(2,1)}, bf16[512,1536]{1,0:T(8,128)(2,1)}, u32[]{:S(2)}, u32[]{:S(2)}) collective-permute-start(bf16[512,1536]{1,0:T(8,128)(2,1)} %constant_dynamic-update-slice_fusion.23.refs_0_), channel_id=1, source_target_pairs={{0,8},{1,9},{2,10},{3,11},{4,12},{5,13},{6,14},{7,15},{8,16},{9,17... | collective-permute-start | bytes 4718600 | tf_op jit(solution)/shard_map/ppermute | solution.py:154
  605.7 34.5 %collective-permute-start.18 = (bf16[32,96,128]{2,1,0:T(8,128)(2,1)S(1)}, bf16[32,96,128]{2,1,0:T(8,128)(2,1)S(1)}, u32[]{:S(2)}, u32[]{:S(2)}) collective-permute-start(bf16[32,96,128]{2,1,0:T(8,128)(2,1)S(1)} %slice.708), channel_id=1, source_target_pairs={{0,2},{1,3},{2,0},{3,1},{4,6},{5,7},{6,4},{7,5},{8,10},{9,11},{10,... | collective-permute-start | bytes 2359304 | tf_op jit(solution)/shard_map/ppermute | solution.py:474
  649.6 46.8 %collective-permute-start.50 = (bf16[512,1536]{1,0:T(8,128)(2,1)}, bf16[512,1536]{1,0:T(8,128)(2,1)}, u32[]{:S(2)}, u32[]{:S(2)}) collective-permute-start(bf16[512,1536]{1,0:T(8,128)(2,1)} %collective-permute-done.49.refs_1_), channel_id=1, source_target_pairs={{0,8},{1,9},{2,10},{3,11},{4,12},{5,13},{6,14},{7,15},{8,16},{9,17... | collective-permute-start | bytes 4718600 | tf_op jit(solution)/shard_map/ppermute | solution.py:154
  649.8 47.4 %collective-permute-start.19 = (bf16[2,1,32,96,128]{4,3,2,0,1:T(8,128)(2,1)S(1)}, bf16[2,1,32,96,128]{4,3,2,0,1:T(8,128)(2,1)}, u32[]{:S(2)}, u32[]{:S(2)}) collective-permute-start(bf16[2,1,32,96,128]{4,3,2,0,1:T(8,128)(2,1)S(1)} %maximum_bitcast_fusion), channel_id=1, source_target_pairs={{0,1},{1,0},{2,3},{3,2},{4,5},{5,4},{6,7},{7,6},{8,9},{9,8},{10,11... | collective-permute-start | bytes 4718600 | tf_op jit(solution)/shard_map/ppermute | solution.py:474
  653.0 82.2 %collective-permute-start.37 = (bf16[384,4096]{1,0:T(8,128)(2,1)}, bf16[384,4096]{1,0:T(8,128)(2,1)}, u32[]{:S(2)}, u32[]{:S(2)}) collective-permute-start(bf16[384,4096]{1,0:T(8,128)(2,1)} %constant_dynamic-update-slice_fusion.13.refs_0_), channel_id=1, source_target_pairs={{0,2},{1,3},{2,0},{3,1},{4,6},{5,7},{6,4},{7,5},{8,10},{9,11},{10,... | collective-permute-start | bytes 9437192 | tf_op jit(solution)/shard_map/ppermute | solution.py:154
  653.1 82.9 %collective-permute-start.44 = (bf16[384,4096]{1,0:T(8,128)(2,1)}, bf16[384,4096]{1,0:T(8,128)(2,1)}, u32[]{:S(2)}, u32[]{:S(2)}) collective-permute-start(bf16[384,4096]{1,0:T(8,128)(2,1)} %constant_dynamic-update-slice_fusion.18.refs_0_), channel_id=1, source_target_pairs={{0,4},{1,5},{2,6},{3,7},{4,0},{5,1},{6,2},{7,3},{8,12},{9,13},{10,... | collective-permute-start | bytes 9437192 | tf_op jit(solution)/shard_map/ppermute | solution.py:154
  665.6 66.9 %collective-permute-start.52 = (bf16[512,1536]{1,0:T(8,128)(2,1)}, bf16[512,1536]{1,0:T(8,128)(2,1)}, u32[]{:S(2)}, u32[]{:S(2)}) collective-permute-start(bf16[512,1536]{1,0:T(8,128)(2,1)} %constant_dynamic-update-slice_fusion.23.refs_0_), channel_id=1, source_target_pairs={{0,1},{1,0},{2,3},{3,2},{4,5},{5,4},{6,7},{7,6},{8,9},{9,8},{10,11... | collective-permute-start | bytes 4718600 | tf_op jit(solution)/shard_map/ppermute | solution.py:154
  696.4 36.5 %collective-permute-start.53 = (bf16[512,1536]{1,0:T(8,128)(2,1)}, bf16[512,1536]{1,0:T(8,128)(2,1)}, u32[]{:S(2)}, u32[]{:S(2)}) collective-permute-start(bf16[512,1536]{1,0:T(8,128)(2,1)} %collective-permute-done.49.refs_1_), channel_id=1, source_target_pairs={{0,1},{1,0},{2,3},{3,2},{4,5},{5,4},{6,7},{7,6},{8,9},{9,8},{10,11... | collective-permute-start | bytes 4718600 | tf_op jit(solution)/shard_map/ppermute | solution.py:154
  697.2 35.8 %collective-permute-start.54 = (bf16[512,1536]{1,0:T(8,128)(2,1)}, bf16[512,1536]{1,0:T(8,128)(2,1)}, u32[]{:S(2)}, u32[]{:S(2)}) collective-permute-start(bf16[512,1536]{1,0:T(8,128)(2,1)} %collective-permute-done.50.refs_2_), channel_id=1, source_target_pairs={{0,1},{1,0},{2,3},{3,2},{4,5},{5,4},{6,7},{7,6},{8,9},{9,8},{10,11... | collective-permute-start | bytes 4718600 | tf_op jit(solution)/shard_map/ppermute | solution.py:154
  732.5 584.2 %collective-permute-start.38 = (bf16[384,4096]{1,0:T(8,128)(2,1)}, bf16[384,4096]{1,0:T(8,128)(2,1)}, u32[]{:S(2)}, u32[]{:S(2)}) collective-permute-start(bf16[384,4096]{1,0:T(8,128)(2,1)} %constant_dynamic-update-slice_fusion.13.refs_0_), channel_id=1, source_target_pairs={{0,1},{1,0},{2,3},{3,2},{4,5},{5,4},{6,7},{7,6},{8,9},{9,8},{10,11... | collective-permute-start | bytes 9437192 | tf_op jit(solution)/shard_map/ppermute | solution.py:154
  732.9 966.9 %collective-permute-start.45 = (bf16[384,4096]{1,0:T(8,128)(2,1)}, bf16[384,4096]{1,0:T(8,128)(2,1)}, u32[]{:S(2)}, u32[]{:S(2)}) collective-permute-start(bf16[384,4096]{1,0:T(8,128)(2,1)} %constant_dynamic-update-slice_fusion.18.refs_0_), channel_id=1, source_target_pairs={{0,1},{1,0},{2,3},{3,2},{4,5},{5,4},{6,7},{7,6},{8,9},{9,8},{10,11... | collective-permute-start | bytes 9437192 | tf_op jit(solution)/shard_map/ppermute | solution.py:154
  733.0 37.6 %collective-permute-start.51 = (bf16[512,1536]{1,0:T(8,128)(2,1)}, bf16[512,1536]{1,0:T(8,128)(2,1)}, u32[]{:S(2)}, u32[]{:S(2)}) collective-permute-start(bf16[512,1536]{1,0:T(8,128)(2,1)} %collective-permute-done.50.refs_2_), channel_id=1, source_target_pairs={{0,8},{1,9},{2,10},{3,11},{4,12},{5,13},{6,14},{7,15},{8,16},{9,17... | collective-permute-start | bytes 4718600 | tf_op jit(solution)/shard_map/ppermute | solution.py:154
  735.2 581.4 %collective-permute-start.39 = (bf16[384,4096]{1,0:T(8,128)(2,1)}, bf16[384,4096]{1,0:T(8,128)(2,1)}, u32[]{:S(2)}, u32[]{:S(2)}) collective-permute-start(bf16[384,4096]{1,0:T(8,128)(2,1)} %collective-permute-done.37.refs_1_), channel_id=1, source_target_pairs={{0,1},{1,0},{2,3},{3,2},{4,5},{5,4},{6,7},{7,6},{8,9},{9,8},{10,11... | collective-permute-start | bytes 9437192 | tf_op jit(solution)/shard_map/ppermute | solution.py:154
  735.9 964.0 %collective-permute-start.46 = (bf16[384,4096]{1,0:T(8,128)(2,1)}, bf16[384,4096]{1,0:T(8,128)(2,1)}, u32[]{:S(2)}, u32[]{:S(2)}) collective-permute-start(bf16[384,4096]{1,0:T(8,128)(2,1)} %collective-permute-done.44.refs_1_), channel_id=1, source_target_pairs={{0,1},{1,0},{2,3},{3,2},{4,5},{5,4},{6,7},{7,6},{8,9},{9,8},{10,11... | collective-permute-start | bytes 9437192 | tf_op jit(solution)/shard_map/ppermute | solution.py:154
  770.7 153.3 %collective-permute-start.55 = (bf16[512,1536]{1,0:T(8,128)(2,1)}, bf16[512,1536]{1,0:T(8,128)(2,1)}, u32[]{:S(2)}, u32[]{:S(2)}) collective-permute-start(bf16[512,1536]{1,0:T(8,128)(2,1)} %collective-permute-done.51.refs_3_), channel_id=1, source_target_pairs={{0,1},{1,0},{2,3},{3,2},{4,5},{5,4},{6,7},{7,6},{8,9},{9,8},{10,11... | collective-permute-start | bytes 4718600 | tf_op jit(solution)/shard_map/ppermute | solution.py:154
  772.9 1310.3 %all-to-all-start.1 = ((bf16[32,96,128]{2,1,0:T(8,128)(2,1)}), bf16[32,96,128]{2,1,0:T(8,128)(2,1)}, u32[]{:S(2)}, u32[]{:S(2)}) async-start(bf16[32,96,128]{2,1,0:T(8,128)(2,1)} %bitcast.61), calls=%async_computation.1 | async-start | bytes 1572864 | tf_op jit(solution)/shard_map/all_to_all | solution.py:471
  2197.9 78.2 %collective-permute-start.70 = (bf16[768,1536]{1,0:T(8,128)(2,1)}, bf16[768,1536]{1,0:T(8,128)(2,1)}, u32[]{:S(2)}, u32[]{:S(2)}) collective-permute-start(bf16[768,1536]{1,0:T(8,128)(2,1)} %convolution_convert_fusion.3), channel_id=1, source_target_pairs={{0,1},{1,0},{2,3},{3,2},{4,5},{5,4},{6,7},{7,6},{8,9},{9,8},{10,11... | collective-permute-start | bytes 7077896 | tf_op jit(solution)/shard_map/ppermute | solution.py:154
  2202.7 159.8 %collective-permute-start.86 = (bf16[768,4096]{1,0:T(8,128)(2,1)}, bf16[768,4096]{1,0:T(8,128)(2,1)}, u32[]{:S(2)}, u32[]{:S(2)}) collective-permute-start(bf16[768,4096]{1,0:T(8,128)(2,1)} %convolution_convert_fusion.1), channel_id=1, source_target_pairs={{0,1},{1,0},{2,3},{3,2},{4,5},{5,4},{6,7},{7,6},{8,9},{9,8},{10,11... | collective-permute-start | bytes 18874376 | tf_op jit(solution)/shard_map/ppermute | solution.py:154
  2270.4 97.4 %collective-permute-start.80 = (bf16[768,4096]{1,0:T(8,128)(2,1)}, bf16[768,4096]{1,0:T(8,128)(2,1)}, u32[]{:S(2)}, u32[]{:S(2)}) collective-permute-start(bf16[768,4096]{1,0:T(8,128)(2,1)} %convolution_convert_fusion.2), channel_id=1, source_target_pairs={{0,1},{1,0},{2,3},{3,2},{4,5},{5,4},{6,7},{7,6},{8,9},{9,8},{10,11... | collective-permute-start | bytes 18874376 | tf_op jit(solution)/shard_map/ppermute | solution.py:154
  2270.8 102.0 %collective-permute-start.92 = (bf16[2048,1536]{1,0:T(8,128)(2,1)}, bf16[2048,1536]{1,0:T(8,128)(2,1)}, u32[]{:S(2)}, u32[]{:S(2)}) collective-permute-start(bf16[2048,1536]{1,0:T(8,128)(2,1)} %convolution_convert_fusion), channel_id=1, source_target_pairs={{0,1},{1,0},{2,3},{3,2},{4,5},{5,4},{6,7},{7,6},{8,9},{9,8},{10,11... | collective-permute-start | bytes 18874376 | tf_op jit(solution)/shard_map/ppermute | solution.py:154
  2305.6 75.1 %all-to-all-start.3 = ((bf16[32,192,128]{2,1,0:T(8,128)(2,1)}), bf16[32,192,128]{2,1,0:T(8,128)(2,1)}, u32[]{:S(2)}, u32[]{:S(2)}) async-start(bf16[32,192,128]{2,1,0:T(8,128)(2,1)} %pad_maximum_fusion.8), calls=%async_computation.3 | async-start | bytes 3145728 | tf_op jit(solution)/shard_map/all_to_all | solution.py:471
  2313.0 37.3 %collective-permute-start.73 = (bf16[192,1536]{1,0:T(8,128)(2,1)S(1)}, bf16[192,1536]{1,0:T(8,128)(2,1)S(1)}, u32[]{:S(2)}, u32[]{:S(2)}) collective-permute-start(bf16[192,1536]{1,0:T(8,128)(2,1)S(1)} %add_convert_fusion.10), channel_id=1, source_target_pairs={{0,24},{1,25},{2,26},{3,27},{4,28},{5,29},{6,30},{7,31},{8,0},{9,1... | collective-permute-start | bytes 1769480 | tf_op jit(solution)/shard_map/ppermute | solution.py:154
  2361.6 55.7 %collective-permute-start.75 = (bf16[48,1536]{1,0:T(8,128)(2,1)}, bf16[48,1536]{1,0:T(8,128)(2,1)}, u32[]{:S(2)}, u32[]{:S(2)}) collective-permute-start(bf16[48,1536]{1,0:T(8,128)(2,1)} %add_convert_fusion.25), channel_id=1, source_target_pairs={{0,4},{1,5},{2,6},{3,7},{4,0},{5,1},{6,2},{7,3},{8,12},{9,13},{10,... | collective-permute-start | bytes 442376 | tf_op jit(solution)/shard_map/ppermute | solution.py:154
  2367.2 67.9 %collective-permute-start.87 = (bf16[384,4096]{1,0:T(8,128)(2,1)}, bf16[384,4096]{1,0:T(8,128)(2,1)}, u32[]{:S(2)}, u32[]{:S(2)}) collective-permute-start(bf16[384,4096]{1,0:T(8,128)(2,1)} %add_convert_fusion), channel_id=1, source_target_pairs={{0,4},{1,5},{2,6},{3,7},{4,0},{5,1},{6,2},{7,3},{8,12},{9,13},{10,... | collective-permute-start | bytes 9437192 | tf_op jit(solution)/shard_map/ppermute | solution.py:154
  2372.4 67.6 %collective-permute-start.81 = (bf16[384,4096]{1,0:T(8,128)(2,1)}, bf16[384,4096]{1,0:T(8,128)(2,1)}, u32[]{:S(2)}, u32[]{:S(2)}) collective-permute-start(bf16[384,4096]{1,0:T(8,128)(2,1)} %add_convert_fusion.1), channel_id=1, source_target_pairs={{0,2},{1,3},{2,0},{3,1},{4,6},{5,7},{6,4},{7,5},{8,10},{9,11},{10,... | collective-permute-start | bytes 9437192 | tf_op jit(solution)/shard_map/ppermute | solution.py:154
  2376.0 44.1 %collective-permute-start.93 = (bf16[512,1536]{1,0:T(8,128)(2,1)}, bf16[512,1536]{1,0:T(8,128)(2,1)}, u32[]{:S(2)}, u32[]{:S(2)}) collective-permute-start(bf16[512,1536]{1,0:T(8,128)(2,1)} %add_convert_fusion.4), channel_id=1, source_target_pairs={{0,24},{1,25},{2,26},{3,27},{4,28},{5,29},{6,30},{7,31},{8,0},{9,1... | collective-permute-start | bytes 4718600 | tf_op jit(solution)/shard_map/ppermute | solution.py:154
  2423.0 39.8 %collective-permute-start.94 = (bf16[512,1536]{1,0:T(8,128)(2,1)S(1)}, bf16[512,1536]{1,0:T(8,128)(2,1)S(1)}, u32[]{:S(2)}, u32[]{:S(2)}) collective-permute-start(bf16[512,1536]{1,0:T(8,128)(2,1)S(1)} %add_convert_fusion.3), channel_id=1, source_target_pairs={{0,24},{1,25},{2,26},{3,27},{4,28},{5,29},{6,30},{7,31},{8,0},{9,1... | collective-permute-start | bytes 4718600 | tf_op jit(solution)/shard_map/ppermute | solution.py:154
  2429.7 39.3 %collective-permute-start.59 = (bf16[384,1536]{1,0:T(8,128)(2,1)S(1)}, bf16[384,1536]{1,0:T(8,128)(2,1)S(1)}, u32[]{:S(2)}, u32[]{:S(2)}) collective-permute-start(bf16[384,1536]{1,0:T(8,128)(2,1)S(1)} %add_convert_fusion.8), channel_id=1, source_target_pairs={{0,2},{1,3},{2,0},{3,1},{4,6},{5,7},{6,4},{7,5},{8,10},{9,11},{10,... | collective-permute-start | bytes 3538952 | tf_op jit(solution)/shard_map/ppermute | solution.py:154
  2432.0 38.5 %collective-permute-start.65 = (bf16[768,768]{1,0:T(8,128)(2,1)S(1)}, bf16[768,768]{1,0:T(8,128)(2,1)S(1)}, u32[]{:S(2)}, u32[]{:S(2)}) collective-permute-start(bf16[768,768]{1,0:T(8,128)(2,1)S(1)} %add_convert_fusion.7), channel_id=1, source_target_pairs={{0,4},{1,5},{2,6},{3,7},{4,0},{5,1},{6,2},{7,3},{8,12},{9,13},{10,... | collective-permute-start | bytes 3538952 | tf_op jit(solution)/shard_map/ppermute | solution.py:154
  2437.8 61.1 %collective-permute-start.88 = (bf16[192,4096]{1,0:T(8,128)(2,1)S(1)}, bf16[192,4096]{1,0:T(8,128)(2,1)S(1)}, u32[]{:S(2)}, u32[]{:S(2)}) collective-permute-start(bf16[192,4096]{1,0:T(8,128)(2,1)S(1)} %add_convert_fusion.5), channel_id=1, source_target_pairs={{0,2},{1,3},{2,0},{3,1},{4,6},{5,7},{6,4},{7,5},{8,10},{9,11},{10,... | collective-permute-start | bytes 4718600 | tf_op jit(solution)/shard_map/ppermute | solution.py:154
  2442.8 62.8 %collective-permute-start.82 = (bf16[192,4096]{1,0:T(8,128)(2,1)S(1)}, bf16[192,4096]{1,0:T(8,128)(2,1)S(1)}, u32[]{:S(2)}, u32[]{:S(2)}) collective-permute-start(bf16[192,4096]{1,0:T(8,128)(2,1)S(1)} %add_convert_fusion.6), channel_id=1, source_target_pairs={{0,4},{1,5},{2,6},{3,7},{4,0},{5,1},{6,2},{7,3},{8,12},{9,13},{10,... | collective-permute-start | bytes 4718600 | tf_op jit(solution)/shard_map/ppermute | solution.py:154
  2464.9 47.5 %collective-permute-start.95 = (bf16[512,1536]{1,0:T(8,128)(2,1)S(1)}, bf16[512,1536]{1,0:T(8,128)(2,1)S(1)}, u32[]{:S(2)}, u32[]{:S(2)}) collective-permute-start(bf16[512,1536]{1,0:T(8,128)(2,1)S(1)} %add_convert_fusion.2), channel_id=1, source_target_pairs={{0,24},{1,25},{2,26},{3,27},{4,28},{5,29},{6,30},{7,31},{8,0},{9,1... | collective-permute-start | bytes 4718600 | tf_op jit(solution)/shard_map/ppermute | solution.py:154
  2469.5 44.8 %collective-permute-start.60 = (bf16[192,1536]{1,0:T(8,128)(2,1)S(1)}, bf16[192,1536]{1,0:T(8,128)(2,1)S(1)}, u32[]{:S(2)}, u32[]{:S(2)}) collective-permute-start(bf16[192,1536]{1,0:T(8,128)(2,1)S(1)} %add_convert_fusion.14), channel_id=1, source_target_pairs={{0,4},{1,5},{2,6},{3,7},{4,0},{5,1},{6,2},{7,3},{8,12},{9,13},{10,... | collective-permute-start | bytes 1769480 | tf_op jit(solution)/shard_map/ppermute | solution.py:154
  2471.0 45.8 %collective-permute-start.66 = (bf16[384,768]{1,0:T(8,128)(2,1)S(1)}, bf16[384,768]{1,0:T(8,128)(2,1)S(1)}, u32[]{:S(2)}, u32[]{:S(2)}) collective-permute-start(bf16[384,768]{1,0:T(8,128)(2,1)S(1)} %add_convert_fusion.13), channel_id=1, source_target_pairs={{0,2},{1,3},{2,0},{3,1},{4,6},{5,7},{6,4},{7,5},{8,10},{9,11},{10,... | collective-permute-start | bytes 1769480 | tf_op jit(solution)/shard_map/ppermute | solution.py:154
  2500.6 37.5 %collective-permute-start.89 = (bf16[48,4096]{1,0:T(8,128)(2,1)S(1)}, bf16[48,4096]{1,0:T(8,128)(2,1)S(1)}, u32[]{:S(2)}, u32[]{:S(2)}) collective-permute-start(bf16[48,4096]{1,0:T(8,128)(2,1)S(1)} %add_convert_fusion.18), channel_id=1, source_target_pairs={{0,24},{1,25},{2,26},{3,27},{4,28},{5,29},{6,30},{7,31},{8,0},{9,1... | collective-permute-start | bytes 1179656 | tf_op jit(solution)/shard_map/ppermute | solution.py:154
  2507.3 32.2 %collective-permute-start.83 = (bf16[48,4096]{1,0:T(8,128)(2,1)S(1)}, bf16[48,4096]{1,0:T(8,128)(2,1)S(1)}, u32[]{:S(2)}, u32[]{:S(2)}) collective-permute-start(bf16[48,4096]{1,0:T(8,128)(2,1)S(1)} %add_convert_fusion.21), channel_id=1, source_target_pairs={{0,24},{1,25},{2,26},{3,27},{4,28},{5,29},{6,30},{7,31},{8,0},{9,1... | collective-permute-start | bytes 1179656 | tf_op jit(solution)/shard_map/ppermute | solution.py:154
  2514.1 47.2 %collective-permute-start.96 = (bf16[256,1536]{1,0:T(8,128)(2,1)S(1)}, bf16[256,1536]{1,0:T(8,128)(2,1)S(1)}, u32[]{:S(2)}, u32[]{:S(2)}) collective-permute-start(bf16[256,1536]{1,0:T(8,128)(2,1)S(1)} %add_convert_fusion.9), channel_id=1, source_target_pairs={{0,2},{1,3},{2,0},{3,1},{4,6},{5,7},{6,4},{7,5},{8,10},{9,11},{10,... | collective-permute-start | bytes 2359304 | tf_op jit(solution)/shard_map/ppermute | solution.py:154
  2544.5 118.6 %collective-permute-start.76 = (f32[73728]{0:T(1024)}, f32[73728]{0:T(1024)}, u32[]{:S(2)}, u32[]{:S(2)}) collective-permute-start(f32[73728]{0:T(1024)} %bitcast.95), channel_id=1, source_target_pairs={{2,0},{5,1},{8,2},{11,3},{14,4},{17,5},{20,6},{23,7},{26,8},{29,9}... | collective-permute-start | bytes 884744 | tf_op jit(solution)/shard_map/ppermute | solution.py:114
  2589.3 83.3 %collective-permute-start.98 = (f32[196608]{0:T(1024)}, f32[196608]{0:T(1024)}, u32[]{:S(2)}, u32[]{:S(2)}) collective-permute-start(f32[196608]{0:T(1024)} %bitcast.101), channel_id=1, source_target_pairs={{2,0},{5,1},{8,2},{11,3},{14,4},{17,5},{20,6},{23,7},{26,8},{29,9}... | collective-permute-start | bytes 2359304 | tf_op jit(solution)/shard_map/ppermute | solution.py:114
  2669.7 29.5 %collective-permute-start.101 = (f32[196608]{0:T(1024)}, f32[196608]{0:T(1024)S(1)}, u32[]{:S(2)}, u32[]{:S(2)}) collective-permute-start(f32[196608]{0:T(1024)} %bitcast.304), channel_id=1, source_target_pairs={{1,0},{4,1},{7,2},{10,3},{13,4},{16,5},{19,6},{22,7},{25,8},{28,9}... | collective-permute-start | bytes 2359304 | tf_op jit(solution)/shard_map/ppermute | solution.py:114
  (129 other events, 3355.4 us)

commit v2 on v1

--- a/solution.py
+++ b/solution.py
@@ -164,37 +164,38 @@
     return jnp.stack(entries).astype(jnp.int32)
 
 
-def place_kernel(table_ref, *refs, lengths, rows):
-    piece_refs, out_ref, sems = (refs[:-2], refs[-2], refs[-1])
-    copies = []
-    for piece_ref, length in zip(piece_refs, lengths):
-        for block in range(length):
-            entry = len(copies)
-            target = pl.ds(pl.multiple_of(table_ref[entry] * rows, rows), rows)
-            copy = pltpu.make_async_copy(
-                piece_ref.at[pl.ds(block * rows, rows), :], out_ref.at[target, :], sems.at[entry]
-            )
-            copy.start()
-            copies.append(copy)
-    for copy in copies:
-        copy.wait()
+def place_kernel(table_ref, *refs, firsts):
+    piece_refs, out_ref = (refs[:-1], refs[-1])
+    entry = pl.program_id(0)
+    for number, piece_ref in enumerate(piece_refs):
+
+        @pl.when((entry >= firsts[number]) & (entry < firsts[number + 1]))
+        def _(piece_ref=piece_ref):
+            out_ref[...] = piece_ref[...]
 
 
 def placed(pieces, table, rows):
     count = table.shape[0]
     width = pieces[0].shape[1]
-    lengths = tuple(piece.shape[0] // rows for piece in pieces)
-    anywhere = pl.BlockSpec(memory_space=pl.ANY)
+    firsts = [0]
+    for piece in pieces:
+        firsts.append(firsts[-1] + piece.shape[0] // rows)
+
+    def block_of(first, last):
+        return pl.BlockSpec(
+            (rows, width), lambda i, table_ref: (jnp.clip(i, first, last - 1) - first, 0)
+        )
+
     return pl.pallas_call(
-        functools.partial(place_kernel, lengths=lengths, rows=rows),
+        functools.partial(place_kernel, firsts=tuple(firsts)),
         grid_spec=pltpu.PrefetchScalarGridSpec(
             num_scalar_prefetch=1,
-            grid=(1,),
-            in_specs=[anywhere] * len(pieces),
-            out_specs=anywhere,
-            scratch_shapes=[pltpu.SemaphoreType.DMA((count,))],
+            grid=(count,),
+            in_specs=[block_of(first, last) for first, last in zip(firsts[:-1], firsts[1:])],
+            out_specs=pl.BlockSpec((rows, width), lambda i, table_ref: (table_ref[i], 0)),
         ),
         out_shape=jax.ShapeDtypeStruct((count * rows, width), pieces[0].dtype),
+        compiler_params=pltpu.CompilerParams(vmem_limit_bytes=32 << 20),
         cost_estimate=pl.CostEstimate(
             flops=0, transcendentals=0, bytes_accessed=4 * count * rows * width
         ),
@@ -238,6 +239,14 @@
         ),
         name="reorder_blocks",
     )(table, value)
+
+
+def summed(value, grid):
+    for axis in reversed(list(grid)):
+        own = value
+        for _ in range(grid[axis] - 1):
+            value = own + shifted(value, axis, 1, grid)
+    return value
 
 
 def sum_scatter(left_cols, right, right_dim, order, index, grid):
@@ -475,13 +484,13 @@
 
     attn_low = attn_master.astype(jnp.bfloat16)
     ffn_low = ffn_master.astype(jnp.bfloat16)
-    gains = lax.psum(
-        jnp.where(
-            index == 0, jnp.stack([attn_low[:D], ffn_low[:D]]).astype(jnp.float32), 0.0
-        ),
-        "seq",
-    )
+    notice = jnp.concatenate(
+        [attn_low[:D], ffn_low[:D], segment_ids.astype(jnp.bfloat16)]
+    ).reshape(1, -1, 128)
+    notices = exchange(jnp.broadcast_to(notice, (count,) + notice.shape[1:]))
+    gains = notices[0, : 2 * D // 128].astype(jnp.float32).reshape(2, D)
     gain_one, gain_two = (gains[0], gains[1])
+    all_ids = notices[:, 2 * D // 128 :].astype(jnp.int32).reshape(-1)
 
     grid = device_grid(count)
     by_axes = (D // count) % 16 == 0
@@ -513,8 +522,6 @@
     gate_weight = gathered(gate_unit, FF, 0)
     up_weight = gathered(up_unit, FF, 1)
     down_weight = gathered(down_unit, D, 2)
-
-    all_ids = lax.all_gather(segment_ids.reshape(1, rows), "seq", axis=0, tiled=True).reshape(-1)
 
     def item_starts(ids):
         return jnp.sum((all_ids < ids[..., None]).astype(jnp.int32), axis=-1)
@@ -749,7 +756,7 @@
     input_norm_grad, grad_one = first_pull(normed_one_grad)
     input_grad = middle_grad + input_norm_grad
 
-    gain_grads = lax.psum(jnp.stack([grad_one, grad_two]), "seq")
+    gain_grads = summed(jnp.stack([grad_one, grad_two]).reshape(-1, 128), grid).reshape(2, D)
     attn_shard = shard_from_units(
         [query_unit, key_value_unit, out_unit], gain_grads[0], index, count
     )

time: 2720 us -> 1190 us (0.44)
  Pallas kernels: 1660 us -> 194 us
  blocking collectives: 125 us -> 0 us
    pallas_call x6, Pallas kernels: 1580 us -> 104 us  [placed(): pl.pallas_call(functools.partial(place_kernel, firsts=tuple(firsts)), gri...]
    psum x2 -> x0, blocking collectives: 90.5 us -> none  [the longest x1 47.6 us: per_device(): gain_grads = lax.psum(jnp.stack([grad_one, grad_two]), 'seq')]
    all_gather x1 -> x0, blocking collectives: 34.9 us -> none  [per_device(): lax.all_gather(segment_ids.reshape(1, rows), 'seq', axis=0, tiled=True)]
    ppermute x82 -> x88, starting transfers between devices: 122 us -> 140 us  [shifted(): return lax.ppermute(value, 'seq', pairs)]
    ppermute x82 -> x88, waiting for transfers between devices: 285 us -> 291 us  [shifted(): return lax.ppermute(value, 'seq', pairs)]
  transfers between devices with their start and end apart: 106 -> 113, of which waited for: 32 -> 36; matrix products, arithmetic and copies ran while one was open for 11% -> 26% of each run, Pallas kernels for 61% -> 16%
where the time goes in v2:
time: 1190 us; the launch traced here: 1170 us
  waiting for transfers between devices  327 us (27%)
  starting transfers between devices  215 us (18%)
  Pallas kernels  194 us (16%)
  matrix products  166 us (14%)
  local copies, waits for them, and re-layouts  154 us (13%)
  other arithmetic  110 us (9%)
    ppermute x88, waiting for transfers between devices, shifted(): return lax.ppermute(value, 'seq', pairs)  291 us
    dot_general x56, matrix products, contract(): lax.dot_general(left, right, (((left_dim,), (right_dim,)), ((), ())), pre...  166 us
    ppermute x88, starting transfers between devices, shifted(): return lax.ppermute(value, 'seq', pairs)  140 us
    pallas_call x6, Pallas kernels, placed(): pl.pallas_call(functools.partial(place_kernel, firsts=tuple(firsts)), gri...  104 us
    pallas_call x2, Pallas kernels, run_kernel(): pl.pallas_call(body, grid_spec=pltpu.PrefetchScalarGridSpec(num_scalar_pr...  71.3 us
    unnamed x225, local copies, waits for them, and re-layouts  48 us
    all_to_all x5, starting transfers between devices, exchange(): return lax.all_to_all(value, 'seq', 0, 0, tiled=True)  26.8 us
    ppermute x6, waiting for transfers between devices, shard_from_units(): lax.ppermute(piece, 'seq', [((3 * i + j) % count, i) for i in range(count)])  24.6 us
  transfers between devices with their start and end apart: 113, of which 36 were waited for; matrix products, arithmetic and copies ran while one was open for 26% of the time, Pallas kernels for 16%

profile of v2, /device:TPU:7, one launch (start us, length us, event | category | flops | bytes accessed | tf_op | source)
XLA Modules:
  0.0 1171.4 jit_solution(15571380683901534261)
XLA Ops:
  9.1 6.4 all-to-all-start
  53.7 6.8 collective-permute-done.11
  74.2 8.4 dynamic-slice_reduce_fusion.2
  90.8 7.6 collective-permute-done.13
  104.5 5.9 collective-permute-done.14
  117.8 8.3 collective-permute-start.16
  126.0 13.6 %collective-permute-done.15.refs_1_ = bf16[768,768]{1,0:T(8,128)(2,1)} collective-permute-done((bf16[768,768]{1,0:T(8,128)(2,1)}, bf16[768,768]{1,0:T(8,128)(2,1)}, u32[]{:S(2)}, u32[]{:S(2)}) %collective-permute-start.15) | collective-permute-done | bytes 1179680 | tf_op jit(solution)/shard_map/ppermute | solution.py:154
  153.8 9.4 place_blocks.7
  174.9 16.4 %place_blocks.6 = bf16[1536,1536]{1,0:T(8,128)(2,1)S(1)} custom-call(s32[32]{0:T(128)S(1)} %stack.138.table_ref, bf16[384,1536]{1,0:T(8,128)(2,1)} %constant_dynamic-update-slice_fusion.refs_0_, bf16[384,1536]{1,0:T(8,128)(2,1)} %collective-permute-done.8.refs_1_, bf16[384,1536]{1,0:T(8,128)(2,1)} %collective-permute-done.9.refs_2_, ...), custom_call_target="tpu_custom_call" | custom-call | bytes 9437184 | tf_op jit(solution)/shard_map/place_blocks/pallas_call | solution.py:189
  195.2 5.2 all-to-all-start.1
  208.1 42.8 %collective-permute-done.42 = bf16[48,4096]{1,0:T(8,128)(2,1)S(1)} collective-permute-done((bf16[48,4096]{1,0:T(8,128)(2,1)}, bf16[48,4096]{1,0:T(8,128)(2,1)S(1)}, u32[]{:S(2)}, u32[]{:S(2)}) %collective-permute-start.42) | collective-permute-done | bytes 393248 | tf_op jit(solution)/shard_map/ppermute | solution.py:154
  253.7 5.6 collective-permute-done.35
  264.1 6.4 collective-permute-start.49
  273.8 16.6 %collective-permute-done.43 = bf16[192,4096]{1,0:T(8,128)(2,1)} collective-permute-done((bf16[192,4096]{1,0:T(8,128)(2,1)}, bf16[192,4096]{1,0:T(8,128)(2,1)}, u32[]{:S(2)}, u32[]{:S(2)}) %collective-permute-start.43) | collective-permute-done | bytes 1572896 | tf_op jit(solution)/shard_map/ppermute | solution.py:154
  297.1 10.1 collective-permute-done.18
  313.0 6.1 collective-permute-start.24
  323.8 8.4 collective-permute-done.24.refs_3_
  335.7 30.2 %collective-permute-done.50.refs_2_ = bf16[512,1536]{1,0:T(8,128)(2,1)} collective-permute-done((bf16[512,1536]{1,0:T(8,128)(2,1)}, bf16[512,1536]{1,0:T(8,128)(2,1)}, u32[]{:S(2)}, u32[]{:S(2)}) %collective-permute-start.50) | collective-permute-done | bytes 1572896 | tf_op jit(solution)/shard_map/ppermute | solution.py:154
  366.7 18.8 %convert_reduce_fusion = s32[4096]{0:T(1024)S(1)} fusion(s32[8192]{0:T(1024)S(1)} %bitcast.343, s32[4096]{0:T(1024)S(1)} %bitcast.346), kind=kLoop, calls=%fused_computation | loop fusion | flops 100659200 | bytes 65536 | tf_op jit(solution)/shard_map/reduce_sum | solution.py:527
  409.8 27.9 %attention_forward.1 = (f32[8,96,512]{2,1,0:T(8,128)}, f32[8,1,512]{2,1,0:T(1,128)S(1)}) custom-call(s32[8]{0:T(128)S(1)} %get-tuple-element.118.low_ref, s32[8]{0:T(128)S(1)} %get-tuple-element.117.high_ref, bf16[8,96,512]{2,1,0:T(8,128)(2,1)S(1)} %copy-done.3, bf16[8192,96]{1,0:T(8,128)(2,1)} %bitcast.311, bf16[8,96,1024]{2,1,0:T(8,128)(2,1)} %reshape.428.value_ref, ...), custom_call_target="tpu_custom_call" | custom-call | flops 20000000000 | bytes 16777216 | tf_op jit(solution)/shard_map/attention_forward/pallas_call | solution.py:387
  455.4 12.5 %place_blocks.8 = bf16[1536,1536]{1,0:T(8,128)(2,1)S(1)} custom-call(s32[32]{0:T(128)S(1)} %stack.148.table_ref, bf16[192,1536]{1,0:T(8,128)(2,1)} %constant_dynamic-update-slice_fusion.10.refs_0_, bf16[192,1536]{1,0:T(8,128)(2,1)} %collective-permute-done.22.refs_1_, bf16[192,1536]{1,0:T(8,128)(2,1)} %collective-permute-done.23.refs_2_, ...), custom_call_target="tpu_custom_call" | custom-call | bytes 9437184 | tf_op jit(solution)/shard_map/place_blocks/pallas_call | solution.py:189
  470.1 22.8 %place_blocks.11 = bf16[4096,1536]{1,0:T(8,128)(2,1)} custom-call(s32[32]{0:T(128)S(1)} %stack.148.table_ref, bf16[512,1536]{1,0:T(8,128)(2,1)} %constant_dynamic-update-slice_fusion.23.refs_0_, bf16[512,1536]{1,0:T(8,128)(2,1)} %collective-permute-done.49.refs_1_, bf16[512,1536]{1,0:T(8,128)(2,1)} %collective-permute-done.50.refs_2_, ...), custom_call_target="tpu_custom_call" | custom-call | bytes 25165824 | tf_op jit(solution)/shard_map/place_blocks/pallas_call | solution.py:189
  503.4 20.6 %place_blocks.9 = bf16[1536,4096]{1,0:T(8,128)(2,1)} custom-call(s32[32]{0:T(128)S(1)} %stack.138.table_ref, bf16[384,4096]{1,0:T(8,128)(2,1)S(1)} %constant_dynamic-update-slice_fusion.13.refs_0_, bf16[384,4096]{1,0:T(8,128)(2,1)} %collective-permute-done.37.refs_1_, bf16[384,4096]{1,0:T(8,128)(2,1)} %collective-permute-done.38.refs_2_, ...), custom_call_target="tpu_custom_call" | custom-call | bytes 25165824 | tf_op jit(solution)/shard_map/place_blocks/pallas_call | solution.py:189
  524.0 22.0 %place_blocks.10 = bf16[1536,4096]{1,0:T(8,128)(2,1)} custom-call(s32[32]{0:T(128)S(1)} %stack.143.table_ref, bf16[384,4096]{1,0:T(8,128)(2,1)} %constant_dynamic-update-slice_fusion.18.refs_0_, bf16[384,4096]{1,0:T(8,128)(2,1)} %collective-permute-done.44.refs_1_, bf16[384,4096]{1,0:T(8,128)(2,1)} %collective-permute-done.45.refs_2_, ...), custom_call_target="tpu_custom_call" | custom-call | bytes 25165824 | tf_op jit(solution)/shard_map/place_blocks/pallas_call | solution.py:189
  560.1 9.8 fusion.215
  569.9 9.8 fusion.214
  579.7 5.6 copy.132
  585.3 5.7 copy.131
  591.1 15.6 %multiply_convert_fusion.1 = (bf16[256,4096]{1,0:T(8,128)(2,1)S(1)}, bf16[256,4096]{1,0:T(8,128)(2,1)}) fusion(f32[256,4096]{1,0:T(8,128)} %fusion.214, f32[256,4096]{1,0:T(8,128)} %fusion.215, bf16[4096,1536]{1,0:T(8,128)(2,1)} %place_blocks.11, bf16[256,1536]{1,0:T(8,128)(2,1)S(1)} %copy-done.26), kind=kOutput, calls=%fused_computation.21 | convolution fusion | flops 3234856960 | bytes 25952256 | tf_op jit(solution)/shard_map/dot_general | solution.py:62
  615.8 7.2 fusion.216
  623.1 10.6 multiply_reduce_fusion
  642.6 4.6 convolution_convert_fusion.6
  652.1 6.4 all-to-all-start.3
  662.3 4.5 convolution_convert_fusion.1
  671.2 4.4 convolution_convert_fusion
  675.5 4.4 convolution_convert_fusion.2
  684.5 43.4 %attention_backward.1 = (f32[8,96,512]{2,1,0:T(8,128)}, f32[8192,96]{1,0:T(8,128)}, f32[8192,96]{1,0:T(8,128)}) custom-call(s32[8]{0:T(128)S(1)} %get-tuple-element.118.low_ref, s32[8]{0:T(128)S(1)} %get-tuple-element.117.high_ref, bf16[8,96,512]{2,1,0:T(8,128)(2,1)S(1)} %copy-done.4, bf16[8,512,96]{2,1,0:T(8,128)(2,1)} %bitcast.293, ...), custom_call_target="tpu_custom_call" | custom-call | flops 49999998976 | bytes 16777216 | tf_op jit(solution)/shard_map/attention_backward/pallas_call | solution.py:387
  727.9 5.3 copy.124
  733.2 5.8 copy.125
  759.5 7.8 collective-permute-done.77
  779.6 4.8 all-to-all-start.4
  795.3 29.0 %collective-permute-done.79 = bf16[192,1536]{1,0:T(8,128)(2,1)S(1)} collective-permute-done((bf16[192,1536]{1,0:T(8,128)(2,1)S(1)}, bf16[192,1536]{1,0:T(8,128)(2,1)S(1)}, u32[]{:S(2)}, u32[]{:S(2)}) %collective-permute-start.79) | collective-permute-done | bytes 589856 | tf_op jit(solution)/shard_map/ppermute | solution.py:154
  828.6 5.0 collective-permute-done.80
  836.6 4.9 add_convert_fusion
  842.1 4.6 add_convert_fusion.1
  850.3 4.6 collective-permute-start.99
  880.7 4.6 reorder_blocks.7
  896.0 6.4 collective-permute-start.100
  917.9 18.5 %collective-permute-done.100 = bf16[512,1536]{1,0:T(8,128)(2,1)S(1)} collective-permute-done((bf16[512,1536]{1,0:T(8,128)(2,1)S(1)}, bf16[512,1536]{1,0:T(8,128)(2,1)S(1)}, u32[]{:S(2)}, u32[]{:S(2)}) %collective-permute-start.100) | collective-permute-done | bytes 1572896 | tf_op jit(solution)/shard_map/ppermute | solution.py:154
  945.3 27.9 %collective-permute-done.94 = bf16[192,4096]{1,0:T(8,128)(2,1)S(1)} collective-permute-done((bf16[192,4096]{1,0:T(8,128)(2,1)S(1)}, bf16[192,4096]{1,0:T(8,128)(2,1)S(1)}, u32[]{:S(2)}, u32[]{:S(2)}) %collective-permute-start.94) | collective-permute-done | bytes 1572896 | tf_op jit(solution)/shard_map/ppermute | solution.py:154
  974.9 5.8 collective-permute-start.95
  992.1 7.3 collective-permute-done.67
  1017.1 6.6 collective-permute-done.96
  1026.6 5.5 collective-permute-done.90
  1041.9 7.1 collective-permute-done.91
  1067.2 8.3 collective-permute-start.58
  1079.9 8.5 collective-permute-done.59
  1101.6 5.3 collective-permute-start.85
  1106.9 4.7 collective-permute-start.83
  1113.8 13.3 %fusion.12 = bf16[256,1536]{0,1:T(8,128)(2,1)} fusion(f32[256,1536]{0,1:T(8,128)S(1)} %copy-done.25, bf16[4096,1536]{1,0:T(8,128)(2,1)} %place_blocks.11, f32[256,4096]{1,0:T(8,128)} %fusion.215, f32[256,4096]{1,0:T(8,128)} %fusion.214), kind=kOutput, calls=%fused_computation.52 | convolution fusion | flops 3228303360 | bytes 23330816 | tf_op jit(solution)/shard_map/dot_general | solution.py:62
  1131.2 4.4 collective-permute-start.106
  1140.0 12.5 %collective-permute-done.106 = f32[196608]{0:T(1024)S(1)} collective-permute-done((f32[196608]{0:T(1024)}, f32[196608]{0:T(1024)S(1)}, u32[]{:S(2)}, u32[]{:S(2)}) %collective-permute-start.106) | collective-permute-done | bytes 786464 | tf_op jit(solution)/shard_map/ppermute | solution.py:114
  1152.5 12.0 %collective-permute-done.107 = f32[196608]{0:T(1024)S(1)} collective-permute-done((f32[196608]{0:T(1024)}, f32[196608]{0:T(1024)S(1)}, u32[]{:S(2)}, u32[]{:S(2)}) %collective-permute-start.107) | collective-permute-done | bytes 786464 | tf_op jit(solution)/shard_map/ppermute | solution.py:114
  1164.5 6.7 multiply_subtract_fusion
  (617 shorter events, 459.8 us)
Async XLA Ops:
  9.1 107.9 %all-to-all-start = ((bf16[32,26,128]{2,1,0:T(8,128)(2,1)}), bf16[32,26,128]{2,1,0:T(8,128)(2,1)}, u32[]{:S(2)}, u32[]{:S(2)}) async-start(bf16[32,26,128]{2,1,0:T(8,128)(2,1)} %broadcast_in_dim.13), calls=%async_computation | async-start | bytes 524288 | tf_op jit(solution)/shard_map/all_to_all | solution.py:480
  31.6 36.2 %collective-permute-start.30 = (bf16[196608]{0:T(1024)(128)(2,1)}, bf16[196608]{0:T(1024)(128)(2,1)S(1)}, u32[]{:S(2)}, u32[]{:S(2)}) collective-permute-start(bf16[196608]{0:T(1024)(128)(2,1)} %get-tuple-element.91), channel_id=1, source_target_pairs={{0,0},{1,3},{2,6},{3,9},{4,12},{5,15},{6,18},{7,21},{8,24},{9,27},... | collective-permute-start | bytes 1179656 | tf_op jit(solution)/shard_map/ppermute | solution.py:90
  33.8 36.7 %collective-permute-start.31 = (bf16[196608]{0:T(1024)(128)(2,1)}, bf16[196608]{0:T(1024)(128)(2,1)S(1)}, u32[]{:S(2)}, u32[]{:S(2)}) collective-permute-start(bf16[196608]{0:T(1024)(128)(2,1)} %get-tuple-element.92), channel_id=1, source_target_pairs={{0,1},{1,4},{2,7},{3,10},{4,13},{5,16},{6,19},{7,22},{8,25},{9,28}... | collective-permute-start | bytes 1179656 | tf_op jit(solution)/shard_map/ppermute | solution.py:90
  36.3 34.7 %collective-permute-start.32 = (bf16[196608]{0:T(1024)(128)(2,1)S(1)}, bf16[196608]{0:T(1024)(128)(2,1)S(1)}, u32[]{:S(2)}, u32[]{:S(2)}) collective-permute-start(bf16[196608]{0:T(1024)(128)(2,1)S(1)} %get-tuple-element.93), channel_id=1, source_target_pairs={{0,2},{1,5},{2,8},{3,11},{4,14},{5,17},{6,20},{7,23},{8,26},{9,29}... | collective-permute-start | bytes 1179656 | tf_op jit(solution)/shard_map/ppermute | solution.py:90
  60.5 57.3 %collective-permute-start.21 = (bf16[96,1536]{1,0:T(8,128)(2,1)}, bf16[96,1536]{1,0:T(8,128)(2,1)}, u32[]{:S(2)}, u32[]{:S(2)}) collective-permute-start(bf16[96,1536]{1,0:T(8,128)(2,1)} %pad_maximum_fusion.18), channel_id=1, source_target_pairs={{0,2},{1,3},{2,0},{3,1},{4,6},{5,7},{6,4},{7,5},{8,10},{9,11},{10,... | collective-permute-start | bytes 884744 | tf_op jit(solution)/shard_map/ppermute | solution.py:154
  83.5 64.0 %collective-permute-start.40 = (bf16[48,4096]{1,0:T(8,128)(2,1)}, bf16[48,4096]{1,0:T(8,128)(2,1)}, u32[]{:S(2)}, u32[]{:S(2)}) collective-permute-start(bf16[48,4096]{1,0:T(8,128)(2,1)} %reshape.434), channel_id=1, source_target_pairs={{0,8},{1,9},{2,10},{3,11},{4,12},{5,13},{6,14},{7,15},{8,16},{9,17... | collective-permute-start | bytes 1179656 | tf_op jit(solution)/shard_map/ppermute | solution.py:154
  87.5 58.0 %collective-permute-start.47 = (bf16[128,1536]{1,0:T(8,128)(2,1)}, bf16[128,1536]{1,0:T(8,128)(2,1)}, u32[]{:S(2)}, u32[]{:S(2)}) collective-permute-start(bf16[128,1536]{1,0:T(8,128)(2,1)} %reshape.435), channel_id=1, source_target_pairs={{0,4},{1,5},{2,6},{3,7},{4,0},{5,1},{6,2},{7,3},{8,12},{9,13},{10,... | collective-permute-start | bytes 1179656 | tf_op jit(solution)/shard_map/ppermute | solution.py:154
  111.2 28.4 %collective-permute-start.15 = (bf16[768,768]{1,0:T(8,128)(2,1)}, bf16[768,768]{1,0:T(8,128)(2,1)}, u32[]{:S(2)}, u32[]{:S(2)}) collective-permute-start(bf16[768,768]{1,0:T(8,128)(2,1)} %constant_dynamic-update-slice_fusion.5.refs_0_), channel_id=1, source_target_pairs={{0,4},{1,5},{2,6},{3,7},{4,0},{5,1},{6,2},{7,3},{8,12},{9,13},{10,... | collective-permute-start | bytes 3538952 | tf_op jit(solution)/shard_map/ppermute | solution.py:154
  116.1 33.2 %collective-permute-start.8 = (bf16[384,1536]{1,0:T(8,128)(2,1)}, bf16[384,1536]{1,0:T(8,128)(2,1)}, u32[]{:S(2)}, u32[]{:S(2)}) collective-permute-start(bf16[384,1536]{1,0:T(8,128)(2,1)} %constant_dynamic-update-slice_fusion.refs_0_), channel_id=1, source_target_pairs={{0,2},{1,3},{2,0},{3,1},{4,6},{5,7},{6,4},{7,5},{8,10},{9,11},{10,... | collective-permute-start | bytes 3538952 | tf_op jit(solution)/shard_map/ppermute | solution.py:154
  117.8 33.9 %collective-permute-start.16 = (bf16[768,768]{1,0:T(8,128)(2,1)}, bf16[768,768]{1,0:T(8,128)(2,1)S(1)}, u32[]{:S(2)}, u32[]{:S(2)}) collective-permute-start(bf16[768,768]{1,0:T(8,128)(2,1)} %constant_dynamic-update-slice_fusion.5.refs_0_), channel_id=1, source_target_pairs={{0,1},{1,0},{2,3},{3,2},{4,5},{5,4},{6,7},{7,6},{8,9},{9,8},{10,11... | collective-permute-start | bytes 3538952 | tf_op jit(solution)/shard_map/ppermute | solution.py:154
  151.7 49.7 %collective-permute-start.22 = (bf16[192,1536]{1,0:T(8,128)(2,1)}, bf16[192,1536]{1,0:T(8,128)(2,1)}, u32[]{:S(2)}, u32[]{:S(2)}) collective-permute-start(bf16[192,1536]{1,0:T(8,128)(2,1)} %constant_dynamic-update-slice_fusion.10.refs_0_), channel_id=1, source_target_pairs={{0,8},{1,9},{2,10},{3,11},{4,12},{5,13},{6,14},{7,15},{8,16},{9,17... | collective-permute-start | bytes 1769480 | tf_op jit(solution)/shard_map/ppermute | solution.py:154
  153.8 108.2 %collective-permute-start.48 = (bf16[256,1536]{1,0:T(8,128)(2,1)}, bf16[256,1536]{1,0:T(8,128)(2,1)}, u32[]{:S(2)}, u32[]{:S(2)}) collective-permute-start(bf16[256,1536]{1,0:T(8,128)(2,1)} %pad_maximum_fusion.13), channel_id=1, source_target_pairs={{0,2},{1,3},{2,0},{3,1},{4,6},{5,7},{6,4},{7,5},{8,10},{9,11},{10,... | collective-permute-start | bytes 2359304 | tf_op jit(solution)/shard_map/ppermute | solution.py:154
  171.5 31.2 %collective-permute-start.41 = (bf16[48,4096]{1,0:T(8,128)(2,1)}, bf16[48,4096]{1,0:T(8,128)(2,1)}, u32[]{:S(2)}, u32[]{:S(2)}) collective-permute-start(bf16[48,4096]{1,0:T(8,128)(2,1)} %collective-permute-done.40), channel_id=1, source_target_pairs={{0,8},{1,9},{2,10},{3,11},{4,12},{5,13},{6,14},{7,15},{8,16},{9,17... | collective-permute-start | bytes 1179656 | tf_op jit(solution)/shard_map/ppermute | solution.py:154
  171.9 32.1 %collective-permute-start.34 = (bf16[48,4096]{1,0:T(8,128)(2,1)}, bf16[48,4096]{1,0:T(8,128)(2,1)}, u32[]{:S(2)}, u32[]{:S(2)}) collective-permute-start(bf16[48,4096]{1,0:T(8,128)(2,1)} %collective-permute-done.33), channel_id=1, source_target_pairs={{0,8},{1,9},{2,10},{3,11},{4,12},{5,13},{6,14},{7,15},{8,16},{9,17... | collective-permute-start | bytes 1179656 | tf_op jit(solution)/shard_map/ppermute | solution.py:154
  195.2 76.1 %all-to-all-start.1 = ((bf16[32,192,128]{2,1,0:T(8,128)(2,1)}), bf16[32,192,128]{2,1,0:T(8,128)(2,1)}, u32[]{:S(2)}, u32[]{:S(2)}) async-start(bf16[32,192,128]{2,1,0:T(8,128)(2,1)} %pad_maximum_fusion.3), calls=%async_computation.1 | async-start | bytes 3145728 | tf_op jit(solution)/shard_map/all_to_all | solution.py:480
  201.4 95.7 %collective-permute-start.23 = (bf16[192,1536]{1,0:T(8,128)(2,1)}, bf16[192,1536]{1,0:T(8,128)(2,1)}, u32[]{:S(2)}, u32[]{:S(2)}) collective-permute-start(bf16[192,1536]{1,0:T(8,128)(2,1)} %collective-permute-done.22.refs_1_), channel_id=1, source_target_pairs={{0,8},{1,9},{2,10},{3,11},{4,12},{5,13},{6,14},{7,15},{8,16},{9,17... | collective-permute-start | bytes 1769480 | tf_op jit(solution)/shard_map/ppermute | solution.py:154
  202.7 48.2 %collective-permute-start.42 = (bf16[48,4096]{1,0:T(8,128)(2,1)}, bf16[48,4096]{1,0:T(8,128)(2,1)S(1)}, u32[]{:S(2)}, u32[]{:S(2)}) collective-permute-start(bf16[48,4096]{1,0:T(8,128)(2,1)} %collective-permute-done.41), channel_id=1, source_target_pairs={{0,8},{1,9},{2,10},{3,11},{4,12},{5,13},{6,14},{7,15},{8,16},{9,17... | collective-permute-start | bytes 1179656 | tf_op jit(solution)/shard_map/ppermute | solution.py:154
  204.0 55.3 %collective-permute-start.35 = (bf16[48,4096]{1,0:T(8,128)(2,1)}, bf16[48,4096]{1,0:T(8,128)(2,1)S(1)}, u32[]{:S(2)}, u32[]{:S(2)}) collective-permute-start(bf16[48,4096]{1,0:T(8,128)(2,1)} %collective-permute-done.34), channel_id=1, source_target_pairs={{0,8},{1,9},{2,10},{3,11},{4,12},{5,13},{6,14},{7,15},{8,16},{9,17... | collective-permute-start | bytes 1179656 | tf_op jit(solution)/shard_map/ppermute | solution.py:154
  253.4 37.1 %collective-permute-start.43 = (bf16[192,4096]{1,0:T(8,128)(2,1)}, bf16[192,4096]{1,0:T(8,128)(2,1)}, u32[]{:S(2)}, u32[]{:S(2)}) collective-permute-start(bf16[192,4096]{1,0:T(8,128)(2,1)} %pad_maximum_fusion.6), channel_id=1, source_target_pairs={{0,2},{1,3},{2,0},{3,1},{4,6},{5,7},{6,4},{7,5},{8,10},{9,11},{10,... | collective-permute-start | bytes 4718600 | tf_op jit(solution)/shard_map/ppermute | solution.py:154
  261.8 57.8 %collective-permute-start.36 = (bf16[192,4096]{1,0:T(8,128)(2,1)}, bf16[192,4096]{1,0:T(8,128)(2,1)}, u32[]{:S(2)}, u32[]{:S(2)}) collective-permute-start(bf16[192,4096]{1,0:T(8,128)(2,1)} %pad_maximum_fusion.5), channel_id=1, source_target_pairs={{0,4},{1,5},{2,6},{3,7},{4,0},{5,1},{6,2},{7,3},{8,12},{9,13},{10,... | collective-permute-start | bytes 4718600 | tf_op jit(solution)/shard_map/ppermute | solution.py:154
  264.1 55.0 %collective-permute-start.49 = (bf16[512,1536]{1,0:T(8,128)(2,1)}, bf16[512,1536]{1,0:T(8,128)(2,1)}, u32[]{:S(2)}, u32[]{:S(2)}) collective-permute-start(bf16[512,1536]{1,0:T(8,128)(2,1)} %constant_dynamic-update-slice_fusion.23.refs_0_), channel_id=1, source_target_pairs={{0,8},{1,9},{2,10},{3,11},{4,12},{5,13},{6,14},{7,15},{8,16},{9,17... | collective-permute-start | bytes 4718600 | tf_op jit(solution)/shard_map/ppermute | solution.py:154
  272.5 34.7 %collective-permute-start.18 = (bf16[32,96,128]{2,1,0:T(8,128)(2,1)S(1)}, bf16[32,96,128]{2,1,0:T(8,128)(2,1)S(1)}, u32[]{:S(2)}, u32[]{:S(2)}) collective-permute-start(bf16[32,96,128]{2,1,0:T(8,128)(2,1)S(1)} %slice.724), channel_id=1, source_target_pairs={{0,2},{1,3},{2,0},{3,1},{4,6},{5,7},{6,4},{7,5},{8,10},{9,11},{10,... | collective-permute-start | bytes 2359304 | tf_op jit(solution)/shard_map/ppermute | solution.py:483
  319.1 46.8 %collective-permute-start.50 = (bf16[512,1536]{1,0:T(8,128)(2,1)}, bf16[512,1536]{1,0:T(8,128)(2,1)}, u32[]{:S(2)}, u32[]{:S(2)}) collective-permute-start(bf16[512,1536]{1,0:T(8,128)(2,1)} %collective-permute-done.49.refs_1_), channel_id=1, source_target_pairs={{0,8},{1,9},{2,10},{3,11},{4,12},{5,13},{6,14},{7,15},{8,16},{9,17... | collective-permute-start | bytes 4718600 | tf_op jit(solution)/shard_map/ppermute | solution.py:154
  319.6 47.0 %collective-permute-start.19 = (bf16[2,1,32,96,128]{4,3,2,0,1:T(8,128)(2,1)}, bf16[2,1,32,96,128]{4,3,2,0,1:T(8,128)(2,1)}, u32[]{:S(2)}, u32[]{:S(2)}) collective-permute-start(bf16[2,1,32,96,128]{4,3,2,0,1:T(8,128)(2,1)} %maximum_bitcast_fusion), channel_id=1, source_target_pairs={{0,1},{1,0},{2,3},{3,2},{4,5},{5,4},{6,7},{7,6},{8,9},{9,8},{10,11... | collective-permute-start | bytes 4718600 | tf_op jit(solution)/shard_map/ppermute | solution.py:483
  322.6 84.9 %collective-permute-start.37 = (bf16[384,4096]{1,0:T(8,128)(2,1)S(1)}, bf16[384,4096]{1,0:T(8,128)(2,1)}, u32[]{:S(2)}, u32[]{:S(2)}) collective-permute-start(bf16[384,4096]{1,0:T(8,128)(2,1)S(1)} %constant_dynamic-update-slice_fusion.13.refs_0_), channel_id=1, source_target_pairs={{0,2},{1,3},{2,0},{3,1},{4,6},{5,7},{6,4},{7,5},{8,10},{9,11},{10,... | collective-permute-start | bytes 9437192 | tf_op jit(solution)/shard_map/ppermute | solution.py:154
  323.4 84.8 %collective-permute-start.44 = (bf16[384,4096]{1,0:T(8,128)(2,1)}, bf16[384,4096]{1,0:T(8,128)(2,1)}, u32[]{:S(2)}, u32[]{:S(2)}) collective-permute-start(bf16[384,4096]{1,0:T(8,128)(2,1)} %constant_dynamic-update-slice_fusion.18.refs_0_), channel_id=1, source_target_pairs={{0,4},{1,5},{2,6},{3,7},{4,0},{5,1},{6,2},{7,3},{8,12},{9,13},{10,... | collective-permute-start | bytes 9437192 | tf_op jit(solution)/shard_map/ppermute | solution.py:154
  335.3 69.4 %collective-permute-start.52 = (bf16[512,1536]{1,0:T(8,128)(2,1)}, bf16[512,1536]{1,0:T(8,128)(2,1)}, u32[]{:S(2)}, u32[]{:S(2)}) collective-permute-start(bf16[512,1536]{1,0:T(8,128)(2,1)} %constant_dynamic-update-slice_fusion.23.refs_0_), channel_id=1, source_target_pairs={{0,1},{1,0},{2,3},{3,2},{4,5},{5,4},{6,7},{7,6},{8,9},{9,8},{10,11... | collective-permute-start | bytes 4718600 | tf_op jit(solution)/shard_map/ppermute | solution.py:154
  365.9 39.3 %collective-permute-start.53 = (bf16[512,1536]{1,0:T(8,128)(2,1)}, bf16[512,1536]{1,0:T(8,128)(2,1)}, u32[]{:S(2)}, u32[]{:S(2)}) collective-permute-start(bf16[512,1536]{1,0:T(8,128)(2,1)} %collective-permute-done.49.refs_1_), channel_id=1, source_target_pairs={{0,1},{1,0},{2,3},{3,2},{4,5},{5,4},{6,7},{7,6},{8,9},{9,8},{10,11... | collective-permute-start | bytes 4718600 | tf_op jit(solution)/shard_map/ppermute | solution.py:154
  366.7 38.6 %collective-permute-start.54 = (bf16[512,1536]{1,0:T(8,128)(2,1)}, bf16[512,1536]{1,0:T(8,128)(2,1)}, u32[]{:S(2)}, u32[]{:S(2)}) collective-permute-start(bf16[512,1536]{1,0:T(8,128)(2,1)} %collective-permute-done.50.refs_2_), channel_id=1, source_target_pairs={{0,1},{1,0},{2,3},{3,2},{4,5},{5,4},{6,7},{7,6},{8,9},{9,8},{10,11... | collective-permute-start | bytes 4718600 | tf_op jit(solution)/shard_map/ppermute | solution.py:154
  404.7 98.6 %collective-permute-start.38 = (bf16[384,4096]{1,0:T(8,128)(2,1)S(1)}, bf16[384,4096]{1,0:T(8,128)(2,1)}, u32[]{:S(2)}, u32[]{:S(2)}) collective-permute-start(bf16[384,4096]{1,0:T(8,128)(2,1)S(1)} %constant_dynamic-update-slice_fusion.13.refs_0_), channel_id=1, source_target_pairs={{0,1},{1,0},{2,3},{3,2},{4,5},{5,4},{6,7},{7,6},{8,9},{9,8},{10,11... | collective-permute-start | bytes 9437192 | tf_op jit(solution)/shard_map/ppermute | solution.py:154
  405.2 118.8 %collective-permute-start.45 = (bf16[384,4096]{1,0:T(8,128)(2,1)}, bf16[384,4096]{1,0:T(8,128)(2,1)}, u32[]{:S(2)}, u32[]{:S(2)}) collective-permute-start(bf16[384,4096]{1,0:T(8,128)(2,1)} %constant_dynamic-update-slice_fusion.18.refs_0_), channel_id=1, source_target_pairs={{0,1},{1,0},{2,3},{3,2},{4,5},{5,4},{6,7},{7,6},{8,9},{9,8},{10,11... | collective-permute-start | bytes 9437192 | tf_op jit(solution)/shard_map/ppermute | solution.py:154
  405.3 37.6 %collective-permute-start.51 = (bf16[512,1536]{1,0:T(8,128)(2,1)}, bf16[512,1536]{1,0:T(8,128)(2,1)}, u32[]{:S(2)}, u32[]{:S(2)}) collective-permute-start(bf16[512,1536]{1,0:T(8,128)(2,1)} %collective-permute-done.50.refs_2_), channel_id=1, source_target_pairs={{0,8},{1,9},{2,10},{3,11},{4,12},{5,13},{6,14},{7,15},{8,16},{9,17... | collective-permute-start | bytes 4718600 | tf_op jit(solution)/shard_map/ppermute | solution.py:154
  407.5 95.9 %collective-permute-start.39 = (bf16[384,4096]{1,0:T(8,128)(2,1)}, bf16[384,4096]{1,0:T(8,128)(2,1)}, u32[]{:S(2)}, u32[]{:S(2)}) collective-permute-start(bf16[384,4096]{1,0:T(8,128)(2,1)} %collective-permute-done.37.refs_1_), channel_id=1, source_target_pairs={{0,1},{1,0},{2,3},{3,2},{4,5},{5,4},{6,7},{7,6},{8,9},{9,8},{10,11... | collective-permute-start | bytes 9437192 | tf_op jit(solution)/shard_map/ppermute | solution.py:154
  408.2 115.8 %collective-permute-start.46 = (bf16[384,4096]{1,0:T(8,128)(2,1)}, bf16[384,4096]{1,0:T(8,128)(2,1)}, u32[]{:S(2)}, u32[]{:S(2)}) collective-permute-start(bf16[384,4096]{1,0:T(8,128)(2,1)} %collective-permute-done.44.refs_1_), channel_id=1, source_target_pairs={{0,1},{1,0},{2,3},{3,2},{4,5},{5,4},{6,7},{7,6},{8,9},{9,8},{10,11... | collective-permute-start | bytes 9437192 | tf_op jit(solution)/shard_map/ppermute | solution.py:154
  445.1 100.9 %all-to-all-start.2 = ((bf16[32,96,128]{2,1,0:T(8,128)(2,1)}), bf16[32,96,128]{2,1,0:T(8,128)(2,1)}, u32[]{:S(2)}, u32[]{:S(2)}) async-start(bf16[32,96,128]{2,1,0:T(8,128)(2,1)} %bitcast.297), calls=%async_computation.2 | async-start | bytes 1572864 | tf_op jit(solution)/shard_map/all_to_all | solution.py:480
  652.1 27.8 %all-to-all-start.3 = ((bf16[32,96,128]{2,1,0:T(8,128)(2,1)}), bf16[32,96,128]{2,1,0:T(8,128)(2,1)}, u32[]{:S(2)}, u32[]{:S(2)}) async-start(bf16[32,96,128]{2,1,0:T(8,128)(2,1)} %bitcast.299), calls=%async_computation.3 | async-start | bytes 1572864 | tf_op jit(solution)/shard_map/all_to_all | solution.py:480
  661.9 88.2 %collective-permute-start.76 = (bf16[768,1536]{1,0:T(8,128)(2,1)}, bf16[768,1536]{1,0:T(8,128)(2,1)}, u32[]{:S(2)}, u32[]{:S(2)}) collective-permute-start(bf16[768,1536]{1,0:T(8,128)(2,1)} %convolution_convert_fusion.3), channel_id=1, source_target_pairs={{0,1},{1,0},{2,3},{3,2},{4,5},{5,4},{6,7},{7,6},{8,9},{9,8},{10,11... | collective-permute-start | bytes 7077896 | tf_op jit(solution)/shard_map/ppermute | solution.py:154
  666.8 169.8 %collective-permute-start.92 = (bf16[768,4096]{1,0:T(8,128)(2,1)}, bf16[768,4096]{1,0:T(8,128)(2,1)}, u32[]{:S(2)}, u32[]{:S(2)}) collective-permute-start(bf16[768,4096]{1,0:T(8,128)(2,1)} %convolution_convert_fusion.1), channel_id=1, source_target_pairs={{0,1},{1,0},{2,3},{3,2},{4,5},{5,4},{6,7},{7,6},{8,9},{9,8},{10,11... | collective-permute-start | bytes 18874376 | tf_op jit(solution)/shard_map/ppermute | solution.py:154
  743.7 98.4 %collective-permute-start.86 = (bf16[768,4096]{1,0:T(8,128)(2,1)}, bf16[768,4096]{1,0:T(8,128)(2,1)}, u32[]{:S(2)}, u32[]{:S(2)}) collective-permute-start(bf16[768,4096]{1,0:T(8,128)(2,1)} %convolution_convert_fusion.2), channel_id=1, source_target_pairs={{0,1},{1,0},{2,3},{3,2},{4,5},{5,4},{6,7},{7,6},{8,9},{9,8},{10,11... | collective-permute-start | bytes 18874376 | tf_op jit(solution)/shard_map/ppermute | solution.py:154
  744.1 103.0 %collective-permute-start.98 = (bf16[2048,1536]{1,0:T(8,128)(2,1)}, bf16[2048,1536]{1,0:T(8,128)(2,1)}, u32[]{:S(2)}, u32[]{:S(2)}) collective-permute-start(bf16[2048,1536]{1,0:T(8,128)(2,1)} %convolution_convert_fusion), channel_id=1, source_target_pairs={{0,1},{1,0},{2,3},{3,2},{4,5},{5,4},{6,7},{7,6},{8,9},{9,8},{10,11... | collective-permute-start | bytes 18874376 | tf_op jit(solution)/shard_map/ppermute | solution.py:154
  779.6 75.3 %all-to-all-start.4 = ((bf16[32,192,128]{2,1,0:T(8,128)(2,1)}), bf16[32,192,128]{2,1,0:T(8,128)(2,1)}, u32[]{:S(2)}, u32[]{:S(2)}) async-start(bf16[32,192,128]{2,1,0:T(8,128)(2,1)} %pad_maximum_fusion.8), calls=%async_computation.4 | async-start | bytes 3145728 | tf_op jit(solution)/shard_map/all_to_all | solution.py:480
  786.3 38.0 %collective-permute-start.79 = (bf16[192,1536]{1,0:T(8,128)(2,1)S(1)}, bf16[192,1536]{1,0:T(8,128)(2,1)S(1)}, u32[]{:S(2)}, u32[]{:S(2)}) collective-permute-start(bf16[192,1536]{1,0:T(8,128)(2,1)S(1)} %add_convert_fusion.10), channel_id=1, source_target_pairs={{0,24},{1,25},{2,26},{3,27},{4,28},{5,29},{6,30},{7,31},{8,0},{9,1... | collective-permute-start | bytes 1769480 | tf_op jit(solution)/shard_map/ppermute | solution.py:154
  835.7 54.5 %collective-permute-start.81 = (bf16[48,1536]{1,0:T(8,128)(2,1)}, bf16[48,1536]{1,0:T(8,128)(2,1)}, u32[]{:S(2)}, u32[]{:S(2)}) collective-permute-start(bf16[48,1536]{1,0:T(8,128)(2,1)} %add_convert_fusion.25), channel_id=1, source_target_pairs={{0,4},{1,5},{2,6},{3,7},{4,0},{5,1},{6,2},{7,3},{8,12},{9,13},{10,... | collective-permute-start | bytes 442376 | tf_op jit(solution)/shard_map/ppermute | solution.py:154
  841.5 67.9 %collective-permute-start.93 = (bf16[384,4096]{1,0:T(8,128)(2,1)}, bf16[384,4096]{1,0:T(8,128)(2,1)}, u32[]{:S(2)}, u32[]{:S(2)}) collective-permute-start(bf16[384,4096]{1,0:T(8,128)(2,1)} %add_convert_fusion), channel_id=1, source_target_pairs={{0,4},{1,5},{2,6},{3,7},{4,0},{5,1},{6,2},{7,3},{8,12},{9,13},{10,... | collective-permute-start | bytes 9437192 | tf_op jit(solution)/shard_map/ppermute | solution.py:154
  846.7 67.6 %collective-permute-start.87 = (bf16[384,4096]{1,0:T(8,128)(2,1)}, bf16[384,4096]{1,0:T(8,128)(2,1)}, u32[]{:S(2)}, u32[]{:S(2)}) collective-permute-start(bf16[384,4096]{1,0:T(8,128)(2,1)} %add_convert_fusion.1), channel_id=1, source_target_pairs={{0,2},{1,3},{2,0},{3,1},{4,6},{5,7},{6,4},{7,5},{8,10},{9,11},{10,... | collective-permute-start | bytes 9437192 | tf_op jit(solution)/shard_map/ppermute | solution.py:154
  850.3 42.7 %collective-permute-start.99 = (bf16[512,1536]{1,0:T(8,128)(2,1)}, bf16[512,1536]{1,0:T(8,128)(2,1)}, u32[]{:S(2)}, u32[]{:S(2)}) collective-permute-start(bf16[512,1536]{1,0:T(8,128)(2,1)} %add_convert_fusion.4), channel_id=1, source_target_pairs={{0,24},{1,25},{2,26},{3,27},{4,28},{5,29},{6,30},{7,31},{8,0},{9,1... | collective-permute-start | bytes 4718600 | tf_op jit(solution)/shard_map/ppermute | solution.py:154
  896.0 40.5 %collective-permute-start.100 = (bf16[512,1536]{1,0:T(8,128)(2,1)S(1)}, bf16[512,1536]{1,0:T(8,128)(2,1)S(1)}, u32[]{:S(2)}, u32[]{:S(2)}) collective-permute-start(bf16[512,1536]{1,0:T(8,128)(2,1)S(1)} %add_convert_fusion.3), channel_id=1, source_target_pairs={{0,24},{1,25},{2,26},{3,27},{4,28},{5,29},{6,30},{7,31},{8,0},{9,1... | collective-permute-start | bytes 4718600 | tf_op jit(solution)/shard_map/ppermute | solution.py:154
  903.3 39.3 %collective-permute-start.65 = (bf16[384,1536]{1,0:T(8,128)(2,1)S(1)}, bf16[384,1536]{1,0:T(8,128)(2,1)S(1)}, u32[]{:S(2)}, u32[]{:S(2)}) collective-permute-start(bf16[384,1536]{1,0:T(8,128)(2,1)S(1)} %add_convert_fusion.8), channel_id=1, source_target_pairs={{0,2},{1,3},{2,0},{3,1},{4,6},{5,7},{6,4},{7,5},{8,10},{9,11},{10,... | collective-permute-start | bytes 3538952 | tf_op jit(solution)/shard_map/ppermute | solution.py:154
  905.4 38.3 %collective-permute-start.71 = (bf16[768,768]{1,0:T(8,128)(2,1)S(1)}, bf16[768,768]{1,0:T(8,128)(2,1)S(1)}, u32[]{:S(2)}, u32[]{:S(2)}) collective-permute-start(bf16[768,768]{1,0:T(8,128)(2,1)S(1)} %add_convert_fusion.7), channel_id=1, source_target_pairs={{0,4},{1,5},{2,6},{3,7},{4,0},{5,1},{6,2},{7,3},{8,12},{9,13},{10,... | collective-permute-start | bytes 3538952 | tf_op jit(solution)/shard_map/ppermute | solution.py:154
  912.1 61.2 %collective-permute-start.94 = (bf16[192,4096]{1,0:T(8,128)(2,1)S(1)}, bf16[192,4096]{1,0:T(8,128)(2,1)S(1)}, u32[]{:S(2)}, u32[]{:S(2)}) collective-permute-start(bf16[192,4096]{1,0:T(8,128)(2,1)S(1)} %add_convert_fusion.5), channel_id=1, source_target_pairs={{0,2},{1,3},{2,0},{3,1},{4,6},{5,7},{6,4},{7,5},{8,10},{9,11},{10,... | collective-permute-start | bytes 4718600 | tf_op jit(solution)/shard_map/ppermute | solution.py:154
  917.1 63.7 %collective-permute-start.88 = (bf16[192,4096]{1,0:T(8,128)(2,1)S(1)}, bf16[192,4096]{1,0:T(8,128)(2,1)S(1)}, u32[]{:S(2)}, u32[]{:S(2)}) collective-permute-start(bf16[192,4096]{1,0:T(8,128)(2,1)S(1)} %add_convert_fusion.6), channel_id=1, source_target_pairs={{0,4},{1,5},{2,6},{3,7},{4,0},{5,1},{6,2},{7,3},{8,12},{9,13},{10,... | collective-permute-start | bytes 4718600 | tf_op jit(solution)/shard_map/ppermute | solution.py:154
  938.5 48.0 %collective-permute-start.101 = (bf16[512,1536]{1,0:T(8,128)(2,1)S(1)}, bf16[512,1536]{1,0:T(8,128)(2,1)S(1)}, u32[]{:S(2)}, u32[]{:S(2)}) collective-permute-start(bf16[512,1536]{1,0:T(8,128)(2,1)S(1)} %add_convert_fusion.2), channel_id=1, source_target_pairs={{0,24},{1,25},{2,26},{3,27},{4,28},{5,29},{6,30},{7,31},{8,0},{9,1... | collective-permute-start | bytes 4718600 | tf_op jit(solution)/shard_map/ppermute | solution.py:154
  943.1 45.4 %collective-permute-start.66 = (bf16[192,1536]{1,0:T(8,128)(2,1)S(1)}, bf16[192,1536]{1,0:T(8,128)(2,1)S(1)}, u32[]{:S(2)}, u32[]{:S(2)}) collective-permute-start(bf16[192,1536]{1,0:T(8,128)(2,1)S(1)} %add_convert_fusion.14), channel_id=1, source_target_pairs={{0,4},{1,5},{2,6},{3,7},{4,0},{5,1},{6,2},{7,3},{8,12},{9,13},{10,... | collective-permute-start | bytes 1769480 | tf_op jit(solution)/shard_map/ppermute | solution.py:154
  944.3 46.9 %collective-permute-start.72 = (bf16[384,768]{1,0:T(8,128)(2,1)S(1)}, bf16[384,768]{1,0:T(8,128)(2,1)S(1)}, u32[]{:S(2)}, u32[]{:S(2)}) collective-permute-start(bf16[384,768]{1,0:T(8,128)(2,1)S(1)} %add_convert_fusion.13), channel_id=1, source_target_pairs={{0,2},{1,3},{2,0},{3,1},{4,6},{5,7},{6,4},{7,5},{8,10},{9,11},{10,... | collective-permute-start | bytes 1769480 | tf_op jit(solution)/shard_map/ppermute | solution.py:154
  974.9 37.1 %collective-permute-start.95 = (bf16[48,4096]{1,0:T(8,128)(2,1)S(1)}, bf16[48,4096]{1,0:T(8,128)(2,1)S(1)}, u32[]{:S(2)}, u32[]{:S(2)}) collective-permute-start(bf16[48,4096]{1,0:T(8,128)(2,1)S(1)} %add_convert_fusion.18), channel_id=1, source_target_pairs={{0,24},{1,25},{2,26},{3,27},{4,28},{5,29},{6,30},{7,31},{8,0},{9,1... | collective-permute-start | bytes 1179656 | tf_op jit(solution)/shard_map/ppermute | solution.py:154
  982.5 31.0 %collective-permute-start.89 = (bf16[48,4096]{1,0:T(8,128)(2,1)S(1)}, bf16[48,4096]{1,0:T(8,128)(2,1)S(1)}, u32[]{:S(2)}, u32[]{:S(2)}) collective-permute-start(bf16[48,4096]{1,0:T(8,128)(2,1)S(1)} %add_convert_fusion.21), channel_id=1, source_target_pairs={{0,24},{1,25},{2,26},{3,27},{4,28},{5,29},{6,30},{7,31},{8,0},{9,1... | collective-permute-start | bytes 1179656 | tf_op jit(solution)/shard_map/ppermute | solution.py:154
  988.2 46.9 %collective-permute-start.102 = (bf16[256,1536]{1,0:T(8,128)(2,1)S(1)}, bf16[256,1536]{1,0:T(8,128)(2,1)S(1)}, u32[]{:S(2)}, u32[]{:S(2)}) collective-permute-start(bf16[256,1536]{1,0:T(8,128)(2,1)S(1)} %add_convert_fusion.9), channel_id=1, source_target_pairs={{0,2},{1,3},{2,0},{3,1},{4,6},{5,7},{6,4},{7,5},{8,10},{9,11},{10,... | collective-permute-start | bytes 2359304 | tf_op jit(solution)/shard_map/ppermute | solution.py:154
  1059.2 52.4 %collective-permute-start.104 = (f32[196608]{0:T(1024)S(1)}, f32[196608]{0:T(1024)S(1)}, u32[]{:S(2)}, u32[]{:S(2)}) collective-permute-start(f32[196608]{0:T(1024)S(1)} %bitcast.321), channel_id=1, source_target_pairs={{2,0},{5,1},{8,2},{11,3},{14,4},{17,5},{20,6},{23,7},{26,8},{29,9}... | collective-permute-start | bytes 2359304 | tf_op jit(solution)/shard_map/ppermute | solution.py:114
  1062.8 44.0 %collective-permute-start.82 = (f32[73728]{0:T(1024)}, f32[73728]{0:T(1024)S(1)}, u32[]{:S(2)}, u32[]{:S(2)}) collective-permute-start(f32[73728]{0:T(1024)} %bitcast.97), channel_id=1, source_target_pairs={{2,0},{5,1},{8,2},{11,3},{14,4},{17,5},{20,6},{23,7},{26,8},{29,9}... | collective-permute-start | bytes 884744 | tf_op jit(solution)/shard_map/ppermute | solution.py:114
  1099.6 31.6 %collective-permute-start.63 = (f32[24,128]{1,0:T(8,128)S(1)}, f32[24,128]{1,0:T(8,128)S(1)}, u32[]{:S(2)}, u32[]{:S(2)}) collective-permute-start(f32[24,128]{1,0:T(8,128)S(1)} %add.3627), channel_id=1, source_target_pairs={{0,8},{1,9},{2,10},{3,11},{4,12},{5,13},{6,14},{7,15},{8,16},{9,17... | collective-permute-start | bytes 36872 | tf_op jit(solution)/shard_map/ppermute | solution.py:154
  1099.7 36.1 %collective-permute-start.84 = (f32[73728]{0:T(1024)}, f32[73728]{0:T(1024)}, u32[]{:S(2)}, u32[]{:S(2)}) collective-permute-start(f32[73728]{0:T(1024)} %bitcast.340), channel_id=1, source_target_pairs={{0,0},{3,1},{6,2},{9,3},{12,4},{15,5},{18,6},{21,7},{24,8},{27,9},... | collective-permute-start | bytes 884744 | tf_op jit(solution)/shard_map/ppermute | solution.py:114
  1101.6 34.2 %collective-permute-start.85 = (f32[73728]{0:T(1024)}, f32[73728]{0:T(1024)}, u32[]{:S(2)}, u32[]{:S(2)}) collective-permute-start(f32[73728]{0:T(1024)} %bitcast.339), channel_id=1, source_target_pairs={{1,0},{4,1},{7,2},{10,3},{13,4},{16,5},{19,6},{22,7},{25,8},{28,9}... | collective-permute-start | bytes 884744 | tf_op jit(solution)/shard_map/ppermute | solution.py:114
  1106.9 28.7 %collective-permute-start.83 = (f32[1536]{0:T(1024)S(1)}, f32[1536]{0:T(1024)S(1)}, u32[]{:S(2)}, u32[]{:S(2)}) collective-permute-start(f32[1536]{0:T(1024)S(1)} %slice.810), channel_id=1, source_target_pairs={{0,1},{1,2},{2,3},{3,4},{4,5},{5,6},{6,7},{7,8},{8,9},{9,10},{10,1... | collective-permute-start | bytes 18440 | tf_op jit(solution)/shard_map/ppermute | solution.py:117
  1135.6 28.9 %collective-permute-start.107 = (f32[196608]{0:T(1024)}, f32[196608]{0:T(1024)S(1)}, u32[]{:S(2)}, u32[]{:S(2)}) collective-permute-start(f32[196608]{0:T(1024)} %bitcast.319), channel_id=1, source_target_pairs={{1,0},{4,1},{7,2},{10,3},{13,4},{16,5},{19,6},{22,7},{25,8},{28,9}... | collective-permute-start | bytes 2359304 | tf_op jit(solution)/shard_map/ppermute | solution.py:114
  (146 other events, 2783.6 us)

commit v3 on v1

--- a/solution.py
+++ b/solution.py
@@ -29,6 +29,7 @@
 QUERY_TILE = 512
 KEY_TILE = 1024
 CHUNK = 8192
+FF_TILE = 512
 SCORE_BASE_TWO = math.log2(math.e) / math.sqrt(HEAD_DIM)
 SCORE_SCALE = 1.0 / math.sqrt(HEAD_DIM)
 
@@ -78,13 +79,37 @@
     return (master_new, first_new, second_new)
 
 
-def units_from_shard(flat_low, index, count):
+def aligned_block(flat_low, index, count):
     edge = D // count
     block = flat_low.shape[0] - edge
-    unit = block // 3
     following = lax.ppermute(flat_low[:D], "seq", [(i + 1, i) for i in range(count - 1)])
     extended = jnp.concatenate([flat_low, following])
-    aligned = lax.dynamic_slice(extended, (D - edge * index,), (block,)).reshape(3, unit)
+    return lax.dynamic_slice(extended, (D - edge * index,), (block,))
+
+
+def tiles_of(unit, width):
+    pieces = unit.reshape(-1, 8, width // 128, 128)
+    return jnp.swapaxes(pieces, 1, 2).reshape(-1, 8, 128)
+
+
+def matrix_of(tiles, width):
+    pieces = tiles.reshape(-1, width // 128, 8, 128)
+    return jnp.swapaxes(pieces, 1, 2).reshape(-1, width)
+
+
+def unit_tiles(block, widths, index, count):
+    units = block.reshape(3, -1)
+    made = []
+    for j in range(3):
+        kind = (3 * index + j) // count
+        made.append(
+            lax.select_n(kind, *[tiles_of(units[j], width) for width in widths])
+        )
+    return jnp.concatenate(made)
+
+
+def units_from_block(block, index, count):
+    aligned = block.reshape(3, -1)
     dealt = jnp.stack(
         [
             lax.ppermute(aligned[j], "seq", [(i, (3 * i + j) % count) for i in range(count)])
@@ -103,25 +128,28 @@
 
 def shard_from_units(units, gain_grad, index, count):
     edge = D // count
-    stacked = jnp.stack(units)
-    unit = stacked.shape[1]
+    units = [unit.astype(jnp.bfloat16) for unit in units]
+    unit = units[0].shape[0]
     returned = []
     for j in range(3):
         inverse = 1 if count % 3 == 1 else 2
         kind = ((j - index) * inverse) % 3
-        piece = lax.dynamic_index_in_dim(stacked, kind, 0, keepdims=False)
+        piece = jnp.where(kind == 0, units[0], jnp.where(kind == 1, units[1], units[2]))
         returned.append(
             lax.ppermute(piece, "seq", [((3 * i + j) % count, i) for i in range(count)])
         )
-    block = jnp.concatenate(returned)
-    before = lax.ppermute(block[-D:], "seq", [(i, i + 1) for i in range(count - 1)])
-    before = jnp.where(index == 0, gain_grad.astype(before.dtype), before)
-    extended = jnp.concatenate([before, block])
+    before = lax.ppermute(returned[2][-D:], "seq", [(i, i + 1) for i in range(count - 1)])
+    before = jnp.where(index == 0, gain_grad, before.astype(jnp.float32))
+    extended = jnp.concatenate([before] + [piece.astype(jnp.float32) for piece in returned])
     return lax.dynamic_slice(extended, (edge * index,), (3 * unit + edge,))
 
 
 AXES = ("z", "y", "x")
-GATHER_ORDERS = (("z", "y", "x"), ("z", "x", "y"), ("y", "x", "z"))
+GATHER_ORDERS = (("core", "x", "y", "z"), ("core", "y", "x", "z"))
+GATE_ORDER = ("core", "x", "z", "y")
+UP_ORDER = ("core", "y", "z", "x")
+DOWN_ORDER = ("core", "x", "y", "z")
+OUT_ORDER = ("core", "y", "x", "z")
 
 
 def device_grid(count):
@@ -164,56 +192,89 @@
     return jnp.stack(entries).astype(jnp.int32)
 
 
-def place_kernel(table_ref, *refs, lengths, rows):
-    piece_refs, out_ref, sems = (refs[:-2], refs[-2], refs[-1])
-    copies = []
+def place_kernel(table_ref, *refs, lengths):
+    pieces = len(lengths)
+    piece_refs, out_ref = (refs[:pieces], refs[pieces])
+    held, in_sems, out_sems = refs[pieces + 1 :]
+    size = held.shape[1]
+    loads = []
     for piece_ref, length in zip(piece_refs, lengths):
         for block in range(length):
-            entry = len(copies)
-            target = pl.ds(pl.multiple_of(table_ref[entry] * rows, rows), rows)
-            copy = pltpu.make_async_copy(
-                piece_ref.at[pl.ds(block * rows, rows), :], out_ref.at[target, :], sems.at[entry]
+            entry = len(loads)
+            load = pltpu.make_async_copy(
+                piece_ref.at[pl.ds(block * size, size)], held.at[entry], in_sems.at[entry]
             )
-            copy.start()
-            copies.append(copy)
-    for copy in copies:
-        copy.wait()
-
-
-def placed(pieces, table, rows):
+            load.start()
+            loads.append(load)
+    stores = []
+    for entry, load in enumerate(loads):
+        load.wait()
+        target = pl.ds(pl.multiple_of(table_ref[entry] * size, size), size)
+        store = pltpu.make_async_copy(held.at[entry], out_ref.at[target], out_sems.at[entry])
+        store.start()
+        stores.append(store)
+    for store in stores:
+        store.wait()
+
+
+def placed(pieces, table):
     count = table.shape[0]
-    width = pieces[0].shape[1]
-    lengths = tuple(piece.shape[0] // rows for piece in pieces)
+    size = sum(piece.shape[0] for piece in pieces) // count
+    shape = pieces[0].shape[1:]
     anywhere = pl.BlockSpec(memory_space=pl.ANY)
     return pl.pallas_call(
-        functools.partial(place_kernel, lengths=lengths, rows=rows),
+        functools.partial(
+            place_kernel, lengths=tuple(piece.shape[0] // size for piece in pieces)
+        ),
         grid_spec=pltpu.PrefetchScalarGridSpec(
             num_scalar_prefetch=1,
             grid=(1,),
             in_specs=[anywhere] * len(pieces),
             out_specs=anywhere,
-            scratch_shapes=[pltpu.SemaphoreType.DMA((count,))],
+            scratch_shapes=[
+                pltpu.VMEM((count, size) + shape, pieces[0].dtype),
+                pltpu.SemaphoreType.DMA((count,)),
+                pltpu.SemaphoreType.DMA((count,)),
+            ],
         ),
-        out_shape=jax.ShapeDtypeStruct((count * rows, width), pieces[0].dtype),
+        out_shape=jax.ShapeDtypeStruct((count * size,) + shape, pieces[0].dtype),
+        compiler_params=pltpu.CompilerParams(vmem_limit_bytes=48 << 20),
         cost_estimate=pl.CostEstimate(
-            flops=0, transcendentals=0, bytes_accessed=4 * count * rows * width
+            flops=0, transcendentals=0, bytes_accessed=4 * count * size * math.prod(shape)
         ),
         name="place_blocks",
     )(table, *pieces)
 
 
-def gather_rows(block, order, index, grid):
-    rows = block.shape[0]
-    held = block
-    for axis in order:
-        arrivals = [held]
-        for _ in range(grid[axis] - 1):
-            arrivals.append(shifted(arrivals[-1], axis, 1, grid))
-        if axis != order[-1]:
-            held = jnp.concatenate(arrivals)
-    pieces = arrivals + [shifted(piece, "core", 1, grid) for piece in arrivals]
-    table = slot_table(index, grid, ("core",) + tuple(reversed(order)))
-    return placed(pieces, table, rows)
+def gather_tiles(block, index, grid, notices, later, beside_of):
+    arrived = [block] + [shifted(block, "z", k, grid) for k in range(1, grid["z"])]
+    arrived, notices = together(arrived, notices)
+    beside = beside_of(notices)
+    half = block.shape[0] // 2
+    held = [
+        jnp.concatenate([each[color * half : (color + 1) * half] for each in arrived])
+        for color in range(2)
+    ]
+    for turn in (2, 1):
+        arrivals = []
+        for color, order in enumerate(GATHER_ORDERS):
+            axis = order[turn]
+            arrivals.append(
+                [held[color]]
+                + [shifted(held[color], axis, k, grid) for k in range(1, grid[axis])]
+            )
+        if turn == 1:
+            arrivals, beside = together(arrivals, beside)
+        else:
+            arrivals, later = together(arrivals, later)
+            held = [jnp.concatenate(each) for each in arrivals]
+    pieces = []
+    tables = []
+    for color, order in enumerate(GATHER_ORDERS):
+        pieces = pieces + arrivals[color]
+        pieces = pieces + [shifted(piece, "core", 1, grid) for piece in arrivals[color]]
+        tables.append(2 * slot_table(index, grid, order) + color)
+    return placed(pieces, jnp.concatenate(tables)), later, beside
 
 
 def reorder_kernel(table_ref, in_ref, out_ref, *, rows):
@@ -240,31 +301,274 @@
     )(table, value)
 
 
-def sum_scatter(left_cols, right, right_dim, order, index, grid):
-    count = math.prod(grid.values())
-    rows = left_cols.shape[0] // count
-    order = ("core",) + tuple(reversed(order))
-    left = reordered(left_cols, slot_table(index, grid, order))
-    received = []
-
-    def partial(first, last):
-        span = slice(first * rows, last * rows)
-        total = contract(left[span], 1, right, right_dim)
-        for part in received:
+class SummedRows:
+
+    def __init__(self, left, right, right_dim, order, grid):
+        self.left = left
+        self.right = right
+        self.right_dim = right_dim
+        self.grid = grid
+        self.rows = left.shape[0] // math.prod(grid.values())
+        self.window = left.shape[0]
+        self.turns = [(axis, slot) for axis in order for slot in range(grid[axis] - 1, 0, -1)]
+        self.received = []
+        self.passing = []
+
+    def partial(self, span):
+        total = contract(self.left[span], 1, self.right, self.right_dim)
+        for part in self.received:
             total = total + part[span]
         return total
 
-    window = count
-    for axis in order:
-        window = window // grid[axis]
-        passing = None
-        for slot in range(grid[axis] - 1, 0, -1):
-            own = partial(slot * window, (slot + 1) * window)
-            total = own if passing is None else own + passing
-            passing = shifted(total.astype(jnp.bfloat16), axis, -1, grid)
-        if passing is not None:
-            received.append(passing)
-    return partial(0, 1)
+    def make(self):
+        axis, slot = self.turns[0]
+        if slot == self.grid[axis] - 1:
+            self.window = self.window // self.grid[axis]
+        total = self.partial(slice(slot * self.window, (slot + 1) * self.window))
+        for part in self.passing:
+            total = total + part
+        self.made = total.astype(jnp.bfloat16)
+
+    def send(self):
+        axis, slot = self.turns.pop(0)
+        arrived = [shifted(self.made, axis, -1, self.grid)]
+        if slot > 1:
+            self.passing = arrived
+        else:
+            self.passing = []
+            self.received = self.received + arrived
+
+    def result(self):
+        return self.partial(slice(0, self.rows)).reshape(-1)
+
+
+def together(values, others):
+    return lax.optimization_barrier((values, others))
+
+
+def made_before(sums, value):
+    for each in sums:
+        each.make()
+    value, made = together(value, [each.made for each in sums])
+    for each, now in zip(sums, made):
+        each.made = now
+    return value
+
+
+def taken_after(sums, value):
+    value, arrived = together(value, [(each.received, each.passing) for each in sums])
+    for each, now in zip(sums, arrived):
+        each.received, each.passing = now
+    return value
+
+
+def one_round(sums):
+    taken_after(sums, ())
+    make_and_send(sums)
+
+
+def make_and_send(sums):
+    for each in sums:
+        each.make()
+        each.send()
+
+
+def feed_forward_kernel(
+    tokens_ref,
+    mixed_piece_ref,
+    gain_ref,
+    out_grad_ref,
+    out_weight_ref,
+    gate_weight_ref,
+    up_weight_ref,
+    down_weight_ref,
+    result_ref,
+    middle_grad_ref,
+    middle_low_ref,
+    dout_piece_ref,
+    gain_grad_ref,
+    gate_grad_ref,
+    up_grad_ref,
+    hidden_col_ref,
+    normed_col_ref,
+    mixed_col_ref,
+    middle_ref,
+    normed_ref,
+    total_ref,
+    normed_grad_ref,
+):
+    step = pl.program_id(0)
+    pieces, _, cols = mixed_piece_ref.shape
+    per_head = pieces // HEADS
+
+    def factor_of(middle):
+        return lax.rsqrt(jnp.mean(middle * middle, axis=-1, keepdims=True) + NORM_EPS)
+
+    def place_of(piece):
+        head, part = divmod(piece, per_head)
+        return (slice(head * HEAD_DIM, (head + 1) * HEAD_DIM), slice(part * cols, (part + 1) * cols))
+
+    @pl.when(step == 0)
+    def _():
+        for piece in range(pieces):
+            mixed_col_ref[place_of(piece)] = mixed_piece_ref[piece]
+        middle = tokens_ref[...].astype(jnp.float32) + contract(
+            mixed_col_ref[...].T, 1, out_weight_ref[...], 0
+        )
+        middle_ref[...] = middle
+        normed = (middle * factor_of(middle) * gain_ref[...]).astype(jnp.bfloat16)
+        normed_ref[...] = normed
+        normed_col_ref[...] = normed.T
+        total_ref[...] = jnp.zeros_like(total_ref)
+        normed_grad_ref[...] = jnp.zeros_like(normed_grad_ref)
+
+    normed = normed_ref[...]
+    gate_weight = gate_weight_ref[...]
+    up_weight = up_weight_ref[...]
+    down_weight = down_weight_ref[...]
+    gate = contract(normed, 1, gate_weight, 0)
+    up = contract(normed, 1, up_weight, 0)
+    sigma = jax.nn.sigmoid(gate)
+    silu = gate * sigma
+    hidden = (silu * up).astype(jnp.bfloat16)
+    hidden_col_ref[...] = hidden.T
+    total_ref[...] += contract(hidden, 1, down_weight, 0)
+    hidden_grad = contract(out_grad_ref[...], 1, down_weight, 1)
+    gate_grad = (hidden_grad * up * sigma * (1.0 + gate * (1.0 - sigma))).astype(jnp.bfloat16)
+    up_grad = (hidden_grad * silu).astype(jnp.bfloat16)
+    gate_grad_ref[...] = gate_grad
+    up_grad_ref[...] = up_grad
+    normed_grad_ref[...] += contract(gate_grad, 1, gate_weight, 1) + contract(
+        up_grad, 1, up_weight, 1
+    )
+
+    @pl.when(step == pl.num_programs(0) - 1)
+    def _():
+        middle = middle_ref[...]
+        factor = factor_of(middle)
+        normed_grad = normed_grad_ref[...]
+        result_ref[...] = (middle + total_ref[...]).astype(jnp.bfloat16)
+        scaled = normed_grad * gain_ref[...]
+        slope = jnp.mean(scaled * middle, axis=-1, keepdims=True)
+        middle_grad = out_grad_ref[...].astype(jnp.float32) + factor * (
+            scaled - middle * (factor * factor * slope)
+        )
+        middle_grad_ref[...] = middle_grad
+        middle_low = middle_grad.astype(jnp.bfloat16)
+        middle_low_ref[...] = middle_low
+        dout_cols = contract(out_weight_ref[...], 1, middle_low, 1).astype(jnp.bfloat16)
+        for piece in range(pieces):
+            dout_piece_ref[piece] = dout_cols[place_of(piece)]
+        gain_grad_ref[...] = jnp.sum(normed_grad * middle * factor, axis=0, keepdims=True)
+
+
+def fixed_spec(shape):
+    return pl.BlockSpec(shape, lambda i, *_: (0,) * len(shape), pipeline_mode=pl.Buffered(1))
+
+
+def feed_forward(tokens, mixed_pieces, gain, out_grad, out, gate, up, down):
+    rows = tokens.shape[0]
+    wide = pl.BlockSpec((rows, FF_TILE), lambda i: (0, i))
+    out_first, gate_first, up_first = (out[1] // D, gate[1] // D, up[1] // D)
+    down_first = down[1] // FF_TILE
+    square = (rows, D)
+    flipped = (D, rows)
+    outs = [
+        (fixed_spec(square), square, jnp.bfloat16),
+        (fixed_spec(square), square, jnp.float32),
+        (fixed_spec(square), square, jnp.bfloat16),
+        (fixed_spec(mixed_pieces.shape), mixed_pieces.shape, jnp.bfloat16),
+        (fixed_spec((1, D)), (1, D), jnp.float32),
+        (wide, (rows, FF), jnp.bfloat16),
+        (wide, (rows, FF), jnp.bfloat16),
+        (pl.BlockSpec((FF_TILE, rows), lambda i: (i, 0)), (FF, rows), jnp.bfloat16),
+        (fixed_spec(flipped), flipped, jnp.bfloat16),
+        (fixed_spec(flipped), flipped, jnp.bfloat16),
+    ]
+    return pl.pallas_call(
+        feed_forward_kernel,
+        grid=(FF // FF_TILE,),
+        in_specs=[
+            fixed_spec(square),
+            fixed_spec(mixed_pieces.shape),
+            fixed_spec((1, D)),
+            fixed_spec(square),
+            pl.BlockSpec((D, D), lambda i: (out_first, 0), pipeline_mode=pl.Buffered(1)),
+            pl.BlockSpec((D, FF_TILE), lambda i: (gate_first, i)),
+            pl.BlockSpec((D, FF_TILE), lambda i: (up_first, i)),
+            pl.BlockSpec((FF_TILE, D), lambda i: (down_first + i, 0)),
+        ],
+        out_specs=[spec for spec, _, _ in outs],
+        out_shape=[jax.ShapeDtypeStruct(shape, kind) for _, shape, kind in outs],
+        scratch_shapes=[
+            pltpu.VMEM(square, jnp.float32),
+            pltpu.VMEM(square, jnp.bfloat16),
+            pltpu.VMEM(square, jnp.float32),
+            pltpu.VMEM(square, jnp.float32),
+        ],
+        compiler_params=pltpu.CompilerParams(vmem_limit_bytes=48 << 20),
+        cost_estimate=pl.CostEstimate(
+            flops=12 * rows * D * FF, transcendentals=rows * FF, bytes_accessed=6 * D * FF
+        ),
+        name="feed_forward",
+    )(tokens, mixed_pieces, gain.reshape(1, D), out_grad, out[0], gate[0], up[0], down[0])
+
+
+def project_kernel(
+    normed_ref, query_weight_ref, key_weight_ref, value_weight_ref, cos_ref, sin_ref, piece_ref
+):
+    normed = normed_ref[...]
+    cosine = cos_ref[...]
+    sine_part = sin_ref[...]
+    query_cols = contract(normed, 1, query_weight_ref[...], 0).T
+    key_cols = contract(normed, 1, key_weight_ref[...], 0).T
+    value_cols = contract(normed, 1, value_weight_ref[...], 0).T
+    key_heads = key_cols.shape[0] // HEAD_DIM
+    pieces, _, cols = piece_ref.shape
+    parts = pieces // (2 * key_heads)
+
+    def head(columns, number):
+        return columns[number * HEAD_DIM : (number + 1) * HEAD_DIM]
+
+    for key_head in range(key_heads):
+        for half in range(2):
+            owner = 2 * key_head + half
+            query = rotate(head(query_cols, owner), cosine, sine_part)
+            if half == 0:
+                other = rotate(head(key_cols, key_head), cosine, sine_part)
+            else:
+                other = head(value_cols, key_head)
+            both = jnp.concatenate([query, other], axis=0).astype(jnp.bfloat16)
+            for part in range(parts):
+                piece_ref[owner * parts + part] = both[:, part * cols : (part + 1) * cols]
+
+
+def project(normed, query, key, value, cosine, sine_part, cols):
+    rows = normed.shape[0]
+    steps = 2
+    pieces = HEADS * rows // cols
+    query_first, key_first, value_first = (query[1] // D, key[1] // D, value[1] // D)
+    query_cols = HEADS * HEAD_DIM // steps
+    key_cols = KV_HEADS * HEAD_DIM // steps
+    return pl.pallas_call(
+        project_kernel,
+        grid=(steps,),
+        in_specs=[
+            fixed_spec(normed.shape),
+            pl.BlockSpec((D, query_cols), lambda i: (query_first, i)),
+            pl.BlockSpec((D, key_cols), lambda i: (key_first, i)),
+            pl.BlockSpec((D, key_cols), lambda i: (value_first, i)),
+            fixed_spec(cosine.shape),
+            fixed_spec(sine_part.shape),
+        ],
+        out_specs=pl.BlockSpec((pieces // steps, 2 * HEAD_DIM, cols), lambda i: (i, 0, 0)),
+        out_shape=jax.ShapeDtypeStruct((pieces, 2 * HEAD_DIM, cols), jnp.bfloat16),
+        compiler_params=pltpu.CompilerParams(vmem_limit_bytes=40 << 20),
+        cost_estimate=pl.CostEstimate(
+            flops=4 * rows * D * 2 * D, transcendentals=0, bytes_accessed=4 * D * 2 * D
+        ),
+        name="project",
+    )(normed, query[0], key[0], value[0], cosine, sine_part)
 
 
 def live_pairs(rel_ref, pos, start, base, queries):
@@ -475,28 +779,39 @@
 
     attn_low = attn_master.astype(jnp.bfloat16)
     ffn_low = ffn_master.astype(jnp.bfloat16)
-    gains = lax.psum(
-        jnp.where(
-            index == 0, jnp.stack([attn_low[:D], ffn_low[:D]]).astype(jnp.float32), 0.0
-        ),
-        "seq",
-    )
-    gain_one, gain_two = (gains[0], gains[1])
+    notice = jnp.concatenate(
+        [attn_low[:D], ffn_low[:D], segment_ids.astype(jnp.bfloat16)]
+    ).reshape(1, -1, 128)
+    notices = exchange(jnp.broadcast_to(notice, (count,) + notice.shape[1:]))
+
+    inputs = tokens.astype(jnp.float32)
+
+    def from_notices(notices):
+        gains = notices[0, : 2 * D // 128].astype(jnp.float32).reshape(2, D)
+        all_ids = notices[:, 2 * D // 128 :].astype(jnp.int32).reshape(-1)
+        held_ids = lax.dynamic_index_in_dim(
+            all_ids.reshape(count, parts, span), part, 1, keepdims=False
+        )
+
+        def item_starts(ids):
+            return jnp.sum((all_ids < ids[..., None]).astype(jnp.int32), axis=-1)
+
+        return (
+            gains[0],
+            gains[1],
+            rms_norm(inputs, gains[0]).astype(jnp.bfloat16),
+            item_starts(held_ids.reshape(-1)),
+            item_starts(all_ids[:: QUERY_TILE // span * rows]) // KEY_TILE,
+        )
 
     grid = device_grid(count)
     by_axes = (D // count) % 16 == 0
 
-    def gathered(unit, width, color):
-        block = unit.reshape(-1, width)
-        if by_axes:
-            return gather_rows(block, GATHER_ORDERS[color], index, grid)
-        return lax.all_gather(block, "seq", axis=0, tiled=True)
-
-    def scattered(left_cols, right, right_dim, color):
-        if by_axes:
-            return sum_scatter(
-                left_cols, right, right_dim, GATHER_ORDERS[color], index, grid
-            ).reshape(-1)
+    def sum_of(left_cols, right, right_dim, order):
+        left = reordered(left_cols, slot_table(index, grid, order))
+        return SummedRows(left, right, right_dim, order, grid)
+
+    def scattered(left_cols, right, right_dim):
         whole = contract(left_cols, 1, right, right_dim).astype(jnp.bfloat16)
         return (
             lax.psum_scatter(whole, "seq", scatter_dimension=0, tiled=True)
@@ -504,48 +819,68 @@
             .astype(jnp.float32)
         )
 
-    q_unit, kv_unit, o_unit = units_from_shard(attn_low, index, count)
-    gate_unit, up_unit, down_unit = units_from_shard(ffn_low, index, count)
-    query_weight = gathered(q_unit, HEADS * HEAD_DIM, 0)
-    key_value_weight = gathered(kv_unit, KV_HEADS * HEAD_DIM, 1)
-    key_weight, value_weight = (key_value_weight[:D], key_value_weight[D:])
-    out_weight = gathered(o_unit, D, 2)
-    gate_weight = gathered(gate_unit, FF, 0)
-    up_weight = gathered(up_unit, FF, 1)
-    down_weight = gathered(down_unit, D, 2)
-
-    all_ids = lax.all_gather(segment_ids.reshape(1, rows), "seq", axis=0, tiled=True).reshape(-1)
-
-    def item_starts(ids):
-        return jnp.sum((all_ids < ids[..., None]).astype(jnp.int32), axis=-1)
-
-    inputs = tokens.astype(jnp.float32)
-    normed_one = rms_norm(inputs, gain_one).astype(jnp.bfloat16)
+    attn_block = aligned_block(attn_low, index, count)
+    ffn_block = aligned_block(ffn_low, index, count)
+    if by_axes:
+        own_tiles = unit_tiles(ffn_block, (FF, FF, D), index, count)
+        attn_tiles, own_tiles, beside = gather_tiles(
+            unit_tiles(attn_block, (D, KV_HEADS * HEAD_DIM, D), index, count),
+            index,
+            grid,
+            notices,
+            own_tiles,
+            from_notices,
+        )
+        ffn_tiles = lax.all_gather(own_tiles, "seq", axis=0, tiled=True)
+        wide_rows = matrix_of(ffn_tiles, FF)
+        gate_weight = (wide_rows, 0)
+        up_weight = (wide_rows, D)
+        down_weight = (matrix_of(ffn_tiles, D), 2 * FF)
+        attn_wide = matrix_of(attn_tiles, D)
+        attn_narrow = matrix_of(attn_tiles, KV_HEADS * HEAD_DIM)
+        query_weight = (attn_wide, 0)
+        key_weight = (attn_narrow, 2 * D)
+        value_weight = (attn_narrow, 3 * D)
+        out_weight = (attn_wide, 2 * D)
+    else:
+
+        def gathered(unit, width):
+            return lax.all_gather(unit.reshape(-1, width), "seq", axis=0, tiled=True)
+
+        q_unit, kv_unit, o_unit = units_from_block(attn_block, index, count)
+        gate_unit, up_unit, down_unit = units_from_block(ffn_block, index, count)
+        query_weight = (gathered(q_unit, HEADS * HEAD_DIM), 0)
+        key_value_weight = gathered(kv_unit, KV_HEADS * HEAD_DIM)
+        key_weight = (key_value_weight, 0)
+        value_weight = (key_value_weight, D)
+        out_weight = (gathered(o_unit, D), 0)
+        gate_weight = (gathered(gate_unit, FF), 0)
+        up_weight = (gathered(up_unit, FF), 0)
+        down_weight = (gathered(down_unit, D), 0)
+
+    gain_one, gain_two, normed_one, held_starts, low = (
+        beside if by_axes else from_notices(notices)
+    )
+
     own_places = index * rows + jnp.arange(rows, dtype=jnp.int32)
     own_cos, own_sin = angle_tables(own_places)
-    query_pre = contract(query_weight, 0, normed_one, 1).reshape(HEADS, HEAD_DIM, rows)
-    key_pre = contract(key_weight, 0, normed_one, 1).reshape(KV_HEADS, HEAD_DIM, rows)
-    value_low = (
-        contract(value_weight, 0, normed_one, 1)
-        .astype(jnp.bfloat16)
-        .reshape(KV_HEADS, HEAD_DIM, rows)
-    )
-    query_low = rotate(query_pre, own_cos, own_sin).astype(jnp.bfloat16)
-    key_low = rotate(key_pre, own_cos, own_sin).astype(jnp.bfloat16)
+
+    cols = span if span % 128 == 0 else rows
 
     def by_owner(value):
-        pieces = value.reshape(HEADS, HEAD_DIM, parts, span)
-        return jnp.swapaxes(pieces, 1, 2).reshape(count, HEAD_DIM, span)
+        if value.shape[0] == count:
+            return value
+        pieces = value.reshape(HEADS, value.shape[1], parts, span)
+        return jnp.swapaxes(pieces, 1, 2).reshape(count, value.shape[1], span)
 
     def by_head(value):
-        pieces = value.reshape(HEADS, parts, HEAD_DIM, span)
-        return jnp.swapaxes(pieces, 1, 2).reshape(HEADS, HEAD_DIM, rows)
-
-    def paired(key_part, value_part):
-        return jnp.stack([key_part, value_part], axis=1).reshape(HEADS, HEAD_DIM, rows)
+        pieces = value.reshape(HEADS, parts, value.shape[1], span)
+        return jnp.swapaxes(pieces, 1, 2).reshape(HEADS, value.shape[1], rows)
 
     received = exchange(
-        jnp.concatenate([by_owner(query_low), by_owner(paired(key_low, value_low))], axis=1)
+        by_owner(
+            project(normed_one, query_weight, key_weight, value_weight, own_cos, own_sin, cols)
+        )
     )
 
     sources = QUERY_TILE // span
@@ -598,14 +933,9 @@
     held_places = (
         rows * jnp.arange(count, dtype=jnp.int32)[:, None] + span * part + within[None, :]
     )
-    held_ids = lax.dynamic_index_in_dim(
-        all_ids.reshape(count, parts, span), part, 1, keepdims=False
-    )
-    held_starts = item_starts(held_ids.reshape(-1))
     pos = held_places.reshape(tiles, 1, QUERY_TILE)
     start = held_starts.reshape(tiles, 1, QUERY_TILE)
     tile_span = sources * rows
-    low = item_starts(all_ids[::tile_span]) // KEY_TILE
     high = (jnp.arange(1, tiles + 1, dtype=jnp.int32) * tile_span + KEY_TILE - 1) // KEY_TILE
 
     chunks = []
@@ -639,45 +969,50 @@
     out_cols = jnp.concatenate([piece[0] for piece in pieces])
     lse = jnp.concatenate([piece[1] for piece in pieces])
 
-    mixed_low = by_head(exchange(from_tiles(out_cols.astype(jnp.bfloat16)))).reshape(
-        HEADS * HEAD_DIM, rows
-    )
-
-    middle = inputs + contract(mixed_low, 0, out_weight, 0)
-    normed_two = rms_norm(middle, gain_two).astype(jnp.bfloat16)
-    gate_rows = contract(normed_two, 1, gate_weight, 0)
-    up_rows = contract(normed_two, 1, up_weight, 0)
-    hidden = (jax.nn.silu(gate_rows) * up_rows).astype(jnp.bfloat16)
-    result = (middle + contract(hidden, 1, down_weight, 0)).astype(jnp.bfloat16)
-    hidden_grad = contract(out_grad, 1, down_weight, 1)
-    sigma_gate = jax.nn.sigmoid(gate_rows)
-    silu_gate = gate_rows * sigma_gate
-    gate_grad = (
-        hidden_grad * up_rows * sigma_gate * (1.0 + gate_rows * (1.0 - sigma_gate))
-    ).astype(jnp.bfloat16)
-    up_grad = (hidden_grad * silu_gate).astype(jnp.bfloat16)
-    normed_two_grad = contract(gate_grad, 1, gate_weight, 1) + contract(up_grad, 1, up_weight, 1)
-    _, norm_pull = jax.vjp(rms_norm, middle, gain_two)
-    middle_norm_grad, grad_two = norm_pull(normed_two_grad)
-    middle_grad = out_grad.astype(jnp.float32) + middle_norm_grad
-    middle_low = middle_grad.astype(jnp.bfloat16)
-
-    dout_cols = to_tiles(
-        exchange(
-            by_owner(
-                contract(out_weight, 1, middle_low, 1)
-                .astype(jnp.bfloat16)
-                .reshape(HEADS, HEAD_DIM, rows)
-            )
-        )
-    )
-    normed_two_cols = normed_two.T
-    ffn_units = [
-        scattered(normed_two_cols, gate_grad, 0, 0),
-        scattered(normed_two_cols, up_grad, 0, 1),
-        scattered(hidden.T, out_grad, 0, 2),
-    ]
-    out_unit = scattered(mixed_low, middle_low, 0, 2)
+    mixed_pieces = exchange(from_tiles(out_cols.astype(jnp.bfloat16)))
+    mixed_pieces, (key_cols, value_rows) = together(mixed_pieces, (key_cols, value_rows))
+    if cols == rows:
+        mixed_pieces = by_head(mixed_pieces)
+
+    (
+        result,
+        middle_grad,
+        middle_low,
+        dout_pieces,
+        grad_two,
+        gate_grad,
+        up_grad,
+        hidden_cols,
+        normed_two_cols,
+        mixed_low,
+    ) = feed_forward(
+        tokens,
+        mixed_pieces,
+        gain_two,
+        out_grad,
+        out_weight,
+        gate_weight,
+        up_weight,
+        down_weight,
+    )
+    dout_received = exchange(by_owner(dout_pieces))
+    if by_axes:
+        gate_sum = sum_of(normed_two_cols, gate_grad, 0, GATE_ORDER)
+        up_sum = sum_of(normed_two_cols, up_grad, 0, UP_ORDER)
+        down_sum = sum_of(hidden_cols, out_grad, 0, DOWN_ORDER)
+        first_sums = [gate_sum, up_sum]
+        make_and_send(first_sums + [down_sum])
+        dout_received = made_before(first_sums, dout_received)
+        for each in first_sums:
+            each.send()
+    else:
+        ffn_units = [
+            scattered(normed_two_cols, gate_grad, 0),
+            scattered(normed_two_cols, up_grad, 0),
+            scattered(hidden_cols, out_grad, 0),
+        ]
+        out_unit = scattered(mixed_low, middle_low, 0)
+    dout_cols = to_tiles(dout_received)
 
     pieces = []
     dkey_rows = jnp.zeros((total, HEAD_DIM), jnp.float32)
@@ -711,6 +1046,10 @@
     def by_slot(value):
         return jnp.transpose(value.reshape(count, parts, span, HEAD_DIM), (1, 0, 3, 2))
 
+    if by_axes:
+        dkey_rows = taken_after(first_sums, dkey_rows)
+        mixed_late, dkey_rows = together(mixed_low, dkey_rows)
+        out_sum = sum_of(mixed_late, middle_low, 0, OUT_ORDER)
     grads = jnp.stack([by_slot(dkey_rows), by_slot(dvalue_rows)])
     bit = parts // 2
     while bit >= 1:
@@ -722,14 +1061,24 @@
     kept_low = jnp.where(half == 0, rotate(kept_kind, held_cos, -held_sin), kept_kind).astype(
         jnp.bfloat16
     )
-    returned = exchange(jnp.concatenate([dquery_held, kept_low], axis=1))
+    sent_back = jnp.concatenate([dquery_held, kept_low], axis=1)
+    if by_axes:
+        early_sums = first_sums + [down_sum]
+        sent_back = made_before(early_sums, sent_back)
+        for each in early_sums:
+            each.send()
+    returned = exchange(sent_back)
+    if by_axes:
+        make_and_send([out_sum])
+        returned = made_before(first_sums, returned)
+        for each in first_sums:
+            each.send()
     dquery_low = by_head(returned[:, :HEAD_DIM]).reshape(HEADS * HEAD_DIM, rows)
     pair_low = by_head(returned[:, HEAD_DIM:]).reshape(KV_HEADS, 2, HEAD_DIM, rows)
     dkey_low = pair_low[:, 0].reshape(KV_HEADS * HEAD_DIM, rows)
     dvalue_low = pair_low[:, 1].reshape(KV_HEADS * HEAD_DIM, rows)
 
     normed_one_cols = normed_one.T
-    query_unit = scattered(normed_one_cols, dquery_low, 1, 0)
     nothing = jnp.zeros_like(normed_one_cols)
     key_value_cols = jnp.concatenate(
         [
@@ -737,23 +1086,55 @@
             jnp.concatenate([nothing, normed_one_cols], axis=1),
         ]
     )
-    key_value_unit = scattered(
-        key_value_cols, jnp.concatenate([dkey_low, dvalue_low], axis=1), 1, 1
-    )
+    key_value_right = jnp.concatenate([dkey_low, dvalue_low], axis=1)
     normed_one_grad = (
-        contract(dquery_low, 0, query_weight, 1)
-        + contract(dkey_low, 0, key_weight, 1)
-        + contract(dvalue_low, 0, value_weight, 1)
+        contract(dquery_low, 0, query_weight[0][:D], 1)
+        + contract(dkey_low, 0, key_weight[0][key_weight[1] : key_weight[1] + D], 1)
+        + contract(dvalue_low, 0, value_weight[0][value_weight[1] : value_weight[1] + D], 1)
     )
     _, first_pull = jax.vjp(rms_norm, inputs, gain_one)
     input_norm_grad, grad_one = first_pull(normed_one_grad)
     input_grad = middle_grad + input_norm_grad
 
-    gain_grads = lax.psum(jnp.stack([grad_one, grad_two]), "seq")
+    gain_grads = jnp.sum(
+        exchange(
+            jnp.broadcast_to(
+                jnp.concatenate([grad_one, grad_two[0]]).reshape(1, -1, 128),
+                (count, 2 * D // 128, 128),
+            )
+        ),
+        axis=0,
+    ).reshape(2, D)
+    if by_axes:
+        query_sum = sum_of(normed_one_cols, dquery_low, 1, GATE_ORDER)
+        key_value_sum = sum_of(key_value_cols, key_value_right, 1, UP_ORDER)
+        last_sums = [query_sum, key_value_sum]
+        make_and_send(last_sums)
+        dquery_low = made_before(last_sums, dquery_low)
+        for each in last_sums:
+            each.send()
+        make_and_send([gate_sum, up_sum, down_sum, out_sum])
+        attn_sums = last_sums + [out_sum]
+        gain_grads, input_grad = taken_after(
+            attn_sums + early_sums, (gain_grads, input_grad)
+        )
+        make_and_send(attn_sums + early_sums)
+        one_round(attn_sums + [down_sum])
+        one_round(attn_sums + [down_sum])
+        ffn_units = [gate_sum.result(), up_sum.result(), down_sum.result()]
+        one_round(attn_sums)
+        query_unit, key_value_unit, out_unit = [each.result() for each in attn_sums]
+    else:
+        query_unit = scattered(normed_one_cols, dquery_low, 1)
+        key_value_unit = scattered(key_value_cols, key_value_right, 1)
+    ffn_shard = shard_from_units(ffn_units, gain_grads[1], index, count)
+    if by_axes:
+        (query_unit, key_value_unit, out_unit), ffn_shard = together(
+            (query_unit, key_value_unit, out_unit), ffn_shard
+        )
     attn_shard = shard_from_units(
         [query_unit, key_value_unit, out_unit], gain_grads[0], index, count
     )
-    ffn_shard = shard_from_units(ffn_units, gain_grads[1], index, count)
     attn_new, attn_one, attn_two = adam_update(
         attn_master, attn_first, attn_second, attn_shard
     )

time: 2720 us -> 929 us (0.34)
  Pallas kernels: 1660 us -> 144 us
  starting transfers between devices: 195 us -> 132 us
  local copies, waits for them, and re-layouts: 135 us -> 73.3 us
  waiting for transfers between devices: 311 us -> 252 us
  matrix products: 169 us -> 120 us
  blocking collectives: 125 us -> 95.6 us
    pallas_call x6 -> x3, Pallas kernels: 1580 us -> 53.3 us  [the longest x1 33.8 us: feed_forward(): pl.pallas_call(feed_forward_kernel, grid=(FF // FF_TILE,), in_specs=[fixe...]
    ppermute x82 -> x47, waiting for transfers between devices: 285 us -> 185 us  [shifted(): return lax.ppermute(value, 'seq', pairs)]
    all_to_all x0 -> x1, blocking collectives: none -> 95.6 us  [exchange(): return lax.all_to_all(value, 'seq', 0, 0, tiled=True)]
    psum x2 -> x0, blocking collectives: 90.5 us -> none  [the longest x1 47.6 us: per_device(): gain_grads = lax.psum(jnp.stack([grad_one, grad_two]), 'seq')]
    ppermute x82 -> x47, starting transfers between devices: 122 us -> 48 us  [shifted(): return lax.ppermute(value, 'seq', pairs)]
    dot_general x56 -> x45, matrix products: 169 us -> 120 us  [contract(): lax.dot_general(left, right, (((left_dim,), (right_dim,)), ((), ())), pre...]
    all_gather x1 -> x0, blocking collectives: 34.9 us -> none  [per_device(): lax.all_gather(segment_ids.reshape(1, rows), 'seq', axis=0, tiled=True)]
    ppermute x4, waiting for transfers between devices: 10.7 us -> 40 us  [swapped(): return lax.ppermute(value, 'seq', [(i, i ^ bit) for i in range(count)])]
  transfers between devices with their start and end apart: 106 -> 67, of which waited for: 32 -> 27; matrix products, arithmetic and copies ran while one was open for 11% -> 28% of each run, Pallas kernels for 61% -> 12%
where the time goes in v3:
time: 929 us; the launch traced here: 923 us
  waiting for transfers between devices  252 us (27%)
  Pallas kernels  144 us (16%)
  starting transfers between devices  132 us (14%)
  matrix products  120 us (13%)
  blocking collectives  95.6 us (10%)
  other arithmetic  89.2 us (10%)
  local copies, waits for them, and re-layouts  73.3 us (8%)
  between operations  16.1 us (2%)
    ppermute x47, waiting for transfers between devices, shifted(): return lax.ppermute(value, 'seq', pairs)  185 us
    dot_general x45, matrix products, contract(): lax.dot_general(left, right, (((left_dim,), (right_dim,)), ((), ())), pre...  120 us
    all_to_all x1, blocking collectives, exchange(): return lax.all_to_all(value, 'seq', 0, 0, tiled=True)  95.6 us
    pallas_call x2, Pallas kernels, run_kernel(): pl.pallas_call(body, grid_spec=pltpu.PrefetchScalarGridSpec(num_scalar_pr...  71.7 us
    ppermute x47, starting transfers between devices, shifted(): return lax.ppermute(value, 'seq', pairs)  48 us
    ppermute x4, waiting for transfers between devices, swapped(): return lax.ppermute(value, 'seq', [(i, i ^ bit) for i in range(count)])  40 us
    all_to_all x5, starting transfers between devices, exchange(): return lax.all_to_all(value, 'seq', 0, 0, tiled=True)  35.5 us
    pallas_call x1, Pallas kernels, feed_forward(): pl.pallas_call(feed_forward_kernel, grid=(FF // FF_TILE,), in_specs=[fixe...  33.8 us
  transfers between devices with their start and end apart: 67, of which 27 were waited for; matrix products, arithmetic and copies ran while one was open for 28% of the time, Pallas kernels for 12%

profile of v3, /device:TPU:7, one launch (start us, length us, event | category | flops | bytes accessed | tf_op | source)
XLA Modules:
  0.0 922.8 jit_solution(10440954430275338413)
XLA Ops:
  15.5 6.3 all-to-all-start
  31.4 18.5 %all-to-all-done = bf16[32,26,128]{2,1,0:T(8,128)(2,1)S(1)} async-done(((bf16[32,26,128]{2,1,0:T(8,128)(2,1)}), bf16[32,26,128]{2,1,0:T(8,128)(2,1)S(1)}, u32[]{:S(2)}, u32[]{:S(2)}) %all-to-all-start) | async-done | bytes 213024 | tf_op jit(solution)/shard_map/all_to_all | solution.py:775
  49.9 9.1 collective-permute-done.2
  68.7 12.7 %collective-permute-done.4 = bf16[432,8,128]{2,1,0:T(8,128)(2,1)} collective-permute-done((bf16[432,8,128]{2,1,0:T(8,128)(2,1)S(1)}, bf16[432,8,128]{2,1,0:T(8,128)(2,1)}, u32[]{:S(2)}, u32[]{:S(2)}) %collective-permute-start.4) | collective-permute-done | bytes 884768 | tf_op jit(solution)/shard_map/ppermute | solution.py:182
  94.0 18.8 %convert_reduce_fusion = s32[4096]{0:T(1024)S(1)} fusion(s32[8192]{0:T(1024)S(1)} %bitcast.312, s32[4096]{0:T(1024)S(1)} %bitcast.316), kind=kLoop, calls=%fused_computation | loop fusion | flops 100659200 | bytes 65536 | tf_op jit(solution)/shard_map/reduce_sum | solution.py:797
  112.8 21.5 %collective-permute-done.7.refs_1_ = bf16[864,8,128]{2,1,0:T(8,128)(2,1)} collective-permute-done((bf16[864,8,128]{2,1,0:T(8,128)(2,1)S(1)}, bf16[864,8,128]{2,1,0:T(8,128)(2,1)}, u32[]{:S(2)}, u32[]{:S(2)}) %collective-permute-start.7) | collective-permute-done | bytes 1769504 | tf_op jit(solution)/shard_map/ppermute | solution.py:182
  134.3 4.5 collective-permute-done.8.refs_5_
  138.8 3.7 collective-permute-start.9
  153.8 13.6 %place_blocks.1 = bf16[6912,8,128]{2,1,0:T(8,128)(2,1)} custom-call(s32[64]{0:T(128)S(1)} %pad_add_fusion.table_ref, bf16[864,8,128]{2,1,0:T(8,128)(2,1)S(1)} %constant_dynamic-update-slice_fusion.refs_0_, bf16[864,8,128]{2,1,0:T(8,128)(2,1)} %collective-permute-done.7.refs_1_, bf16[864,8,128]{2,1,0:T(8,128)(2,1)} %collective-permute-done.9.refs_2_, ...), custom_call_target="tpu_custom_call" | custom-call | bytes 28311552 | tf_op jit(solution)/shard_map/place_blocks/pallas_call | solution.py:225
  167.5 5.9 project.1
  173.4 95.6 %all_to_all.30 = bf16[32,192,128]{2,1,0:T(8,128)(2,1)S(1)} all-to-all(bf16[32,192,128]{2,1,0:T(8,128)(2,1)S(1)} %project.1), channel_id=1, replica_groups=mesh['seq'=32] {'seq'}, dimensions={0} | all-to-all | bytes 3145728 | tf_op jit(solution)/shard_map/all_to_all | solution.py:775
  270.5 28.5 %collective-permute-done.13 = bf16[32,96,128]{2,1,0:T(8,128)(2,1)S(1)} collective-permute-done((bf16[32,96,128]{2,1,0:T(8,128)(2,1)S(1)}, bf16[32,96,128]{2,1,0:T(8,128)(2,1)S(1)}, u32[]{:S(2)}, u32[]{:S(2)}) %collective-permute-start.13) | collective-permute-done | bytes 786464 | tf_op jit(solution)/shard_map/ppermute | solution.py:778
  307.1 3.8 pad_maximum_fusion.1
  310.9 3.8 copy.140
  314.7 4.2 copy.178
  318.9 3.8 reshape.477.value_ref
  322.9 28.1 %attention_forward.1 = (f32[8,96,512]{2,1,0:T(8,128)}, f32[8,1,512]{2,1,0:T(1,128)S(1)}) custom-call(s32[8]{0:T(128)S(1)} %and_select_fusion.1.low_ref, s32[8]{0:T(128)S(1)} %and_select_fusion.high_ref, bf16[8,96,512]{2,1,0:T(8,128)(2,1)S(1)} %copy.142.query_ref, bf16[8192,96]{1,0:T(8,128)(2,1)} %bitcast.280, bf16[8,96,1024]{2,1,0:T(8,128)(2,1)} %reshape.477.value_ref, ...), custom_call_target="tpu_custom_call" | custom-call | flops 20000000000 | bytes 16777216 | tf_op jit(solution)/shard_map/attention_forward/pallas_call | solution.py:682
  353.6 6.9 all-to-all-start.2
  363.9 3.8 reshape.480.key_col_ref
  367.8 4.0 copy.144
  371.7 8.5 all-to-all-done.2.mixed_piece_ref
  380.3 33.8 %feed_forward.1 = (bf16[256,1536]{1,0:T(8,128)(2,1)}, f32[256,1536]{1,0:T(8,128)}, bf16[256,1536]{1,0:T(8,128)(2,1)S(1)}, bf16[32,96,128]{2,1,0:T(8,128)(2,1)}, ...) custom-call(bf16[256,1536]{1,0:T(8,128)(2,1)S(1)} %copy-done.2, ...), custom_call_target="tpu_custom_call" | custom-call | flops 19327352832 | bytes 37748736 | tf_op jit(solution)/shard_map/feed_forward/pallas_call | solution.py:488
  418.7 6.2 convolution_convert_fusion.2
  429.3 6.2 convolution_convert_fusion.1
  435.5 4.1 all-to-all-start.3
  439.5 3.7 reorder_blocks.8
  443.3 5.8 convolution_convert_fusion
  449.5 4.9 add_convert_fusion.2
  454.4 4.6 add_convert_fusion.1
  464.7 43.6 %attention_backward.1 = (f32[8,96,512]{2,1,0:T(8,128)}, f32[8192,96]{1,0:T(8,128)}, f32[8192,96]{1,0:T(8,128)}) custom-call(s32[8]{0:T(128)S(1)} %and_select_fusion.1.low_ref, s32[8]{0:T(128)S(1)} %and_select_fusion.high_ref, bf16[8,96,512]{2,1,0:T(8,128)(2,1)S(1)} %copy-done.4, bf16[8,512,96]{2,1,0:T(8,128)(2,1)} %bitcast.269, ...), custom_call_target="tpu_custom_call" | custom-call | flops 49999998976 | bytes 16777216 | tf_op jit(solution)/shard_map/attention_backward/pallas_call | solution.py:682
  508.3 5.3 copy.149
  513.6 19.3 %collective-permute-done.17 = bf16[384,4096]{1,0:T(8,128)(2,1)} collective-permute-done((bf16[384,4096]{1,0:T(8,128)(2,1)}, bf16[384,4096]{1,0:T(8,128)(2,1)}, u32[]{:S(2)}, u32[]{:S(2)}) %collective-permute-start.17) | collective-permute-done | bytes 3145760 | tf_op jit(solution)/shard_map/ppermute | solution.py:182
  533.3 5.3 copy.148
  538.6 3.4 fusion.36
  544.8 3.5 fusion.85
  548.4 4.8 add_convert_fusion
  568.5 9.7 %collective-permute-done.20 = bf16[32,96,128]{2,1,0:T(8,128)(2,1)S(1)} collective-permute-done((bf16[32,96,128]{2,1,0:T(8,128)(2,1)S(1)}, bf16[32,96,128]{2,1,0:T(8,128)(2,1)S(1)}, u32[]{:S(2)}, u32[]{:S(2)}) %collective-permute-start.20) | collective-permute-done | bytes 786464 | tf_op jit(solution)/shard_map/ppermute | solution.py:778
  578.6 3.3 fusion.88
  583.5 5.8 all-to-all-start.4
  594.1 4.4 reorder_blocks.10
  600.5 3.1 collective-permute-start.22
  614.7 18.8 %collective-permute-done.22 = bf16[96,4096]{1,0:T(8,128)(2,1)} collective-permute-done((bf16[96,4096]{1,0:T(8,128)(2,1)}, bf16[96,4096]{1,0:T(8,128)(2,1)}, u32[]{:S(2)}, u32[]{:S(2)}) %collective-permute-start.22) | collective-permute-done | bytes 786464 | tf_op jit(solution)/shard_map/ppermute | solution.py:182
  633.5 3.2 fusion.15
  636.7 13.6 %collective-permute-done.23 = bf16[96,4096]{1,0:T(8,128)(2,1)S(1)} collective-permute-done((bf16[96,4096]{1,0:T(8,128)(2,1)}, bf16[96,4096]{1,0:T(8,128)(2,1)S(1)}, u32[]{:S(2)}, u32[]{:S(2)}) %collective-permute-start.23) | collective-permute-done | bytes 786464 | tf_op jit(solution)/shard_map/ppermute | solution.py:182
  675.5 12.4 %all-to-all-start.5 = ((f32[32,24,128]{2,1,0:T(8,128)}), f32[32,24,128]{2,1,0:T(8,128)}, u32[]{:S(2)}, u32[]{:S(2)}) async-start(f32[32,24,128]{2,1,0:T(8,128)} %broadcast_in_dim.16), calls=%async_computation.5 | async-start | bytes 786432 | tf_op jit(solution)/shard_map/all_to_all | solution.py:775
  687.9 3.1 collective-permute-start.30
  701.1 4.1 add_convert_fusion.3
  705.2 7.9 collective-permute-done.30
  718.4 3.3 add_convert_fusion.4
  725.1 4.9 collective-permute-done.32
  738.0 8.9 collective-permute-done.31
  746.9 16.9 %collective-permute-done.33 = bf16[96,4096]{1,0:T(8,128)(2,1)} collective-permute-done((bf16[96,4096]{1,0:T(8,128)(2,1)}, bf16[96,4096]{1,0:T(8,128)(2,1)}, u32[]{:S(2)}, u32[]{:S(2)}) %collective-permute-start.33) | collective-permute-done | bytes 786464 | tf_op jit(solution)/shard_map/ppermute | solution.py:182
  763.7 9.5 %collective-permute-done.27 = bf16[768,768]{1,0:T(8,128)(2,1)} collective-permute-done((bf16[768,768]{1,0:T(8,128)(2,1)}, bf16[768,768]{1,0:T(8,128)(2,1)}, u32[]{:S(2)}, u32[]{:S(2)}) %collective-permute-start.27) | collective-permute-done | bytes 1179680 | tf_op jit(solution)/shard_map/ppermute | solution.py:182
  789.7 5.1 collective-permute-done.50
  809.3 13.1 %collective-permute-done.42 = bf16[48,1536]{1,0:T(8,128)(2,1)S(1)} collective-permute-done((bf16[48,1536]{1,0:T(8,128)(2,1)S(1)}, bf16[48,1536]{1,0:T(8,128)(2,1)S(1)}, u32[]{:S(2)}, u32[]{:S(2)}) %collective-permute-start.42) | collective-permute-done | bytes 147488 | tf_op jit(solution)/shard_map/ppermute | solution.py:182
  823.6 4.1 collective-permute-start.44
  831.9 9.1 collective-permute-done.46
  856.9 3.6 collective-permute-start.55
  860.4 9.2 %collective-permute-start.56 = (bf16[196608]{0:T(1024)(128)(2,1)S(1)}, bf16[196608]{0:T(1024)(128)(2,1)}, u32[]{:S(2)}, u32[]{:S(2)}) collective-permute-start(bf16[196608]{0:T(1024)(128)(2,1)S(1)} %get-tuple-element.301), channel_id=1, source_target_pairs={{1,0},{4,1},{7,2},{10,3},{13,4},{16,5},{19,6},{22,7},{25,8},{28,9}... | collective-permute-start | bytes 1179656 | tf_op jit(solution)/shard_map/ppermute | solution.py:139
  872.2 8.2 collective-permute-start.54
  883.4 3.3 fusion.44
  886.7 8.4 collective-permute-start.57
  900.2 5.5 collective-permute-start.58
  905.6 7.3 multiply_subtract_fusion
  (433 shorter events, 236.9 us)
Async XLA Ops:
  8.4 13.5 %collective-permute-start = (bf16[1536]{0:T(1024)(128)(2,1)S(1)}, bf16[1536]{0:T(1024)(128)(2,1)S(1)}, u32[]{:S(2)}, u32[]{:S(2)}) collective-permute-start(bf16[1536]{0:T(1024)(128)(2,1)S(1)} %slice.874), channel_id=1, source_target_pairs={{1,0},{2,1},{3,2},{4,3},{5,4},{6,5},{7,6},{8,7},{9,8},{10,9},{11,1... | collective-permute-start | bytes 9224 | tf_op jit(solution)/shard_map/ppermute | solution.py:85
  12.8 15.7 %collective-permute-start.6 = (bf16[1536]{0:T(1024)(128)(2,1)S(1)}, bf16[1536]{0:T(1024)(128)(2,1)S(1)}, u32[]{:S(2)}, u32[]{:S(2)}) collective-permute-start(bf16[1536]{0:T(1024)(128)(2,1)S(1)} %slice.878), channel_id=1, source_target_pairs={{1,0},{2,1},{3,2},{4,3},{5,4},{6,5},{7,6},{8,7},{9,8},{10,9},{11,1... | collective-permute-start | bytes 9224 | tf_op jit(solution)/shard_map/ppermute | solution.py:85
  15.5 34.4 %all-to-all-start = ((bf16[32,26,128]{2,1,0:T(8,128)(2,1)}), bf16[32,26,128]{2,1,0:T(8,128)(2,1)S(1)}, u32[]{:S(2)}, u32[]{:S(2)}) async-start(bf16[32,26,128]{2,1,0:T(8,128)(2,1)} %broadcast_in_dim.13), calls=%async_computation | async-start | bytes 524288 | tf_op jit(solution)/shard_map/all_to_all | solution.py:775
  21.9 358.4 %all-gather.2.cloned.1.call-start = ((), (), s32[]{:S(2)}) async-start(), calls=%async_computation.6 | async-start | bytes 38928384 | tf_op jit(solution)/shard_map/all_gather | solution.py:834
  23.8 26.0 %collective-permute-start.1 = (bf16[216,8,128]{2,1,0:T(8,128)(2,1)S(1)}, bf16[216,8,128]{2,1,0:T(8,128)(2,1)S(1)}, u32[]{:S(2)}, u32[]{:S(2)}) collective-permute-start(bf16[216,8,128]{2,1,0:T(8,128)(2,1)S(1)} %pad_maximum_fusion.9), channel_id=1, source_target_pairs={{0,8},{1,9},{2,10},{3,11},{4,12},{5,13},{6,14},{7,15},{8,16},{9,17... | collective-permute-start | bytes 1327112 | tf_op jit(solution)/shard_map/ppermute | solution.py:182
  25.1 33.9 %collective-permute-start.2 = (bf16[216,8,128]{2,1,0:T(8,128)(2,1)S(1)}, bf16[216,8,128]{2,1,0:T(8,128)(2,1)}, u32[]{:S(2)}, u32[]{:S(2)}) collective-permute-start(bf16[216,8,128]{2,1,0:T(8,128)(2,1)S(1)} %pad_maximum_fusion.9), channel_id=1, source_target_pairs={{0,16},{1,17},{2,18},{3,19},{4,20},{5,21},{6,22},{7,23},{8,24},{9,... | collective-permute-start | bytes 1327112 | tf_op jit(solution)/shard_map/ppermute | solution.py:182
  27.3 31.7 %collective-permute-start.3 = (bf16[216,8,128]{2,1,0:T(8,128)(2,1)S(1)}, bf16[216,8,128]{2,1,0:T(8,128)(2,1)}, u32[]{:S(2)}, u32[]{:S(2)}) collective-permute-start(bf16[216,8,128]{2,1,0:T(8,128)(2,1)S(1)} %pad_maximum_fusion.9), channel_id=1, source_target_pairs={{0,24},{1,25},{2,26},{3,27},{4,28},{5,29},{6,30},{7,31},{8,0},{9,1... | collective-permute-start | bytes 1327112 | tf_op jit(solution)/shard_map/ppermute | solution.py:182
  61.4 20.0 %collective-permute-start.4 = (bf16[432,8,128]{2,1,0:T(8,128)(2,1)S(1)}, bf16[432,8,128]{2,1,0:T(8,128)(2,1)}, u32[]{:S(2)}, u32[]{:S(2)}) collective-permute-start(bf16[432,8,128]{2,1,0:T(8,128)(2,1)S(1)} %pad_maximum_fusion.5), channel_id=1, source_target_pairs={{0,4},{1,5},{2,6},{3,7},{4,0},{5,1},{6,2},{7,3},{8,12},{9,13},{10,... | collective-permute-start | bytes 2654216 | tf_op jit(solution)/shard_map/ppermute | solution.py:182
  62.7 19.8 %collective-permute-start.5 = (bf16[432,8,128]{2,1,0:T(8,128)(2,1)}, bf16[432,8,128]{2,1,0:T(8,128)(2,1)}, u32[]{:S(2)}, u32[]{:S(2)}) collective-permute-start(bf16[432,8,128]{2,1,0:T(8,128)(2,1)} %pad_maximum_fusion.6), channel_id=1, source_target_pairs={{0,2},{1,3},{2,0},{3,1},{4,6},{5,7},{6,4},{7,5},{8,10},{9,11},{10,... | collective-permute-start | bytes 2654216 | tf_op jit(solution)/shard_map/ppermute | solution.py:182
  88.2 46.2 %collective-permute-start.7 = (bf16[864,8,128]{2,1,0:T(8,128)(2,1)S(1)}, bf16[864,8,128]{2,1,0:T(8,128)(2,1)}, u32[]{:S(2)}, u32[]{:S(2)}) collective-permute-start(bf16[864,8,128]{2,1,0:T(8,128)(2,1)S(1)} %constant_dynamic-update-slice_fusion.refs_0_), channel_id=1, source_target_pairs={{0,2},{1,3},{2,0},{3,1},{4,6},{5,7},{6,4},{7,5},{8,10},{9,11},{10,... | collective-permute-start | bytes 5308424 | tf_op jit(solution)/shard_map/ppermute | solution.py:182
  92.8 46.0 %collective-permute-start.8 = (bf16[864,8,128]{2,1,0:T(8,128)(2,1)}, bf16[864,8,128]{2,1,0:T(8,128)(2,1)}, u32[]{:S(2)}, u32[]{:S(2)}) collective-permute-start(bf16[864,8,128]{2,1,0:T(8,128)(2,1)} %constant_dynamic-update-slice_fusion.2.refs_4_), channel_id=1, source_target_pairs={{0,4},{1,5},{2,6},{3,7},{4,0},{5,1},{6,2},{7,3},{8,12},{9,13},{10,... | collective-permute-start | bytes 5308424 | tf_op jit(solution)/shard_map/ppermute | solution.py:182
  138.8 9.7 %collective-permute-start.9 = (bf16[864,8,128]{2,1,0:T(8,128)(2,1)S(1)}, bf16[864,8,128]{2,1,0:T(8,128)(2,1)}, u32[]{:S(2)}, u32[]{:S(2)}) collective-permute-start(bf16[864,8,128]{2,1,0:T(8,128)(2,1)S(1)} %constant_dynamic-update-slice_fusion.refs_0_), channel_id=1, source_target_pairs={{0,1},{1,0},{2,3},{3,2},{4,5},{5,4},{6,7},{7,6},{8,9},{9,8},{10,11... | collective-permute-start | bytes 5308424 | tf_op jit(solution)/shard_map/ppermute | solution.py:182
  142.6 8.7 collective-permute-start.11
  143.1 10.7 %collective-permute-start.12 = (bf16[864,8,128]{2,1,0:T(8,128)(2,1)}, bf16[864,8,128]{2,1,0:T(8,128)(2,1)}, u32[]{:S(2)}, u32[]{:S(2)}) collective-permute-start(bf16[864,8,128]{2,1,0:T(8,128)(2,1)} %collective-permute-done.8.refs_5_), channel_id=1, source_target_pairs={{0,1},{1,0},{2,3},{3,2},{4,5},{5,4},{6,7},{7,6},{8,9},{9,8},{10,11... | collective-permute-start | bytes 5308424 | tf_op jit(solution)/shard_map/ppermute | solution.py:182
  270.1 28.8 %collective-permute-start.13 = (bf16[32,96,128]{2,1,0:T(8,128)(2,1)S(1)}, bf16[32,96,128]{2,1,0:T(8,128)(2,1)S(1)}, u32[]{:S(2)}, u32[]{:S(2)}) collective-permute-start(bf16[32,96,128]{2,1,0:T(8,128)(2,1)S(1)} %slice.885), channel_id=1, source_target_pairs={{0,2},{1,3},{2,0},{3,1},{4,6},{5,7},{6,4},{7,5},{8,10},{9,11},{10,... | collective-permute-start | bytes 2359304 | tf_op jit(solution)/shard_map/ppermute | solution.py:778
  353.6 26.7 %all-to-all-start.2 = ((bf16[32,96,128]{2,1,0:T(8,128)(2,1)}), bf16[32,96,128]{2,1,0:T(8,128)(2,1)S(1)}, u32[]{:S(2)}, u32[]{:S(2)}) async-start(bf16[32,96,128]{2,1,0:T(8,128)(2,1)} %bitcast.276), calls=%async_computation.2 | async-start | bytes 1572864 | tf_op jit(solution)/shard_map/all_to_all | solution.py:775
  424.9 24.6 %collective-permute-start.15 = (bf16[768,4096]{1,0:T(8,128)(2,1)}, bf16[768,4096]{1,0:T(8,128)(2,1)}, u32[]{:S(2)}, u32[]{:S(2)}) collective-permute-start(bf16[768,4096]{1,0:T(8,128)(2,1)} %convolution_convert_fusion.2), channel_id=1, source_target_pairs={{0,1},{1,0},{2,3},{3,2},{4,5},{5,4},{6,7},{7,6},{8,9},{9,8},{10,11... | collective-permute-start | bytes 18874376 | tf_op jit(solution)/shard_map/ppermute | solution.py:182
  435.4 18.9 %collective-permute-start.16 = (bf16[768,4096]{1,0:T(8,128)(2,1)}, bf16[768,4096]{1,0:T(8,128)(2,1)}, u32[]{:S(2)}, u32[]{:S(2)}) collective-permute-start(bf16[768,4096]{1,0:T(8,128)(2,1)} %convolution_convert_fusion.1), channel_id=1, source_target_pairs={{0,1},{1,0},{2,3},{3,2},{4,5},{5,4},{6,7},{7,6},{8,9},{9,8},{10,11... | collective-permute-start | bytes 18874376 | tf_op jit(solution)/shard_map/ppermute | solution.py:182
  435.5 23.9 %all-to-all-start.3 = ((bf16[32,96,128]{2,1,0:T(8,128)(2,1)}), bf16[32,96,128]{2,1,0:T(8,128)(2,1)}, u32[]{:S(2)}, u32[]{:S(2)}) async-start(bf16[32,96,128]{2,1,0:T(8,128)(2,1)} %get-tuple-element.143), calls=%async_computation.3 | async-start | bytes 1572864 | tf_op jit(solution)/shard_map/all_to_all | solution.py:775
  449.1 99.3 %collective-permute-start.21 = (bf16[2048,1536]{1,0:T(8,128)(2,1)}, bf16[2048,1536]{1,0:T(8,128)(2,1)}, u32[]{:S(2)}, u32[]{:S(2)}) collective-permute-start(bf16[2048,1536]{1,0:T(8,128)(2,1)} %convolution_convert_fusion), channel_id=1, source_target_pairs={{0,1},{1,0},{2,3},{3,2},{4,5},{5,4},{6,7},{7,6},{8,9},{9,8},{10,11... | collective-permute-start | bytes 18874376 | tf_op jit(solution)/shard_map/ppermute | solution.py:182
  463.9 69.0 %collective-permute-start.17 = (bf16[384,4096]{1,0:T(8,128)(2,1)}, bf16[384,4096]{1,0:T(8,128)(2,1)}, u32[]{:S(2)}, u32[]{:S(2)}) collective-permute-start(bf16[384,4096]{1,0:T(8,128)(2,1)} %add_convert_fusion.2), channel_id=1, source_target_pairs={{0,2},{1,3},{2,0},{3,1},{4,6},{5,7},{6,4},{7,5},{8,10},{9,11},{10,... | collective-permute-start | bytes 9437192 | tf_op jit(solution)/shard_map/ppermute | solution.py:182
  464.4 68.9 %collective-permute-start.18 = (bf16[384,4096]{1,0:T(8,128)(2,1)}, bf16[384,4096]{1,0:T(8,128)(2,1)}, u32[]{:S(2)}, u32[]{:S(2)}) collective-permute-start(bf16[384,4096]{1,0:T(8,128)(2,1)} %add_convert_fusion.1), channel_id=1, source_target_pairs={{0,4},{1,5},{2,6},{3,7},{4,0},{5,1},{6,2},{7,3},{8,12},{9,13},{10,... | collective-permute-start | bytes 9437192 | tf_op jit(solution)/shard_map/ppermute | solution.py:182
  542.0 14.0 %collective-permute-start.19 = (bf16[2,1,32,96,128]{4,3,2,1,0:T(8,128)(2,1)}, bf16[2,1,32,96,128]{4,3,2,1,0:T(8,128)(2,1)}, u32[]{:S(2)}, u32[]{:S(2)}) collective-permute-start(bf16[2,1,32,96,128]{4,3,2,1,0:T(8,128)(2,1)} %fusion.36), channel_id=1, source_target_pairs={{0,1},{1,0},{2,3},{3,2},{4,5},{5,4},{6,7},{7,6},{8,9},{9,8},{10,11... | collective-permute-start | bytes 4718600 | tf_op jit(solution)/shard_map/ppermute | solution.py:778
  559.0 19.2 %collective-permute-start.20 = (bf16[32,96,128]{2,1,0:T(8,128)(2,1)S(1)}, bf16[32,96,128]{2,1,0:T(8,128)(2,1)S(1)}, u32[]{:S(2)}, u32[]{:S(2)}) collective-permute-start(bf16[32,96,128]{2,1,0:T(8,128)(2,1)S(1)} %fusion.95), channel_id=1, source_target_pairs={{0,2},{1,3},{2,0},{3,1},{4,6},{5,7},{6,4},{7,5},{8,10},{9,11},{10,... | collective-permute-start | bytes 2359304 | tf_op jit(solution)/shard_map/ppermute | solution.py:778
  562.2 49.1 %collective-permute-start.28 = (bf16[768,1536]{1,0:T(8,128)(2,1)}, bf16[768,1536]{1,0:T(8,128)(2,1)}, u32[]{:S(2)}, u32[]{:S(2)}) collective-permute-start(bf16[768,1536]{1,0:T(8,128)(2,1)} %convolution_convert_fusion.3), channel_id=1, source_target_pairs={{0,1},{1,0},{2,3},{3,2},{4,5},{5,4},{6,7},{7,6},{8,9},{9,8},{10,11... | collective-permute-start | bytes 7077896 | tf_op jit(solution)/shard_map/ppermute | solution.py:182
  583.5 69.9 %all-to-all-start.4 = ((bf16[32,192,128]{2,1,0:T(8,128)(2,1)}), bf16[32,192,128]{2,1,0:T(8,128)(2,1)}, u32[]{:S(2)}, u32[]{:S(2)}) async-start(bf16[32,192,128]{2,1,0:T(8,128)(2,1)} %pad_maximum_fusion.3), calls=%async_computation.4 | async-start | bytes 3145728 | tf_op jit(solution)/shard_map/all_to_all | solution.py:775
  600.5 33.0 %collective-permute-start.22 = (bf16[96,4096]{1,0:T(8,128)(2,1)}, bf16[96,4096]{1,0:T(8,128)(2,1)}, u32[]{:S(2)}, u32[]{:S(2)}) collective-permute-start(bf16[96,4096]{1,0:T(8,128)(2,1)} %fusion.13), channel_id=1, source_target_pairs={{0,24},{1,25},{2,26},{3,27},{4,28},{5,29},{6,30},{7,31},{8,0},{9,1... | collective-permute-start | bytes 2359304 | tf_op jit(solution)/shard_map/ppermute | solution.py:182
  605.6 44.8 %collective-permute-start.23 = (bf16[96,4096]{1,0:T(8,128)(2,1)}, bf16[96,4096]{1,0:T(8,128)(2,1)S(1)}, u32[]{:S(2)}, u32[]{:S(2)}) collective-permute-start(bf16[96,4096]{1,0:T(8,128)(2,1)} %fusion.14), channel_id=1, source_target_pairs={{0,24},{1,25},{2,26},{3,27},{4,28},{5,29},{6,30},{7,31},{8,0},{9,1... | collective-permute-start | bytes 2359304 | tf_op jit(solution)/shard_map/ppermute | solution.py:182
  614.2 119.1 %collective-permute-start.29 = (bf16[384,1536]{1,0:T(8,128)(2,1)}, bf16[384,1536]{1,0:T(8,128)(2,1)}, u32[]{:S(2)}, u32[]{:S(2)}) collective-permute-start(bf16[384,1536]{1,0:T(8,128)(2,1)} %fusion.37), channel_id=1, source_target_pairs={{0,4},{1,5},{2,6},{3,7},{4,0},{5,1},{6,2},{7,3},{8,12},{9,13},{10,... | collective-permute-start | bytes 3538952 | tf_op jit(solution)/shard_map/ppermute | solution.py:182
  614.4 86.2 %collective-permute-start.34 = (bf16[1024,1536]{1,0:T(8,128)(2,1)}, bf16[1024,1536]{1,0:T(8,128)(2,1)}, u32[]{:S(2)}, u32[]{:S(2)}) collective-permute-start(bf16[1024,1536]{1,0:T(8,128)(2,1)} %add_convert_fusion), channel_id=1, source_target_pairs={{0,2},{1,3},{2,0},{3,1},{4,6},{5,7},{6,4},{7,5},{8,10},{9,11},{10,... | collective-permute-start | bytes 9437192 | tf_op jit(solution)/shard_map/ppermute | solution.py:182
  661.4 60.4 %collective-permute-start.24 = (bf16[768,1536]{1,0:T(8,128)(2,1)}, bf16[768,1536]{1,0:T(8,128)(2,1)}, u32[]{:S(2)}, u32[]{:S(2)}) collective-permute-start(bf16[768,1536]{1,0:T(8,128)(2,1)} %convolution_convert_fusion.5), channel_id=1, source_target_pairs={{0,1},{1,0},{2,3},{3,2},{4,5},{5,4},{6,7},{7,6},{8,9},{9,8},{10,11... | collective-permute-start | bytes 7077896 | tf_op jit(solution)/shard_map/ppermute | solution.py:182
  665.0 51.4 %collective-permute-start.25 = (bf16[1536,768]{1,0:T(8,128)(2,1)}, bf16[1536,768]{1,0:T(8,128)(2,1)}, u32[]{:S(2)}, u32[]{:S(2)}) collective-permute-start(bf16[1536,768]{1,0:T(8,128)(2,1)} %convolution_convert_fusion.4), channel_id=1, source_target_pairs={{0,1},{1,0},{2,3},{3,2},{4,5},{5,4},{6,7},{7,6},{8,9},{9,8},{10,11... | collective-permute-start | bytes 7077896 | tf_op jit(solution)/shard_map/ppermute | solution.py:182
  675.5 61.3 %all-to-all-start.5 = ((f32[32,24,128]{2,1,0:T(8,128)}), f32[32,24,128]{2,1,0:T(8,128)}, u32[]{:S(2)}, u32[]{:S(2)}) async-start(f32[32,24,128]{2,1,0:T(8,128)} %broadcast_in_dim.16), calls=%async_computation.5 | async-start | bytes 786432 | tf_op jit(solution)/shard_map/all_to_all | solution.py:775
  687.9 25.2 %collective-permute-start.30 = (bf16[96,4096]{1,0:T(8,128)(2,1)}, bf16[96,4096]{1,0:T(8,128)(2,1)S(1)}, u32[]{:S(2)}, u32[]{:S(2)}) collective-permute-start(bf16[96,4096]{1,0:T(8,128)(2,1)} %fusion.15), channel_id=1, source_target_pairs={{0,24},{1,25},{2,26},{3,27},{4,28},{5,29},{6,30},{7,31},{8,0},{9,1... | collective-permute-start | bytes 2359304 | tf_op jit(solution)/shard_map/ppermute | solution.py:182
  700.7 29.3 %collective-permute-start.32 = (bf16[96,4096]{1,0:T(8,128)(2,1)S(1)}, bf16[96,4096]{1,0:T(8,128)(2,1)S(1)}, u32[]{:S(2)}, u32[]{:S(2)}) collective-permute-start(bf16[96,4096]{1,0:T(8,128)(2,1)S(1)} %copy-done.41), channel_id=1, source_target_pairs={{0,24},{1,25},{2,26},{3,27},{4,28},{5,29},{6,30},{7,31},{8,0},{9,1... | collective-permute-start | bytes 2359304 | tf_op jit(solution)/shard_map/ppermute | solution.py:182
  713.1 50.7 %collective-permute-start.35 = (bf16[512,1536]{1,0:T(8,128)(2,1)}, bf16[512,1536]{1,0:T(8,128)(2,1)}, u32[]{:S(2)}, u32[]{:S(2)}) collective-permute-start(bf16[512,1536]{1,0:T(8,128)(2,1)} %add_convert_fusion.3), channel_id=1, source_target_pairs={{0,4},{1,5},{2,6},{3,7},{4,0},{5,1},{6,2},{7,3},{8,12},{9,13},{10,... | collective-permute-start | bytes 4718600 | tf_op jit(solution)/shard_map/ppermute | solution.py:182
  716.3 30.5 %collective-permute-start.31 = (bf16[96,4096]{1,0:T(8,128)(2,1)}, bf16[96,4096]{1,0:T(8,128)(2,1)}, u32[]{:S(2)}, u32[]{:S(2)}) collective-permute-start(bf16[96,4096]{1,0:T(8,128)(2,1)} %fusion.17), channel_id=1, source_target_pairs={{0,24},{1,25},{2,26},{3,27},{4,28},{5,29},{6,30},{7,31},{8,0},{9,1... | collective-permute-start | bytes 2359304 | tf_op jit(solution)/shard_map/ppermute | solution.py:182
  724.8 38.9 %collective-permute-start.26 = (bf16[384,1536]{1,0:T(8,128)(2,1)}, bf16[384,1536]{1,0:T(8,128)(2,1)}, u32[]{:S(2)}, u32[]{:S(2)}) collective-permute-start(bf16[384,1536]{1,0:T(8,128)(2,1)} %add_convert_fusion.5), channel_id=1, source_target_pairs={{0,2},{1,3},{2,0},{3,1},{4,6},{5,7},{6,4},{7,5},{8,10},{9,11},{10,... | collective-permute-start | bytes 3538952 | tf_op jit(solution)/shard_map/ppermute | solution.py:182
  730.0 43.2 %collective-permute-start.27 = (bf16[768,768]{1,0:T(8,128)(2,1)}, bf16[768,768]{1,0:T(8,128)(2,1)}, u32[]{:S(2)}, u32[]{:S(2)}) collective-permute-start(bf16[768,768]{1,0:T(8,128)(2,1)} %add_convert_fusion.4), channel_id=1, source_target_pairs={{0,4},{1,5},{2,6},{3,7},{4,0},{5,1},{6,2},{7,3},{8,12},{9,13},{10,... | collective-permute-start | bytes 3538952 | tf_op jit(solution)/shard_map/ppermute | solution.py:182
  733.3 30.4 %collective-permute-start.33 = (bf16[96,4096]{1,0:T(8,128)(2,1)}, bf16[96,4096]{1,0:T(8,128)(2,1)}, u32[]{:S(2)}, u32[]{:S(2)}) collective-permute-start(bf16[96,4096]{1,0:T(8,128)(2,1)} %fusion.18), channel_id=1, source_target_pairs={{0,24},{1,25},{2,26},{3,27},{4,28},{5,29},{6,30},{7,31},{8,0},{9,1... | collective-permute-start | bytes 2359304 | tf_op jit(solution)/shard_map/ppermute | solution.py:182
  774.7 23.3 %collective-permute-start.36 = (bf16[96,1536]{1,0:T(8,128)(2,1)S(1)}, bf16[96,1536]{1,0:T(8,128)(2,1)S(1)}, u32[]{:S(2)}, u32[]{:S(2)}) collective-permute-start(bf16[96,1536]{1,0:T(8,128)(2,1)S(1)} %add_convert_fusion.15), channel_id=1, source_target_pairs={{0,24},{1,25},{2,26},{3,27},{4,28},{5,29},{6,30},{7,31},{8,0},{9,1... | collective-permute-start | bytes 884744 | tf_op jit(solution)/shard_map/ppermute | solution.py:182
  778.9 19.1 %collective-permute-start.37 = (bf16[192,768]{1,0:T(8,128)(2,1)S(1)}, bf16[192,768]{1,0:T(8,128)(2,1)S(1)}, u32[]{:S(2)}, u32[]{:S(2)}) collective-permute-start(bf16[192,768]{1,0:T(8,128)(2,1)S(1)} %add_convert_fusion.14), channel_id=1, source_target_pairs={{0,24},{1,25},{2,26},{3,27},{4,28},{5,29},{6,30},{7,31},{8,0},{9,1... | collective-permute-start | bytes 884744 | tf_op jit(solution)/shard_map/ppermute | solution.py:182
  782.0 16.0 %collective-permute-start.38 = (bf16[192,1536]{1,0:T(8,128)(2,1)S(1)}, bf16[192,1536]{1,0:T(8,128)(2,1)S(1)}, u32[]{:S(2)}, u32[]{:S(2)}) collective-permute-start(bf16[192,1536]{1,0:T(8,128)(2,1)S(1)} %fusion.41), channel_id=1, source_target_pairs={{0,2},{1,3},{2,0},{3,1},{4,6},{5,7},{6,4},{7,5},{8,10},{9,11},{10,... | collective-permute-start | bytes 1769480 | tf_op jit(solution)/shard_map/ppermute | solution.py:182
  783.9 14.1 %collective-permute-start.39 = (bf16[128,1536]{1,0:T(8,128)(2,1)S(1)}, bf16[128,1536]{1,0:T(8,128)(2,1)S(1)}, u32[]{:S(2)}, u32[]{:S(2)}) collective-permute-start(bf16[128,1536]{1,0:T(8,128)(2,1)S(1)} %add_convert_fusion.9), channel_id=1, source_target_pairs={{0,24},{1,25},{2,26},{3,27},{4,28},{5,29},{6,30},{7,31},{8,0},{9,1... | collective-permute-start | bytes 1179656 | tf_op jit(solution)/shard_map/ppermute | solution.py:182
  794.8 12.5 %collective-permute-start.51 = (bf16[48,4096]{1,0:T(8,128)(2,1)S(1)}, bf16[48,4096]{1,0:T(8,128)(2,1)S(1)}, u32[]{:S(2)}, u32[]{:S(2)}) collective-permute-start(bf16[48,4096]{1,0:T(8,128)(2,1)S(1)} %fusion.32), channel_id=1, source_target_pairs={{0,2},{1,3},{2,0},{3,1},{4,6},{5,7},{6,4},{7,5},{8,10},{9,11},{10,... | collective-permute-start | bytes 1179656 | tf_op jit(solution)/shard_map/ppermute | solution.py:182
  799.3 23.1 %collective-permute-start.40 = (bf16[96,1536]{1,0:T(8,128)(2,1)S(1)}, bf16[96,1536]{1,0:T(8,128)(2,1)S(1)}, u32[]{:S(2)}, u32[]{:S(2)}) collective-permute-start(bf16[96,1536]{1,0:T(8,128)(2,1)S(1)} %add_convert_fusion.13), channel_id=1, source_target_pairs={{0,24},{1,25},{2,26},{3,27},{4,28},{5,29},{6,30},{7,31},{8,0},{9,1... | collective-permute-start | bytes 884744 | tf_op jit(solution)/shard_map/ppermute | solution.py:182
  802.5 19.8 %collective-permute-start.41 = (bf16[192,768]{1,0:T(8,128)(2,1)S(1)}, bf16[192,768]{1,0:T(8,128)(2,1)S(1)}, u32[]{:S(2)}, u32[]{:S(2)}) collective-permute-start(bf16[192,768]{1,0:T(8,128)(2,1)S(1)} %add_convert_fusion.12), channel_id=1, source_target_pairs={{0,24},{1,25},{2,26},{3,27},{4,28},{5,29},{6,30},{7,31},{8,0},{9,1... | collective-permute-start | bytes 884744 | tf_op jit(solution)/shard_map/ppermute | solution.py:182
  804.1 18.3 %collective-permute-start.43 = (bf16[128,1536]{1,0:T(8,128)(2,1)S(1)}, bf16[128,1536]{1,0:T(8,128)(2,1)S(1)}, u32[]{:S(2)}, u32[]{:S(2)}) collective-permute-start(bf16[128,1536]{1,0:T(8,128)(2,1)S(1)} %add_convert_fusion.8), channel_id=1, source_target_pairs={{0,24},{1,25},{2,26},{3,27},{4,28},{5,29},{6,30},{7,31},{8,0},{9,1... | collective-permute-start | bytes 1179656 | tf_op jit(solution)/shard_map/ppermute | solution.py:182
  806.6 15.7 %collective-permute-start.42 = (bf16[48,1536]{1,0:T(8,128)(2,1)S(1)}, bf16[48,1536]{1,0:T(8,128)(2,1)S(1)}, u32[]{:S(2)}, u32[]{:S(2)}) collective-permute-start(bf16[48,1536]{1,0:T(8,128)(2,1)S(1)} %fusion.61), channel_id=1, source_target_pairs={{0,24},{1,25},{2,26},{3,27},{4,28},{5,29},{6,30},{7,31},{8,0},{9,1... | collective-permute-start | bytes 442376 | tf_op jit(solution)/shard_map/ppermute | solution.py:182
  823.6 17.4 %collective-permute-start.44 = (bf16[96,1536]{1,0:T(8,128)(2,1)S(1)}, bf16[96,1536]{1,0:T(8,128)(2,1)S(1)}, u32[]{:S(2)}, u32[]{:S(2)}) collective-permute-start(bf16[96,1536]{1,0:T(8,128)(2,1)S(1)} %add_convert_fusion.11), channel_id=1, source_target_pairs={{0,24},{1,25},{2,26},{3,27},{4,28},{5,29},{6,30},{7,31},{8,0},{9,1... | collective-permute-start | bytes 884744 | tf_op jit(solution)/shard_map/ppermute | solution.py:182
  828.8 12.2 %collective-permute-start.45 = (bf16[192,768]{1,0:T(8,128)(2,1)S(1)}, bf16[192,768]{1,0:T(8,128)(2,1)S(1)}, u32[]{:S(2)}, u32[]{:S(2)}) collective-permute-start(bf16[192,768]{1,0:T(8,128)(2,1)S(1)} %add_convert_fusion.10), channel_id=1, source_target_pairs={{0,24},{1,25},{2,26},{3,27},{4,28},{5,29},{6,30},{7,31},{8,0},{9,1... | collective-permute-start | bytes 884744 | tf_op jit(solution)/shard_map/ppermute | solution.py:182
  830.2 10.7 %collective-permute-start.46 = (bf16[48,1536]{1,0:T(8,128)(2,1)S(1)}, bf16[48,1536]{1,0:T(8,128)(2,1)S(1)}, u32[]{:S(2)}, u32[]{:S(2)}) collective-permute-start(bf16[48,1536]{1,0:T(8,128)(2,1)S(1)} %fusion.60), channel_id=1, source_target_pairs={{0,24},{1,25},{2,26},{3,27},{4,28},{5,29},{6,30},{7,31},{8,0},{9,1... | collective-permute-start | bytes 442376 | tf_op jit(solution)/shard_map/ppermute | solution.py:182
  831.8 20.3 %collective-permute-start.52 = (bf16[128,1536]{1,0:T(8,128)(2,1)S(1)}, bf16[128,1536]{1,0:T(8,128)(2,1)S(1)}, u32[]{:S(2)}, u32[]{:S(2)}) collective-permute-start(bf16[128,1536]{1,0:T(8,128)(2,1)S(1)} %add_convert_fusion.7), channel_id=1, source_target_pairs={{0,24},{1,25},{2,26},{3,27},{4,28},{5,29},{6,30},{7,31},{8,0},{9,1... | collective-permute-start | bytes 1179656 | tf_op jit(solution)/shard_map/ppermute | solution.py:182
  843.2 17.2 %collective-permute-start.47 = (bf16[48,1536]{1,0:T(8,128)(2,1)}, bf16[48,1536]{1,0:T(8,128)(2,1)}, u32[]{:S(2)}, u32[]{:S(2)}) collective-permute-start(bf16[48,1536]{1,0:T(8,128)(2,1)} %add_convert_fusion.17), channel_id=1, source_target_pairs={{0,4},{1,5},{2,6},{3,7},{4,0},{5,1},{6,2},{7,3},{8,12},{9,13},{10,... | collective-permute-start | bytes 442376 | tf_op jit(solution)/shard_map/ppermute | solution.py:182
  845.6 34.9 %collective-permute-start.48 = (bf16[96,768]{1,0:T(8,128)(2,1)}, bf16[96,768]{1,0:T(8,128)(2,1)}, u32[]{:S(2)}, u32[]{:S(2)}) collective-permute-start(bf16[96,768]{1,0:T(8,128)(2,1)} %add_convert_fusion.16), channel_id=1, source_target_pairs={{0,2},{1,3},{2,0},{3,1},{4,6},{5,7},{6,4},{7,5},{8,10},{9,11},{10,... | collective-permute-start | bytes 442376 | tf_op jit(solution)/shard_map/ppermute | solution.py:182
  849.2 21.6 %collective-permute-start.49 = (bf16[48,1536]{1,0:T(8,128)(2,1)}, bf16[48,1536]{1,0:T(8,128)(2,1)}, u32[]{:S(2)}, u32[]{:S(2)}) collective-permute-start(bf16[48,1536]{1,0:T(8,128)(2,1)} %fusion.59), channel_id=1, source_target_pairs={{0,24},{1,25},{2,26},{3,27},{4,28},{5,29},{6,30},{7,31},{8,0},{9,1... | collective-permute-start | bytes 442376 | tf_op jit(solution)/shard_map/ppermute | solution.py:182
  854.9 17.2 %collective-permute-start.53 = (bf16[196608]{0:T(1024)(128)(2,1)S(1)}, bf16[196608]{0:T(1024)(128)(2,1)S(1)}, u32[]{:S(2)}, u32[]{:S(2)}) collective-permute-start(bf16[196608]{0:T(1024)(128)(2,1)S(1)} %get-tuple-element.303), channel_id=1, source_target_pairs={{2,0},{5,1},{8,2},{11,3},{14,4},{17,5},{20,6},{23,7},{26,8},{29,9}... | collective-permute-start | bytes 1179656 | tf_op jit(solution)/shard_map/ppermute | solution.py:139
  856.9 25.4 %collective-permute-start.55 = (bf16[196608]{0:T(1024)(128)(2,1)}, bf16[196608]{0:T(1024)(128)(2,1)S(1)}, u32[]{:S(2)}, u32[]{:S(2)}) collective-permute-start(bf16[196608]{0:T(1024)(128)(2,1)} %get-tuple-element.302), channel_id=1, source_target_pairs={{0,0},{3,1},{6,2},{9,3},{12,4},{15,5},{18,6},{21,7},{24,8},{27,9},... | collective-permute-start | bytes 1179656 | tf_op jit(solution)/shard_map/ppermute | solution.py:139
  860.4 21.8 %collective-permute-start.56 = (bf16[196608]{0:T(1024)(128)(2,1)S(1)}, bf16[196608]{0:T(1024)(128)(2,1)}, u32[]{:S(2)}, u32[]{:S(2)}) collective-permute-start(bf16[196608]{0:T(1024)(128)(2,1)S(1)} %get-tuple-element.301), channel_id=1, source_target_pairs={{1,0},{4,1},{7,2},{10,3},{13,4},{16,5},{19,6},{22,7},{25,8},{28,9}... | collective-permute-start | bytes 1179656 | tf_op jit(solution)/shard_map/ppermute | solution.py:139
  872.2 11.1 %collective-permute-start.54 = (bf16[1536]{0:T(1024)(128)(2,1)S(1)}, bf16[1536]{0:T(1024)(128)(2,1)S(1)}, u32[]{:S(2)}, u32[]{:S(2)}) collective-permute-start(bf16[1536]{0:T(1024)(128)(2,1)S(1)} %slice.955), channel_id=1, source_target_pairs={{0,1},{1,2},{2,3},{3,4},{4,5},{5,6},{6,7},{7,8},{8,9},{9,10},{10,1... | collective-permute-start | bytes 9224 | tf_op jit(solution)/shard_map/ppermute | solution.py:141
  886.7 13.4 %collective-permute-start.57 = (bf16[73728]{0:T(1024)(128)(2,1)S(1)}, bf16[73728]{0:T(1024)(128)(2,1)S(1)}, u32[]{:S(2)}, u32[]{:S(2)}) collective-permute-start(bf16[73728]{0:T(1024)(128)(2,1)S(1)} %get-tuple-element.315), channel_id=1, source_target_pairs={{2,0},{5,1},{8,2},{11,3},{14,4},{17,5},{20,6},{23,7},{26,8},{29,9}... | collective-permute-start | bytes 442376 | tf_op jit(solution)/shard_map/ppermute | solution.py:139
  898.2 14.8 %collective-permute-start.60 = (bf16[73728]{0:T(1024)(128)(2,1)S(1)}, bf16[73728]{0:T(1024)(128)(2,1)S(1)}, u32[]{:S(2)}, u32[]{:S(2)}) collective-permute-start(bf16[73728]{0:T(1024)(128)(2,1)S(1)} %get-tuple-element.313), channel_id=1, source_target_pairs={{1,0},{4,1},{7,2},{10,3},{13,4},{16,5},{19,6},{22,7},{25,8},{28,9}... | collective-permute-start | bytes 442376 | tf_op jit(solution)/shard_map/ppermute | solution.py:139
  898.2 14.8 %collective-permute-start.59 = (bf16[73728]{0:T(1024)(128)(2,1)S(1)}, bf16[73728]{0:T(1024)(128)(2,1)S(1)}, u32[]{:S(2)}, u32[]{:S(2)}) collective-permute-start(bf16[73728]{0:T(1024)(128)(2,1)S(1)} %get-tuple-element.314), channel_id=1, source_target_pairs={{0,0},{3,1},{6,2},{9,3},{12,4},{15,5},{18,6},{21,7},{24,8},{27,9},... | collective-permute-start | bytes 442376 | tf_op jit(solution)/shard_map/ppermute | solution.py:139
  900.2 12.9 %collective-permute-start.58 = (bf16[1536]{0:T(1024)(128)(2,1)S(1)}, bf16[1536]{0:T(1024)(128)(2,1)S(1)}, u32[]{:S(2)}, u32[]{:S(2)}) collective-permute-start(bf16[1536]{0:T(1024)(128)(2,1)S(1)} %slice.956), channel_id=1, source_target_pairs={{0,1},{1,2},{2,3},{3,4},{4,5},{5,6},{6,7},{7,8},{8,9},{9,10},{10,1... | collective-permute-start | bytes 9224 | tf_op jit(solution)/shard_map/ppermute | solution.py:141
  (76 other events, 763.3 us)
Sparse Core Ops, SparseCore 0:
  82.7 257.6 all-gather.1

commit v4 on v3

--- a/solution.py
+++ b/solution.py
@@ -29,6 +29,7 @@
 QUERY_TILE = 512
 KEY_TILE = 1024
 CHUNK = 8192
+LANES = 128
 FF_TILE = 512
 SCORE_BASE_TWO = math.log2(math.e) / math.sqrt(HEAD_DIM)
 SCORE_SCALE = 1.0 / math.sqrt(HEAD_DIM)
@@ -148,7 +149,7 @@
 GATHER_ORDERS = (("core", "x", "y", "z"), ("core", "y", "x", "z"))
 GATE_ORDER = ("core", "x", "z", "y")
 UP_ORDER = ("core", "y", "z", "x")
-DOWN_ORDER = ("core", "x", "y", "z")
+DOWN_ORDER = ("core", "y", "x", "z")
 OUT_ORDER = ("core", "y", "x", "z")
 
 
@@ -340,6 +341,33 @@
 
     def result(self):
         return self.partial(slice(0, self.rows)).reshape(-1)
+
+
+class SummedWhole:
+
+    def __init__(self, value, grid):
+        self.value = value
+        self.grid = grid
+        self.turns = []
+        for axis in ("core", "x", "y", "z"):
+            step = grid[axis] // 2
+            while step >= 1:
+                self.turns.append((axis, step))
+                step = step // 2
+        self.received = []
+        self.passing = []
+
+    def make(self):
+        for part in self.received:
+            self.value = self.value + part
+        self.made = self.value
+
+    def send(self):
+        axis, step = self.turns.pop(0)
+        self.received = [shifted(self.made, axis, step, self.grid)]
+
+    def result(self):
+        return self.value + self.received[0]
 
 
 def together(values, others):
@@ -577,13 +605,44 @@
     return (rel >= start - base) & (rel <= pos - base)
 
 
-def forward_kernel(
-    low_ref, high_ref, query_ref, key_ref, value_ref, pos_ref, start_ref, rel_ref, out_ref, lse_ref
-):
+def side_by_side(ref):
+    return jnp.concatenate([ref[piece] for piece in range(ref.shape[0])], axis=1)
+
+
+def stacked_rows(ref):
+    return jnp.concatenate([ref[piece].T for piece in range(ref.shape[0])], axis=0)
+
+
+def forward_kernel(low_ref, high_ref, half_ref, query_ref, *refs, slots):
+    own_refs, other_refs = (refs[:slots], refs[slots : 2 * slots])
+    pos_ref, start_ref, rel_ref, out_ref, piece_ref, lse_ref, key_ref, value_ref = refs[2 * slots :]
     tile = pl.program_id(0)
-    query_cols = query_ref[0]
+    keys = rel_ref.shape[0]
+    per_slot = keys // (slots * LANES)
+
+    def lay_out(key_refs, value_refs):
+        def body(step, carried):
+            for slot in range(slots):
+                for piece in range(per_slot):
+                    place = (slot * per_slot + piece) * LANES
+                    source = step * per_slot + piece
+                    rows = pl.ds(pl.multiple_of(step * keys + place, LANES), LANES)
+                    key_ref[rows, :] = key_refs[slot][source].T
+                    value_ref[step, :, place : place + LANES] = value_refs[slot][source]
+            return carried
+
+        lax.fori_loop(0, value_ref.shape[0], body, 0)
+
+    @pl.when((tile == 0) & (half_ref[0] == 0))
+    def _():
+        lay_out(own_refs, other_refs)
+
+    @pl.when((tile == 0) & (half_ref[0] != 0))
+    def _():
+        lay_out(other_refs, own_refs)
+
+    query_cols = side_by_side(query_ref)
     queries = query_cols.shape[1]
-    keys = rel_ref.shape[0]
     pos = pos_ref[0]
     start = start_ref[0]
 
@@ -606,7 +665,10 @@
         jnp.zeros((HEAD_DIM, queries), jnp.float32),
     )
     run_max, run_total, mixed = lax.fori_loop(low_ref[tile], high_ref[tile], body, start_state)
-    out_ref[0] = mixed / run_total
+    mixed = mixed / run_total
+    out_ref[0] = mixed
+    for piece in range(piece_ref.shape[0]):
+        piece_ref[piece] = mixed[:, piece * LANES : (piece + 1) * LANES].astype(jnp.bfloat16)
     lse_ref[0] = run_max * SCORE_BASE_TWO + jnp.log2(run_total)
 
 
@@ -614,9 +676,7 @@
     low_ref,
     high_ref,
     query_ref,
-    query_row_ref,
     dout_ref,
-    dout_row_ref,
     out_ref,
     lse_ref,
     key_ref,
@@ -625,7 +685,11 @@
     pos_ref,
     start_ref,
     rel_ref,
+    cos_ref,
+    sin_ref,
     dquery_ref,
+    kept_ref,
+    sent_ref,
     dkey_ref,
     dvalue_ref,
 ):
@@ -636,10 +700,10 @@
         dkey_ref[...] = jnp.zeros_like(dkey_ref)
         dvalue_ref[...] = jnp.zeros_like(dvalue_ref)
 
-    query_cols = query_ref[0]
-    query_rows = query_row_ref[0]
-    dout_cols = dout_ref[0]
-    dout_rows = dout_row_ref[0]
+    query_cols = side_by_side(query_ref)
+    query_rows = stacked_rows(query_ref)
+    dout_cols = side_by_side(dout_ref)
+    dout_rows = stacked_rows(dout_ref)
     queries = query_cols.shape[1]
     keys = rel_ref.shape[0]
     pos = pos_ref[0]
@@ -661,11 +725,34 @@
     dquery = lax.fori_loop(
         low_ref[tile], high_ref[tile], body, jnp.zeros((HEAD_DIM, queries), jnp.float32)
     )
-    dquery_ref[0] = dquery * SCORE_SCALE
+    dquery = dquery * SCORE_SCALE
+    for piece in range(dquery_ref.shape[0]):
+        dquery_ref[piece] = rotate(
+            dquery[:, piece * LANES : (piece + 1) * LANES], cos_ref[piece], -sin_ref[piece]
+        ).astype(jnp.bfloat16)
 
     @pl.when(tile == pl.num_programs(0) - 1)
     def _():
-        dkey_ref[...] = dkey_ref[...] * SCORE_SCALE
+        kept_slots = kept_ref.shape[1]
+        per_slot = keys // (2 * kept_slots * LANES)
+
+        def lay_out(step, carried):
+            for slot in range(2 * kept_slots):
+                for piece in range(per_slot):
+                    place = (slot * per_slot + piece) * LANES
+                    source = step * per_slot + piece
+                    rows = pl.ds(pl.multiple_of(step * keys + place, LANES), LANES)
+                    found = (dkey_ref[rows, :].T * SCORE_SCALE, dvalue_ref[rows, :].T)
+                    for kind in range(2):
+                        if slot < kept_slots:
+                            kept_ref[kind, slot, source] = found[kind]
+                        else:
+                            sent_ref[kind, slot - kept_slots, source] = found[kind].astype(
+                                sent_ref.dtype
+                            )
+            return carried
+
+        lax.fori_loop(0, dkey_ref.shape[0] // keys, lay_out, 0)
 
 
 def whole_spec(array):
@@ -676,76 +763,114 @@
     return pl.BlockSpec((1,) + array.shape[1:], lambda i, *_: (i,) + (0,) * (array.ndim - 1))
 
 
-def run_kernel(body, name, bounds, inputs, outputs, flops):
-    spec = lambda item: tile_spec(item[0]) if item[1] else whole_spec(item[0])
-    grid = next(array.shape[0] for array, cut in inputs if cut)
+def piece_spec(array):
+    per_tile = QUERY_TILE // LANES
+    return pl.BlockSpec((per_tile, min(array.shape[1], HEAD_DIM), LANES), lambda i, *_: (i, 0, 0))
+
+
+def run_kernel(body, name, scalars, grid, inputs, outputs, scratch, flops):
     return pl.pallas_call(
         body,
         grid_spec=pltpu.PrefetchScalarGridSpec(
-            num_scalar_prefetch=2,
+            num_scalar_prefetch=len(scalars),
             grid=(grid,),
-            in_specs=[spec(item) for item in inputs],
-            out_specs=[spec(item) for item in outputs],
+            in_specs=[spec for _, spec in inputs],
+            out_specs=[spec for _, spec in outputs],
+            scratch_shapes=scratch,
         ),
-        out_shape=[item[0] for item in outputs],
+        out_shape=[shape for shape, _ in outputs],
         compiler_params=pltpu.CompilerParams(vmem_limit_bytes=52 << 20),
         cost_estimate=pl.CostEstimate(
             flops=flops, transcendentals=flops // 400, bytes_accessed=16 << 20
         ),
         name=name,
-    )(*bounds, *[item[0] for item in inputs])
-
-
-def attend(query_cols, key_rows, value_cols, pos, start, rel, low, high):
-    tiles, _, queries = query_cols.shape
+    )(*scalars, *[array for array, _ in inputs])
+
+
+def attend(query_pieces, own, other, half, pos, start, rel, low, high):
+    tiles, _, queries = pos.shape
+    key_total = own[0].shape[0] * LANES * len(own)
+    key_tile = rel.shape[0]
+    kind = jax.ShapeDtypeStruct
+    pieces = kind((tiles * queries // LANES, HEAD_DIM, LANES), jnp.bfloat16)
+    outputs = [
+        kind((tiles, HEAD_DIM, queries), jnp.float32),
+        pieces,
+        kind((tiles, 1, queries), jnp.float32),
+        kind((key_total, HEAD_DIM), jnp.bfloat16),
+        kind((key_total // key_tile, HEAD_DIM, key_tile), jnp.bfloat16),
+    ]
     return run_kernel(
-        forward_kernel,
+        functools.partial(forward_kernel, slots=len(own)),
         "attention_forward",
-        (low, high),
+        (low, high, half),
+        tiles,
+        [(query_pieces, piece_spec(query_pieces))]
+        + [(each, fixed_spec(each.shape)) for each in own + other]
+        + [(pos, tile_spec(pos)), (start, tile_spec(start)), (rel, fixed_spec(rel.shape))],
         [
-            (query_cols, True),
-            (key_rows, False),
-            (value_cols, False),
-            (pos, True),
-            (start, True),
-            (rel, False),
+            (outputs[0], tile_spec(outputs[0])),
+            (outputs[1], piece_spec(outputs[1])),
+            (outputs[2], tile_spec(outputs[2])),
+            (outputs[3], fixed_spec(outputs[3].shape)),
+            (outputs[4], fixed_spec(outputs[4].shape)),
         ],
-        [
-            (jax.ShapeDtypeStruct((tiles, HEAD_DIM, queries), jnp.float32), True),
-            (jax.ShapeDtypeStruct((tiles, 1, queries), jnp.float32), True),
-        ],
+        [],
         20_000_000_000,
     )
 
 
 def attend_back(
-    query_cols, dout_cols, out_cols, lse, key_rows, key_cols, value_rows, pos, start, rel, low, high
+    query_pieces,
+    dout_pieces,
+    out_cols,
+    lse,
+    key_rows,
+    key_cols,
+    value_rows,
+    pos,
+    start,
+    rel,
+    cosine,
+    sine_part,
+    low,
+    high,
+    slots,
+    sent_kind,
 ):
-    tiles, _, queries = query_cols.shape
-    grads = jax.ShapeDtypeStruct(key_rows.shape, jnp.float32)
+    tiles, _, queries = pos.shape
+    sources = key_rows.shape[0] // (slots * LANES)
+    grads = (2, slots // 2, sources, HEAD_DIM, LANES)
+    outputs = [
+        jax.ShapeDtypeStruct((tiles * queries // LANES, HEAD_DIM, LANES), jnp.bfloat16),
+        jax.ShapeDtypeStruct(grads, jnp.float32),
+        jax.ShapeDtypeStruct(grads, sent_kind),
+    ]
     return run_kernel(
         backward_kernel,
         "attention_backward",
         (low, high),
+        tiles,
         [
-            (query_cols, True),
-            (jnp.swapaxes(query_cols, 1, 2), True),
-            (dout_cols, True),
-            (jnp.swapaxes(dout_cols, 1, 2), True),
-            (out_cols, True),
-            (lse, True),
-            (key_rows, False),
-            (key_cols, False),
-            (value_rows, False),
-            (pos, True),
-            (start, True),
-            (rel, False),
+            (query_pieces, piece_spec(query_pieces)),
+            (dout_pieces, piece_spec(dout_pieces)),
+            (out_cols, tile_spec(out_cols)),
+            (lse, tile_spec(lse)),
+            (key_rows, fixed_spec(key_rows.shape)),
+            (key_cols, fixed_spec(key_cols.shape)),
+            (value_rows, fixed_spec(value_rows.shape)),
+            (pos, tile_spec(pos)),
+            (start, tile_spec(start)),
+            (rel, fixed_spec(rel.shape)),
+            (cosine, piece_spec(cosine)),
+            (sine_part, piece_spec(sine_part)),
         ],
         [
-            (jax.ShapeDtypeStruct((tiles, HEAD_DIM, queries), jnp.float32), True),
-            (grads, False),
-            (grads, False),
+            (outputs[0], piece_spec(outputs[0])),
+            (outputs[1], fixed_spec(grads)),
+            (outputs[2], fixed_spec(grads)),
         ],
+        [pltpu.VMEM(key_rows.shape, jnp.float32)] * 2,
         50_000_000_000,
     )
 
@@ -883,53 +1008,37 @@
         )
     )
 
+    merged = LANES // span
+
+    def to_pieces(value):
+        if merged == 1:
+            return value
+        pieces = value.reshape(count // merged, merged, value.shape[1], span)
+        return jnp.swapaxes(pieces, 1, 2).reshape(count // merged, value.shape[1], LANES)
+
+    def from_pieces(value):
+        if merged == 1:
+            return value
+        pieces = value.reshape(count // merged, value.shape[1], merged, span)
+        return jnp.swapaxes(pieces, 1, 2).reshape(count, value.shape[1], span)
+
+    own_kind = received[:, HEAD_DIM:]
+    both_kinds = [[own_kind], [swapped(own_kind, parts)]]
+    bit = 1
+    while bit < parts:
+        both_kinds = [kind + [swapped(each, bit) for each in kind] for kind in both_kinds]
+        bit = bit * 2
+    own, other = [[to_pieces(each) for each in kind] for kind in both_kinds]
+    query_pieces = to_pieces(received)
     sources = QUERY_TILE // span
     tiles = count // sources
-
-    def to_tiles(value):
-        pieces = value.reshape(tiles, sources, value.shape[1], span)
-        return jnp.swapaxes(pieces, 1, 2).reshape(tiles, value.shape[1], QUERY_TILE)
-
-    def from_tiles(value):
-        pieces = value.reshape(tiles, value.shape[1], sources, span)
-        return jnp.swapaxes(pieces, 1, 2).reshape(count, value.shape[1], span)
-
-    query_cols = to_tiles(received[:, :HEAD_DIM])
-    own_kind = received[:, HEAD_DIM:]
-    other_kind = swapped(own_kind, parts)
-    pair = jnp.stack(
-        [
-            jnp.where(half == 0, own_kind, other_kind),
-            jnp.where(half == 0, other_kind, own_kind),
-        ]
-    )[:, None]
-    bit = 1
-    while bit < parts:
-        pair = jnp.concatenate([pair, swapped(pair, bit)], axis=1)
-        bit = bit * 2
-    key_all, value_all = (pair[0], pair[1])
-    devices_per_tile = KEY_TILE // rows
-    key_tiles = count // devices_per_tile
-
-    def key_columns(value):
-        pieces = value.reshape(parts, key_tiles, devices_per_tile, HEAD_DIM, span)
-        return jnp.transpose(pieces, (1, 3, 2, 0, 4)).reshape(key_tiles, HEAD_DIM, KEY_TILE)
-
-    def key_rows_of(value):
-        return jnp.transpose(value, (1, 0, 3, 2)).reshape(total, HEAD_DIM)
-
-    key_cols = key_columns(key_all)
-    value_cols = key_columns(value_all)
-    key_rows = key_rows_of(key_all)
-    value_rows = key_rows_of(value_all)
-    slot_parts = part ^ jnp.arange(parts, dtype=jnp.int32)
     within = jnp.arange(span, dtype=jnp.int32)
     rel = (
-        rows * jnp.arange(devices_per_tile, dtype=jnp.int32)[:, None, None]
-        + span * slot_parts[None, :, None]
+        span * (part ^ jnp.arange(parts, dtype=jnp.int32))[:, None, None]
+        + rows * jnp.arange(KEY_TILE // rows, dtype=jnp.int32)[None, :, None]
         + within[None, None, :]
     ).reshape(KEY_TILE, 1)
-    rel = jnp.broadcast_to(rel, (KEY_TILE, 128))
+    rel = jnp.broadcast_to(rel, (KEY_TILE, LANES))
     held_places = (
         rows * jnp.arange(count, dtype=jnp.int32)[:, None] + span * part + within[None, :]
     )
@@ -940,37 +1049,46 @@
 
     chunks = []
     chunk = min(CHUNK, total)
+    per_tile = QUERY_TILE // LANES
     for first in range(0, total, chunk):
+        of_tiles = slice(first // tile_span, (first + chunk) // tile_span)
+        of_queries = slice(of_tiles.start * per_tile, of_tiles.stop * per_tile)
         first_key = max(0, first - SEG_MOST) // KEY_TILE
         last_key = (first + chunk) // KEY_TILE
-        chunks.append(
-            (
-                slice(first // tile_span, (first + chunk) // tile_span),
-                slice(first_key, last_key),
-                slice(first_key * KEY_TILE, last_key * KEY_TILE),
-            )
-        )
-
-    pieces = []
-    for of_tiles, of_key_tiles, of_keys in chunks:
-        shift = of_key_tiles.start * KEY_TILE
-        pieces.append(
+        per_piece = merged * rows
+        of_keys = slice(
+            first_key * KEY_TILE // per_piece, last_key * KEY_TILE // per_piece
+        )
+        chunks.append((of_tiles, of_queries, first_key, of_keys))
+
+    attended = []
+    for of_tiles, of_queries, first_key, of_keys in chunks:
+        shift = first_key * KEY_TILE
+        attended.append(
             attend(
-                query_cols[of_tiles],
-                key_rows[of_keys],
-                value_cols[of_key_tiles],
+                query_pieces[of_queries],
+                [each[of_keys] for each in own],
+                [each[of_keys] for each in other],
+                half.reshape(1),
                 pos[of_tiles] - shift,
                 start[of_tiles] - shift,
                 rel,
-                low[of_tiles] - of_key_tiles.start,
-                high[of_tiles] - of_key_tiles.start,
+                low[of_tiles] - first_key,
+                high[of_tiles] - first_key,
             )
         )
-    out_cols = jnp.concatenate([piece[0] for piece in pieces])
-    lse = jnp.concatenate([piece[1] for piece in pieces])
-
-    mixed_pieces = exchange(from_tiles(out_cols.astype(jnp.bfloat16)))
-    mixed_pieces, (key_cols, value_rows) = together(mixed_pieces, (key_cols, value_rows))
+    mixed_pieces = exchange(
+        from_pieces(jnp.concatenate([piece[1] for piece in attended]))
+    )
+    held = []
+    for out_cols, _, lse, key_rows, value_cols in attended:
+        key_cols = jnp.swapaxes(key_rows.reshape(-1, KEY_TILE, HEAD_DIM), 1, 2)
+        value_rows = jnp.swapaxes(value_cols, 1, 2).reshape(-1, HEAD_DIM)
+        held.append((out_cols, lse, key_rows, key_cols, value_rows))
+    held_cos, held_sin = [to_pieces(table) for table in angle_tables(held_places)]
+    mixed_pieces, (held, held_cos, held_sin) = together(
+        mixed_pieces, (held, held_cos, held_sin)
+    )
     if cols == rows:
         mixed_pieces = by_head(mixed_pieces)
 
@@ -1012,54 +1130,53 @@
             scattered(hidden_cols, out_grad, 0),
         ]
         out_unit = scattered(mixed_low, middle_low, 0)
-    dout_cols = to_tiles(dout_received)
-
-    pieces = []
-    dkey_rows = jnp.zeros((total, HEAD_DIM), jnp.float32)
-    dvalue_rows = jnp.zeros((total, HEAD_DIM), jnp.float32)
-    for of_tiles, of_key_tiles, of_keys in chunks:
-        shift = of_key_tiles.start * KEY_TILE
-        dquery_piece, dkey_piece, dvalue_piece = attend_back(
-            query_cols[of_tiles],
-            dout_cols[of_tiles],
-            out_cols[of_tiles],
-            lse[of_tiles],
-            key_rows[of_keys],
-            key_cols[of_key_tiles],
-            value_rows[of_keys],
+    dout_pieces = to_pieces(dout_received)
+
+    one_chunk = len(chunks) == 1
+    dquery_pieces = []
+    summed = [jnp.zeros((2, max(parts // 2, 1), count // merged, HEAD_DIM, LANES), jnp.float32)] * 2
+    for (of_tiles, of_queries, first_key, of_keys), kept_values in zip(chunks, held):
+        shift = first_key * KEY_TILE
+        dquery_piece, *found = attend_back(
+            query_pieces[of_queries],
+            dout_pieces[of_queries],
+            *kept_values,
             pos[of_tiles] - shift,
             start[of_tiles] - shift,
             rel,
-            low[of_tiles] - of_key_tiles.start,
-            high[of_tiles] - of_key_tiles.start,
-        )
-        pieces.append(dquery_piece)
-        if len(chunks) == 1:
-            dkey_rows, dvalue_rows = (dkey_piece, dvalue_piece)
+            held_cos[of_queries],
+            held_sin[of_queries],
+            low[of_tiles] - first_key,
+            high[of_tiles] - first_key,
+            parts,
+            jnp.bfloat16 if one_chunk else jnp.float32,
+        )
+        dquery_pieces.append(dquery_piece)
+        if one_chunk:
+            summed = found
         else:
-            dkey_rows = dkey_rows.at[of_keys].add(dkey_piece)
-            dvalue_rows = dvalue_rows.at[of_keys].add(dvalue_piece)
-    dquery_rot = from_tiles(jnp.concatenate(pieces))
-    held_cos, held_sin = angle_tables(held_places)
-    dquery_held = rotate(dquery_rot, held_cos, -held_sin).astype(jnp.bfloat16)
-
-    def by_slot(value):
-        return jnp.transpose(value.reshape(count, parts, span, HEAD_DIM), (1, 0, 3, 2))
-
+            summed = [
+                whole.at[:, :, of_keys].add(piece) for whole, piece in zip(summed, found)
+            ]
+    dquery_held = from_pieces(jnp.concatenate(dquery_pieces))
+    grads, sent = summed
     if by_axes:
-        dkey_rows = taken_after(first_sums, dkey_rows)
-        mixed_late, dkey_rows = together(mixed_low, dkey_rows)
+        mixed_late, grads = together(mixed_low, grads)
         out_sum = sum_of(mixed_late, middle_low, 0, OUT_ORDER)
-    grads = jnp.stack([by_slot(dkey_rows), by_slot(dvalue_rows)])
-    bit = parts // 2
+    grads = grads + swapped(sent.astype(jnp.bfloat16), parts // 2)
+    bit = parts // 4
     while bit >= 1:
         grads = grads[:, :bit] + swapped(grads[:, bit:].astype(jnp.bfloat16), bit)
         bit = bit // 2
+    if by_axes:
+        grads = taken_after(first_sums, grads)
     dkey_held, dvalue_held = (grads[0, 0], grads[1, 0])
     sent_kind = jnp.where(half == 0, dvalue_held, dkey_held).astype(jnp.bfloat16)
     kept_kind = jnp.where(half == 0, dkey_held, dvalue_held) + swapped(sent_kind, parts)
-    kept_low = jnp.where(half == 0, rotate(kept_kind, held_cos, -held_sin), kept_kind).astype(
-        jnp.bfloat16
+    kept_low = from_pieces(
+        jnp.where(half == 0, rotate(kept_kind, held_cos, -held_sin), kept_kind).astype(
+            jnp.bfloat16
+        )
     )
     sent_back = jnp.concatenate([dquery_held, kept_low], axis=1)
     if by_axes:
@@ -1070,7 +1187,7 @@
     returned = exchange(sent_back)
     if by_axes:
         make_and_send([out_sum])
-        returned = made_before(first_sums, returned)
+        returned = taken_after([down_sum], made_before(first_sums, returned))
         for each in first_sums:
             each.send()
     dquery_low = by_head(returned[:, :HEAD_DIM]).reshape(HEADS * HEAD_DIM, rows)
@@ -1087,51 +1204,51 @@
         ]
     )
     key_value_right = jnp.concatenate([dkey_low, dvalue_low], axis=1)
-    normed_one_grad = (
-        contract(dquery_low, 0, query_weight[0][:D], 1)
-        + contract(dkey_low, 0, key_weight[0][key_weight[1] : key_weight[1] + D], 1)
-        + contract(dvalue_low, 0, value_weight[0][value_weight[1] : value_weight[1] + D], 1)
-    )
-    _, first_pull = jax.vjp(rms_norm, inputs, gain_one)
-    input_norm_grad, grad_one = first_pull(normed_one_grad)
-    input_grad = middle_grad + input_norm_grad
-
-    gain_grads = jnp.sum(
-        exchange(
-            jnp.broadcast_to(
-                jnp.concatenate([grad_one, grad_two[0]]).reshape(1, -1, 128),
-                (count, 2 * D // 128, 128),
-            )
-        ),
-        axis=0,
-    ).reshape(2, D)
     if by_axes:
         query_sum = sum_of(normed_one_cols, dquery_low, 1, GATE_ORDER)
         key_value_sum = sum_of(key_value_cols, key_value_right, 1, UP_ORDER)
         last_sums = [query_sum, key_value_sum]
         make_and_send(last_sums)
-        dquery_low = made_before(last_sums, dquery_low)
+        for each in last_sums:
+            each.make()
+        taken_after(early_sums + [out_sum], [each.made for each in last_sums])
         for each in last_sums:
             each.send()
+        dquery_late = taken_after(last_sums, dquery_low)
         make_and_send([gate_sum, up_sum, down_sum, out_sum])
+        normed_one_grad = (
+            contract(dquery_late, 0, query_weight[0][:D], 1)
+            + contract(dkey_low, 0, key_weight[0][key_weight[1] : key_weight[1] + D], 1)
+            + contract(dvalue_low, 0, value_weight[0][value_weight[1] : value_weight[1] + D], 1)
+        )
+        _, first_pull = jax.vjp(rms_norm, inputs, gain_one)
+        input_norm_grad, grad_one = first_pull(normed_one_grad)
+        input_grad = middle_grad + input_norm_grad
+
+        gain_sum = SummedWhole(jnp.concatenate([grad_one, grad_two[0]]).reshape(-1, 128), grid)
         attn_sums = last_sums + [out_sum]
-        gain_grads, input_grad = taken_after(
-            attn_sums + early_sums, (gain_grads, input_grad)
-        )
-        make_and_send(attn_sums + early_sums)
-        one_round(attn_sums + [down_sum])
-        one_round(attn_sums + [down_sum])
+        make_and_send([gain_sum])
+        one_round(attn_sums + early_sums + [gain_sum])
+        one_round(attn_sums + [down_sum, gain_sum])
+        one_round(attn_sums + [down_sum, gain_sum])
         ffn_units = [gate_sum.result(), up_sum.result(), down_sum.result()]
-        one_round(attn_sums)
+        one_round(attn_sums + [gain_sum])
+        gain_grads = gain_sum.result().reshape(2, D)
         query_unit, key_value_unit, out_unit = [each.result() for each in attn_sums]
     else:
         query_unit = scattered(normed_one_cols, dquery_low, 1)
         key_value_unit = scattered(key_value_cols, key_value_right, 1)
+        normed_one_grad = (
+            contract(dquery_low, 0, query_weight[0][:D], 1)
+            + contract(dkey_low, 0, key_weight[0][key_weight[1] : key_weight[1] + D], 1)
+            + contract(dvalue_low, 0, value_weight[0][value_weight[1] : value_weight[1] + D], 1)
+        )
+        _, first_pull = jax.vjp(rms_norm, inputs, gain_one)
+        input_norm_grad, grad_one = first_pull(normed_one_grad)
+        input_grad = middle_grad + input_norm_grad
+
+        gain_grads = lax.psum(jnp.stack([grad_one, grad_two[0]]), "seq")
     ffn_shard = shard_from_units(ffn_units, gain_grads[1], index, count)
-    if by_axes:
-        (query_unit, key_value_unit, out_unit), ffn_shard = together(
-            (query_unit, key_value_unit, out_unit), ffn_shard
-        )
     attn_shard = shard_from_units(
         [query_unit, key_value_unit, out_unit], gain_grads[0], index, count
     )

time: 929 us -> 876 us (0.943)
  local copies, waits for them, and re-layouts: 73.3 us -> 42.9 us
  other arithmetic: 89.2 us -> 69.6 us
  matrix products: 120 us -> 103 us
  waiting for transfers between devices: 252 us -> 268 us
    reshape x12 -> x1, local copies, waits for them, and re-layouts: 24.5 us -> 3.93 us  [per_device(): key_cols = jnp.swapaxes(key_rows.reshape(-1, KEY_TILE, HEAD_DIM), 1, 2)]
    dot_general x45, matrix products: 120 us -> 103 us  [contract(): lax.dot_general(left, right, (((left_dim,), (right_dim,)), ((), ())), pre...]
    all_to_all x5 -> x4, waiting for transfers between devices: 27.4 us -> 41 us  [exchange(): return lax.all_to_all(value, 'seq', 0, 0, tiled=True)]
    ppermute x47 -> x52, starting transfers between devices: 48 us -> 56.4 us  [shifted(): return lax.ppermute(value, 'seq', pairs)]
    ppermute x47 -> x52, waiting for transfers between devices: 185 us -> 178 us  [shifted(): return lax.ppermute(value, 'seq', pairs)]
    ppermute x4 -> x5, waiting for transfers between devices: 40 us -> 44.5 us  [swapped(): return lax.ppermute(value, 'seq', [(i, i ^ bit) for i in range(count)])]
    all_to_all x5 -> x4, starting transfers between devices: 35.5 us -> 32.5 us  [exchange(): return lax.all_to_all(value, 'seq', 0, 0, tiled=True)]
  transfers between devices with their start and end apart: 67 -> 72, of which waited for: 27 -> 29; matrix products, arithmetic and copies ran while one was open for 28% -> 21% of each run, Pallas kernels for 12% -> 13%
where the time goes in v4:
time: 876 us; the launch traced here: 871 us
  waiting for transfers between devices  268 us (31%)
  Pallas kernels  147 us (17%)
  starting transfers between devices  133 us (15%)
  matrix products  103 us (12%)
  blocking collectives  89.8 us (10%)
  other arithmetic  69.6 us (8%)
  local copies, waits for them, and re-layouts  42.9 us (5%)
  between operations  16 us (2%)
    ppermute x52, waiting for transfers between devices, shifted(): return lax.ppermute(value, 'seq', pairs)  178 us
    dot_general x45, matrix products, contract(): lax.dot_general(left, right, (((left_dim,), (right_dim,)), ((), ())), pre...  103 us
    all_to_all x1, blocking collectives, exchange(): return lax.all_to_all(value, 'seq', 0, 0, tiled=True)  89.8 us
    pallas_call x2, Pallas kernels, run_kernel(): pl.pallas_call(body, grid_spec=pltpu.PrefetchScalarGridSpec(num_scalar_pr...  75.2 us
    ppermute x52, starting transfers between devices, shifted(): return lax.ppermute(value, 'seq', pairs)  56.4 us
    ppermute x5, waiting for transfers between devices, swapped(): return lax.ppermute(value, 'seq', [(i, i ^ bit) for i in range(count)])  44.5 us
    all_to_all x4, waiting for transfers between devices, exchange(): return lax.all_to_all(value, 'seq', 0, 0, tiled=True)  41 us
    pallas_call x1, Pallas kernels, feed_forward(): pl.pallas_call(feed_forward_kernel, grid=(FF // FF_TILE,), in_specs=[fixe...  33.7 us
  transfers between devices with their start and end apart: 72, of which 29 were waited for; matrix products, arithmetic and copies ran while one was open for 21% of the time, Pallas kernels for 13%

profile of v4, /device:TPU:7, one launch (start us, length us, event | category | flops | bytes accessed | tf_op | source)
XLA Modules:
  0.0 870.7 jit_solution(4086723707134965047)
XLA Ops:
  14.4 6.3 all-to-all-start
  27.5 2.8 fusion.71
  30.3 18.5 %all-to-all-done = bf16[32,26,128]{2,1,0:T(8,128)(2,1)S(1)} async-done(((bf16[32,26,128]{2,1,0:T(8,128)(2,1)}), bf16[32,26,128]{2,1,0:T(8,128)(2,1)S(1)}, u32[]{:S(2)}, u32[]{:S(2)}) %all-to-all-start) | async-done | bytes 213024 | tf_op jit(solution)/shard_map/all_to_all | solution.py:900
  48.8 9.1 %collective-permute-done.2 = bf16[216,8,128]{2,1,0:T(8,128)(2,1)} collective-permute-done((bf16[216,8,128]{2,1,0:T(8,128)(2,1)S(1)}, bf16[216,8,128]{2,1,0:T(8,128)(2,1)}, u32[]{:S(2)}, u32[]{:S(2)}) %collective-permute-start.2) | collective-permute-done | bytes 442400 | tf_op jit(solution)/shard_map/ppermute | solution.py:183
  68.4 11.9 %collective-permute-done.5 = bf16[432,8,128]{2,1,0:T(8,128)(2,1)} collective-permute-done((bf16[432,8,128]{2,1,0:T(8,128)(2,1)S(1)}, bf16[432,8,128]{2,1,0:T(8,128)(2,1)}, u32[]{:S(2)}, u32[]{:S(2)}) %collective-permute-start.5) | collective-permute-done | bytes 884768 | tf_op jit(solution)/shard_map/ppermute | solution.py:183
  91.2 18.8 %convert_reduce_fusion = s32[4096]{0:T(1024)S(1)} fusion(s32[8192]{0:T(1024)S(1)} %bitcast.263, s32[4096]{0:T(1024)S(1)} %bitcast.270), kind=kLoop, calls=%fused_computation | loop fusion | flops 100659200 | bytes 65536 | tf_op jit(solution)/shard_map/reduce_sum | solution.py:922
  110.0 23.5 %collective-permute-done.8.refs_5_ = bf16[864,8,128]{2,1,0:T(8,128)(2,1)} collective-permute-done((bf16[864,8,128]{2,1,0:T(8,128)(2,1)}, bf16[864,8,128]{2,1,0:T(8,128)(2,1)}, u32[]{:S(2)}, u32[]{:S(2)}) %collective-permute-start.8) | collective-permute-done | bytes 1769504 | tf_op jit(solution)/shard_map/ppermute | solution.py:183
  135.8 3.7 collective-permute-start.10
  143.3 5.1 collective-permute-done.11.refs_6_
  150.9 13.6 %place_blocks.1 = bf16[6912,8,128]{2,1,0:T(8,128)(2,1)} custom-call(s32[64]{0:T(128)S(1)} %pad_add_fusion.table_ref, bf16[864,8,128]{2,1,0:T(8,128)(2,1)S(1)} %constant_dynamic-update-slice_fusion.refs_0_, bf16[864,8,128]{2,1,0:T(8,128)(2,1)} %collective-permute-done.7.refs_1_, bf16[864,8,128]{2,1,0:T(8,128)(2,1)} %collective-permute-done.9.refs_2_, ...), custom_call_target="tpu_custom_call" | custom-call | bytes 28311552 | tf_op jit(solution)/shard_map/place_blocks/pallas_call | solution.py:226
  164.5 5.8 project.1
  170.3 89.8 %all_to_all.25.query_ref = bf16[32,192,128]{2,1,0:T(8,128)(2,1)S(1)} all-to-all(bf16[32,192,128]{2,1,0:T(8,128)(2,1)S(1)} %project.1), channel_id=1, replica_groups=mesh['seq'=32] {'seq'}, dimensions={0} | all-to-all | bytes 3145728 | tf_op jit(solution)/shard_map/all_to_all | solution.py:900
  262.5 33.5 %collective-permute-done.14.refs_2_ = bf16[32,96,128]{2,1,0:T(8,128)(2,1)S(1)} collective-permute-done((bf16[32,96,128]{2,1,0:T(8,128)(2,1)S(1)}, bf16[32,96,128]{2,1,0:T(8,128)(2,1)S(1)}, u32[]{:S(2)}, u32[]{:S(2)}) %collective-permute-start.14) | collective-permute-done | bytes 786464 | tf_op jit(solution)/shard_map/ppermute | solution.py:903
  300.8 30.7 %attention_forward.1 = (f32[8,96,512]{2,1,0:T(8,128)}, bf16[32,96,128]{2,1,0:T(8,128)(2,1)}, f32[8,1,512]{2,1,0:T(1,128)S(1)}, bf16[8192,96]{1,0:T(8,128)(2,1)}, bf16[8,96,1024]{2,1,0:T(8,128)(2,1)}) custom-call(s32[8]{0:T(128)S(1)} %and_select_fusion.1.low_ref, s32[8]{0:T(128)S(1)} %and_select_fusion.high_ref, s32[1]{0:T(128)} %bitcast.32.half_ref, ...), custom_call_target="tpu_custom_call" | custom-call | flops 20000000000 | bytes 16777216 | tf_op jit(solution)/shard_map/attention_forward/pallas_call | solution.py:772
  331.5 13.9 %all-to-all-start.2 = ((bf16[32,96,128]{2,1,0:T(8,128)(2,1)}), bf16[32,96,128]{2,1,0:T(8,128)(2,1)S(1)}, u32[]{:S(2)}, u32[]{:S(2)}) async-start(bf16[32,96,128]{2,1,0:T(8,128)(2,1)} %get-tuple-element.159), calls=%async_computation.2 | async-start | bytes 1572864 | tf_op jit(solution)/shard_map/all_to_all | solution.py:900
  346.2 3.9 multiply_sine_fusion
  352.5 3.9 copy.106
  356.4 8.6 all-to-all-done.2.mixed_piece_ref
  365.0 33.7 %feed_forward.1 = (bf16[256,1536]{1,0:T(8,128)(2,1)}, f32[256,1536]{1,0:T(8,128)}, bf16[256,1536]{1,0:T(8,128)(2,1)S(1)}, bf16[32,96,128]{2,1,0:T(8,128)(2,1)}, ...) custom-call(bf16[256,1536]{1,0:T(8,128)(2,1)S(1)} %copy-done.2, ...), custom_call_target="tpu_custom_call" | custom-call | flops 19327352832 | bytes 37748736 | tf_op jit(solution)/shard_map/feed_forward/pallas_call | solution.py:516
  403.2 6.2 convolution_convert_fusion.1
  413.8 6.1 convolution_convert_fusion.2
  419.9 4.6 all-to-all-start.3
  424.5 3.8 reorder_blocks.8
  428.3 5.8 convolution_convert_fusion
  434.4 4.9 add_convert_fusion.1
  439.4 4.7 add_convert_fusion.2
  445.9 44.5 %attention_backward.1 = (bf16[32,96,128]{2,1,0:T(8,128)(2,1)S(1)}, f32[2,1,32,96,128]{4,3,2,1,0:T(8,128)}, bf16[2,1,32,96,128]{4,3,2,1,0:T(8,128)(2,1)}) custom-call(s32[8]{0:T(128)S(1)} %and_select_fusion.1.low_ref, s32[8]{0:T(128)S(1)} %and_select_fusion.high_ref, bf16[32,192,128]{2,1,0:T(8,128)(2,1)} %copy-done.20, bf16[32,96,128]{2,1,0:T(8,128)(2,1)} %copy-done.40, ...), custom_call_target="tpu_custom_call" | custom-call | flops 49999998976 | bytes 16777216 | tf_op jit(solution)/shard_map/attention_backward/pallas_call | solution.py:772
  491.0 3.4 collective-permute-done.18
  494.4 2.8 convert_add_fusion
  497.2 15.8 %collective-permute-done.19 = bf16[384,4096]{1,0:T(8,128)(2,1)} collective-permute-done((bf16[384,4096]{1,0:T(8,128)(2,1)}, bf16[384,4096]{1,0:T(8,128)(2,1)}, u32[]{:S(2)}, u32[]{:S(2)}) %collective-permute-start.19) | collective-permute-done | bytes 3145760 | tf_op jit(solution)/shard_map/ppermute | solution.py:183
  514.5 5.0 add_convert_fusion
  519.5 3.1 fusion.14
  522.5 2.9 fusion.13
  525.5 5.8 collective-permute-done.21
  535.8 7.6 all-to-all-start.4
  548.1 4.4 reorder_blocks.10
  552.5 3.0 copy.113
  555.5 3.1 collective-permute-start.24
  567.8 19.8 %collective-permute-done.24 = bf16[96,4096]{1,0:T(8,128)(2,1)S(1)} collective-permute-done((bf16[96,4096]{1,0:T(8,128)(2,1)}, bf16[96,4096]{1,0:T(8,128)(2,1)S(1)}, u32[]{:S(2)}, u32[]{:S(2)}) %collective-permute-start.24) | collective-permute-done | bytes 786464 | tf_op jit(solution)/shard_map/ppermute | solution.py:183
  587.6 3.6 fusion.16
  591.2 13.3 %collective-permute-done.23 = bf16[96,4096]{1,0:T(8,128)(2,1)S(1)} collective-permute-done((bf16[96,4096]{1,0:T(8,128)(2,1)}, bf16[96,4096]{1,0:T(8,128)(2,1)S(1)}, u32[]{:S(2)}, u32[]{:S(2)}) %collective-permute-start.23) | collective-permute-done | bytes 786464 | tf_op jit(solution)/shard_map/ppermute | solution.py:183
  604.5 3.0 fusion.15
  607.5 13.8 %all-to-all-done.4 = bf16[32,192,128]{2,1,0:T(8,128)(2,1)} async-done(((bf16[32,192,128]{2,1,0:T(8,128)(2,1)}), bf16[32,192,128]{2,1,0:T(8,128)(2,1)}, u32[]{:S(2)}, u32[]{:S(2)}) %all-to-all-start.4) | async-done | bytes 1572896 | tf_op jit(solution)/shard_map/all_to_all | solution.py:900
  625.0 4.5 convolution_convert_fusion.4
  632.8 4.3 collective-permute-start.30
  640.0 3.8 fusion.44
  650.5 3.2 collective-permute-done.30
  653.8 16.9 %collective-permute-done.31 = bf16[96,4096]{1,0:T(8,128)(2,1)S(1)} collective-permute-done((bf16[96,4096]{1,0:T(8,128)(2,1)S(1)}, bf16[96,4096]{1,0:T(8,128)(2,1)S(1)}, u32[]{:S(2)}, u32[]{:S(2)}) %collective-permute-start.31) | collective-permute-done | bytes 786464 | tf_op jit(solution)/shard_map/ppermute | solution.py:183
  670.6 3.8 add_convert_fusion.3
  676.5 4.1 collective-permute-start.35
  685.1 4.1 fusion.63
  696.0 16.9 %collective-permute-done.34 = bf16[96,4096]{1,0:T(8,128)(2,1)S(1)} collective-permute-done((bf16[96,4096]{1,0:T(8,128)(2,1)S(1)}, bf16[96,4096]{1,0:T(8,128)(2,1)S(1)}, u32[]{:S(2)}, u32[]{:S(2)}) %collective-permute-start.34) | collective-permute-done | bytes 786464 | tf_op jit(solution)/shard_map/ppermute | solution.py:183
  714.8 4.1 collective-permute-start.41
  727.2 12.8 %collective-permute-done.61 = bf16[48,4096]{1,0:T(8,128)(2,1)S(1)} collective-permute-done((bf16[48,4096]{1,0:T(8,128)(2,1)S(1)}, bf16[48,4096]{1,0:T(8,128)(2,1)S(1)}, u32[]{:S(2)}, u32[]{:S(2)}) %collective-permute-start.61) | collective-permute-done | bytes 393248 | tf_op jit(solution)/shard_map/ppermute | solution.py:183
  749.8 3.2 collective-permute-start.45
  756.4 11.5 %collective-permute-done.45 = bf16[48,1536]{1,0:T(8,128)(2,1)S(1)} collective-permute-done((bf16[48,1536]{1,0:T(8,128)(2,1)S(1)}, bf16[48,1536]{1,0:T(8,128)(2,1)S(1)}, u32[]{:S(2)}, u32[]{:S(2)}) %collective-permute-start.45) | collective-permute-done | bytes 147488 | tf_op jit(solution)/shard_map/ppermute | solution.py:183
  777.7 6.4 collective-permute-done.48
  785.1 3.2 collective-permute-start.55
  809.0 4.2 collective-permute-start.56
  817.2 19.5 %collective-permute-start.66 = (bf16[196608]{0:T(1024)(128)(2,1)}, bf16[196608]{0:T(1024)(128)(2,1)S(1)}, u32[]{:S(2)}, u32[]{:S(2)}) collective-permute-start(bf16[196608]{0:T(1024)(128)(2,1)} %get-tuple-element.330), channel_id=1, source_target_pairs={{1,0},{4,1},{7,2},{10,3},{13,4},{16,5},{19,6},{22,7},{25,8},{28,9}... | collective-permute-start | bytes 1179656 | tf_op jit(solution)/shard_map/ppermute | solution.py:140
  842.0 3.0 fusion.64
  844.9 3.2 copy.114
  848.2 5.1 collective-permute-done.59
  855.5 5.4 multiply_subtract_fusion
  (414 shorter events, 183.2 us)
Async XLA Ops:
  9.1 18.4 %collective-permute-start.6 = (bf16[1536]{0:T(1024)(128)(2,1)S(1)}, bf16[1536]{0:T(1024)(128)(2,1)S(1)}, u32[]{:S(2)}, u32[]{:S(2)}) collective-permute-start(bf16[1536]{0:T(1024)(128)(2,1)S(1)} %slice.819), channel_id=1, source_target_pairs={{1,0},{2,1},{3,2},{4,3},{5,4},{6,5},{7,6},{8,7},{9,8},{10,9},{11,1... | collective-permute-start | bytes 9224 | tf_op jit(solution)/shard_map/ppermute | solution.py:86
  11.7 9.1 %collective-permute-start = (bf16[1536]{0:T(1024)(128)(2,1)S(1)}, bf16[1536]{0:T(1024)(128)(2,1)S(1)}, u32[]{:S(2)}, u32[]{:S(2)}) collective-permute-start(bf16[1536]{0:T(1024)(128)(2,1)S(1)} %slice.815), channel_id=1, source_target_pairs={{1,0},{2,1},{3,2},{4,3},{5,4},{6,5},{7,6},{8,7},{9,8},{10,9},{11,1... | collective-permute-start | bytes 9224 | tf_op jit(solution)/shard_map/ppermute | solution.py:86
  14.4 34.4 %all-to-all-start = ((bf16[32,26,128]{2,1,0:T(8,128)(2,1)}), bf16[32,26,128]{2,1,0:T(8,128)(2,1)S(1)}, u32[]{:S(2)}, u32[]{:S(2)}) async-start(bf16[32,26,128]{2,1,0:T(8,128)(2,1)} %broadcast_in_dim.9), calls=%async_computation | async-start | bytes 524288 | tf_op jit(solution)/shard_map/all_to_all | solution.py:900
  20.8 344.2 %all-gather.2.cloned.1.call-start = ((), (), s32[]{:S(2)}) async-start(), calls=%async_computation.5 | async-start | bytes 38928384 | tf_op jit(solution)/shard_map/all_gather | solution.py:959
  22.8 26.0 %collective-permute-start.1 = (bf16[216,8,128]{2,1,0:T(8,128)(2,1)S(1)}, bf16[216,8,128]{2,1,0:T(8,128)(2,1)S(1)}, u32[]{:S(2)}, u32[]{:S(2)}) collective-permute-start(bf16[216,8,128]{2,1,0:T(8,128)(2,1)S(1)} %pad_maximum_fusion.5), channel_id=1, source_target_pairs={{0,8},{1,9},{2,10},{3,11},{4,12},{5,13},{6,14},{7,15},{8,16},{9,17... | collective-permute-start | bytes 1327112 | tf_op jit(solution)/shard_map/ppermute | solution.py:183
  24.0 33.9 %collective-permute-start.2 = (bf16[216,8,128]{2,1,0:T(8,128)(2,1)S(1)}, bf16[216,8,128]{2,1,0:T(8,128)(2,1)}, u32[]{:S(2)}, u32[]{:S(2)}) collective-permute-start(bf16[216,8,128]{2,1,0:T(8,128)(2,1)S(1)} %pad_maximum_fusion.5), channel_id=1, source_target_pairs={{0,16},{1,17},{2,18},{3,19},{4,20},{5,21},{6,22},{7,23},{8,24},{9,... | collective-permute-start | bytes 1327112 | tf_op jit(solution)/shard_map/ppermute | solution.py:183
  26.2 31.7 %collective-permute-start.3 = (bf16[216,8,128]{2,1,0:T(8,128)(2,1)S(1)}, bf16[216,8,128]{2,1,0:T(8,128)(2,1)}, u32[]{:S(2)}, u32[]{:S(2)}) collective-permute-start(bf16[216,8,128]{2,1,0:T(8,128)(2,1)S(1)} %pad_maximum_fusion.5), channel_id=1, source_target_pairs={{0,24},{1,25},{2,26},{3,27},{4,28},{5,29},{6,30},{7,31},{8,0},{9,1... | collective-permute-start | bytes 1327112 | tf_op jit(solution)/shard_map/ppermute | solution.py:183
  60.3 20.0 %collective-permute-start.5 = (bf16[432,8,128]{2,1,0:T(8,128)(2,1)S(1)}, bf16[432,8,128]{2,1,0:T(8,128)(2,1)}, u32[]{:S(2)}, u32[]{:S(2)}) collective-permute-start(bf16[432,8,128]{2,1,0:T(8,128)(2,1)S(1)} %pad_maximum_fusion.3), channel_id=1, source_target_pairs={{0,2},{1,3},{2,0},{3,1},{4,6},{5,7},{6,4},{7,5},{8,10},{9,11},{10,... | collective-permute-start | bytes 2654216 | tf_op jit(solution)/shard_map/ppermute | solution.py:183
  61.6 19.8 %collective-permute-start.4 = (bf16[432,8,128]{2,1,0:T(8,128)(2,1)}, bf16[432,8,128]{2,1,0:T(8,128)(2,1)}, u32[]{:S(2)}, u32[]{:S(2)}) collective-permute-start(bf16[432,8,128]{2,1,0:T(8,128)(2,1)} %pad_maximum_fusion.2), channel_id=1, source_target_pairs={{0,4},{1,5},{2,6},{3,7},{4,0},{5,1},{6,2},{7,3},{8,12},{9,13},{10,... | collective-permute-start | bytes 2654216 | tf_op jit(solution)/shard_map/ppermute | solution.py:183
  87.2 46.3 %collective-permute-start.8 = (bf16[864,8,128]{2,1,0:T(8,128)(2,1)}, bf16[864,8,128]{2,1,0:T(8,128)(2,1)}, u32[]{:S(2)}, u32[]{:S(2)}) collective-permute-start(bf16[864,8,128]{2,1,0:T(8,128)(2,1)} %constant_dynamic-update-slice_fusion.2.refs_4_), channel_id=1, source_target_pairs={{0,4},{1,5},{2,6},{3,7},{4,0},{5,1},{6,2},{7,3},{8,12},{9,13},{10,... | collective-permute-start | bytes 5308424 | tf_op jit(solution)/shard_map/ppermute | solution.py:183
  90.0 45.9 %collective-permute-start.7 = (bf16[864,8,128]{2,1,0:T(8,128)(2,1)S(1)}, bf16[864,8,128]{2,1,0:T(8,128)(2,1)}, u32[]{:S(2)}, u32[]{:S(2)}) collective-permute-start(bf16[864,8,128]{2,1,0:T(8,128)(2,1)S(1)} %constant_dynamic-update-slice_fusion.refs_0_), channel_id=1, source_target_pairs={{0,2},{1,3},{2,0},{3,1},{4,6},{5,7},{6,4},{7,5},{8,10},{9,11},{10,... | collective-permute-start | bytes 5308424 | tf_op jit(solution)/shard_map/ppermute | solution.py:183
  139.6 11.2 %collective-permute-start.12 = (bf16[864,8,128]{2,1,0:T(8,128)(2,1)}, bf16[864,8,128]{2,1,0:T(8,128)(2,1)}, u32[]{:S(2)}, u32[]{:S(2)}) collective-permute-start(bf16[864,8,128]{2,1,0:T(8,128)(2,1)} %collective-permute-done.8.refs_5_), channel_id=1, source_target_pairs={{0,1},{1,0},{2,3},{3,2},{4,5},{5,4},{6,7},{7,6},{8,9},{9,8},{10,11... | collective-permute-start | bytes 5308424 | tf_op jit(solution)/shard_map/ppermute | solution.py:183
  140.1 10.7 %collective-permute-start.9 = (bf16[864,8,128]{2,1,0:T(8,128)(2,1)S(1)}, bf16[864,8,128]{2,1,0:T(8,128)(2,1)}, u32[]{:S(2)}, u32[]{:S(2)}) collective-permute-start(bf16[864,8,128]{2,1,0:T(8,128)(2,1)S(1)} %constant_dynamic-update-slice_fusion.refs_0_), channel_id=1, source_target_pairs={{0,1},{1,0},{2,3},{3,2},{4,5},{5,4},{6,7},{7,6},{8,9},{9,8},{10,11... | collective-permute-start | bytes 5308424 | tf_op jit(solution)/shard_map/ppermute | solution.py:183
  260.2 35.8 %collective-permute-start.14 = (bf16[32,96,128]{2,1,0:T(8,128)(2,1)S(1)}, bf16[32,96,128]{2,1,0:T(8,128)(2,1)S(1)}, u32[]{:S(2)}, u32[]{:S(2)}) collective-permute-start(bf16[32,96,128]{2,1,0:T(8,128)(2,1)S(1)} %slice.825.refs_0_), channel_id=1, source_target_pairs={{0,2},{1,3},{2,0},{3,1},{4,6},{5,7},{6,4},{7,5},{8,10},{9,11},{10,... | collective-permute-start | bytes 2359304 | tf_op jit(solution)/shard_map/ppermute | solution.py:903
  261.6 37.2 %collective-permute-start.13 = (bf16[32,96,128]{2,1,0:T(8,128)(2,1)S(1)}, bf16[32,96,128]{2,1,0:T(8,128)(2,1)S(1)}, u32[]{:S(2)}, u32[]{:S(2)}) collective-permute-start(bf16[32,96,128]{2,1,0:T(8,128)(2,1)S(1)} %slice.825.refs_0_), channel_id=1, source_target_pairs={{0,1},{1,0},{2,3},{3,2},{4,5},{5,4},{6,7},{7,6},{8,9},{9,8},{10,11... | collective-permute-start | bytes 2359304 | tf_op jit(solution)/shard_map/ppermute | solution.py:903
  331.5 33.5 %all-to-all-start.2 = ((bf16[32,96,128]{2,1,0:T(8,128)(2,1)}), bf16[32,96,128]{2,1,0:T(8,128)(2,1)S(1)}, u32[]{:S(2)}, u32[]{:S(2)}) async-start(bf16[32,96,128]{2,1,0:T(8,128)(2,1)} %get-tuple-element.159), calls=%async_computation.2 | async-start | bytes 1572864 | tf_op jit(solution)/shard_map/all_to_all | solution.py:900
  409.4 25.0 %collective-permute-start.17 = (bf16[768,4096]{1,0:T(8,128)(2,1)}, bf16[768,4096]{1,0:T(8,128)(2,1)}, u32[]{:S(2)}, u32[]{:S(2)}) collective-permute-start(bf16[768,4096]{1,0:T(8,128)(2,1)} %convolution_convert_fusion.1), channel_id=1, source_target_pairs={{0,1},{1,0},{2,3},{3,2},{4,5},{5,4},{6,7},{7,6},{8,9},{9,8},{10,11... | collective-permute-start | bytes 18874376 | tf_op jit(solution)/shard_map/ppermute | solution.py:183
  419.9 19.4 %collective-permute-start.16 = (bf16[768,4096]{1,0:T(8,128)(2,1)}, bf16[768,4096]{1,0:T(8,128)(2,1)}, u32[]{:S(2)}, u32[]{:S(2)}) collective-permute-start(bf16[768,4096]{1,0:T(8,128)(2,1)} %convolution_convert_fusion.2), channel_id=1, source_target_pairs={{0,1},{1,0},{2,3},{3,2},{4,5},{5,4},{6,7},{7,6},{8,9},{9,8},{10,11... | collective-permute-start | bytes 18874376 | tf_op jit(solution)/shard_map/ppermute | solution.py:183
  419.9 24.2 %all-to-all-start.3 = ((bf16[32,96,128]{2,1,0:T(8,128)(2,1)}), bf16[32,96,128]{2,1,0:T(8,128)(2,1)S(1)}, u32[]{:S(2)}, u32[]{:S(2)}) async-start(bf16[32,96,128]{2,1,0:T(8,128)(2,1)} %get-tuple-element.169), calls=%async_computation.3 | async-start | bytes 1572864 | tf_op jit(solution)/shard_map/all_to_all | solution.py:900
  434.1 80.4 %collective-permute-start.22 = (bf16[2048,1536]{1,0:T(8,128)(2,1)}, bf16[2048,1536]{1,0:T(8,128)(2,1)}, u32[]{:S(2)}, u32[]{:S(2)}) collective-permute-start(bf16[2048,1536]{1,0:T(8,128)(2,1)} %convolution_convert_fusion), channel_id=1, source_target_pairs={{0,1},{1,0},{2,3},{3,2},{4,5},{5,4},{6,7},{7,6},{8,9},{9,8},{10,11... | collective-permute-start | bytes 18874376 | tf_op jit(solution)/shard_map/ppermute | solution.py:183
  444.1 68.9 %collective-permute-start.19 = (bf16[384,4096]{1,0:T(8,128)(2,1)}, bf16[384,4096]{1,0:T(8,128)(2,1)}, u32[]{:S(2)}, u32[]{:S(2)}) collective-permute-start(bf16[384,4096]{1,0:T(8,128)(2,1)} %add_convert_fusion.2), channel_id=1, source_target_pairs={{0,2},{1,3},{2,0},{3,1},{4,6},{5,7},{6,4},{7,5},{8,10},{9,11},{10,... | collective-permute-start | bytes 9437192 | tf_op jit(solution)/shard_map/ppermute | solution.py:183
  445.0 68.9 %collective-permute-start.20 = (bf16[384,4096]{1,0:T(8,128)(2,1)}, bf16[384,4096]{1,0:T(8,128)(2,1)}, u32[]{:S(2)}, u32[]{:S(2)}) collective-permute-start(bf16[384,4096]{1,0:T(8,128)(2,1)} %add_convert_fusion.1), channel_id=1, source_target_pairs={{0,4},{1,5},{2,6},{3,7},{4,0},{5,1},{6,2},{7,3},{8,12},{9,13},{10,... | collective-permute-start | bytes 9437192 | tf_op jit(solution)/shard_map/ppermute | solution.py:183
  514.1 17.2 %collective-permute-start.21 = (bf16[32,96,128]{2,1,0:T(8,128)(2,1)S(1)}, bf16[32,96,128]{2,1,0:T(8,128)(2,1)S(1)}, u32[]{:S(2)}, u32[]{:S(2)}) collective-permute-start(bf16[32,96,128]{2,1,0:T(8,128)(2,1)S(1)} %fusion.77), channel_id=1, source_target_pairs={{0,2},{1,3},{2,0},{3,1},{4,6},{5,7},{6,4},{7,5},{8,10},{9,11},{10,... | collective-permute-start | bytes 2359304 | tf_op jit(solution)/shard_map/ppermute | solution.py:903
  533.5 87.8 %collective-permute-start.25 = (bf16[1024,1536]{1,0:T(8,128)(2,1)}, bf16[1024,1536]{1,0:T(8,128)(2,1)}, u32[]{:S(2)}, u32[]{:S(2)}) collective-permute-start(bf16[1024,1536]{1,0:T(8,128)(2,1)} %add_convert_fusion), channel_id=1, source_target_pairs={{0,4},{1,5},{2,6},{3,7},{4,0},{5,1},{6,2},{7,3},{8,12},{9,13},{10,... | collective-permute-start | bytes 9437192 | tf_op jit(solution)/shard_map/ppermute | solution.py:183
  535.8 85.5 %all-to-all-start.4 = ((bf16[32,192,128]{2,1,0:T(8,128)(2,1)}), bf16[32,192,128]{2,1,0:T(8,128)(2,1)}, u32[]{:S(2)}, u32[]{:S(2)}) async-start(bf16[32,192,128]{2,1,0:T(8,128)(2,1)} %pad_maximum_fusion), calls=%async_computation.4 | async-start | bytes 3145728 | tf_op jit(solution)/shard_map/all_to_all | solution.py:900
  555.5 32.1 %collective-permute-start.24 = (bf16[96,4096]{1,0:T(8,128)(2,1)}, bf16[96,4096]{1,0:T(8,128)(2,1)S(1)}, u32[]{:S(2)}, u32[]{:S(2)}) collective-permute-start(bf16[96,4096]{1,0:T(8,128)(2,1)} %fusion.14), channel_id=1, source_target_pairs={{0,24},{1,25},{2,26},{3,27},{4,28},{5,29},{6,30},{7,31},{8,0},{9,1... | collective-permute-start | bytes 2359304 | tf_op jit(solution)/shard_map/ppermute | solution.py:183
  560.7 43.8 %collective-permute-start.23 = (bf16[96,4096]{1,0:T(8,128)(2,1)}, bf16[96,4096]{1,0:T(8,128)(2,1)S(1)}, u32[]{:S(2)}, u32[]{:S(2)}) collective-permute-start(bf16[96,4096]{1,0:T(8,128)(2,1)} %fusion.13), channel_id=1, source_target_pairs={{0,24},{1,25},{2,26},{3,27},{4,28},{5,29},{6,30},{7,31},{8,0},{9,1... | collective-permute-start | bytes 2359304 | tf_op jit(solution)/shard_map/ppermute | solution.py:183
  629.6 17.4 %collective-permute-start.28 = (bf16[1536,768]{1,0:T(8,128)(2,1)}, bf16[1536,768]{1,0:T(8,128)(2,1)}, u32[]{:S(2)}, u32[]{:S(2)}) collective-permute-start(bf16[1536,768]{1,0:T(8,128)(2,1)} %convolution_convert_fusion.4), channel_id=1, source_target_pairs={{0,1},{1,0},{2,3},{3,2},{4,5},{5,4},{6,7},{7,6},{8,9},{9,8},{10,11... | collective-permute-start | bytes 7077896 | tf_op jit(solution)/shard_map/ppermute | solution.py:183
  631.4 18.5 %collective-permute-start.26 = (bf16[768,1536]{1,0:T(8,128)(2,1)S(1)}, bf16[768,1536]{1,0:T(8,128)(2,1)S(1)}, u32[]{:S(2)}, u32[]{:S(2)}) collective-permute-start(bf16[768,1536]{1,0:T(8,128)(2,1)S(1)} %convolution_convert_fusion.5), channel_id=1, source_target_pairs={{0,1},{1,0},{2,3},{3,2},{4,5},{5,4},{6,7},{7,6},{8,9},{9,8},{10,11... | collective-permute-start | bytes 7077896 | tf_op jit(solution)/shard_map/ppermute | solution.py:183
  632.5 17.9 %collective-permute-start.32 = (bf16[768,1536]{1,0:T(8,128)(2,1)S(1)}, bf16[768,1536]{1,0:T(8,128)(2,1)S(1)}, u32[]{:S(2)}, u32[]{:S(2)}) collective-permute-start(bf16[768,1536]{1,0:T(8,128)(2,1)S(1)} %convolution_convert_fusion.3), channel_id=1, source_target_pairs={{0,1},{1,0},{2,3},{3,2},{4,5},{5,4},{6,7},{7,6},{8,9},{9,8},{10,11... | collective-permute-start | bytes 7077896 | tf_op jit(solution)/shard_map/ppermute | solution.py:183
  632.8 20.9 %collective-permute-start.30 = (bf16[96,4096]{1,0:T(8,128)(2,1)S(1)}, bf16[96,4096]{1,0:T(8,128)(2,1)S(1)}, u32[]{:S(2)}, u32[]{:S(2)}) collective-permute-start(bf16[96,4096]{1,0:T(8,128)(2,1)S(1)} %copy-done.39), channel_id=1, source_target_pairs={{0,24},{1,25},{2,26},{3,27},{4,28},{5,29},{6,30},{7,31},{8,0},{9,1... | collective-permute-start | bytes 2359304 | tf_op jit(solution)/shard_map/ppermute | solution.py:183
  637.1 33.5 %collective-permute-start.31 = (bf16[96,4096]{1,0:T(8,128)(2,1)S(1)}, bf16[96,4096]{1,0:T(8,128)(2,1)S(1)}, u32[]{:S(2)}, u32[]{:S(2)}) collective-permute-start(bf16[96,4096]{1,0:T(8,128)(2,1)S(1)} %copy-done.38), channel_id=1, source_target_pairs={{0,24},{1,25},{2,26},{3,27},{4,28},{5,29},{6,30},{7,31},{8,0},{9,1... | collective-permute-start | bytes 2359304 | tf_op jit(solution)/shard_map/ppermute | solution.py:183
  649.1 35.0 %collective-permute-start.29 = (bf16[768,768]{1,0:T(8,128)(2,1)S(1)}, bf16[768,768]{1,0:T(8,128)(2,1)S(1)}, u32[]{:S(2)}, u32[]{:S(2)}) collective-permute-start(bf16[768,768]{1,0:T(8,128)(2,1)S(1)} %add_convert_fusion.4), channel_id=1, source_target_pairs={{0,4},{1,5},{2,6},{3,7},{4,0},{5,1},{6,2},{7,3},{8,12},{9,13},{10,... | collective-permute-start | bytes 3538952 | tf_op jit(solution)/shard_map/ppermute | solution.py:183
  650.4 34.7 %collective-permute-start.27 = (bf16[384,1536]{1,0:T(8,128)(2,1)S(1)}, bf16[384,1536]{1,0:T(8,128)(2,1)}, u32[]{:S(2)}, u32[]{:S(2)}) collective-permute-start(bf16[384,1536]{1,0:T(8,128)(2,1)S(1)} %add_convert_fusion.5), channel_id=1, source_target_pairs={{0,2},{1,3},{2,0},{3,1},{4,6},{5,7},{6,4},{7,5},{8,10},{9,11},{10,... | collective-permute-start | bytes 3538952 | tf_op jit(solution)/shard_map/ppermute | solution.py:183
  674.4 38.5 %collective-permute-start.36 = (bf16[512,1536]{1,0:T(8,128)(2,1)}, bf16[512,1536]{1,0:T(8,128)(2,1)S(1)}, u32[]{:S(2)}, u32[]{:S(2)}) collective-permute-start(bf16[512,1536]{1,0:T(8,128)(2,1)} %add_convert_fusion.3), channel_id=1, source_target_pairs={{0,2},{1,3},{2,0},{3,1},{4,6},{5,7},{6,4},{7,5},{8,10},{9,11},{10,... | collective-permute-start | bytes 4718600 | tf_op jit(solution)/shard_map/ppermute | solution.py:183
  676.5 19.5 %collective-permute-start.35 = (bf16[96,4096]{1,0:T(8,128)(2,1)S(1)}, bf16[96,4096]{1,0:T(8,128)(2,1)S(1)}, u32[]{:S(2)}, u32[]{:S(2)}) collective-permute-start(bf16[96,4096]{1,0:T(8,128)(2,1)S(1)} %fusion.18), channel_id=1, source_target_pairs={{0,24},{1,25},{2,26},{3,27},{4,28},{5,29},{6,30},{7,31},{8,0},{9,1... | collective-permute-start | bytes 2359304 | tf_op jit(solution)/shard_map/ppermute | solution.py:183
  681.1 31.8 %collective-permute-start.33 = (bf16[384,1536]{1,0:T(8,128)(2,1)S(1)}, bf16[384,1536]{1,0:T(8,128)(2,1)S(1)}, u32[]{:S(2)}, u32[]{:S(2)}) collective-permute-start(bf16[384,1536]{1,0:T(8,128)(2,1)S(1)} %fusion.34), channel_id=1, source_target_pairs={{0,4},{1,5},{2,6},{3,7},{4,0},{5,1},{6,2},{7,3},{8,12},{9,13},{10,... | collective-permute-start | bytes 3538952 | tf_op jit(solution)/shard_map/ppermute | solution.py:183
  684.1 28.8 %collective-permute-start.34 = (bf16[96,4096]{1,0:T(8,128)(2,1)S(1)}, bf16[96,4096]{1,0:T(8,128)(2,1)S(1)}, u32[]{:S(2)}, u32[]{:S(2)}) collective-permute-start(bf16[96,4096]{1,0:T(8,128)(2,1)S(1)} %fusion.17), channel_id=1, source_target_pairs={{0,24},{1,25},{2,26},{3,27},{4,28},{5,29},{6,30},{7,31},{8,0},{9,1... | collective-permute-start | bytes 2359304 | tf_op jit(solution)/shard_map/ppermute | solution.py:183
  689.3 23.6 %collective-permute-start.37 = (f32[24,128]{1,0:T(8,128)S(1)}, f32[24,128]{1,0:T(8,128)S(1)}, u32[]{:S(2)}, u32[]{:S(2)}) collective-permute-start(f32[24,128]{1,0:T(8,128)S(1)} %pad_maximum_fusion.6), channel_id=1, source_target_pairs={{0,1},{1,0},{2,3},{3,2},{4,5},{5,4},{6,7},{7,6},{8,9},{9,8},{10,11... | collective-permute-start | bytes 36872 | tf_op jit(solution)/shard_map/ppermute | solution.py:183
  714.8 29.5 %collective-permute-start.41 = (bf16[128,1536]{1,0:T(8,128)(2,1)S(1)}, bf16[128,1536]{1,0:T(8,128)(2,1)S(1)}, u32[]{:S(2)}, u32[]{:S(2)}) collective-permute-start(bf16[128,1536]{1,0:T(8,128)(2,1)S(1)} %add_convert_fusion.9), channel_id=1, source_target_pairs={{0,24},{1,25},{2,26},{3,27},{4,28},{5,29},{6,30},{7,31},{8,0},{9,1... | collective-permute-start | bytes 1179656 | tf_op jit(solution)/shard_map/ppermute | solution.py:183
  719.2 25.1 %collective-permute-start.40 = (bf16[192,1536]{1,0:T(8,128)(2,1)S(1)}, bf16[192,1536]{1,0:T(8,128)(2,1)S(1)}, u32[]{:S(2)}, u32[]{:S(2)}) collective-permute-start(bf16[192,1536]{1,0:T(8,128)(2,1)S(1)} %fusion.38), channel_id=1, source_target_pairs={{0,2},{1,3},{2,0},{3,1},{4,6},{5,7},{6,4},{7,5},{8,10},{9,11},{10,... | collective-permute-start | bytes 1769480 | tf_op jit(solution)/shard_map/ppermute | solution.py:183
  722.1 22.3 %collective-permute-start.39 = (bf16[192,768]{1,0:T(8,128)(2,1)S(1)}, bf16[192,768]{1,0:T(8,128)(2,1)S(1)}, u32[]{:S(2)}, u32[]{:S(2)}) collective-permute-start(bf16[192,768]{1,0:T(8,128)(2,1)S(1)} %add_convert_fusion.14), channel_id=1, source_target_pairs={{0,24},{1,25},{2,26},{3,27},{4,28},{5,29},{6,30},{7,31},{8,0},{9,1... | collective-permute-start | bytes 884744 | tf_op jit(solution)/shard_map/ppermute | solution.py:183
  723.6 20.7 %collective-permute-start.38 = (bf16[96,1536]{1,0:T(8,128)(2,1)S(1)}, bf16[96,1536]{1,0:T(8,128)(2,1)S(1)}, u32[]{:S(2)}, u32[]{:S(2)}) collective-permute-start(bf16[96,1536]{1,0:T(8,128)(2,1)S(1)} %add_convert_fusion.15), channel_id=1, source_target_pairs={{0,24},{1,25},{2,26},{3,27},{4,28},{5,29},{6,30},{7,31},{8,0},{9,1... | collective-permute-start | bytes 884744 | tf_op jit(solution)/shard_map/ppermute | solution.py:183
  725.4 14.7 %collective-permute-start.61 = (bf16[48,4096]{1,0:T(8,128)(2,1)S(1)}, bf16[48,4096]{1,0:T(8,128)(2,1)S(1)}, u32[]{:S(2)}, u32[]{:S(2)}) collective-permute-start(bf16[48,4096]{1,0:T(8,128)(2,1)S(1)} %fusion.32), channel_id=1, source_target_pairs={{0,2},{1,3},{2,0},{3,1},{4,6},{5,7},{6,4},{7,5},{8,10},{9,11},{10,... | collective-permute-start | bytes 1179656 | tf_op jit(solution)/shard_map/ppermute | solution.py:183
  744.4 12.0 %collective-permute-start.47 = (f32[24,128]{1,0:T(8,128)S(1)}, f32[24,128]{1,0:T(8,128)S(1)}, u32[]{:S(2)}, u32[]{:S(2)}) collective-permute-start(f32[24,128]{1,0:T(8,128)S(1)} %add.2654), channel_id=1, source_target_pairs={{0,4},{1,5},{2,6},{3,7},{4,0},{5,1},{6,2},{7,3},{8,12},{9,13},{10,... | collective-permute-start | bytes 36872 | tf_op jit(solution)/shard_map/ppermute | solution.py:183
  746.1 21.8 %collective-permute-start.46 = (bf16[128,1536]{1,0:T(8,128)(2,1)S(1)}, bf16[128,1536]{1,0:T(8,128)(2,1)S(1)}, u32[]{:S(2)}, u32[]{:S(2)}) collective-permute-start(bf16[128,1536]{1,0:T(8,128)(2,1)S(1)} %add_convert_fusion.8), channel_id=1, source_target_pairs={{0,24},{1,25},{2,26},{3,27},{4,28},{5,29},{6,30},{7,31},{8,0},{9,1... | collective-permute-start | bytes 1179656 | tf_op jit(solution)/shard_map/ppermute | solution.py:183
  747.6 20.3 %collective-permute-start.44 = (bf16[192,768]{1,0:T(8,128)(2,1)S(1)}, bf16[192,768]{1,0:T(8,128)(2,1)S(1)}, u32[]{:S(2)}, u32[]{:S(2)}) collective-permute-start(bf16[192,768]{1,0:T(8,128)(2,1)S(1)} %add_convert_fusion.12), channel_id=1, source_target_pairs={{0,24},{1,25},{2,26},{3,27},{4,28},{5,29},{6,30},{7,31},{8,0},{9,1... | collective-permute-start | bytes 884744 | tf_op jit(solution)/shard_map/ppermute | solution.py:183
  748.8 19.1 %collective-permute-start.43 = (bf16[96,1536]{1,0:T(8,128)(2,1)S(1)}, bf16[96,1536]{1,0:T(8,128)(2,1)S(1)}, u32[]{:S(2)}, u32[]{:S(2)}) collective-permute-start(bf16[96,1536]{1,0:T(8,128)(2,1)S(1)} %add_convert_fusion.13), channel_id=1, source_target_pairs={{0,24},{1,25},{2,26},{3,27},{4,28},{5,29},{6,30},{7,31},{8,0},{9,1... | collective-permute-start | bytes 884744 | tf_op jit(solution)/shard_map/ppermute | solution.py:183
  749.8 18.1 %collective-permute-start.45 = (bf16[48,1536]{1,0:T(8,128)(2,1)S(1)}, bf16[48,1536]{1,0:T(8,128)(2,1)S(1)}, u32[]{:S(2)}, u32[]{:S(2)}) collective-permute-start(bf16[48,1536]{1,0:T(8,128)(2,1)S(1)} %fusion.59), channel_id=1, source_target_pairs={{0,24},{1,25},{2,26},{3,27},{4,28},{5,29},{6,30},{7,31},{8,0},{9,1... | collective-permute-start | bytes 442376 | tf_op jit(solution)/shard_map/ppermute | solution.py:183
  768.0 9.4 %collective-permute-start.51 = (f32[24,128]{1,0:T(8,128)S(1)}, f32[24,128]{1,0:T(8,128)S(1)}, u32[]{:S(2)}, u32[]{:S(2)}) collective-permute-start(f32[24,128]{1,0:T(8,128)S(1)} %add.2668), channel_id=1, source_target_pairs={{0,16},{1,17},{2,18},{3,19},{4,20},{5,21},{6,22},{7,23},{8,24},{9,... | collective-permute-start | bytes 36872 | tf_op jit(solution)/shard_map/ppermute | solution.py:183
  768.3 9.1 %collective-permute-start.50 = (bf16[48,1536]{1,0:T(8,128)(2,1)S(1)}, bf16[48,1536]{1,0:T(8,128)(2,1)S(1)}, u32[]{:S(2)}, u32[]{:S(2)}) collective-permute-start(bf16[48,1536]{1,0:T(8,128)(2,1)S(1)} %fusion.58), channel_id=1, source_target_pairs={{0,24},{1,25},{2,26},{3,27},{4,28},{5,29},{6,30},{7,31},{8,0},{9,1... | collective-permute-start | bytes 442376 | tf_op jit(solution)/shard_map/ppermute | solution.py:183
  774.2 9.9 %collective-permute-start.48 = (bf16[96,1536]{1,0:T(8,128)(2,1)S(1)}, bf16[96,1536]{1,0:T(8,128)(2,1)S(1)}, u32[]{:S(2)}, u32[]{:S(2)}) collective-permute-start(bf16[96,1536]{1,0:T(8,128)(2,1)S(1)} %add_convert_fusion.11), channel_id=1, source_target_pairs={{0,24},{1,25},{2,26},{3,27},{4,28},{5,29},{6,30},{7,31},{8,0},{9,1... | collective-permute-start | bytes 884744 | tf_op jit(solution)/shard_map/ppermute | solution.py:183
  777.3 17.1 %collective-permute-start.62 = (bf16[128,1536]{1,0:T(8,128)(2,1)S(1)}, bf16[128,1536]{1,0:T(8,128)(2,1)S(1)}, u32[]{:S(2)}, u32[]{:S(2)}) collective-permute-start(bf16[128,1536]{1,0:T(8,128)(2,1)S(1)} %add_convert_fusion.7), channel_id=1, source_target_pairs={{0,24},{1,25},{2,26},{3,27},{4,28},{5,29},{6,30},{7,31},{8,0},{9,1... | collective-permute-start | bytes 1179656 | tf_op jit(solution)/shard_map/ppermute | solution.py:183
  784.1 53.4 %collective-permute-start.52 = (f32[24,128]{1,0:T(8,128)S(1)}, f32[24,128]{1,0:T(8,128)S(1)}, u32[]{:S(2)}, u32[]{:S(2)}) collective-permute-start(f32[24,128]{1,0:T(8,128)S(1)} %add.2679), channel_id=1, source_target_pairs={{0,8},{1,9},{2,10},{3,11},{4,12},{5,13},{6,14},{7,15},{8,16},{9,17... | collective-permute-start | bytes 36872 | tf_op jit(solution)/shard_map/ppermute | solution.py:183
  785.1 17.1 %collective-permute-start.55 = (bf16[48,1536]{1,0:T(8,128)(2,1)}, bf16[48,1536]{1,0:T(8,128)(2,1)}, u32[]{:S(2)}, u32[]{:S(2)}) collective-permute-start(bf16[48,1536]{1,0:T(8,128)(2,1)} %fusion.56), channel_id=1, source_target_pairs={{0,24},{1,25},{2,26},{3,27},{4,28},{5,29},{6,30},{7,31},{8,0},{9,1... | collective-permute-start | bytes 442376 | tf_op jit(solution)/shard_map/ppermute | solution.py:183
  790.3 15.2 %collective-permute-start.54 = (bf16[96,768]{1,0:T(8,128)(2,1)}, bf16[96,768]{1,0:T(8,128)(2,1)}, u32[]{:S(2)}, u32[]{:S(2)}) collective-permute-start(bf16[96,768]{1,0:T(8,128)(2,1)} %add_convert_fusion.17), channel_id=1, source_target_pairs={{0,2},{1,3},{2,0},{3,1},{4,6},{5,7},{6,4},{7,5},{8,10},{9,11},{10,... | collective-permute-start | bytes 442376 | tf_op jit(solution)/shard_map/ppermute | solution.py:183
  793.3 13.6 %collective-permute-start.53 = (bf16[48,1536]{1,0:T(8,128)(2,1)}, bf16[48,1536]{1,0:T(8,128)(2,1)}, u32[]{:S(2)}, u32[]{:S(2)}) collective-permute-start(bf16[48,1536]{1,0:T(8,128)(2,1)} %add_convert_fusion.19), channel_id=1, source_target_pairs={{0,4},{1,5},{2,6},{3,7},{4,0},{5,1},{6,2},{7,3},{8,12},{9,13},{10,... | collective-permute-start | bytes 442376 | tf_op jit(solution)/shard_map/ppermute | solution.py:183
  800.2 36.5 %collective-permute-start.63 = (bf16[196608]{0:T(1024)(128)(2,1)}, bf16[196608]{0:T(1024)(128)(2,1)}, u32[]{:S(2)}, u32[]{:S(2)}) collective-permute-start(bf16[196608]{0:T(1024)(128)(2,1)} %get-tuple-element.332), channel_id=1, source_target_pairs={{2,0},{5,1},{8,2},{11,3},{14,4},{17,5},{20,6},{23,7},{26,8},{29,9}... | collective-permute-start | bytes 1179656 | tf_op jit(solution)/shard_map/ppermute | solution.py:140
  813.3 26.7 %collective-permute-start.58 = (bf16[73728]{0:T(1024)(128)(2,1)S(1)}, bf16[73728]{0:T(1024)(128)(2,1)S(1)}, u32[]{:S(2)}, u32[]{:S(2)}) collective-permute-start(bf16[73728]{0:T(1024)(128)(2,1)S(1)} %get-tuple-element.339), channel_id=1, source_target_pairs={{0,0},{3,1},{6,2},{9,3},{12,4},{15,5},{18,6},{21,7},{24,8},{27,9},... | collective-permute-start | bytes 442376 | tf_op jit(solution)/shard_map/ppermute | solution.py:140
  815.2 40.0 %collective-permute-start.65 = (bf16[196608]{0:T(1024)(128)(2,1)}, bf16[196608]{0:T(1024)(128)(2,1)S(1)}, u32[]{:S(2)}, u32[]{:S(2)}) collective-permute-start(bf16[196608]{0:T(1024)(128)(2,1)} %get-tuple-element.331), channel_id=1, source_target_pairs={{0,0},{3,1},{6,2},{9,3},{12,4},{15,5},{18,6},{21,7},{24,8},{27,9},... | collective-permute-start | bytes 1179656 | tf_op jit(solution)/shard_map/ppermute | solution.py:140
  817.2 38.2 %collective-permute-start.66 = (bf16[196608]{0:T(1024)(128)(2,1)}, bf16[196608]{0:T(1024)(128)(2,1)S(1)}, u32[]{:S(2)}, u32[]{:S(2)}) collective-permute-start(bf16[196608]{0:T(1024)(128)(2,1)} %get-tuple-element.330), channel_id=1, source_target_pairs={{1,0},{4,1},{7,2},{10,3},{13,4},{16,5},{19,6},{22,7},{25,8},{28,9}... | collective-permute-start | bytes 1179656 | tf_op jit(solution)/shard_map/ppermute | solution.py:140
  836.7 16.5 %collective-permute-start.59 = (bf16[73728]{0:T(1024)(128)(2,1)}, bf16[73728]{0:T(1024)(128)(2,1)}, u32[]{:S(2)}, u32[]{:S(2)}) collective-permute-start(bf16[73728]{0:T(1024)(128)(2,1)} %get-tuple-element.338), channel_id=1, source_target_pairs={{1,0},{4,1},{7,2},{10,3},{13,4},{16,5},{19,6},{22,7},{25,8},{28,9}... | collective-permute-start | bytes 442376 | tf_op jit(solution)/shard_map/ppermute | solution.py:140
  837.5 17.9 %collective-permute-start.57 = (bf16[1536]{0:T(1024)(128)(2,1)S(1)}, bf16[1536]{0:T(1024)(128)(2,1)S(1)}, u32[]{:S(2)}, u32[]{:S(2)}) collective-permute-start(bf16[1536]{0:T(1024)(128)(2,1)S(1)} %slice.875), channel_id=1, source_target_pairs={{0,1},{1,2},{2,3},{3,4},{4,5},{5,6},{6,7},{7,8},{8,9},{9,10},{10,1... | collective-permute-start | bytes 9224 | tf_op jit(solution)/shard_map/ppermute | solution.py:142
  840.0 15.4 %collective-permute-start.64 = (bf16[1536]{0:T(1024)(128)(2,1)S(1)}, bf16[1536]{0:T(1024)(128)(2,1)S(1)}, u32[]{:S(2)}, u32[]{:S(2)}) collective-permute-start(bf16[1536]{0:T(1024)(128)(2,1)S(1)} %slice.883), channel_id=1, source_target_pairs={{0,1},{1,2},{2,3},{3,4},{4,5},{5,6},{6,7},{7,8},{8,9},{9,10},{10,1... | collective-permute-start | bytes 9224 | tf_op jit(solution)/shard_map/ppermute | solution.py:142
  (76 other events, 1095.4 us)
Sparse Core Ops, SparseCore 0:
  81.6 265.4 all-gather.1

commit v5 on v4

--- a/solution.py
+++ b/solution.py
@@ -1211,7 +1211,8 @@
         make_and_send(last_sums)
         for each in last_sums:
             each.make()
-        taken_after(early_sums + [out_sum], [each.made for each in last_sums])
+        for other_sum in early_sums + [out_sum]:
+            taken_after([other_sum], [each.made for each in last_sums])
         for each in last_sums:
             each.send()
         dquery_late = taken_after(last_sums, dquery_low)

time: 876 us -> 867 us (0.990)
  Pallas kernels: 147 us -> 134 us
    pallas_call x2, Pallas kernels: 75.2 us -> 62 us  [run_kernel(): pl.pallas_call(body, grid_spec=pltpu.PrefetchScalarGridSpec(num_scalar_pr...]
  transfers between devices with their start and end apart: 72 -> 72, of which waited for: 29 -> 29; matrix products, arithmetic and copies ran while one was open for 21% -> 21% of each run, Pallas kernels for 13% -> 11%
where the time goes in v5:
time: 867 us; the launch traced here: 859 us
  waiting for transfers between devices  271 us (31%)
  starting transfers between devices  135 us (16%)
  Pallas kernels  134 us (15%)
  matrix products  101 us (12%)
  blocking collectives  89.8 us (10%)
  other arithmetic  69.6 us (8%)
  local copies, waits for them, and re-layouts  43.4 us (5%)
  between operations  16 us (2%)
    ppermute x52, waiting for transfers between devices, shifted(): return lax.ppermute(value, 'seq', pairs)  181 us
    dot_general x45, matrix products, contract(): lax.dot_general(left, right, (((left_dim,), (right_dim,)), ((), ())), pre...  101 us
    all_to_all x1, blocking collectives, exchange(): return lax.all_to_all(value, 'seq', 0, 0, tiled=True)  89.8 us
    pallas_call x2, Pallas kernels, run_kernel(): pl.pallas_call(body, grid_spec=pltpu.PrefetchScalarGridSpec(num_scalar_pr...  62 us
    ppermute x52, starting transfers between devices, shifted(): return lax.ppermute(value, 'seq', pairs)  55.7 us
    ppermute x5, waiting for transfers between devices, swapped(): return lax.ppermute(value, 'seq', [(i, i ^ bit) for i in range(count)])  44.6 us
    all_to_all x4, waiting for transfers between devices, exchange(): return lax.all_to_all(value, 'seq', 0, 0, tiled=True)  41.6 us
    pallas_call x1, Pallas kernels, feed_forward(): pl.pallas_call(feed_forward_kernel, grid=(FF // FF_TILE,), in_specs=[fixe...  33.7 us
  transfers between devices with their start and end apart: 72, of which 29 were waited for; matrix products, arithmetic and copies ran while one was open for 21% of the time, Pallas kernels for 11%

profile of v5, /device:TPU:7, one launch (start us, length us, event | category | flops | bytes accessed | tf_op | source)
XLA Modules:
  0.0 859.0 jit_solution(15054152782004523492)
XLA Ops:
  14.4 6.3 all-to-all-start
  27.5 2.8 fusion.73
  30.3 18.5 %all-to-all-done = bf16[32,26,128]{2,1,0:T(8,128)(2,1)S(1)} async-done(((bf16[32,26,128]{2,1,0:T(8,128)(2,1)}), bf16[32,26,128]{2,1,0:T(8,128)(2,1)S(1)}, u32[]{:S(2)}, u32[]{:S(2)}) %all-to-all-start) | async-done | bytes 213024 | tf_op jit(solution)/shard_map/all_to_all | solution.py:900
  48.8 9.1 %collective-permute-done.2 = bf16[216,8,128]{2,1,0:T(8,128)(2,1)} collective-permute-done((bf16[216,8,128]{2,1,0:T(8,128)(2,1)S(1)}, bf16[216,8,128]{2,1,0:T(8,128)(2,1)}, u32[]{:S(2)}, u32[]{:S(2)}) %collective-permute-start.2) | collective-permute-done | bytes 442400 | tf_op jit(solution)/shard_map/ppermute | solution.py:183
  68.4 11.9 %collective-permute-done.5 = bf16[432,8,128]{2,1,0:T(8,128)(2,1)} collective-permute-done((bf16[432,8,128]{2,1,0:T(8,128)(2,1)S(1)}, bf16[432,8,128]{2,1,0:T(8,128)(2,1)}, u32[]{:S(2)}, u32[]{:S(2)}) %collective-permute-start.5) | collective-permute-done | bytes 884768 | tf_op jit(solution)/shard_map/ppermute | solution.py:183
  91.3 18.8 %convert_reduce_fusion = s32[4096]{0:T(1024)S(1)} fusion(s32[8192]{0:T(1024)S(1)} %bitcast.263, s32[4096]{0:T(1024)S(1)} %bitcast.270), kind=kLoop, calls=%fused_computation | loop fusion | flops 100659200 | bytes 65536 | tf_op jit(solution)/shard_map/reduce_sum | solution.py:922
  110.0 23.5 %collective-permute-done.8.refs_5_ = bf16[864,8,128]{2,1,0:T(8,128)(2,1)} collective-permute-done((bf16[864,8,128]{2,1,0:T(8,128)(2,1)}, bf16[864,8,128]{2,1,0:T(8,128)(2,1)}, u32[]{:S(2)}, u32[]{:S(2)}) %collective-permute-start.8) | collective-permute-done | bytes 1769504 | tf_op jit(solution)/shard_map/ppermute | solution.py:183
  135.9 3.7 collective-permute-start.10
  143.3 5.1 collective-permute-done.11.refs_6_
  150.9 13.6 %place_blocks.1 = bf16[6912,8,128]{2,1,0:T(8,128)(2,1)} custom-call(s32[64]{0:T(128)S(1)} %pad_add_fusion.table_ref, bf16[864,8,128]{2,1,0:T(8,128)(2,1)S(1)} %constant_dynamic-update-slice_fusion.refs_0_, bf16[864,8,128]{2,1,0:T(8,128)(2,1)} %collective-permute-done.7.refs_1_, bf16[864,8,128]{2,1,0:T(8,128)(2,1)} %collective-permute-done.9.refs_2_, ...), custom_call_target="tpu_custom_call" | custom-call | bytes 28311552 | tf_op jit(solution)/shard_map/place_blocks/pallas_call | solution.py:226
  164.5 5.8 project.1
  170.3 89.8 %all_to_all.25.query_ref = bf16[32,192,128]{2,1,0:T(8,128)(2,1)S(1)} all-to-all(bf16[32,192,128]{2,1,0:T(8,128)(2,1)S(1)} %project.1), channel_id=1, replica_groups=mesh['seq'=32] {'seq'}, dimensions={0} | all-to-all | bytes 3145728 | tf_op jit(solution)/shard_map/all_to_all | solution.py:900
  262.5 33.5 %collective-permute-done.14.refs_2_ = bf16[32,96,128]{2,1,0:T(8,128)(2,1)S(1)} collective-permute-done((bf16[32,96,128]{2,1,0:T(8,128)(2,1)S(1)}, bf16[32,96,128]{2,1,0:T(8,128)(2,1)S(1)}, u32[]{:S(2)}, u32[]{:S(2)}) %collective-permute-start.14) | collective-permute-done | bytes 786464 | tf_op jit(solution)/shard_map/ppermute | solution.py:903
  300.8 25.2 %attention_forward.1 = (f32[8,96,512]{2,1,0:T(8,128)}, bf16[32,96,128]{2,1,0:T(8,128)(2,1)}, f32[8,1,512]{2,1,0:T(1,128)S(1)}, bf16[8192,96]{1,0:T(8,128)(2,1)}, bf16[8,96,1024]{2,1,0:T(8,128)(2,1)}) custom-call(s32[8]{0:T(128)S(1)} %and_select_fusion.1.low_ref, s32[8]{0:T(128)S(1)} %and_select_fusion.high_ref, s32[1]{0:T(128)} %bitcast.32.half_ref, ...), custom_call_target="tpu_custom_call" | custom-call | flops 20000000000 | bytes 16777216 | tf_op jit(solution)/shard_map/attention_forward/pallas_call | solution.py:772
  326.0 13.9 %all-to-all-start.2 = ((bf16[32,96,128]{2,1,0:T(8,128)(2,1)}), bf16[32,96,128]{2,1,0:T(8,128)(2,1)S(1)}, u32[]{:S(2)}, u32[]{:S(2)}) async-start(bf16[32,96,128]{2,1,0:T(8,128)(2,1)} %get-tuple-element.159), calls=%async_computation.2 | async-start | bytes 1572864 | tf_op jit(solution)/shard_map/all_to_all | solution.py:900
  340.6 3.8 multiply_sine_fusion
  346.9 3.9 copy.106
  350.8 9.2 %all-to-all-done.2.mixed_piece_ref = bf16[32,96,128]{2,1,0:T(8,128)(2,1)S(1)} async-done(((bf16[32,96,128]{2,1,0:T(8,128)(2,1)}), bf16[32,96,128]{2,1,0:T(8,128)(2,1)S(1)}, u32[]{:S(2)}, u32[]{:S(2)}) %all-to-all-start.2) | async-done | bytes 786464 | tf_op jit(solution)/shard_map/all_to_all | solution.py:900
  360.0 33.7 %feed_forward.1 = (bf16[256,1536]{1,0:T(8,128)(2,1)}, f32[256,1536]{1,0:T(8,128)}, bf16[256,1536]{1,0:T(8,128)(2,1)S(1)}, bf16[32,96,128]{2,1,0:T(8,128)(2,1)}, ...) custom-call(bf16[256,1536]{1,0:T(8,128)(2,1)S(1)} %copy-done.2, ...), custom_call_target="tpu_custom_call" | custom-call | flops 19327352832 | bytes 37748736 | tf_op jit(solution)/shard_map/feed_forward/pallas_call | solution.py:516
  395.5 2.7 reorder_blocks.7
  398.2 6.2 convolution_convert_fusion.1
  408.3 6.1 convolution_convert_fusion.2
  414.4 5.1 all-to-all-start.3
  419.5 3.8 reorder_blocks.8
  423.3 5.8 convolution_convert_fusion
  429.4 4.9 add_convert_fusion.1
  434.4 4.7 add_convert_fusion.2
  440.9 36.8 %attention_backward.1 = (bf16[32,96,128]{2,1,0:T(8,128)(2,1)S(1)}, f32[2,1,32,96,128]{4,3,2,1,0:T(8,128)}, bf16[2,1,32,96,128]{4,3,2,1,0:T(8,128)(2,1)}) custom-call(s32[8]{0:T(128)S(1)} %and_select_fusion.1.low_ref, s32[8]{0:T(128)S(1)} %and_select_fusion.high_ref, bf16[32,192,128]{2,1,0:T(8,128)(2,1)} %copy-done.20, bf16[32,96,128]{2,1,0:T(8,128)(2,1)} %copy-done.40, ...), custom_call_target="tpu_custom_call" | custom-call | flops 49999998976 | bytes 16777216 | tf_op jit(solution)/shard_map/attention_backward/pallas_call | solution.py:772
  478.3 3.4 collective-permute-done.18
  481.7 2.8 convert_add_fusion
  484.5 23.6 %collective-permute-done.19 = bf16[384,4096]{1,0:T(8,128)(2,1)} collective-permute-done((bf16[384,4096]{1,0:T(8,128)(2,1)}, bf16[384,4096]{1,0:T(8,128)(2,1)}, u32[]{:S(2)}, u32[]{:S(2)}) %collective-permute-start.19) | collective-permute-done | bytes 3145760 | tf_op jit(solution)/shard_map/ppermute | solution.py:183
  509.5 4.9 add_convert_fusion
  514.4 3.1 fusion.14
  517.4 2.9 fusion.13
  520.4 5.9 collective-permute-done.21
  530.8 7.6 all-to-all-start.4
  543.1 4.5 reorder_blocks.10
  547.6 3.0 copy.113
  550.6 3.1 collective-permute-start.24
  562.9 19.8 %collective-permute-done.24 = bf16[96,4096]{1,0:T(8,128)(2,1)S(1)} collective-permute-done((bf16[96,4096]{1,0:T(8,128)(2,1)}, bf16[96,4096]{1,0:T(8,128)(2,1)S(1)}, u32[]{:S(2)}, u32[]{:S(2)}) %collective-permute-start.24) | collective-permute-done | bytes 786464 | tf_op jit(solution)/shard_map/ppermute | solution.py:183
  582.7 3.6 fusion.16
  586.2 13.3 %collective-permute-done.23 = bf16[96,4096]{1,0:T(8,128)(2,1)S(1)} collective-permute-done((bf16[96,4096]{1,0:T(8,128)(2,1)}, bf16[96,4096]{1,0:T(8,128)(2,1)S(1)}, u32[]{:S(2)}, u32[]{:S(2)}) %collective-permute-start.23) | collective-permute-done | bytes 786464 | tf_op jit(solution)/shard_map/ppermute | solution.py:183
  599.5 3.0 fusion.15
  602.5 13.8 %all-to-all-done.4 = bf16[32,192,128]{2,1,0:T(8,128)(2,1)} async-done(((bf16[32,192,128]{2,1,0:T(8,128)(2,1)}), bf16[32,192,128]{2,1,0:T(8,128)(2,1)}, u32[]{:S(2)}, u32[]{:S(2)}) %all-to-all-start.4) | async-done | bytes 1572896 | tf_op jit(solution)/shard_map/all_to_all | solution.py:900
  620.1 3.1 convolution_convert_fusion.4
  626.5 4.3 collective-permute-start.34
  634.9 3.7 fusion.46
  643.5 4.2 fusion.35
  650.8 13.5 %collective-permute-done.32 = bf16[96,4096]{1,0:T(8,128)(2,1)S(1)} collective-permute-done((bf16[96,4096]{1,0:T(8,128)(2,1)S(1)}, bf16[96,4096]{1,0:T(8,128)(2,1)S(1)}, u32[]{:S(2)}, u32[]{:S(2)}) %collective-permute-start.32) | collective-permute-done | bytes 786464 | tf_op jit(solution)/shard_map/ppermute | solution.py:183
  664.3 4.0 collective-permute-start.35
  672.9 4.2 fusion.65
  680.8 3.2 collective-permute-done.35
  684.0 16.9 %collective-permute-done.33 = bf16[96,4096]{1,0:T(8,128)(2,1)S(1)} collective-permute-done((bf16[96,4096]{1,0:T(8,128)(2,1)S(1)}, bf16[96,4096]{1,0:T(8,128)(2,1)S(1)}, u32[]{:S(2)}, u32[]{:S(2)}) %collective-permute-start.33) | collective-permute-done | bytes 786464 | tf_op jit(solution)/shard_map/ppermute | solution.py:183
  717.0 11.1 %collective-permute-done.61 = bf16[48,4096]{1,0:T(8,128)(2,1)S(1)} collective-permute-done((bf16[48,4096]{1,0:T(8,128)(2,1)S(1)}, bf16[48,4096]{1,0:T(8,128)(2,1)S(1)}, u32[]{:S(2)}, u32[]{:S(2)}) %collective-permute-start.61) | collective-permute-done | bytes 393248 | tf_op jit(solution)/shard_map/ppermute | solution.py:183
  744.4 11.5 %collective-permute-done.45 = bf16[48,1536]{1,0:T(8,128)(2,1)S(1)} collective-permute-done((bf16[48,1536]{1,0:T(8,128)(2,1)S(1)}, bf16[48,1536]{1,0:T(8,128)(2,1)S(1)}, u32[]{:S(2)}, u32[]{:S(2)}) %collective-permute-start.45) | collective-permute-done | bytes 147488 | tf_op jit(solution)/shard_map/ppermute | solution.py:183
  765.7 6.2 collective-permute-done.48
  772.9 3.2 collective-permute-start.55
  797.3 4.2 collective-permute-start.56
  806.0 16.7 %collective-permute-start.66 = (bf16[196608]{0:T(1024)(128)(2,1)}, bf16[196608]{0:T(1024)(128)(2,1)S(1)}, u32[]{:S(2)}, u32[]{:S(2)}) collective-permute-start(bf16[196608]{0:T(1024)(128)(2,1)} %get-tuple-element.330), channel_id=1, source_target_pairs={{1,0},{4,1},{7,2},{10,3},{13,4},{16,5},{19,6},{22,7},{25,8},{28,9}... | collective-permute-start | bytes 1179656 | tf_op jit(solution)/shard_map/ppermute | solution.py:140
  823.5 6.5 collective-permute-start.57
  832.0 3.0 fusion.66
  834.9 3.2 copy.114
  838.2 3.4 collective-permute-done.59
  843.8 5.4 multiply_subtract_fusion
  (416 shorter events, 184.7 us)
Async XLA Ops:
  9.1 18.4 %collective-permute-start.6 = (bf16[1536]{0:T(1024)(128)(2,1)S(1)}, bf16[1536]{0:T(1024)(128)(2,1)S(1)}, u32[]{:S(2)}, u32[]{:S(2)}) collective-permute-start(bf16[1536]{0:T(1024)(128)(2,1)S(1)} %slice.819), channel_id=1, source_target_pairs={{1,0},{2,1},{3,2},{4,3},{5,4},{6,5},{7,6},{8,7},{9,8},{10,9},{11,1... | collective-permute-start | bytes 9224 | tf_op jit(solution)/shard_map/ppermute | solution.py:86
  11.7 9.1 %collective-permute-start = (bf16[1536]{0:T(1024)(128)(2,1)S(1)}, bf16[1536]{0:T(1024)(128)(2,1)S(1)}, u32[]{:S(2)}, u32[]{:S(2)}) collective-permute-start(bf16[1536]{0:T(1024)(128)(2,1)S(1)} %slice.815), channel_id=1, source_target_pairs={{1,0},{2,1},{3,2},{4,3},{5,4},{6,5},{7,6},{8,7},{9,8},{10,9},{11,1... | collective-permute-start | bytes 9224 | tf_op jit(solution)/shard_map/ppermute | solution.py:86
  14.4 34.4 %all-to-all-start = ((bf16[32,26,128]{2,1,0:T(8,128)(2,1)}), bf16[32,26,128]{2,1,0:T(8,128)(2,1)S(1)}, u32[]{:S(2)}, u32[]{:S(2)}) async-start(bf16[32,26,128]{2,1,0:T(8,128)(2,1)} %broadcast_in_dim.9), calls=%async_computation | async-start | bytes 524288 | tf_op jit(solution)/shard_map/all_to_all | solution.py:900
  20.8 339.2 %all-gather.2.cloned.1.call-start = ((), (), s32[]{:S(2)}) async-start(), calls=%async_computation.5 | async-start | bytes 38928384 | tf_op jit(solution)/shard_map/all_gather | solution.py:959
  22.8 26.0 %collective-permute-start.1 = (bf16[216,8,128]{2,1,0:T(8,128)(2,1)S(1)}, bf16[216,8,128]{2,1,0:T(8,128)(2,1)S(1)}, u32[]{:S(2)}, u32[]{:S(2)}) collective-permute-start(bf16[216,8,128]{2,1,0:T(8,128)(2,1)S(1)} %pad_maximum_fusion.5), channel_id=1, source_target_pairs={{0,8},{1,9},{2,10},{3,11},{4,12},{5,13},{6,14},{7,15},{8,16},{9,17... | collective-permute-start | bytes 1327112 | tf_op jit(solution)/shard_map/ppermute | solution.py:183
  24.0 33.9 %collective-permute-start.2 = (bf16[216,8,128]{2,1,0:T(8,128)(2,1)S(1)}, bf16[216,8,128]{2,1,0:T(8,128)(2,1)}, u32[]{:S(2)}, u32[]{:S(2)}) collective-permute-start(bf16[216,8,128]{2,1,0:T(8,128)(2,1)S(1)} %pad_maximum_fusion.5), channel_id=1, source_target_pairs={{0,16},{1,17},{2,18},{3,19},{4,20},{5,21},{6,22},{7,23},{8,24},{9,... | collective-permute-start | bytes 1327112 | tf_op jit(solution)/shard_map/ppermute | solution.py:183
  26.2 31.7 %collective-permute-start.3 = (bf16[216,8,128]{2,1,0:T(8,128)(2,1)S(1)}, bf16[216,8,128]{2,1,0:T(8,128)(2,1)}, u32[]{:S(2)}, u32[]{:S(2)}) collective-permute-start(bf16[216,8,128]{2,1,0:T(8,128)(2,1)S(1)} %pad_maximum_fusion.5), channel_id=1, source_target_pairs={{0,24},{1,25},{2,26},{3,27},{4,28},{5,29},{6,30},{7,31},{8,0},{9,1... | collective-permute-start | bytes 1327112 | tf_op jit(solution)/shard_map/ppermute | solution.py:183
  60.3 20.0 %collective-permute-start.5 = (bf16[432,8,128]{2,1,0:T(8,128)(2,1)S(1)}, bf16[432,8,128]{2,1,0:T(8,128)(2,1)}, u32[]{:S(2)}, u32[]{:S(2)}) collective-permute-start(bf16[432,8,128]{2,1,0:T(8,128)(2,1)S(1)} %pad_maximum_fusion.3), channel_id=1, source_target_pairs={{0,2},{1,3},{2,0},{3,1},{4,6},{5,7},{6,4},{7,5},{8,10},{9,11},{10,... | collective-permute-start | bytes 2654216 | tf_op jit(solution)/shard_map/ppermute | solution.py:183
  61.6 19.8 %collective-permute-start.4 = (bf16[432,8,128]{2,1,0:T(8,128)(2,1)}, bf16[432,8,128]{2,1,0:T(8,128)(2,1)}, u32[]{:S(2)}, u32[]{:S(2)}) collective-permute-start(bf16[432,8,128]{2,1,0:T(8,128)(2,1)} %pad_maximum_fusion.2), channel_id=1, source_target_pairs={{0,4},{1,5},{2,6},{3,7},{4,0},{5,1},{6,2},{7,3},{8,12},{9,13},{10,... | collective-permute-start | bytes 2654216 | tf_op jit(solution)/shard_map/ppermute | solution.py:183
  87.2 46.3 %collective-permute-start.8 = (bf16[864,8,128]{2,1,0:T(8,128)(2,1)}, bf16[864,8,128]{2,1,0:T(8,128)(2,1)}, u32[]{:S(2)}, u32[]{:S(2)}) collective-permute-start(bf16[864,8,128]{2,1,0:T(8,128)(2,1)} %constant_dynamic-update-slice_fusion.2.refs_4_), channel_id=1, source_target_pairs={{0,4},{1,5},{2,6},{3,7},{4,0},{5,1},{6,2},{7,3},{8,12},{9,13},{10,... | collective-permute-start | bytes 5308424 | tf_op jit(solution)/shard_map/ppermute | solution.py:183
  90.0 45.9 %collective-permute-start.7 = (bf16[864,8,128]{2,1,0:T(8,128)(2,1)S(1)}, bf16[864,8,128]{2,1,0:T(8,128)(2,1)}, u32[]{:S(2)}, u32[]{:S(2)}) collective-permute-start(bf16[864,8,128]{2,1,0:T(8,128)(2,1)S(1)} %constant_dynamic-update-slice_fusion.refs_0_), channel_id=1, source_target_pairs={{0,2},{1,3},{2,0},{3,1},{4,6},{5,7},{6,4},{7,5},{8,10},{9,11},{10,... | collective-permute-start | bytes 5308424 | tf_op jit(solution)/shard_map/ppermute | solution.py:183
  139.6 8.7 %collective-permute-start.11 = (bf16[864,8,128]{2,1,0:T(8,128)(2,1)}, bf16[864,8,128]{2,1,0:T(8,128)(2,1)}, u32[]{:S(2)}, u32[]{:S(2)}) collective-permute-start(bf16[864,8,128]{2,1,0:T(8,128)(2,1)} %constant_dynamic-update-slice_fusion.2.refs_4_), channel_id=1, source_target_pairs={{0,1},{1,0},{2,3},{3,2},{4,5},{5,4},{6,7},{7,6},{8,9},{9,8},{10,11... | collective-permute-start | bytes 5308424 | tf_op jit(solution)/shard_map/ppermute | solution.py:183
  139.6 11.2 %collective-permute-start.12 = (bf16[864,8,128]{2,1,0:T(8,128)(2,1)}, bf16[864,8,128]{2,1,0:T(8,128)(2,1)}, u32[]{:S(2)}, u32[]{:S(2)}) collective-permute-start(bf16[864,8,128]{2,1,0:T(8,128)(2,1)} %collective-permute-done.8.refs_5_), channel_id=1, source_target_pairs={{0,1},{1,0},{2,3},{3,2},{4,5},{5,4},{6,7},{7,6},{8,9},{9,8},{10,11... | collective-permute-start | bytes 5308424 | tf_op jit(solution)/shard_map/ppermute | solution.py:183
  140.1 10.7 %collective-permute-start.9 = (bf16[864,8,128]{2,1,0:T(8,128)(2,1)S(1)}, bf16[864,8,128]{2,1,0:T(8,128)(2,1)}, u32[]{:S(2)}, u32[]{:S(2)}) collective-permute-start(bf16[864,8,128]{2,1,0:T(8,128)(2,1)S(1)} %constant_dynamic-update-slice_fusion.refs_0_), channel_id=1, source_target_pairs={{0,1},{1,0},{2,3},{3,2},{4,5},{5,4},{6,7},{7,6},{8,9},{9,8},{10,11... | collective-permute-start | bytes 5308424 | tf_op jit(solution)/shard_map/ppermute | solution.py:183
  260.2 35.8 %collective-permute-start.14 = (bf16[32,96,128]{2,1,0:T(8,128)(2,1)S(1)}, bf16[32,96,128]{2,1,0:T(8,128)(2,1)S(1)}, u32[]{:S(2)}, u32[]{:S(2)}) collective-permute-start(bf16[32,96,128]{2,1,0:T(8,128)(2,1)S(1)} %slice.825.refs_0_), channel_id=1, source_target_pairs={{0,2},{1,3},{2,0},{3,1},{4,6},{5,7},{6,4},{7,5},{8,10},{9,11},{10,... | collective-permute-start | bytes 2359304 | tf_op jit(solution)/shard_map/ppermute | solution.py:903
  261.6 37.2 %collective-permute-start.13 = (bf16[32,96,128]{2,1,0:T(8,128)(2,1)S(1)}, bf16[32,96,128]{2,1,0:T(8,128)(2,1)S(1)}, u32[]{:S(2)}, u32[]{:S(2)}) collective-permute-start(bf16[32,96,128]{2,1,0:T(8,128)(2,1)S(1)} %slice.825.refs_0_), channel_id=1, source_target_pairs={{0,1},{1,0},{2,3},{3,2},{4,5},{5,4},{6,7},{7,6},{8,9},{9,8},{10,11... | collective-permute-start | bytes 2359304 | tf_op jit(solution)/shard_map/ppermute | solution.py:903
  326.0 34.0 %all-to-all-start.2 = ((bf16[32,96,128]{2,1,0:T(8,128)(2,1)}), bf16[32,96,128]{2,1,0:T(8,128)(2,1)S(1)}, u32[]{:S(2)}, u32[]{:S(2)}) async-start(bf16[32,96,128]{2,1,0:T(8,128)(2,1)} %get-tuple-element.159), calls=%async_computation.2 | async-start | bytes 1572864 | tf_op jit(solution)/shard_map/all_to_all | solution.py:900
  404.4 25.0 %collective-permute-start.17 = (bf16[768,4096]{1,0:T(8,128)(2,1)}, bf16[768,4096]{1,0:T(8,128)(2,1)}, u32[]{:S(2)}, u32[]{:S(2)}) collective-permute-start(bf16[768,4096]{1,0:T(8,128)(2,1)} %convolution_convert_fusion.1), channel_id=1, source_target_pairs={{0,1},{1,0},{2,3},{3,2},{4,5},{5,4},{6,7},{7,6},{8,9},{9,8},{10,11... | collective-permute-start | bytes 18874376 | tf_op jit(solution)/shard_map/ppermute | solution.py:183
  414.4 19.9 %collective-permute-start.16 = (bf16[768,4096]{1,0:T(8,128)(2,1)}, bf16[768,4096]{1,0:T(8,128)(2,1)}, u32[]{:S(2)}, u32[]{:S(2)}) collective-permute-start(bf16[768,4096]{1,0:T(8,128)(2,1)} %convolution_convert_fusion.2), channel_id=1, source_target_pairs={{0,1},{1,0},{2,3},{3,2},{4,5},{5,4},{6,7},{7,6},{8,9},{9,8},{10,11... | collective-permute-start | bytes 18874376 | tf_op jit(solution)/shard_map/ppermute | solution.py:183
  414.4 24.7 %all-to-all-start.3 = ((bf16[32,96,128]{2,1,0:T(8,128)(2,1)}), bf16[32,96,128]{2,1,0:T(8,128)(2,1)S(1)}, u32[]{:S(2)}, u32[]{:S(2)}) async-start(bf16[32,96,128]{2,1,0:T(8,128)(2,1)} %get-tuple-element.169), calls=%async_computation.3 | async-start | bytes 1572864 | tf_op jit(solution)/shard_map/all_to_all | solution.py:900
  429.0 80.4 %collective-permute-start.22 = (bf16[2048,1536]{1,0:T(8,128)(2,1)}, bf16[2048,1536]{1,0:T(8,128)(2,1)}, u32[]{:S(2)}, u32[]{:S(2)}) collective-permute-start(bf16[2048,1536]{1,0:T(8,128)(2,1)} %convolution_convert_fusion), channel_id=1, source_target_pairs={{0,1},{1,0},{2,3},{3,2},{4,5},{5,4},{6,7},{7,6},{8,9},{9,8},{10,11... | collective-permute-start | bytes 18874376 | tf_op jit(solution)/shard_map/ppermute | solution.py:183
  439.1 68.9 %collective-permute-start.19 = (bf16[384,4096]{1,0:T(8,128)(2,1)}, bf16[384,4096]{1,0:T(8,128)(2,1)}, u32[]{:S(2)}, u32[]{:S(2)}) collective-permute-start(bf16[384,4096]{1,0:T(8,128)(2,1)} %add_convert_fusion.2), channel_id=1, source_target_pairs={{0,2},{1,3},{2,0},{3,1},{4,6},{5,7},{6,4},{7,5},{8,10},{9,11},{10,... | collective-permute-start | bytes 9437192 | tf_op jit(solution)/shard_map/ppermute | solution.py:183
  440.0 68.9 %collective-permute-start.20 = (bf16[384,4096]{1,0:T(8,128)(2,1)}, bf16[384,4096]{1,0:T(8,128)(2,1)}, u32[]{:S(2)}, u32[]{:S(2)}) collective-permute-start(bf16[384,4096]{1,0:T(8,128)(2,1)} %add_convert_fusion.1), channel_id=1, source_target_pairs={{0,4},{1,5},{2,6},{3,7},{4,0},{5,1},{6,2},{7,3},{8,12},{9,13},{10,... | collective-permute-start | bytes 9437192 | tf_op jit(solution)/shard_map/ppermute | solution.py:183
  509.1 17.2 %collective-permute-start.21 = (bf16[32,96,128]{2,1,0:T(8,128)(2,1)S(1)}, bf16[32,96,128]{2,1,0:T(8,128)(2,1)S(1)}, u32[]{:S(2)}, u32[]{:S(2)}) collective-permute-start(bf16[32,96,128]{2,1,0:T(8,128)(2,1)S(1)} %fusion.79), channel_id=1, source_target_pairs={{0,2},{1,3},{2,0},{3,1},{4,6},{5,7},{6,4},{7,5},{8,10},{9,11},{10,... | collective-permute-start | bytes 2359304 | tf_op jit(solution)/shard_map/ppermute | solution.py:903
  528.5 87.8 %collective-permute-start.25 = (bf16[1024,1536]{1,0:T(8,128)(2,1)}, bf16[1024,1536]{1,0:T(8,128)(2,1)}, u32[]{:S(2)}, u32[]{:S(2)}) collective-permute-start(bf16[1024,1536]{1,0:T(8,128)(2,1)} %add_convert_fusion), channel_id=1, source_target_pairs={{0,4},{1,5},{2,6},{3,7},{4,0},{5,1},{6,2},{7,3},{8,12},{9,13},{10,... | collective-permute-start | bytes 9437192 | tf_op jit(solution)/shard_map/ppermute | solution.py:183
  530.8 85.5 %all-to-all-start.4 = ((bf16[32,192,128]{2,1,0:T(8,128)(2,1)}), bf16[32,192,128]{2,1,0:T(8,128)(2,1)}, u32[]{:S(2)}, u32[]{:S(2)}) async-start(bf16[32,192,128]{2,1,0:T(8,128)(2,1)} %pad_maximum_fusion), calls=%async_computation.4 | async-start | bytes 3145728 | tf_op jit(solution)/shard_map/all_to_all | solution.py:900
  550.6 32.0 %collective-permute-start.24 = (bf16[96,4096]{1,0:T(8,128)(2,1)}, bf16[96,4096]{1,0:T(8,128)(2,1)S(1)}, u32[]{:S(2)}, u32[]{:S(2)}) collective-permute-start(bf16[96,4096]{1,0:T(8,128)(2,1)} %fusion.14), channel_id=1, source_target_pairs={{0,24},{1,25},{2,26},{3,27},{4,28},{5,29},{6,30},{7,31},{8,0},{9,1... | collective-permute-start | bytes 2359304 | tf_op jit(solution)/shard_map/ppermute | solution.py:183
  555.8 43.7 %collective-permute-start.23 = (bf16[96,4096]{1,0:T(8,128)(2,1)}, bf16[96,4096]{1,0:T(8,128)(2,1)S(1)}, u32[]{:S(2)}, u32[]{:S(2)}) collective-permute-start(bf16[96,4096]{1,0:T(8,128)(2,1)} %fusion.13), channel_id=1, source_target_pairs={{0,24},{1,25},{2,26},{3,27},{4,28},{5,29},{6,30},{7,31},{8,0},{9,1... | collective-permute-start | bytes 2359304 | tf_op jit(solution)/shard_map/ppermute | solution.py:183
  623.2 17.5 %collective-permute-start.28 = (bf16[1536,768]{1,0:T(8,128)(2,1)S(1)}, bf16[1536,768]{1,0:T(8,128)(2,1)S(1)}, u32[]{:S(2)}, u32[]{:S(2)}) collective-permute-start(bf16[1536,768]{1,0:T(8,128)(2,1)S(1)} %convolution_convert_fusion.4), channel_id=1, source_target_pairs={{0,1},{1,0},{2,3},{3,2},{4,5},{5,4},{6,7},{7,6},{8,9},{9,8},{10,11... | collective-permute-start | bytes 7077896 | tf_op jit(solution)/shard_map/ppermute | solution.py:183
  625.0 17.8 %collective-permute-start.26 = (bf16[768,1536]{1,0:T(8,128)(2,1)S(1)}, bf16[768,1536]{1,0:T(8,128)(2,1)S(1)}, u32[]{:S(2)}, u32[]{:S(2)}) collective-permute-start(bf16[768,1536]{1,0:T(8,128)(2,1)S(1)} %convolution_convert_fusion.5), channel_id=1, source_target_pairs={{0,1},{1,0},{2,3},{3,2},{4,5},{5,4},{6,7},{7,6},{8,9},{9,8},{10,11... | collective-permute-start | bytes 7077896 | tf_op jit(solution)/shard_map/ppermute | solution.py:183
  626.2 42.1 %collective-permute-start.30 = (bf16[768,1536]{1,0:T(8,128)(2,1)S(1)}, bf16[768,1536]{1,0:T(8,128)(2,1)S(1)}, u32[]{:S(2)}, u32[]{:S(2)}) collective-permute-start(bf16[768,1536]{1,0:T(8,128)(2,1)S(1)} %convolution_convert_fusion.3), channel_id=1, source_target_pairs={{0,1},{1,0},{2,3},{3,2},{4,5},{5,4},{6,7},{7,6},{8,9},{9,8},{10,11... | collective-permute-start | bytes 7077896 | tf_op jit(solution)/shard_map/ppermute | solution.py:183
  626.5 21.1 %collective-permute-start.34 = (bf16[96,4096]{1,0:T(8,128)(2,1)S(1)}, bf16[96,4096]{1,0:T(8,128)(2,1)S(1)}, u32[]{:S(2)}, u32[]{:S(2)}) collective-permute-start(bf16[96,4096]{1,0:T(8,128)(2,1)S(1)} %copy-done.39), channel_id=1, source_target_pairs={{0,24},{1,25},{2,26},{3,27},{4,28},{5,29},{6,30},{7,31},{8,0},{9,1... | collective-permute-start | bytes 2359304 | tf_op jit(solution)/shard_map/ppermute | solution.py:183
  630.8 33.5 %collective-permute-start.32 = (bf16[96,4096]{1,0:T(8,128)(2,1)S(1)}, bf16[96,4096]{1,0:T(8,128)(2,1)S(1)}, u32[]{:S(2)}, u32[]{:S(2)}) collective-permute-start(bf16[96,4096]{1,0:T(8,128)(2,1)S(1)} %copy-done.38), channel_id=1, source_target_pairs={{0,24},{1,25},{2,26},{3,27},{4,28},{5,29},{6,30},{7,31},{8,0},{9,1... | collective-permute-start | bytes 2359304 | tf_op jit(solution)/shard_map/ppermute | solution.py:183
  642.1 29.8 %collective-permute-start.29 = (bf16[768,768]{1,0:T(8,128)(2,1)S(1)}, bf16[768,768]{1,0:T(8,128)(2,1)S(1)}, u32[]{:S(2)}, u32[]{:S(2)}) collective-permute-start(bf16[768,768]{1,0:T(8,128)(2,1)S(1)} %add_convert_fusion.3), channel_id=1, source_target_pairs={{0,4},{1,5},{2,6},{3,7},{4,0},{5,1},{6,2},{7,3},{8,12},{9,13},{10,... | collective-permute-start | bytes 3538952 | tf_op jit(solution)/shard_map/ppermute | solution.py:183
  643.4 29.5 %collective-permute-start.27 = (bf16[384,1536]{1,0:T(8,128)(2,1)S(1)}, bf16[384,1536]{1,0:T(8,128)(2,1)}, u32[]{:S(2)}, u32[]{:S(2)}) collective-permute-start(bf16[384,1536]{1,0:T(8,128)(2,1)S(1)} %add_convert_fusion.4), channel_id=1, source_target_pairs={{0,2},{1,3},{2,0},{3,1},{4,6},{5,7},{6,4},{7,5},{8,10},{9,11},{10,... | collective-permute-start | bytes 3538952 | tf_op jit(solution)/shard_map/ppermute | solution.py:183
  647.6 56.0 %collective-permute-start.36 = (bf16[512,1536]{1,0:T(8,128)(2,1)}, bf16[512,1536]{1,0:T(8,128)(2,1)S(1)}, u32[]{:S(2)}, u32[]{:S(2)}) collective-permute-start(bf16[512,1536]{1,0:T(8,128)(2,1)} %fusion.35), channel_id=1, source_target_pairs={{0,2},{1,3},{2,0},{3,1},{4,6},{5,7},{6,4},{7,5},{8,10},{9,11},{10,... | collective-permute-start | bytes 4718600 | tf_op jit(solution)/shard_map/ppermute | solution.py:183
  664.3 19.7 %collective-permute-start.35 = (bf16[96,4096]{1,0:T(8,128)(2,1)S(1)}, bf16[96,4096]{1,0:T(8,128)(2,1)S(1)}, u32[]{:S(2)}, u32[]{:S(2)}) collective-permute-start(bf16[96,4096]{1,0:T(8,128)(2,1)S(1)} %fusion.18), channel_id=1, source_target_pairs={{0,24},{1,25},{2,26},{3,27},{4,28},{5,29},{6,30},{7,31},{8,0},{9,1... | collective-permute-start | bytes 2359304 | tf_op jit(solution)/shard_map/ppermute | solution.py:183
  668.8 32.0 %collective-permute-start.31 = (bf16[384,1536]{1,0:T(8,128)(2,1)S(1)}, bf16[384,1536]{1,0:T(8,128)(2,1)S(1)}, u32[]{:S(2)}, u32[]{:S(2)}) collective-permute-start(bf16[384,1536]{1,0:T(8,128)(2,1)S(1)} %fusion.36), channel_id=1, source_target_pairs={{0,4},{1,5},{2,6},{3,7},{4,0},{5,1},{6,2},{7,3},{8,12},{9,13},{10,... | collective-permute-start | bytes 3538952 | tf_op jit(solution)/shard_map/ppermute | solution.py:183
  671.9 29.0 %collective-permute-start.33 = (bf16[96,4096]{1,0:T(8,128)(2,1)S(1)}, bf16[96,4096]{1,0:T(8,128)(2,1)S(1)}, u32[]{:S(2)}, u32[]{:S(2)}) collective-permute-start(bf16[96,4096]{1,0:T(8,128)(2,1)S(1)} %fusion.17), channel_id=1, source_target_pairs={{0,24},{1,25},{2,26},{3,27},{4,28},{5,29},{6,30},{7,31},{8,0},{9,1... | collective-permute-start | bytes 2359304 | tf_op jit(solution)/shard_map/ppermute | solution.py:183
  677.1 23.8 %collective-permute-start.37 = (f32[24,128]{1,0:T(8,128)S(1)}, f32[24,128]{1,0:T(8,128)S(1)}, u32[]{:S(2)}, u32[]{:S(2)}) collective-permute-start(f32[24,128]{1,0:T(8,128)S(1)} %pad_maximum_fusion.6), channel_id=1, source_target_pairs={{0,1},{1,0},{2,3},{3,2},{4,5},{5,4},{6,7},{7,6},{8,9},{9,8},{10,11... | collective-permute-start | bytes 36872 | tf_op jit(solution)/shard_map/ppermute | solution.py:183
  705.1 27.0 %collective-permute-start.41 = (bf16[128,1536]{1,0:T(8,128)(2,1)S(1)}, bf16[128,1536]{1,0:T(8,128)(2,1)S(1)}, u32[]{:S(2)}, u32[]{:S(2)}) collective-permute-start(bf16[128,1536]{1,0:T(8,128)(2,1)S(1)} %add_convert_fusion.8), channel_id=1, source_target_pairs={{0,24},{1,25},{2,26},{3,27},{4,28},{5,29},{6,30},{7,31},{8,0},{9,1... | collective-permute-start | bytes 1179656 | tf_op jit(solution)/shard_map/ppermute | solution.py:183
  707.2 24.9 %collective-permute-start.40 = (bf16[192,1536]{1,0:T(8,128)(2,1)S(1)}, bf16[192,1536]{1,0:T(8,128)(2,1)S(1)}, u32[]{:S(2)}, u32[]{:S(2)}) collective-permute-start(bf16[192,1536]{1,0:T(8,128)(2,1)S(1)} %fusion.40), channel_id=1, source_target_pairs={{0,2},{1,3},{2,0},{3,1},{4,6},{5,7},{6,4},{7,5},{8,10},{9,11},{10,... | collective-permute-start | bytes 1769480 | tf_op jit(solution)/shard_map/ppermute | solution.py:183
  708.7 23.4 %collective-permute-start.39 = (bf16[192,768]{1,0:T(8,128)(2,1)S(1)}, bf16[192,768]{1,0:T(8,128)(2,1)S(1)}, u32[]{:S(2)}, u32[]{:S(2)}) collective-permute-start(bf16[192,768]{1,0:T(8,128)(2,1)S(1)} %add_convert_fusion.13), channel_id=1, source_target_pairs={{0,24},{1,25},{2,26},{3,27},{4,28},{5,29},{6,30},{7,31},{8,0},{9,1... | collective-permute-start | bytes 884744 | tf_op jit(solution)/shard_map/ppermute | solution.py:183
  710.2 21.9 %collective-permute-start.38 = (bf16[96,1536]{1,0:T(8,128)(2,1)S(1)}, bf16[96,1536]{1,0:T(8,128)(2,1)S(1)}, u32[]{:S(2)}, u32[]{:S(2)}) collective-permute-start(bf16[96,1536]{1,0:T(8,128)(2,1)S(1)} %add_convert_fusion.14), channel_id=1, source_target_pairs={{0,24},{1,25},{2,26},{3,27},{4,28},{5,29},{6,30},{7,31},{8,0},{9,1... | collective-permute-start | bytes 884744 | tf_op jit(solution)/shard_map/ppermute | solution.py:183
  713.9 14.3 %collective-permute-start.61 = (bf16[48,4096]{1,0:T(8,128)(2,1)S(1)}, bf16[48,4096]{1,0:T(8,128)(2,1)S(1)}, u32[]{:S(2)}, u32[]{:S(2)}) collective-permute-start(bf16[48,4096]{1,0:T(8,128)(2,1)S(1)} %fusion.32), channel_id=1, source_target_pairs={{0,2},{1,3},{2,0},{3,1},{4,6},{5,7},{6,4},{7,5},{8,10},{9,11},{10,... | collective-permute-start | bytes 1179656 | tf_op jit(solution)/shard_map/ppermute | solution.py:183
  732.1 12.3 %collective-permute-start.47 = (f32[24,128]{1,0:T(8,128)S(1)}, f32[24,128]{1,0:T(8,128)S(1)}, u32[]{:S(2)}, u32[]{:S(2)}) collective-permute-start(f32[24,128]{1,0:T(8,128)S(1)} %add.2654), channel_id=1, source_target_pairs={{0,4},{1,5},{2,6},{3,7},{4,0},{5,1},{6,2},{7,3},{8,12},{9,13},{10,... | collective-permute-start | bytes 36872 | tf_op jit(solution)/shard_map/ppermute | solution.py:183
  734.1 21.8 %collective-permute-start.46 = (bf16[128,1536]{1,0:T(8,128)(2,1)S(1)}, bf16[128,1536]{1,0:T(8,128)(2,1)S(1)}, u32[]{:S(2)}, u32[]{:S(2)}) collective-permute-start(bf16[128,1536]{1,0:T(8,128)(2,1)S(1)} %add_convert_fusion.7), channel_id=1, source_target_pairs={{0,24},{1,25},{2,26},{3,27},{4,28},{5,29},{6,30},{7,31},{8,0},{9,1... | collective-permute-start | bytes 1179656 | tf_op jit(solution)/shard_map/ppermute | solution.py:183
  735.4 20.5 %collective-permute-start.44 = (bf16[192,768]{1,0:T(8,128)(2,1)S(1)}, bf16[192,768]{1,0:T(8,128)(2,1)S(1)}, u32[]{:S(2)}, u32[]{:S(2)}) collective-permute-start(bf16[192,768]{1,0:T(8,128)(2,1)S(1)} %add_convert_fusion.11), channel_id=1, source_target_pairs={{0,24},{1,25},{2,26},{3,27},{4,28},{5,29},{6,30},{7,31},{8,0},{9,1... | collective-permute-start | bytes 884744 | tf_op jit(solution)/shard_map/ppermute | solution.py:183
  738.3 17.6 %collective-permute-start.43 = (bf16[96,1536]{1,0:T(8,128)(2,1)S(1)}, bf16[96,1536]{1,0:T(8,128)(2,1)S(1)}, u32[]{:S(2)}, u32[]{:S(2)}) collective-permute-start(bf16[96,1536]{1,0:T(8,128)(2,1)S(1)} %add_convert_fusion.12), channel_id=1, source_target_pairs={{0,24},{1,25},{2,26},{3,27},{4,28},{5,29},{6,30},{7,31},{8,0},{9,1... | collective-permute-start | bytes 884744 | tf_op jit(solution)/shard_map/ppermute | solution.py:183
  739.1 16.9 %collective-permute-start.45 = (bf16[48,1536]{1,0:T(8,128)(2,1)S(1)}, bf16[48,1536]{1,0:T(8,128)(2,1)S(1)}, u32[]{:S(2)}, u32[]{:S(2)}) collective-permute-start(bf16[48,1536]{1,0:T(8,128)(2,1)S(1)} %fusion.61), channel_id=1, source_target_pairs={{0,24},{1,25},{2,26},{3,27},{4,28},{5,29},{6,30},{7,31},{8,0},{9,1... | collective-permute-start | bytes 442376 | tf_op jit(solution)/shard_map/ppermute | solution.py:183
  755.9 9.2 %collective-permute-start.51 = (f32[24,128]{1,0:T(8,128)S(1)}, f32[24,128]{1,0:T(8,128)S(1)}, u32[]{:S(2)}, u32[]{:S(2)}) collective-permute-start(f32[24,128]{1,0:T(8,128)S(1)} %add.2668), channel_id=1, source_target_pairs={{0,16},{1,17},{2,18},{3,19},{4,20},{5,21},{6,22},{7,23},{8,24},{9,... | collective-permute-start | bytes 36872 | tf_op jit(solution)/shard_map/ppermute | solution.py:183
  762.2 9.7 %collective-permute-start.48 = (bf16[96,1536]{1,0:T(8,128)(2,1)S(1)}, bf16[96,1536]{1,0:T(8,128)(2,1)S(1)}, u32[]{:S(2)}, u32[]{:S(2)}) collective-permute-start(bf16[96,1536]{1,0:T(8,128)(2,1)S(1)} %add_convert_fusion.10), channel_id=1, source_target_pairs={{0,24},{1,25},{2,26},{3,27},{4,28},{5,29},{6,30},{7,31},{8,0},{9,1... | collective-permute-start | bytes 884744 | tf_op jit(solution)/shard_map/ppermute | solution.py:183
  765.0 17.7 %collective-permute-start.62 = (bf16[128,1536]{1,0:T(8,128)(2,1)S(1)}, bf16[128,1536]{1,0:T(8,128)(2,1)S(1)}, u32[]{:S(2)}, u32[]{:S(2)}) collective-permute-start(bf16[128,1536]{1,0:T(8,128)(2,1)S(1)} %add_convert_fusion.6), channel_id=1, source_target_pairs={{0,24},{1,25},{2,26},{3,27},{4,28},{5,29},{6,30},{7,31},{8,0},{9,1... | collective-permute-start | bytes 1179656 | tf_op jit(solution)/shard_map/ppermute | solution.py:183
  771.9 51.6 %collective-permute-start.52 = (f32[24,128]{1,0:T(8,128)S(1)}, f32[24,128]{1,0:T(8,128)S(1)}, u32[]{:S(2)}, u32[]{:S(2)}) collective-permute-start(f32[24,128]{1,0:T(8,128)S(1)} %add.2679), channel_id=1, source_target_pairs={{0,8},{1,9},{2,10},{3,11},{4,12},{5,13},{6,14},{7,15},{8,16},{9,17... | collective-permute-start | bytes 36872 | tf_op jit(solution)/shard_map/ppermute | solution.py:183
  772.9 17.6 %collective-permute-start.55 = (bf16[48,1536]{1,0:T(8,128)(2,1)}, bf16[48,1536]{1,0:T(8,128)(2,1)}, u32[]{:S(2)}, u32[]{:S(2)}) collective-permute-start(bf16[48,1536]{1,0:T(8,128)(2,1)} %fusion.58), channel_id=1, source_target_pairs={{0,24},{1,25},{2,26},{3,27},{4,28},{5,29},{6,30},{7,31},{8,0},{9,1... | collective-permute-start | bytes 442376 | tf_op jit(solution)/shard_map/ppermute | solution.py:183
  778.0 15.7 %collective-permute-start.54 = (bf16[96,768]{1,0:T(8,128)(2,1)}, bf16[96,768]{1,0:T(8,128)(2,1)}, u32[]{:S(2)}, u32[]{:S(2)}) collective-permute-start(bf16[96,768]{1,0:T(8,128)(2,1)} %add_convert_fusion.16), channel_id=1, source_target_pairs={{0,2},{1,3},{2,0},{3,1},{4,6},{5,7},{6,4},{7,5},{8,10},{9,11},{10,... | collective-permute-start | bytes 442376 | tf_op jit(solution)/shard_map/ppermute | solution.py:183
  780.9 14.2 %collective-permute-start.53 = (bf16[48,1536]{1,0:T(8,128)(2,1)}, bf16[48,1536]{1,0:T(8,128)(2,1)}, u32[]{:S(2)}, u32[]{:S(2)}) collective-permute-start(bf16[48,1536]{1,0:T(8,128)(2,1)} %add_convert_fusion.18), channel_id=1, source_target_pairs={{0,4},{1,5},{2,6},{3,7},{4,0},{5,1},{6,2},{7,3},{8,12},{9,13},{10,... | collective-permute-start | bytes 442376 | tf_op jit(solution)/shard_map/ppermute | solution.py:183
  788.5 34.2 %collective-permute-start.63 = (bf16[196608]{0:T(1024)(128)(2,1)}, bf16[196608]{0:T(1024)(128)(2,1)}, u32[]{:S(2)}, u32[]{:S(2)}) collective-permute-start(bf16[196608]{0:T(1024)(128)(2,1)} %get-tuple-element.332), channel_id=1, source_target_pairs={{2,0},{5,1},{8,2},{11,3},{14,4},{17,5},{20,6},{23,7},{26,8},{29,9}... | collective-permute-start | bytes 1179656 | tf_op jit(solution)/shard_map/ppermute | solution.py:140
  801.6 28.4 %collective-permute-start.58 = (bf16[73728]{0:T(1024)(128)(2,1)S(1)}, bf16[73728]{0:T(1024)(128)(2,1)S(1)}, u32[]{:S(2)}, u32[]{:S(2)}) collective-permute-start(bf16[73728]{0:T(1024)(128)(2,1)S(1)} %get-tuple-element.339), channel_id=1, source_target_pairs={{0,0},{3,1},{6,2},{9,3},{12,4},{15,5},{18,6},{21,7},{24,8},{27,9},... | collective-permute-start | bytes 442376 | tf_op jit(solution)/shard_map/ppermute | solution.py:140
  804.1 39.5 %collective-permute-start.65 = (bf16[196608]{0:T(1024)(128)(2,1)}, bf16[196608]{0:T(1024)(128)(2,1)S(1)}, u32[]{:S(2)}, u32[]{:S(2)}) collective-permute-start(bf16[196608]{0:T(1024)(128)(2,1)} %get-tuple-element.331), channel_id=1, source_target_pairs={{0,0},{3,1},{6,2},{9,3},{12,4},{15,5},{18,6},{21,7},{24,8},{27,9},... | collective-permute-start | bytes 1179656 | tf_op jit(solution)/shard_map/ppermute | solution.py:140
  806.0 37.6 %collective-permute-start.66 = (bf16[196608]{0:T(1024)(128)(2,1)}, bf16[196608]{0:T(1024)(128)(2,1)S(1)}, u32[]{:S(2)}, u32[]{:S(2)}) collective-permute-start(bf16[196608]{0:T(1024)(128)(2,1)} %get-tuple-element.330), channel_id=1, source_target_pairs={{1,0},{4,1},{7,2},{10,3},{13,4},{16,5},{19,6},{22,7},{25,8},{28,9}... | collective-permute-start | bytes 1179656 | tf_op jit(solution)/shard_map/ppermute | solution.py:140
  822.7 18.9 %collective-permute-start.59 = (bf16[73728]{0:T(1024)(128)(2,1)}, bf16[73728]{0:T(1024)(128)(2,1)}, u32[]{:S(2)}, u32[]{:S(2)}) collective-permute-start(bf16[73728]{0:T(1024)(128)(2,1)} %get-tuple-element.338), channel_id=1, source_target_pairs={{1,0},{4,1},{7,2},{10,3},{13,4},{16,5},{19,6},{22,7},{25,8},{28,9}... | collective-permute-start | bytes 442376 | tf_op jit(solution)/shard_map/ppermute | solution.py:140
  823.5 20.2 %collective-permute-start.57 = (bf16[1536]{0:T(1024)(128)(2,1)S(1)}, bf16[1536]{0:T(1024)(128)(2,1)S(1)}, u32[]{:S(2)}, u32[]{:S(2)}) collective-permute-start(bf16[1536]{0:T(1024)(128)(2,1)S(1)} %slice.875), channel_id=1, source_target_pairs={{0,1},{1,2},{2,3},{3,4},{4,5},{5,6},{6,7},{7,8},{8,9},{9,10},{10,1... | collective-permute-start | bytes 9224 | tf_op jit(solution)/shard_map/ppermute | solution.py:142
  830.0 13.7 %collective-permute-start.64 = (bf16[1536]{0:T(1024)(128)(2,1)S(1)}, bf16[1536]{0:T(1024)(128)(2,1)S(1)}, u32[]{:S(2)}, u32[]{:S(2)}) collective-permute-start(bf16[1536]{0:T(1024)(128)(2,1)S(1)} %slice.883), channel_id=1, source_target_pairs={{0,1},{1,2},{2,3},{3,4},{4,5},{5,6},{6,7},{7,8},{8,9},{9,10},{10,1... | collective-permute-start | bytes 9224 | tf_op jit(solution)/shard_map/ppermute | solution.py:142
  (77 other events, 1019.7 us)
Sparse Core Ops, SparseCore 0:
  81.6 265.4 all-gather.1

commit v6 on v5

--- a/solution.py
+++ b/solution.py
@@ -1230,8 +1230,9 @@
         attn_sums = last_sums + [out_sum]
         make_and_send([gain_sum])
         one_round(attn_sums + early_sums + [gain_sum])
-        one_round(attn_sums + [down_sum, gain_sum])
-        one_round(attn_sums + [down_sum, gain_sum])
+        for _ in range(2):
+            one_round(attn_sums + [gain_sum])
+            make_and_send([down_sum])
         ffn_units = [gate_sum.result(), up_sum.result(), down_sum.result()]
         one_round(attn_sums + [gain_sum])
         gain_grads = gain_sum.result().reshape(2, D)

time: 867 us -> 860 us (level)
  waiting for transfers between devices: 271 us -> 253 us
  Pallas kernels: 134 us -> 145 us
    ppermute x52, waiting for transfers between devices: 181 us -> 162 us  [shifted(): return lax.ppermute(value, 'seq', pairs)]
    ppermute x52, starting transfers between devices: 55.7 us -> 68.5 us  [shifted(): return lax.ppermute(value, 'seq', pairs)]
    ppermute x6, starting transfers between devices: 27.3 us -> 15 us  [shard_from_units(): lax.ppermute(piece, 'seq', [((3 * i + j) % count, i) for i in range(count)])]
    pallas_call x2, Pallas kernels: 62 us -> 72.5 us  [run_kernel(): pl.pallas_call(body, grid_spec=pltpu.PrefetchScalarGridSpec(num_scalar_pr...]
  transfers between devices with their start and end apart: 72 -> 72, of which waited for: 29 -> 31; matrix products, arithmetic and copies ran while one was open for 21% -> 22% of each run, Pallas kernels for 11% -> 13%
where the time goes in v6:
time: 860 us; the launch traced here: 853 us
  waiting for transfers between devices  253 us (29%)
  Pallas kernels  145 us (17%)
  starting transfers between devices  133 us (15%)
  matrix products  105 us (12%)
  blocking collectives  89.8 us (10%)
  other arithmetic  71.1 us (8%)
  local copies, waits for them, and re-layouts  40.9 us (5%)
  between operations  15.9 us (2%)
    ppermute x52, waiting for transfers between devices, shifted(): return lax.ppermute(value, 'seq', pairs)  162 us
    dot_general x45, matrix products, contract(): lax.dot_general(left, right, (((left_dim,), (right_dim,)), ((), ())), pre...  105 us
    all_to_all x1, blocking collectives, exchange(): return lax.all_to_all(value, 'seq', 0, 0, tiled=True)  89.8 us
    pallas_call x2, Pallas kernels, run_kernel(): pl.pallas_call(body, grid_spec=pltpu.PrefetchScalarGridSpec(num_scalar_pr...  72.5 us
    ppermute x52, starting transfers between devices, shifted(): return lax.ppermute(value, 'seq', pairs)  68.5 us
    ppermute x5, waiting for transfers between devices, swapped(): return lax.ppermute(value, 'seq', [(i, i ^ bit) for i in range(count)])  44.7 us
    all_to_all x4, waiting for transfers between devices, exchange(): return lax.all_to_all(value, 'seq', 0, 0, tiled=True)  41.2 us
    pallas_call x1, Pallas kernels, feed_forward(): pl.pallas_call(feed_forward_kernel, grid=(FF // FF_TILE,), in_specs=[fixe...  33.7 us
  transfers between devices with their start and end apart: 72, of which 31 were waited for; matrix products, arithmetic and copies ran while one was open for 22% of the time, Pallas kernels for 13%

profile of v6, /device:TPU:7, one launch (start us, length us, event | category | flops | bytes accessed | tf_op | source)
XLA Modules:
  0.0 853.2 jit_solution(11948029469069354973)
XLA Ops:
  14.4 6.3 all-to-all-start
  30.3 18.5 %all-to-all-done = bf16[32,26,128]{2,1,0:T(8,128)(2,1)S(1)} async-done(((bf16[32,26,128]{2,1,0:T(8,128)(2,1)}), bf16[32,26,128]{2,1,0:T(8,128)(2,1)S(1)}, u32[]{:S(2)}, u32[]{:S(2)}) %all-to-all-start) | async-done | bytes 213024 | tf_op jit(solution)/shard_map/all_to_all | solution.py:900
  48.8 9.1 %collective-permute-done.2 = bf16[216,8,128]{2,1,0:T(8,128)(2,1)} collective-permute-done((bf16[216,8,128]{2,1,0:T(8,128)(2,1)S(1)}, bf16[216,8,128]{2,1,0:T(8,128)(2,1)}, u32[]{:S(2)}, u32[]{:S(2)}) %collective-permute-start.2) | collective-permute-done | bytes 442400 | tf_op jit(solution)/shard_map/ppermute | solution.py:183
  68.4 11.9 %collective-permute-done.5 = bf16[432,8,128]{2,1,0:T(8,128)(2,1)} collective-permute-done((bf16[432,8,128]{2,1,0:T(8,128)(2,1)S(1)}, bf16[432,8,128]{2,1,0:T(8,128)(2,1)}, u32[]{:S(2)}, u32[]{:S(2)}) %collective-permute-start.5) | collective-permute-done | bytes 884768 | tf_op jit(solution)/shard_map/ppermute | solution.py:183
  91.2 18.8 %convert_reduce_fusion = s32[4096]{0:T(1024)S(1)} fusion(s32[8192]{0:T(1024)S(1)} %bitcast.263, s32[4096]{0:T(1024)S(1)} %bitcast.270), kind=kLoop, calls=%fused_computation | loop fusion | flops 100659200 | bytes 65536 | tf_op jit(solution)/shard_map/reduce_sum | solution.py:922
  110.0 23.5 %collective-permute-done.8.refs_5_ = bf16[864,8,128]{2,1,0:T(8,128)(2,1)} collective-permute-done((bf16[864,8,128]{2,1,0:T(8,128)(2,1)}, bf16[864,8,128]{2,1,0:T(8,128)(2,1)}, u32[]{:S(2)}, u32[]{:S(2)}) %collective-permute-start.8) | collective-permute-done | bytes 1769504 | tf_op jit(solution)/shard_map/ppermute | solution.py:183
  135.8 3.7 collective-permute-start.10
  143.2 5.1 collective-permute-done.11.refs_6_
  150.8 13.6 %place_blocks.1 = bf16[6912,8,128]{2,1,0:T(8,128)(2,1)} custom-call(s32[64]{0:T(128)S(1)} %pad_add_fusion.table_ref, bf16[864,8,128]{2,1,0:T(8,128)(2,1)S(1)} %constant_dynamic-update-slice_fusion.refs_0_, bf16[864,8,128]{2,1,0:T(8,128)(2,1)} %collective-permute-done.7.refs_1_, bf16[864,8,128]{2,1,0:T(8,128)(2,1)} %collective-permute-done.9.refs_2_, ...), custom_call_target="tpu_custom_call" | custom-call | bytes 28311552 | tf_op jit(solution)/shard_map/place_blocks/pallas_call | solution.py:226
  164.5 5.8 project.1
  170.3 89.8 %all_to_all.25.query_ref = bf16[32,192,128]{2,1,0:T(8,128)(2,1)S(1)} all-to-all(bf16[32,192,128]{2,1,0:T(8,128)(2,1)S(1)} %project.1), channel_id=1, replica_groups=mesh['seq'=32] {'seq'}, dimensions={0} | all-to-all | bytes 3145728 | tf_op jit(solution)/shard_map/all_to_all | solution.py:900
  262.4 33.6 %collective-permute-done.14.refs_2_ = bf16[32,96,128]{2,1,0:T(8,128)(2,1)S(1)} collective-permute-done((bf16[32,96,128]{2,1,0:T(8,128)(2,1)S(1)}, bf16[32,96,128]{2,1,0:T(8,128)(2,1)S(1)}, u32[]{:S(2)}, u32[]{:S(2)}) %collective-permute-start.14) | collective-permute-done | bytes 786464 | tf_op jit(solution)/shard_map/ppermute | solution.py:903
  300.7 29.6 %attention_forward.1 = (f32[8,96,512]{2,1,0:T(8,128)}, bf16[32,96,128]{2,1,0:T(8,128)(2,1)}, f32[8,1,512]{2,1,0:T(1,128)S(1)}, bf16[8192,96]{1,0:T(8,128)(2,1)}, bf16[8,96,1024]{2,1,0:T(8,128)(2,1)}) custom-call(s32[8]{0:T(128)S(1)} %and_select_fusion.1.low_ref, s32[8]{0:T(128)S(1)} %and_select_fusion.high_ref, s32[1]{0:T(128)} %bitcast.32.half_ref, ...), custom_call_target="tpu_custom_call" | custom-call | flops 20000000000 | bytes 16777216 | tf_op jit(solution)/shard_map/attention_forward/pallas_call | solution.py:772
  330.3 14.1 %all-to-all-start.2 = ((bf16[32,96,128]{2,1,0:T(8,128)(2,1)}), bf16[32,96,128]{2,1,0:T(8,128)(2,1)S(1)}, u32[]{:S(2)}, u32[]{:S(2)}) async-start(bf16[32,96,128]{2,1,0:T(8,128)(2,1)} %get-tuple-element.151), calls=%async_computation.2 | async-start | bytes 1572864 | tf_op jit(solution)/shard_map/all_to_all | solution.py:900
  345.1 3.8 multiply_sine_fusion
  351.4 3.9 copy.106
  355.3 8.7 %all-to-all-done.2.mixed_piece_ref = bf16[32,96,128]{2,1,0:T(8,128)(2,1)S(1)} async-done(((bf16[32,96,128]{2,1,0:T(8,128)(2,1)}), bf16[32,96,128]{2,1,0:T(8,128)(2,1)S(1)}, u32[]{:S(2)}, u32[]{:S(2)}) %all-to-all-start.2) | async-done | bytes 786464 | tf_op jit(solution)/shard_map/all_to_all | solution.py:900
  364.0 33.7 %feed_forward.1 = (bf16[256,1536]{1,0:T(8,128)(2,1)}, f32[256,1536]{1,0:T(8,128)}, bf16[256,1536]{1,0:T(8,128)(2,1)S(1)}, bf16[32,96,128]{2,1,0:T(8,128)(2,1)}, ...) custom-call(bf16[256,1536]{1,0:T(8,128)(2,1)S(1)} %copy-done.2, ...), custom_call_target="tpu_custom_call" | custom-call | flops 19327352832 | bytes 37748736 | tf_op jit(solution)/shard_map/feed_forward/pallas_call | solution.py:516
  402.2 6.2 convolution_convert_fusion.1
  412.8 6.2 convolution_convert_fusion.2
  418.9 4.6 all-to-all-start.3
  423.5 3.8 reorder_blocks.8
  427.3 5.8 convolution_convert_fusion
  433.4 4.9 add_convert_fusion.1
  438.3 4.7 add_convert_fusion.2
  444.9 43.0 %attention_backward.1 = (bf16[32,96,128]{2,1,0:T(8,128)(2,1)S(1)}, f32[2,1,32,96,128]{4,3,2,1,0:T(8,128)}, bf16[2,1,32,96,128]{4,3,2,1,0:T(8,128)(2,1)}) custom-call(s32[8]{0:T(128)S(1)} %and_select_fusion.1.low_ref, s32[8]{0:T(128)S(1)} %and_select_fusion.high_ref, bf16[32,192,128]{2,1,0:T(8,128)(2,1)} %copy-done.20, bf16[32,96,128]{2,1,0:T(8,128)(2,1)} %copy-done.39, ...), custom_call_target="tpu_custom_call" | custom-call | flops 49999998976 | bytes 16777216 | tf_op jit(solution)/shard_map/attention_backward/pallas_call | solution.py:772
  488.5 3.4 collective-permute-done.18
  494.7 17.4 %collective-permute-done.19 = bf16[384,4096]{1,0:T(8,128)(2,1)} collective-permute-done((bf16[384,4096]{1,0:T(8,128)(2,1)}, bf16[384,4096]{1,0:T(8,128)(2,1)}, u32[]{:S(2)}, u32[]{:S(2)}) %collective-permute-start.19) | collective-permute-done | bytes 3145760 | tf_op jit(solution)/shard_map/ppermute | solution.py:183
  513.5 4.9 add_convert_fusion
  518.4 3.1 fusion.14
  521.4 2.9 fusion.13
  524.4 5.9 collective-permute-done.21
  534.8 7.5 all-to-all-start.4
  547.0 4.4 reorder_blocks.10
  551.4 3.0 copy.113
  554.5 3.1 collective-permute-start.24
  566.8 19.8 %collective-permute-done.24 = bf16[96,4096]{1,0:T(8,128)(2,1)S(1)} collective-permute-done((bf16[96,4096]{1,0:T(8,128)(2,1)}, bf16[96,4096]{1,0:T(8,128)(2,1)S(1)}, u32[]{:S(2)}, u32[]{:S(2)}) %collective-permute-start.24) | collective-permute-done | bytes 786464 | tf_op jit(solution)/shard_map/ppermute | solution.py:183
  586.6 3.6 fusion.16
  590.2 13.3 %collective-permute-done.23 = bf16[96,4096]{1,0:T(8,128)(2,1)S(1)} collective-permute-done((bf16[96,4096]{1,0:T(8,128)(2,1)}, bf16[96,4096]{1,0:T(8,128)(2,1)S(1)}, u32[]{:S(2)}, u32[]{:S(2)}) %collective-permute-start.23) | collective-permute-done | bytes 786464 | tf_op jit(solution)/shard_map/ppermute | solution.py:183
  603.4 3.0 fusion.15
  606.4 13.9 %all-to-all-done.4 = bf16[32,192,128]{2,1,0:T(8,128)(2,1)} async-done(((bf16[32,192,128]{2,1,0:T(8,128)(2,1)}), bf16[32,192,128]{2,1,0:T(8,128)(2,1)}, u32[]{:S(2)}, u32[]{:S(2)}) %all-to-all-start.4) | async-done | bytes 1572896 | tf_op jit(solution)/shard_map/all_to_all | solution.py:900
  624.1 3.1 convolution_convert_fusion.4
  630.5 4.2 collective-permute-start.34
  639.1 3.7 fusion.46
  644.8 3.6 add_convert_fusion.3
  649.8 4.1 fusion.35
  657.1 11.1 %collective-permute-done.32 = bf16[96,4096]{1,0:T(8,128)(2,1)S(1)} collective-permute-done((bf16[96,4096]{1,0:T(8,128)(2,1)S(1)}, bf16[96,4096]{1,0:T(8,128)(2,1)S(1)}, u32[]{:S(2)}, u32[]{:S(2)}) %collective-permute-start.32) | collective-permute-done | bytes 786464 | tf_op jit(solution)/shard_map/ppermute | solution.py:183
  668.2 4.0 collective-permute-start.35
  676.2 4.6 fusion.65
  680.8 3.6 collective-permute-start.37
  687.9 16.9 %collective-permute-done.33 = bf16[96,4096]{1,0:T(8,128)(2,1)S(1)} collective-permute-done((bf16[96,4096]{1,0:T(8,128)(2,1)S(1)}, bf16[96,4096]{1,0:T(8,128)(2,1)S(1)}, u32[]{:S(2)}, u32[]{:S(2)}) %collective-permute-start.33) | collective-permute-done | bytes 786464 | tf_op jit(solution)/shard_map/ppermute | solution.py:183
  704.8 5.1 collective-permute-done.36
  742.7 3.5 collective-permute-start.62
  746.3 4.0 collective-permute-done.43
  750.3 6.3 collective-permute-done.42
  775.8 5.4 collective-permute-done.46
  784.0 8.9 %collective-permute-start.53 = (bf16[48,1536]{1,0:T(8,128)(2,1)S(1)}, bf16[48,1536]{1,0:T(8,128)(2,1)S(1)}, u32[]{:S(2)}, u32[]{:S(2)}) collective-permute-start(bf16[48,1536]{1,0:T(8,128)(2,1)S(1)} %fusion.58), channel_id=1, source_target_pairs={{0,24},{1,25},{2,26},{3,27},{4,28},{5,29},{6,30},{7,31},{8,0},{9,1... | collective-permute-start | bytes 442376 | tf_op jit(solution)/shard_map/ppermute | solution.py:183
  805.9 4.2 collective-permute-start.56
  812.1 4.7 collective-permute-start.66
  817.5 5.2 collective-permute-start.55
  824.7 3.0 fusion.66
  827.6 3.2 copy.114
  830.9 4.9 collective-permute-done.57
  838.0 5.4 multiply_subtract_fusion
  (412 shorter events, 192.7 us)
Async XLA Ops:
  9.1 18.4 %collective-permute-start.6 = (bf16[1536]{0:T(1024)(128)(2,1)S(1)}, bf16[1536]{0:T(1024)(128)(2,1)S(1)}, u32[]{:S(2)}, u32[]{:S(2)}) collective-permute-start(bf16[1536]{0:T(1024)(128)(2,1)S(1)} %slice.819), channel_id=1, source_target_pairs={{1,0},{2,1},{3,2},{4,3},{5,4},{6,5},{7,6},{8,7},{9,8},{10,9},{11,1... | collective-permute-start | bytes 9224 | tf_op jit(solution)/shard_map/ppermute | solution.py:86
  11.7 9.1 %collective-permute-start = (bf16[1536]{0:T(1024)(128)(2,1)S(1)}, bf16[1536]{0:T(1024)(128)(2,1)S(1)}, u32[]{:S(2)}, u32[]{:S(2)}) collective-permute-start(bf16[1536]{0:T(1024)(128)(2,1)S(1)} %slice.815), channel_id=1, source_target_pairs={{1,0},{2,1},{3,2},{4,3},{5,4},{6,5},{7,6},{8,7},{9,8},{10,9},{11,1... | collective-permute-start | bytes 9224 | tf_op jit(solution)/shard_map/ppermute | solution.py:86
  14.4 34.4 %all-to-all-start = ((bf16[32,26,128]{2,1,0:T(8,128)(2,1)}), bf16[32,26,128]{2,1,0:T(8,128)(2,1)S(1)}, u32[]{:S(2)}, u32[]{:S(2)}) async-start(bf16[32,26,128]{2,1,0:T(8,128)(2,1)} %broadcast_in_dim.9), calls=%async_computation | async-start | bytes 524288 | tf_op jit(solution)/shard_map/all_to_all | solution.py:900
  20.8 343.2 %all-gather.2.cloned.1.call-start = ((), (), s32[]{:S(2)}) async-start(), calls=%async_computation.5 | async-start | bytes 38928384 | tf_op jit(solution)/shard_map/all_gather | solution.py:959
  22.8 26.0 %collective-permute-start.1 = (bf16[216,8,128]{2,1,0:T(8,128)(2,1)S(1)}, bf16[216,8,128]{2,1,0:T(8,128)(2,1)S(1)}, u32[]{:S(2)}, u32[]{:S(2)}) collective-permute-start(bf16[216,8,128]{2,1,0:T(8,128)(2,1)S(1)} %pad_maximum_fusion.5), channel_id=1, source_target_pairs={{0,8},{1,9},{2,10},{3,11},{4,12},{5,13},{6,14},{7,15},{8,16},{9,17... | collective-permute-start | bytes 1327112 | tf_op jit(solution)/shard_map/ppermute | solution.py:183
  24.0 33.9 %collective-permute-start.2 = (bf16[216,8,128]{2,1,0:T(8,128)(2,1)S(1)}, bf16[216,8,128]{2,1,0:T(8,128)(2,1)}, u32[]{:S(2)}, u32[]{:S(2)}) collective-permute-start(bf16[216,8,128]{2,1,0:T(8,128)(2,1)S(1)} %pad_maximum_fusion.5), channel_id=1, source_target_pairs={{0,16},{1,17},{2,18},{3,19},{4,20},{5,21},{6,22},{7,23},{8,24},{9,... | collective-permute-start | bytes 1327112 | tf_op jit(solution)/shard_map/ppermute | solution.py:183
  26.2 31.7 %collective-permute-start.3 = (bf16[216,8,128]{2,1,0:T(8,128)(2,1)S(1)}, bf16[216,8,128]{2,1,0:T(8,128)(2,1)}, u32[]{:S(2)}, u32[]{:S(2)}) collective-permute-start(bf16[216,8,128]{2,1,0:T(8,128)(2,1)S(1)} %pad_maximum_fusion.5), channel_id=1, source_target_pairs={{0,24},{1,25},{2,26},{3,27},{4,28},{5,29},{6,30},{7,31},{8,0},{9,1... | collective-permute-start | bytes 1327112 | tf_op jit(solution)/shard_map/ppermute | solution.py:183
  60.3 20.0 %collective-permute-start.5 = (bf16[432,8,128]{2,1,0:T(8,128)(2,1)S(1)}, bf16[432,8,128]{2,1,0:T(8,128)(2,1)}, u32[]{:S(2)}, u32[]{:S(2)}) collective-permute-start(bf16[432,8,128]{2,1,0:T(8,128)(2,1)S(1)} %pad_maximum_fusion.3), channel_id=1, source_target_pairs={{0,2},{1,3},{2,0},{3,1},{4,6},{5,7},{6,4},{7,5},{8,10},{9,11},{10,... | collective-permute-start | bytes 2654216 | tf_op jit(solution)/shard_map/ppermute | solution.py:183
  61.6 19.8 %collective-permute-start.4 = (bf16[432,8,128]{2,1,0:T(8,128)(2,1)}, bf16[432,8,128]{2,1,0:T(8,128)(2,1)}, u32[]{:S(2)}, u32[]{:S(2)}) collective-permute-start(bf16[432,8,128]{2,1,0:T(8,128)(2,1)} %pad_maximum_fusion.2), channel_id=1, source_target_pairs={{0,4},{1,5},{2,6},{3,7},{4,0},{5,1},{6,2},{7,3},{8,12},{9,13},{10,... | collective-permute-start | bytes 2654216 | tf_op jit(solution)/shard_map/ppermute | solution.py:183
  87.2 46.3 %collective-permute-start.8 = (bf16[864,8,128]{2,1,0:T(8,128)(2,1)}, bf16[864,8,128]{2,1,0:T(8,128)(2,1)}, u32[]{:S(2)}, u32[]{:S(2)}) collective-permute-start(bf16[864,8,128]{2,1,0:T(8,128)(2,1)} %constant_dynamic-update-slice_fusion.2.refs_4_), channel_id=1, source_target_pairs={{0,4},{1,5},{2,6},{3,7},{4,0},{5,1},{6,2},{7,3},{8,12},{9,13},{10,... | collective-permute-start | bytes 5308424 | tf_op jit(solution)/shard_map/ppermute | solution.py:183
  89.9 45.9 %collective-permute-start.7 = (bf16[864,8,128]{2,1,0:T(8,128)(2,1)S(1)}, bf16[864,8,128]{2,1,0:T(8,128)(2,1)}, u32[]{:S(2)}, u32[]{:S(2)}) collective-permute-start(bf16[864,8,128]{2,1,0:T(8,128)(2,1)S(1)} %constant_dynamic-update-slice_fusion.refs_0_), channel_id=1, source_target_pairs={{0,2},{1,3},{2,0},{3,1},{4,6},{5,7},{6,4},{7,5},{8,10},{9,11},{10,... | collective-permute-start | bytes 5308424 | tf_op jit(solution)/shard_map/ppermute | solution.py:183
  139.6 11.2 %collective-permute-start.12 = (bf16[864,8,128]{2,1,0:T(8,128)(2,1)}, bf16[864,8,128]{2,1,0:T(8,128)(2,1)}, u32[]{:S(2)}, u32[]{:S(2)}) collective-permute-start(bf16[864,8,128]{2,1,0:T(8,128)(2,1)} %collective-permute-done.8.refs_5_), channel_id=1, source_target_pairs={{0,1},{1,0},{2,3},{3,2},{4,5},{5,4},{6,7},{7,6},{8,9},{9,8},{10,11... | collective-permute-start | bytes 5308424 | tf_op jit(solution)/shard_map/ppermute | solution.py:183
  140.1 10.7 %collective-permute-start.9 = (bf16[864,8,128]{2,1,0:T(8,128)(2,1)S(1)}, bf16[864,8,128]{2,1,0:T(8,128)(2,1)}, u32[]{:S(2)}, u32[]{:S(2)}) collective-permute-start(bf16[864,8,128]{2,1,0:T(8,128)(2,1)S(1)} %constant_dynamic-update-slice_fusion.refs_0_), channel_id=1, source_target_pairs={{0,1},{1,0},{2,3},{3,2},{4,5},{5,4},{6,7},{7,6},{8,9},{9,8},{10,11... | collective-permute-start | bytes 5308424 | tf_op jit(solution)/shard_map/ppermute | solution.py:183
  260.1 35.8 %collective-permute-start.14 = (bf16[32,96,128]{2,1,0:T(8,128)(2,1)S(1)}, bf16[32,96,128]{2,1,0:T(8,128)(2,1)S(1)}, u32[]{:S(2)}, u32[]{:S(2)}) collective-permute-start(bf16[32,96,128]{2,1,0:T(8,128)(2,1)S(1)} %slice.825.refs_0_), channel_id=1, source_target_pairs={{0,2},{1,3},{2,0},{3,1},{4,6},{5,7},{6,4},{7,5},{8,10},{9,11},{10,... | collective-permute-start | bytes 2359304 | tf_op jit(solution)/shard_map/ppermute | solution.py:903
  261.5 37.2 %collective-permute-start.13 = (bf16[32,96,128]{2,1,0:T(8,128)(2,1)S(1)}, bf16[32,96,128]{2,1,0:T(8,128)(2,1)S(1)}, u32[]{:S(2)}, u32[]{:S(2)}) collective-permute-start(bf16[32,96,128]{2,1,0:T(8,128)(2,1)S(1)} %slice.825.refs_0_), channel_id=1, source_target_pairs={{0,1},{1,0},{2,3},{3,2},{4,5},{5,4},{6,7},{7,6},{8,9},{9,8},{10,11... | collective-permute-start | bytes 2359304 | tf_op jit(solution)/shard_map/ppermute | solution.py:903
  330.3 33.7 %all-to-all-start.2 = ((bf16[32,96,128]{2,1,0:T(8,128)(2,1)}), bf16[32,96,128]{2,1,0:T(8,128)(2,1)S(1)}, u32[]{:S(2)}, u32[]{:S(2)}) async-start(bf16[32,96,128]{2,1,0:T(8,128)(2,1)} %get-tuple-element.151), calls=%async_computation.2 | async-start | bytes 1572864 | tf_op jit(solution)/shard_map/all_to_all | solution.py:900
  408.4 25.0 %collective-permute-start.17 = (bf16[768,4096]{1,0:T(8,128)(2,1)}, bf16[768,4096]{1,0:T(8,128)(2,1)}, u32[]{:S(2)}, u32[]{:S(2)}) collective-permute-start(bf16[768,4096]{1,0:T(8,128)(2,1)} %convolution_convert_fusion.1), channel_id=1, source_target_pairs={{0,1},{1,0},{2,3},{3,2},{4,5},{5,4},{6,7},{7,6},{8,9},{9,8},{10,11... | collective-permute-start | bytes 18874376 | tf_op jit(solution)/shard_map/ppermute | solution.py:183
  418.9 19.4 %collective-permute-start.16 = (bf16[768,4096]{1,0:T(8,128)(2,1)}, bf16[768,4096]{1,0:T(8,128)(2,1)}, u32[]{:S(2)}, u32[]{:S(2)}) collective-permute-start(bf16[768,4096]{1,0:T(8,128)(2,1)} %convolution_convert_fusion.2), channel_id=1, source_target_pairs={{0,1},{1,0},{2,3},{3,2},{4,5},{5,4},{6,7},{7,6},{8,9},{9,8},{10,11... | collective-permute-start | bytes 18874376 | tf_op jit(solution)/shard_map/ppermute | solution.py:183
  418.9 24.2 %all-to-all-start.3 = ((bf16[32,96,128]{2,1,0:T(8,128)(2,1)}), bf16[32,96,128]{2,1,0:T(8,128)(2,1)S(1)}, u32[]{:S(2)}, u32[]{:S(2)}) async-start(bf16[32,96,128]{2,1,0:T(8,128)(2,1)} %get-tuple-element.161), calls=%async_computation.3 | async-start | bytes 1572864 | tf_op jit(solution)/shard_map/all_to_all | solution.py:900
  433.1 80.4 %collective-permute-start.22 = (bf16[2048,1536]{1,0:T(8,128)(2,1)}, bf16[2048,1536]{1,0:T(8,128)(2,1)}, u32[]{:S(2)}, u32[]{:S(2)}) collective-permute-start(bf16[2048,1536]{1,0:T(8,128)(2,1)} %convolution_convert_fusion), channel_id=1, source_target_pairs={{0,1},{1,0},{2,3},{3,2},{4,5},{5,4},{6,7},{7,6},{8,9},{9,8},{10,11... | collective-permute-start | bytes 18874376 | tf_op jit(solution)/shard_map/ppermute | solution.py:183
  443.1 68.9 %collective-permute-start.19 = (bf16[384,4096]{1,0:T(8,128)(2,1)}, bf16[384,4096]{1,0:T(8,128)(2,1)}, u32[]{:S(2)}, u32[]{:S(2)}) collective-permute-start(bf16[384,4096]{1,0:T(8,128)(2,1)} %add_convert_fusion.2), channel_id=1, source_target_pairs={{0,2},{1,3},{2,0},{3,1},{4,6},{5,7},{6,4},{7,5},{8,10},{9,11},{10,... | collective-permute-start | bytes 9437192 | tf_op jit(solution)/shard_map/ppermute | solution.py:183
  444.0 68.9 %collective-permute-start.20 = (bf16[384,4096]{1,0:T(8,128)(2,1)}, bf16[384,4096]{1,0:T(8,128)(2,1)}, u32[]{:S(2)}, u32[]{:S(2)}) collective-permute-start(bf16[384,4096]{1,0:T(8,128)(2,1)} %add_convert_fusion.1), channel_id=1, source_target_pairs={{0,4},{1,5},{2,6},{3,7},{4,0},{5,1},{6,2},{7,3},{8,12},{9,13},{10,... | collective-permute-start | bytes 9437192 | tf_op jit(solution)/shard_map/ppermute | solution.py:183
  513.1 17.2 %collective-permute-start.21 = (bf16[32,96,128]{2,1,0:T(8,128)(2,1)S(1)}, bf16[32,96,128]{2,1,0:T(8,128)(2,1)S(1)}, u32[]{:S(2)}, u32[]{:S(2)}) collective-permute-start(bf16[32,96,128]{2,1,0:T(8,128)(2,1)S(1)} %fusion.79), channel_id=1, source_target_pairs={{0,2},{1,3},{2,0},{3,1},{4,6},{5,7},{6,4},{7,5},{8,10},{9,11},{10,... | collective-permute-start | bytes 2359304 | tf_op jit(solution)/shard_map/ppermute | solution.py:903
  532.5 87.8 %collective-permute-start.25 = (bf16[1024,1536]{1,0:T(8,128)(2,1)}, bf16[1024,1536]{1,0:T(8,128)(2,1)}, u32[]{:S(2)}, u32[]{:S(2)}) collective-permute-start(bf16[1024,1536]{1,0:T(8,128)(2,1)} %add_convert_fusion), channel_id=1, source_target_pairs={{0,4},{1,5},{2,6},{3,7},{4,0},{5,1},{6,2},{7,3},{8,12},{9,13},{10,... | collective-permute-start | bytes 9437192 | tf_op jit(solution)/shard_map/ppermute | solution.py:183
  534.8 85.5 %all-to-all-start.4 = ((bf16[32,192,128]{2,1,0:T(8,128)(2,1)}), bf16[32,192,128]{2,1,0:T(8,128)(2,1)}, u32[]{:S(2)}, u32[]{:S(2)}) async-start(bf16[32,192,128]{2,1,0:T(8,128)(2,1)} %pad_maximum_fusion), calls=%async_computation.4 | async-start | bytes 3145728 | tf_op jit(solution)/shard_map/all_to_all | solution.py:900
  554.5 32.1 %collective-permute-start.24 = (bf16[96,4096]{1,0:T(8,128)(2,1)}, bf16[96,4096]{1,0:T(8,128)(2,1)S(1)}, u32[]{:S(2)}, u32[]{:S(2)}) collective-permute-start(bf16[96,4096]{1,0:T(8,128)(2,1)} %fusion.14), channel_id=1, source_target_pairs={{0,24},{1,25},{2,26},{3,27},{4,28},{5,29},{6,30},{7,31},{8,0},{9,1... | collective-permute-start | bytes 2359304 | tf_op jit(solution)/shard_map/ppermute | solution.py:183
  559.7 43.8 %collective-permute-start.23 = (bf16[96,4096]{1,0:T(8,128)(2,1)}, bf16[96,4096]{1,0:T(8,128)(2,1)S(1)}, u32[]{:S(2)}, u32[]{:S(2)}) collective-permute-start(bf16[96,4096]{1,0:T(8,128)(2,1)} %fusion.13), channel_id=1, source_target_pairs={{0,24},{1,25},{2,26},{3,27},{4,28},{5,29},{6,30},{7,31},{8,0},{9,1... | collective-permute-start | bytes 2359304 | tf_op jit(solution)/shard_map/ppermute | solution.py:183
  627.2 17.6 %collective-permute-start.28 = (bf16[1536,768]{1,0:T(8,128)(2,1)S(1)}, bf16[1536,768]{1,0:T(8,128)(2,1)S(1)}, u32[]{:S(2)}, u32[]{:S(2)}) collective-permute-start(bf16[1536,768]{1,0:T(8,128)(2,1)S(1)} %convolution_convert_fusion.4), channel_id=1, source_target_pairs={{0,1},{1,0},{2,3},{3,2},{4,5},{5,4},{6,7},{7,6},{8,9},{9,8},{10,11... | collective-permute-start | bytes 7077896 | tf_op jit(solution)/shard_map/ppermute | solution.py:183
  629.0 20.1 %collective-permute-start.26 = (bf16[768,1536]{1,0:T(8,128)(2,1)S(1)}, bf16[768,1536]{1,0:T(8,128)(2,1)S(1)}, u32[]{:S(2)}, u32[]{:S(2)}) collective-permute-start(bf16[768,1536]{1,0:T(8,128)(2,1)S(1)} %convolution_convert_fusion.5), channel_id=1, source_target_pairs={{0,1},{1,0},{2,3},{3,2},{4,5},{5,4},{6,7},{7,6},{8,9},{9,8},{10,11... | collective-permute-start | bytes 7077896 | tf_op jit(solution)/shard_map/ppermute | solution.py:183
  630.2 42.0 %collective-permute-start.30 = (bf16[768,1536]{1,0:T(8,128)(2,1)S(1)}, bf16[768,1536]{1,0:T(8,128)(2,1)S(1)}, u32[]{:S(2)}, u32[]{:S(2)}) collective-permute-start(bf16[768,1536]{1,0:T(8,128)(2,1)S(1)} %convolution_convert_fusion.3), channel_id=1, source_target_pairs={{0,1},{1,0},{2,3},{3,2},{4,5},{5,4},{6,7},{7,6},{8,9},{9,8},{10,11... | collective-permute-start | bytes 7077896 | tf_op jit(solution)/shard_map/ppermute | solution.py:183
  630.5 23.4 %collective-permute-start.34 = (bf16[96,4096]{1,0:T(8,128)(2,1)S(1)}, bf16[96,4096]{1,0:T(8,128)(2,1)S(1)}, u32[]{:S(2)}, u32[]{:S(2)}) collective-permute-start(bf16[96,4096]{1,0:T(8,128)(2,1)S(1)} %copy-done.38), channel_id=1, source_target_pairs={{0,24},{1,25},{2,26},{3,27},{4,28},{5,29},{6,30},{7,31},{8,0},{9,1... | collective-permute-start | bytes 2359304 | tf_op jit(solution)/shard_map/ppermute | solution.py:183
  634.7 33.5 %collective-permute-start.32 = (bf16[96,4096]{1,0:T(8,128)(2,1)S(1)}, bf16[96,4096]{1,0:T(8,128)(2,1)S(1)}, u32[]{:S(2)}, u32[]{:S(2)}) collective-permute-start(bf16[96,4096]{1,0:T(8,128)(2,1)S(1)} %copy-done.37), channel_id=1, source_target_pairs={{0,24},{1,25},{2,26},{3,27},{4,28},{5,29},{6,30},{7,31},{8,0},{9,1... | collective-permute-start | bytes 2359304 | tf_op jit(solution)/shard_map/ppermute | solution.py:183
  648.4 27.4 %collective-permute-start.29 = (bf16[768,768]{1,0:T(8,128)(2,1)}, bf16[768,768]{1,0:T(8,128)(2,1)S(1)}, u32[]{:S(2)}, u32[]{:S(2)}) collective-permute-start(bf16[768,768]{1,0:T(8,128)(2,1)} %add_convert_fusion.3), channel_id=1, source_target_pairs={{0,4},{1,5},{2,6},{3,7},{4,0},{5,1},{6,2},{7,3},{8,12},{9,13},{10,... | collective-permute-start | bytes 3538952 | tf_op jit(solution)/shard_map/ppermute | solution.py:183
  649.7 26.5 %collective-permute-start.27 = (bf16[384,1536]{1,0:T(8,128)(2,1)S(1)}, bf16[384,1536]{1,0:T(8,128)(2,1)S(1)}, u32[]{:S(2)}, u32[]{:S(2)}) collective-permute-start(bf16[384,1536]{1,0:T(8,128)(2,1)S(1)} %add_convert_fusion.4), channel_id=1, source_target_pairs={{0,2},{1,3},{2,0},{3,1},{4,6},{5,7},{6,4},{7,5},{8,10},{9,11},{10,... | collective-permute-start | bytes 3538952 | tf_op jit(solution)/shard_map/ppermute | solution.py:183
  653.9 56.0 %collective-permute-start.36 = (bf16[512,1536]{1,0:T(8,128)(2,1)}, bf16[512,1536]{1,0:T(8,128)(2,1)S(1)}, u32[]{:S(2)}, u32[]{:S(2)}) collective-permute-start(bf16[512,1536]{1,0:T(8,128)(2,1)} %fusion.35), channel_id=1, source_target_pairs={{0,2},{1,3},{2,0},{3,1},{4,6},{5,7},{6,4},{7,5},{8,10},{9,11},{10,... | collective-permute-start | bytes 4718600 | tf_op jit(solution)/shard_map/ppermute | solution.py:183
  668.2 19.7 %collective-permute-start.35 = (bf16[96,4096]{1,0:T(8,128)(2,1)S(1)}, bf16[96,4096]{1,0:T(8,128)(2,1)S(1)}, u32[]{:S(2)}, u32[]{:S(2)}) collective-permute-start(bf16[96,4096]{1,0:T(8,128)(2,1)S(1)} %fusion.18), channel_id=1, source_target_pairs={{0,24},{1,25},{2,26},{3,27},{4,28},{5,29},{6,30},{7,31},{8,0},{9,1... | collective-permute-start | bytes 2359304 | tf_op jit(solution)/shard_map/ppermute | solution.py:183
  672.7 32.0 %collective-permute-start.31 = (bf16[384,1536]{1,0:T(8,128)(2,1)S(1)}, bf16[384,1536]{1,0:T(8,128)(2,1)S(1)}, u32[]{:S(2)}, u32[]{:S(2)}) collective-permute-start(bf16[384,1536]{1,0:T(8,128)(2,1)S(1)} %fusion.36), channel_id=1, source_target_pairs={{0,4},{1,5},{2,6},{3,7},{4,0},{5,1},{6,2},{7,3},{8,12},{9,13},{10,... | collective-permute-start | bytes 3538952 | tf_op jit(solution)/shard_map/ppermute | solution.py:183
  675.8 29.0 %collective-permute-start.33 = (bf16[96,4096]{1,0:T(8,128)(2,1)S(1)}, bf16[96,4096]{1,0:T(8,128)(2,1)S(1)}, u32[]{:S(2)}, u32[]{:S(2)}) collective-permute-start(bf16[96,4096]{1,0:T(8,128)(2,1)S(1)} %fusion.17), channel_id=1, source_target_pairs={{0,24},{1,25},{2,26},{3,27},{4,28},{5,29},{6,30},{7,31},{8,0},{9,1... | collective-permute-start | bytes 2359304 | tf_op jit(solution)/shard_map/ppermute | solution.py:183
  680.8 24.0 %collective-permute-start.37 = (f32[24,128]{1,0:T(8,128)S(1)}, f32[24,128]{1,0:T(8,128)S(1)}, u32[]{:S(2)}, u32[]{:S(2)}) collective-permute-start(f32[24,128]{1,0:T(8,128)S(1)} %pad_maximum_fusion.6), channel_id=1, source_target_pairs={{0,1},{1,0},{2,3},{3,2},{4,5},{5,4},{6,7},{7,6},{8,9},{9,8},{10,11... | collective-permute-start | bytes 36872 | tf_op jit(solution)/shard_map/ppermute | solution.py:183
  711.3 9.4 %collective-permute-start.60 = (bf16[128,1536]{1,0:T(8,128)(2,1)S(1)}, bf16[128,1536]{1,0:T(8,128)(2,1)S(1)}, u32[]{:S(2)}, u32[]{:S(2)}) collective-permute-start(bf16[128,1536]{1,0:T(8,128)(2,1)S(1)} %add_convert_fusion.8), channel_id=1, source_target_pairs={{0,24},{1,25},{2,26},{3,27},{4,28},{5,29},{6,30},{7,31},{8,0},{9,1... | collective-permute-start | bytes 1179656 | tf_op jit(solution)/shard_map/ppermute | solution.py:183
  713.3 10.2 %collective-permute-start.59 = (bf16[48,4096]{1,0:T(8,128)(2,1)S(1)}, bf16[48,4096]{1,0:T(8,128)(2,1)S(1)}, u32[]{:S(2)}, u32[]{:S(2)}) collective-permute-start(bf16[48,4096]{1,0:T(8,128)(2,1)S(1)} %fusion.32), channel_id=1, source_target_pairs={{0,2},{1,3},{2,0},{3,1},{4,6},{5,7},{6,4},{7,5},{8,10},{9,11},{10,... | collective-permute-start | bytes 1179656 | tf_op jit(solution)/shard_map/ppermute | solution.py:183
  715.2 12.2 %collective-permute-start.58 = (bf16[48,4096]{1,0:T(8,128)(2,1)S(1)}, bf16[48,4096]{1,0:T(8,128)(2,1)S(1)}, u32[]{:S(2)}, u32[]{:S(2)}) collective-permute-start(bf16[48,4096]{1,0:T(8,128)(2,1)S(1)} %fusion.30), channel_id=1, source_target_pairs={{0,4},{1,5},{2,6},{3,7},{4,0},{5,1},{6,2},{7,3},{8,12},{9,13},{10,... | collective-permute-start | bytes 1179656 | tf_op jit(solution)/shard_map/ppermute | solution.py:183
  715.9 15.5 %collective-permute-start.41 = (f32[24,128]{1,0:T(8,128)S(1)}, f32[24,128]{1,0:T(8,128)S(1)}, u32[]{:S(2)}, u32[]{:S(2)}) collective-permute-start(f32[24,128]{1,0:T(8,128)S(1)} %fusion.198), channel_id=1, source_target_pairs={{0,2},{1,3},{2,0},{3,1},{4,6},{5,7},{6,4},{7,5},{8,10},{9,11},{10,... | collective-permute-start | bytes 36872 | tf_op jit(solution)/shard_map/ppermute | solution.py:183
  717.7 17.0 %collective-permute-start.40 = (bf16[192,1536]{1,0:T(8,128)(2,1)S(1)}, bf16[192,1536]{1,0:T(8,128)(2,1)S(1)}, u32[]{:S(2)}, u32[]{:S(2)}) collective-permute-start(bf16[192,1536]{1,0:T(8,128)(2,1)S(1)} %fusion.40), channel_id=1, source_target_pairs={{0,2},{1,3},{2,0},{3,1},{4,6},{5,7},{6,4},{7,5},{8,10},{9,11},{10,... | collective-permute-start | bytes 1769480 | tf_op jit(solution)/shard_map/ppermute | solution.py:183
  720.8 10.6 %collective-permute-start.39 = (bf16[192,768]{1,0:T(8,128)(2,1)S(1)}, bf16[192,768]{1,0:T(8,128)(2,1)S(1)}, u32[]{:S(2)}, u32[]{:S(2)}) collective-permute-start(bf16[192,768]{1,0:T(8,128)(2,1)S(1)} %add_convert_fusion.13), channel_id=1, source_target_pairs={{0,24},{1,25},{2,26},{3,27},{4,28},{5,29},{6,30},{7,31},{8,0},{9,1... | collective-permute-start | bytes 884744 | tf_op jit(solution)/shard_map/ppermute | solution.py:183
  727.4 14.0 %collective-permute-start.61 = (bf16[128,1536]{1,0:T(8,128)(2,1)S(1)}, bf16[128,1536]{1,0:T(8,128)(2,1)S(1)}, u32[]{:S(2)}, u32[]{:S(2)}) collective-permute-start(bf16[128,1536]{1,0:T(8,128)(2,1)S(1)} %add_convert_fusion.7), channel_id=1, source_target_pairs={{0,24},{1,25},{2,26},{3,27},{4,28},{5,29},{6,30},{7,31},{8,0},{9,1... | collective-permute-start | bytes 1179656 | tf_op jit(solution)/shard_map/ppermute | solution.py:183
  734.7 11.5 %collective-permute-start.45 = (f32[24,128]{1,0:T(8,128)S(1)}, f32[24,128]{1,0:T(8,128)S(1)}, u32[]{:S(2)}, u32[]{:S(2)}) collective-permute-start(f32[24,128]{1,0:T(8,128)S(1)} %add.2651), channel_id=1, source_target_pairs={{0,4},{1,5},{2,6},{3,7},{4,0},{5,1},{6,2},{7,3},{8,12},{9,13},{10,... | collective-permute-start | bytes 36872 | tf_op jit(solution)/shard_map/ppermute | solution.py:183
  735.5 10.8 %collective-permute-start.44 = (bf16[48,1536]{1,0:T(8,128)(2,1)S(1)}, bf16[48,1536]{1,0:T(8,128)(2,1)S(1)}, u32[]{:S(2)}, u32[]{:S(2)}) collective-permute-start(bf16[48,1536]{1,0:T(8,128)(2,1)S(1)} %fusion.61), channel_id=1, source_target_pairs={{0,24},{1,25},{2,26},{3,27},{4,28},{5,29},{6,30},{7,31},{8,0},{9,1... | collective-permute-start | bytes 442376 | tf_op jit(solution)/shard_map/ppermute | solution.py:183
  738.7 11.6 %collective-permute-start.43 = (bf16[192,768]{1,0:T(8,128)(2,1)S(1)}, bf16[192,768]{1,0:T(8,128)(2,1)S(1)}, u32[]{:S(2)}, u32[]{:S(2)}) collective-permute-start(bf16[192,768]{1,0:T(8,128)(2,1)S(1)} %add_convert_fusion.11), channel_id=1, source_target_pairs={{0,24},{1,25},{2,26},{3,27},{4,28},{5,29},{6,30},{7,31},{8,0},{9,1... | collective-permute-start | bytes 884744 | tf_op jit(solution)/shard_map/ppermute | solution.py:183
  741.1 15.6 %collective-permute-start.42 = (bf16[96,1536]{1,0:T(8,128)(2,1)S(1)}, bf16[96,1536]{1,0:T(8,128)(2,1)S(1)}, u32[]{:S(2)}, u32[]{:S(2)}) collective-permute-start(bf16[96,1536]{1,0:T(8,128)(2,1)S(1)} %add_convert_fusion.12), channel_id=1, source_target_pairs={{0,24},{1,25},{2,26},{3,27},{4,28},{5,29},{6,30},{7,31},{8,0},{9,1... | collective-permute-start | bytes 884744 | tf_op jit(solution)/shard_map/ppermute | solution.py:183
  742.7 25.1 %collective-permute-start.62 = (bf16[128,1536]{1,0:T(8,128)(2,1)S(1)}, bf16[128,1536]{1,0:T(8,128)(2,1)S(1)}, u32[]{:S(2)}, u32[]{:S(2)}) collective-permute-start(bf16[128,1536]{1,0:T(8,128)(2,1)S(1)} %add_convert_fusion.6), channel_id=1, source_target_pairs={{0,24},{1,25},{2,26},{3,27},{4,28},{5,29},{6,30},{7,31},{8,0},{9,1... | collective-permute-start | bytes 1179656 | tf_op jit(solution)/shard_map/ppermute | solution.py:183
  756.7 19.2 %collective-permute-start.49 = (f32[24,128]{1,0:T(8,128)S(1)}, f32[24,128]{1,0:T(8,128)S(1)}, u32[]{:S(2)}, u32[]{:S(2)}) collective-permute-start(f32[24,128]{1,0:T(8,128)S(1)} %add.2661), channel_id=1, source_target_pairs={{0,16},{1,17},{2,18},{3,19},{4,20},{5,21},{6,22},{7,23},{8,24},{9,... | collective-permute-start | bytes 36872 | tf_op jit(solution)/shard_map/ppermute | solution.py:183
  759.6 16.2 %collective-permute-start.48 = (bf16[48,1536]{1,0:T(8,128)(2,1)}, bf16[48,1536]{1,0:T(8,128)(2,1)}, u32[]{:S(2)}, u32[]{:S(2)}) collective-permute-start(bf16[48,1536]{1,0:T(8,128)(2,1)} %fusion.60), channel_id=1, source_target_pairs={{0,24},{1,25},{2,26},{3,27},{4,28},{5,29},{6,30},{7,31},{8,0},{9,1... | collective-permute-start | bytes 442376 | tf_op jit(solution)/shard_map/ppermute | solution.py:183
  763.5 12.4 %collective-permute-start.47 = (bf16[192,768]{1,0:T(8,128)(2,1)}, bf16[192,768]{1,0:T(8,128)(2,1)}, u32[]{:S(2)}, u32[]{:S(2)}) collective-permute-start(bf16[192,768]{1,0:T(8,128)(2,1)} %add_convert_fusion.9), channel_id=1, source_target_pairs={{0,24},{1,25},{2,26},{3,27},{4,28},{5,29},{6,30},{7,31},{8,0},{9,1... | collective-permute-start | bytes 884744 | tf_op jit(solution)/shard_map/ppermute | solution.py:183
  765.3 16.0 %collective-permute-start.46 = (bf16[96,1536]{1,0:T(8,128)(2,1)}, bf16[96,1536]{1,0:T(8,128)(2,1)}, u32[]{:S(2)}, u32[]{:S(2)}) collective-permute-start(bf16[96,1536]{1,0:T(8,128)(2,1)} %add_convert_fusion.10), channel_id=1, source_target_pairs={{0,24},{1,25},{2,26},{3,27},{4,28},{5,29},{6,30},{7,31},{8,0},{9,1... | collective-permute-start | bytes 884744 | tf_op jit(solution)/shard_map/ppermute | solution.py:183
  773.9 42.9 %collective-permute-start.63 = (bf16[196608]{0:T(1024)(128)(2,1)}, bf16[196608]{0:T(1024)(128)(2,1)}, u32[]{:S(2)}, u32[]{:S(2)}) collective-permute-start(bf16[196608]{0:T(1024)(128)(2,1)} %get-tuple-element.316), channel_id=1, source_target_pairs={{2,0},{5,1},{8,2},{11,3},{14,4},{17,5},{20,6},{23,7},{26,8},{29,9}... | collective-permute-start | bytes 1179656 | tf_op jit(solution)/shard_map/ppermute | solution.py:140
  781.3 36.2 %collective-permute-start.50 = (f32[24,128]{1,0:T(8,128)S(1)}, f32[24,128]{1,0:T(8,128)S(1)}, u32[]{:S(2)}, u32[]{:S(2)}) collective-permute-start(f32[24,128]{1,0:T(8,128)S(1)} %add.2672), channel_id=1, source_target_pairs={{0,8},{1,9},{2,10},{3,11},{4,12},{5,13},{6,14},{7,15},{8,16},{9,17... | collective-permute-start | bytes 36872 | tf_op jit(solution)/shard_map/ppermute | solution.py:183
  784.0 14.6 %collective-permute-start.53 = (bf16[48,1536]{1,0:T(8,128)(2,1)S(1)}, bf16[48,1536]{1,0:T(8,128)(2,1)S(1)}, u32[]{:S(2)}, u32[]{:S(2)}) collective-permute-start(bf16[48,1536]{1,0:T(8,128)(2,1)S(1)} %fusion.58), channel_id=1, source_target_pairs={{0,24},{1,25},{2,26},{3,27},{4,28},{5,29},{6,30},{7,31},{8,0},{9,1... | collective-permute-start | bytes 442376 | tf_op jit(solution)/shard_map/ppermute | solution.py:183
  805.9 16.8 %collective-permute-start.56 = (bf16[73728]{0:T(1024)(128)(2,1)S(1)}, bf16[73728]{0:T(1024)(128)(2,1)S(1)}, u32[]{:S(2)}, u32[]{:S(2)}) collective-permute-start(bf16[73728]{0:T(1024)(128)(2,1)S(1)} %get-tuple-element.323), channel_id=1, source_target_pairs={{0,0},{3,1},{6,2},{9,3},{12,4},{15,5},{18,6},{21,7},{24,8},{27,9},... | collective-permute-start | bytes 442376 | tf_op jit(solution)/shard_map/ppermute | solution.py:140
  810.1 27.6 %collective-permute-start.65 = (bf16[196608]{0:T(1024)(128)(2,1)}, bf16[196608]{0:T(1024)(128)(2,1)S(1)}, u32[]{:S(2)}, u32[]{:S(2)}) collective-permute-start(bf16[196608]{0:T(1024)(128)(2,1)} %get-tuple-element.315), channel_id=1, source_target_pairs={{0,0},{3,1},{6,2},{9,3},{12,4},{15,5},{18,6},{21,7},{24,8},{27,9},... | collective-permute-start | bytes 1179656 | tf_op jit(solution)/shard_map/ppermute | solution.py:140
  812.1 25.7 %collective-permute-start.66 = (bf16[196608]{0:T(1024)(128)(2,1)}, bf16[196608]{0:T(1024)(128)(2,1)S(1)}, u32[]{:S(2)}, u32[]{:S(2)}) collective-permute-start(bf16[196608]{0:T(1024)(128)(2,1)} %get-tuple-element.314), channel_id=1, source_target_pairs={{1,0},{4,1},{7,2},{10,3},{13,4},{16,5},{19,6},{22,7},{25,8},{28,9}... | collective-permute-start | bytes 1179656 | tf_op jit(solution)/shard_map/ppermute | solution.py:140
  816.8 19.0 %collective-permute-start.57 = (bf16[73728]{0:T(1024)(128)(2,1)}, bf16[73728]{0:T(1024)(128)(2,1)}, u32[]{:S(2)}, u32[]{:S(2)}) collective-permute-start(bf16[73728]{0:T(1024)(128)(2,1)} %get-tuple-element.322), channel_id=1, source_target_pairs={{1,0},{4,1},{7,2},{10,3},{13,4},{16,5},{19,6},{22,7},{25,8},{28,9}... | collective-permute-start | bytes 442376 | tf_op jit(solution)/shard_map/ppermute | solution.py:140
  817.5 20.4 %collective-permute-start.55 = (bf16[1536]{0:T(1024)(128)(2,1)S(1)}, bf16[1536]{0:T(1024)(128)(2,1)S(1)}, u32[]{:S(2)}, u32[]{:S(2)}) collective-permute-start(bf16[1536]{0:T(1024)(128)(2,1)S(1)} %slice.873), channel_id=1, source_target_pairs={{0,1},{1,2},{2,3},{3,4},{4,5},{5,6},{6,7},{7,8},{8,9},{9,10},{10,1... | collective-permute-start | bytes 9224 | tf_op jit(solution)/shard_map/ppermute | solution.py:142
  822.7 15.2 %collective-permute-start.64 = (bf16[1536]{0:T(1024)(128)(2,1)S(1)}, bf16[1536]{0:T(1024)(128)(2,1)S(1)}, u32[]{:S(2)}, u32[]{:S(2)}) collective-permute-start(bf16[1536]{0:T(1024)(128)(2,1)S(1)} %slice.883), channel_id=1, source_target_pairs={{0,1},{1,2},{2,3},{3,4},{4,5},{5,6},{6,7},{7,8},{8,9},{9,10},{10,1... | collective-permute-start | bytes 9224 | tf_op jit(solution)/shard_map/ppermute | solution.py:142
  (75 other events, 994.3 us)
Sparse Core Ops, SparseCore 0:
  81.6 265.5 all-gather.1
